TPU v7x, 512 devices: a whole 4x8x8 slice. The times are simulated.
512 devices in a mesh: space: 32 (over y, z_hi), filt: 16 (over z_lo, x, core).
Axes of the slice: x: 4, y: 8, z: 8 (z_hi: 4, z_lo: 2; z = z_hi * 2 + z_lo), core: 2. Of those that a mesh axis runs over, the one named last changes fastest.
Arguments:
- activations: bfloat16 [64, 32, 128, 128], P('space', None, 'filt'), may hold values from -6 to 6
- weight: bfloat16 [3, 3, 3, 128, 128], P(None, None, None, None, 'filt'), may hold values from -0.109375 to 0.109375
- grad_out: bfloat16 [64, 32, 128, 128], P('space', None, 'filt'), may hold values from -6 to 6
Outputs:
- output: float32 [64, 32, 128, 128], P('space', None, 'filt')
- grad_in: float32 [64, 32, 128, 128], P('space', None, 'filt')
- weight_grad: float32 [3, 3, 3, 128, 128], P(None, None, None, None, 'filt')
All inputs are finite; a program needn't handle non-finite values.
Results may differ from a plain program's by a relative error of at most 0.0003.
Values may be sent and summed in bfloat16 or wider, within the bound.
No kernel may reach another device: no remote copies, remote signals or barrier semaphores. Data moves between devices by JAX's collectives and lax.ppermute only.
A program may use at most 64 MiB of HBM per device.

v0:
```python
import jax
import jax.numpy as jnp
from jax import lax
from jax.sharding import PartitionSpec as P


def padded_2(array, sides, width):
    for axis, dim in sides:
        devices, length = (lax.axis_size(axis), array.shape[dim])
        up = [(i, (i + 1) % devices) for i in range(devices - 1)]
        down = [(j, i) for i, j in up]
        last = lax.slice_in_dim(array, length - width, length, axis=dim)
        initial = lax.slice_in_dim(array, 0, width, axis=dim)
        before = lax.ppermute(last, axis, up)
        after = lax.ppermute(initial, axis, down)
        array = jnp.concatenate([before, array, after], axis=dim)
    return array


def correlate(padded, kernel):
    depth_len = padded.shape[0] - 2
    row_len = padded.shape[1] - 2
    col_len = padded.shape[2] - 2
    width_in = kernel.shape[3]
    width_out = kernel.shape[4]
    summed = jnp.zeros((depth_len, row_len, col_len, width_out), jnp.float32)
    for shift_a in range(3):
        flat_kernel = kernel[shift_a].transpose(2, 0, 1, 3).reshape(width_in, 9 * width_out)
        product = jnp.einsum(
            "zhwi,ij->zhwj",
            padded[shift_a : shift_a + depth_len],
            flat_kernel,
            preferred_element_type=jnp.float32,
        )
        product = product.reshape(depth_len, row_len + 2, col_len + 2, 9, width_out)
        for shift_b in range(3):
            for shift_c in range(3):
                summed = (
                    summed
                    + product[
                        :,
                        shift_b : shift_b + row_len,
                        shift_c : shift_c + col_len,
                        3 * shift_b + shift_c,
                    ]
                )
    return summed


def stacked_grads(grads):
    layers = []
    for shift_b in range(3):
        for shift_c in range(3):
            layers.append(
                jnp.pad(grads, ((0, 0), (shift_b, 2 - shift_b), (shift_c, 2 - shift_c), (0, 0)))
            )
    stacked = jnp.stack(layers, axis=3)
    return stacked.reshape(stacked.shape[0], stacked.shape[1], stacked.shape[2], 9 * grads.shape[3])


def filter_grad(padded, stacked):
    depth_len = stacked.shape[0]
    width_in = padded.shape[3]
    width_out = stacked.shape[3] // 9
    planes = [
        jnp.einsum(
            "zhwi,zhwj->ij",
            padded[shift_a : shift_a + depth_len],
            stacked,
            preferred_element_type=jnp.float32,
        )
        for shift_a in range(3)
    ]
    result = jnp.stack(planes, 0).reshape(3, width_in, 3, 3, width_out)
    return result.transpose(0, 2, 3, 1, 4)


def block_pad(values):
    haloed = padded_2(values, (("space", 0), ("filt", 1)), 1)
    return jnp.pad(haloed, ((0, 0), (0, 0), (1, 1), (0, 0)))


def body(activations, weight, grad_out):
    depth_len, row_len, group_width, col_len = activations.shape
    norm_factor = float(depth_len * lax.axis_size("space") * row_len * col_len) ** (-0.5)
    blocks_x, blocks_g = (
        lax.all_to_all(activations, "filt", split_axis=1, concat_axis=2, tiled=True),
        lax.all_to_all(grad_out, "filt", split_axis=1, concat_axis=2, tiled=True),
    )
    blocks_x = blocks_x.transpose(0, 1, 3, 2)
    blocks_g = blocks_g.transpose(0, 1, 3, 2)
    full_weight = lax.all_gather(weight, "filt", axis=4, tiled=True)
    padded_x = block_pad(blocks_x)
    padded_g = block_pad(blocks_g)
    out_block = correlate(padded_x, full_weight).transpose(0, 1, 3, 2)
    flipped = jnp.flip(full_weight, (0, 1, 2)).transpose(0, 1, 2, 4, 3)
    grad_block = correlate(padded_g, flipped).transpose(0, 1, 3, 2)
    partial_grad = filter_grad(padded_x, stacked_grads(blocks_g))
    output, grad_in = (
        lax.all_to_all(out_block, "filt", split_axis=2, concat_axis=1, tiled=True),
        lax.all_to_all(grad_block, "filt", split_axis=2, concat_axis=1, tiled=True),
    )
    shared = lax.psum_scatter(partial_grad, "filt", scatter_dimension=4, tiled=True)
    weight_grad = lax.psum(shared, "space") * norm_factor
    return (output, grad_in, weight_grad)


def solution(mesh):
    return jax.shard_map(
        body,
        mesh=mesh,
        in_specs=(
            P("space", None, "filt", None),
            P(None, None, None, None, "filt"),
            P("space", None, "filt", None),
        ),
        out_specs=(
            P("space", None, "filt", None),
            P("space", None, "filt", None),
            P(None, None, None, None, "filt"),
        ),
        check_vma=False,
    )
```

profile of v0, /device:TPU:6, one launch (start us, length us, event | category | flops | bytes accessed | tf_op | source)
XLA Modules:
  0.0 573.2 jit_solution(8670351523516555453)
XLA Ops:
  7.2 1.6 copy.125
  8.7 9.2 %all-to-all-start.2 = ((bf16[2,32,8,128]{3,2,0,1:T(8,128)(2,1)}), bf16[2,32,8,128]{3,2,0,1:T(8,128)(2,1)S(1)}, u32[]{:S(2)}, u32[]{:S(2)}) async-start(bf16[2,32,8,128]{3,2,0,1:T(8,128)(2,1)} %copy.125), calls=%async_computation.2 | async-start | bytes 262144 | tf_op jit(solution)/shard_map/all_to_all | solution.py:88
  17.9 17.9 %all_gather.3 = bf16[3,3,3,128,128]{3,4,2,1,0:T(8,128)(2,1)S(1)} all-gather(bf16[3,3,3,128,8]{3,4,2,1,0:T(8,128)(2,1)} %param.4), channel_id=1, replica_groups=mesh['space'=32,'filt'=16] {'filt'}, dimensions={4}, use_global_device_ids=true | all-gather | bytes 940032 | tf_op jit(solution)/shard_map/all_gather | solution.py:92
  35.8 1.6 copy.108
  40.3 1.0 fusion.48
  41.3 8.2 %all-to-all-start = ((bf16[2,32,8,128]{3,2,0,1:T(8,128)(2,1)}), bf16[2,32,8,128]{3,2,0,1:T(8,128)(2,1)S(1)}, u32[]{:S(2)}, u32[]{:S(2)}) async-start(bf16[2,32,8,128]{3,2,0,1:T(8,128)(2,1)} %copy.108), calls=%async_computation | async-start | bytes 262144 | tf_op jit(solution)/shard_map/all_to_all | solution.py:87
  50.3 3.8 all-to-all-done
  54.9 1.3 collective-permute-start.1
  56.2 6.1 %collective-permute-start = (bf16[1,2,128,128]{3,2,1,0:T(8,128)(2,1)}, bf16[1,2,128,128]{3,2,1,0:T(8,128)(2,1)}, u32[]{:S(2)}, u32[]{:S(2)}) collective-permute-start(bf16[1,2,128,128]{3,2,1,0:T(8,128)(2,1)} %get-tuple-element.30), channel_id=1, source_target_pairs={{0,16},{16,32},{32,48},{48,64},{64,80},{80,96},{96,112},{112,128},... | collective-permute-start | bytes 196616 | tf_op jit(solution)/shard_map/ppermute | solution.py:14
  62.3 1.3 collective-permute-start.5
  63.6 6.1 %collective-permute-start.4 = (bf16[1,2,128,128]{3,2,1,0:T(8,128)(2,1)}, bf16[1,2,128,128]{3,2,1,0:T(8,128)(2,1)}, u32[]{:S(2)}, u32[]{:S(2)}) collective-permute-start(bf16[1,2,128,128]{3,2,1,0:T(8,128)(2,1)} %get-tuple-element.28), channel_id=1, source_target_pairs={{0,16},{16,32},{32,48},{48,64},{64,80},{80,96},{96,112},{112,128},... | collective-permute-start | bytes 196616 | tf_op jit(solution)/shard_map/ppermute | solution.py:14
  70.2 3.8 copy.145
  74.0 4.9 reshape.75
  78.9 4.5 reshape.119
  84.4 1.9 collective-permute-start.3
  86.3 2.4 collective-permute-start.2
  90.4 3.1 collective-permute-start.7
  93.5 3.3 collective-permute-start.6
  96.8 1.0 select_maximum_fusion.4
  97.8 1.0 slice_bitcast_fusion.31
  101.7 1.3 fusion.34
  103.0 1.8 copy.122
  104.8 8.0 %all-to-all-start.1 = ((f32[2,2,128,128]{3,1,0,2:T(2,128)}), f32[2,2,128,128]{3,1,0,2:T(2,128)}, u32[]{:S(2)}, u32[]{:S(2)}) async-start(f32[2,2,128,128]{3,1,0,2:T(2,128)} %copy.122), calls=%async_computation.1 | async-start | bytes 524288 | tf_op jit(solution)/shard_map/all_to_all | solution.py:100
  113.0 1.6 convolution_bitcast_fusion
  116.3 2.6 copy.153
  118.9 1.2 select_maximum_fusion
  124.5 5.7 all-to-all-start.3
  130.2 1.3 dynamic-slice
  132.1 123.0 %all-reduce.17.cloned.1.call-done = f32[3,3,3,128,128]{3,2,1,0,4:T(4,128)} async-done(((f32[3,3,3,128,128]{3,2,1,0,4:T(4,128)}), f32[3,3,3,128,128]{3,2,1,0,4:T(4,128)}) %all-reduce.17.cloned.1.call-update) | async-done | bytes 1769488
  255.1 1.6 constant_dynamic-slice_fusion
  256.7 1.0 copy.202
  259.2 305.6 %all-reduce.15.cloned.1.call-done = f32[3,3,3,128,8]{3,2,1,0,4:T(4,128)} async-done(((f32[3,3,3,128,8]{3,2,1,0,4:T(4,128)}), f32[3,3,3,128,8]{3,2,1,0,4:T(4,128)}) %all-reduce.15.cloned.1.call-update) | async-done | bytes 110608 | tf_op jit(solution)/shard_map/psum | solution.py:104
  (71 shorter events, 19.8 us)
Async XLA Ops:
  8.7 32.5 %all-to-all-start.2 = ((bf16[2,32,8,128]{3,2,0,1:T(8,128)(2,1)}), bf16[2,32,8,128]{3,2,0,1:T(8,128)(2,1)S(1)}, u32[]{:S(2)}, u32[]{:S(2)}) async-start(bf16[2,32,8,128]{3,2,0,1:T(8,128)(2,1)} %copy.125), calls=%async_computation.2 | async-start | bytes 262144 | tf_op jit(solution)/shard_map/all_to_all | solution.py:88
  41.3 12.8 %all-to-all-start = ((bf16[2,32,8,128]{3,2,0,1:T(8,128)(2,1)}), bf16[2,32,8,128]{3,2,0,1:T(8,128)(2,1)S(1)}, u32[]{:S(2)}, u32[]{:S(2)}) async-start(bf16[2,32,8,128]{3,2,0,1:T(8,128)(2,1)} %copy.108), calls=%async_computation | async-start | bytes 262144 | tf_op jit(solution)/shard_map/all_to_all | solution.py:87
  54.9 28.5 %collective-permute-start.1 = (bf16[1,2,128,128]{3,2,1,0:T(8,128)(2,1)}, bf16[1,2,128,128]{3,2,1,0:T(8,128)(2,1)}, u32[]{:S(2)}, u32[]{:S(2)}) collective-permute-start(bf16[1,2,128,128]{3,2,1,0:T(8,128)(2,1)} %get-tuple-element.31), channel_id=1, source_target_pairs={{16,0},{32,16},{48,32},{64,48},{80,64},{96,80},{112,96},{128,112},... | collective-permute-start | bytes 196616 | tf_op jit(solution)/shard_map/ppermute | solution.py:15
  56.2 27.2 %collective-permute-start = (bf16[1,2,128,128]{3,2,1,0:T(8,128)(2,1)}, bf16[1,2,128,128]{3,2,1,0:T(8,128)(2,1)}, u32[]{:S(2)}, u32[]{:S(2)}) collective-permute-start(bf16[1,2,128,128]{3,2,1,0:T(8,128)(2,1)} %get-tuple-element.30), channel_id=1, source_target_pairs={{0,16},{16,32},{32,48},{48,64},{64,80},{80,96},{96,112},{112,128},... | collective-permute-start | bytes 196616 | tf_op jit(solution)/shard_map/ppermute | solution.py:14
  62.3 26.4 %collective-permute-start.5 = (bf16[1,2,128,128]{3,2,1,0:T(8,128)(2,1)}, bf16[1,2,128,128]{3,2,1,0:T(8,128)(2,1)S(1)}, u32[]{:S(2)}, u32[]{:S(2)}) collective-permute-start(bf16[1,2,128,128]{3,2,1,0:T(8,128)(2,1)} %get-tuple-element.29), channel_id=1, source_target_pairs={{16,0},{32,16},{48,32},{64,48},{80,64},{96,80},{112,96},{128,112},... | collective-permute-start | bytes 196616 | tf_op jit(solution)/shard_map/ppermute | solution.py:15
  63.6 25.2 %collective-permute-start.4 = (bf16[1,2,128,128]{3,2,1,0:T(8,128)(2,1)}, bf16[1,2,128,128]{3,2,1,0:T(8,128)(2,1)}, u32[]{:S(2)}, u32[]{:S(2)}) collective-permute-start(bf16[1,2,128,128]{3,2,1,0:T(8,128)(2,1)} %get-tuple-element.28), channel_id=1, source_target_pairs={{0,16},{16,32},{32,48},{48,64},{64,80},{80,96},{96,112},{112,128},... | collective-permute-start | bytes 196616 | tf_op jit(solution)/shard_map/ppermute | solution.py:14
  83.4 15.5 %copy-start = (bf16[1,3,3,128,128]{3,4,2,1,0:T(8,128)(2,1)S(1)}, bf16[1,3,3,128,128]{3,4,2,1,0:T(8,128)(2,1)}, u32[]{:S(2)}) copy-start(bf16[1,3,3,128,128]{3,4,2,1,0:T(8,128)(2,1)} %get-tuple-element.19) | copy-start | bytes 884740
  84.4 12.4 %collective-permute-start.3 = (bf16[4,1,128,128]{3,2,1,0:T(8,128)(2,1)S(1)}, bf16[4,1,128,128]{3,2,1,0:T(8,128)(2,1)S(1)}, u32[]{:S(2)}, u32[]{:S(2)}) collective-permute-start(bf16[4,1,128,128]{3,2,1,0:T(8,128)(2,1)S(1)} %get-tuple-element.27), channel_id=1, source_target_pairs={{1,0},{2,1},{3,2},{4,3},{5,4},{6,5},{7,6},{8,7},{9,8},{10,9},{11,1... | collective-permute-start | bytes 393224 | tf_op jit(solution)/shard_map/ppermute | solution.py:15
  86.3 10.5 %collective-permute-start.2 = (bf16[4,1,128,128]{3,2,1,0:T(8,128)(2,1)S(1)}, bf16[4,1,128,128]{3,2,1,0:T(8,128)(2,1)S(1)}, u32[]{:S(2)}, u32[]{:S(2)}) collective-permute-start(bf16[4,1,128,128]{3,2,1,0:T(8,128)(2,1)S(1)} %get-tuple-element.26), channel_id=1, source_target_pairs={{0,1},{1,2},{2,3},{3,4},{4,5},{5,6},{6,7},{7,8},{8,9},{9,10},{10,1... | collective-permute-start | bytes 393224 | tf_op jit(solution)/shard_map/ppermute | solution.py:14
  90.4 28.6 %collective-permute-start.7 = (bf16[4,1,128,128]{3,2,1,0:T(8,128)(2,1)}, bf16[4,1,128,128]{3,2,1,0:T(8,128)(2,1)}, u32[]{:S(2)}, u32[]{:S(2)}) collective-permute-start(bf16[4,1,128,128]{3,2,1,0:T(8,128)(2,1)} %get-tuple-element.25), channel_id=1, source_target_pairs={{1,0},{2,1},{3,2},{4,3},{5,4},{6,5},{7,6},{8,7},{9,8},{10,9},{11,1... | collective-permute-start | bytes 393224 | tf_op jit(solution)/shard_map/ppermute | solution.py:15
  93.5 25.4 %collective-permute-start.6 = (bf16[4,1,128,128]{3,2,1,0:T(8,128)(2,1)}, bf16[4,1,128,128]{3,2,1,0:T(8,128)(2,1)}, u32[]{:S(2)}, u32[]{:S(2)}) collective-permute-start(bf16[4,1,128,128]{3,2,1,0:T(8,128)(2,1)} %get-tuple-element.24), channel_id=1, source_target_pairs={{0,1},{1,2},{2,3},{3,4},{4,5},{5,6},{6,7},{7,8},{8,9},{9,10},{10,1... | collective-permute-start | bytes 393224 | tf_op jit(solution)/shard_map/ppermute | solution.py:14
  98.8 1.0 copy-start.3
  99.8 1.0 copy-start.2
  104.8 19.7 %all-to-all-start.1 = ((f32[2,2,128,128]{3,1,0,2:T(2,128)}), f32[2,2,128,128]{3,1,0,2:T(2,128)}, u32[]{:S(2)}, u32[]{:S(2)}) async-start(f32[2,2,128,128]{3,1,0,2:T(2,128)} %copy.122), calls=%async_computation.1 | async-start | bytes 524288 | tf_op jit(solution)/shard_map/all_to_all | solution.py:100
  112.8 142.3 %all-reduce.17.cloned.1.call-start = ((), (), s32[]{:S(2)}) async-start(), calls=%async_computation.5 | async-start | bytes 4718592
  113.0 1.6 copy-start.7
  114.6 1.0 copy-start.6
  118.9 1.2 copy-start.1
  120.1 1.0 copy-start.4
  121.1 1.0 copy-start.5
  124.5 134.0 %all-to-all-start.3 = ((f32[2,2,128,128]{3,1,0,2:T(2,128)}), f32[2,2,128,128]{3,1,0,2:T(2,128)S(1)}, u32[]{:S(2)}, u32[]{:S(2)}) async-start(f32[2,2,128,128]{3,1,0,2:T(2,128)} %copy.142), calls=%async_computation.3 | async-start | bytes 524288 | tf_op jit(solution)/shard_map/all_to_all | solution.py:101
  130.2 434.6 %all-reduce.15.cloned.1.call-start = ((), (), s32[]{:S(2)}) async-start(), calls=%async_computation.4 | async-start | bytes 294912 | tf_op jit(solution)/shard_map/psum | solution.py:104
Sparse Core Ops, SparseCore 0:
  119.0 136.0 all-reduce.16
  258.0 306.7 all-reduce.14
where the time goes:
time: 575 us; the launch traced here: 573 us
  waiting for transfers between devices  432 us (75%)
  starting transfers between devices  56.8 us (10%)
  local copies, waits for them, and re-layouts  35.8 us (6%)
  blocking collectives  17.9 us (3%)
  between operations  15 us (3%)
  matrix products  8.31 us (1%)
  other arithmetic  7.08 us (1%)
    psum x1, waiting for transfers between devices, body(): weight_grad = lax.psum(shared, 'space') * norm_factor  306 us
    unnamed x3, waiting for transfers between devices  123 us
    all_gather x1, blocking collectives, body(): full_weight = lax.all_gather(weight, 'filt', axis=4, tiled=True)  17.9 us
    ppermute x4, starting transfers between devices, padded_2(): before = lax.ppermute(last, axis, up)  17.8 us
  transfers between devices with their start and end apart: 14, of which 3 were waited for; matrix products, arithmetic and copies ran while one was open for 8% of the time, Pallas kernels for 0%

commit v1 on v0

v1 whole, which is shorter than its diff:
```python
import functools

import jax
import jax.numpy as jnp
from jax import lax
from jax.experimental import pallas as pl
from jax.experimental.pallas import tpu as pltpu
from jax.sharding import Mesh
from jax.sharding import PartitionSpec as P

SPACE = ("y", "zh")
FILT = ("zl", "x", "core")
CHIPS = ("zl", "x")
BF, F32 = jnp.bfloat16, jnp.float32


def vmem_specs(n):
    return [pl.BlockSpec(memory_space=pltpu.VMEM)] * n


def call(kernel, outs, ins, scratch=(), smem=0, flops=0, name=None):
    specs = [pl.BlockSpec(memory_space=pltpu.SMEM)] * smem + vmem_specs(len(ins) - smem)
    moved = sum(a.size * a.dtype.itemsize for a in ins) + sum(o.size * o.dtype.itemsize for o in outs)
    return pl.pallas_call(
        kernel,
        out_shape=tuple(outs),
        in_specs=specs,
        out_specs=tuple(vmem_specs(len(outs))),
        scratch_shapes=list(scratch),
        cost_estimate=pl.CostEstimate(flops=flops, transcendentals=0, bytes_accessed=moved),
        name=name,
    )(*ins)


def pack_kernel(x_ref, g_ref, o_ref):
    n, _, nz, nr = o_ref.shape[:4]
    step = nr - 2
    rows = x_ref.shape[1]
    zero = jnp.zeros(x_ref.shape[2:], x_ref.dtype)
    for k, ref in enumerate((x_ref, g_ref)):
        for z in range(nz):
            for d in range(n):
                for r in range(nr):
                    h = d * step + r - 1
                    o_ref[d, k, z, r] = ref[z, h] if 0 <= h < rows else zero


def shifted(value):
    lane = lax.broadcasted_iota(jnp.int32, value.shape, 1)
    w = value.shape[1]
    left = jnp.where(lane == 0, 0.0, pltpu.roll(value, 1, 1))
    right = jnp.where(lane == w - 1, 0.0, pltpu.roll(value, w - 1, 1))
    return left.astype(BF), value.astype(BF), right.astype(BF)


def block_of(plane_ref, k, r, z=None):
    n = plane_ref.shape[0]
    if z is None:
        parts = [plane_ref[d, k, r].astype(F32) for d in range(n)]
    else:
        parts = [plane_ref[d, k, z, r].astype(F32) for d in range(n)]
    return jnp.concatenate(parts, 0)


def planes(own_ref, before_ref, after_ref):
    yield before_ref, None
    yield own_ref, 0
    yield own_ref, 1
    yield after_ref, None


def build(own_ref, before_ref, after_ref, k, s_ref):
    nr = own_ref.shape[3]
    nh = nr - 2
    ch = own_ref.shape[0] * own_ref.shape[4]
    w = own_ref.shape[5]
    for p, (ref, z) in enumerate(planes(own_ref, before_ref, after_ref)):
        for r in range(nr):
            for c, v in enumerate(shifted(block_of(ref, k, r, z))):
                for h in range(nh):
                    b = r - h
                    if 0 <= b < 3:
                        s_ref[p, pl.ds((3 * b + c) * ch, ch), pl.ds(h * w, w)] = v


def wgrad_kernel(core_ref, own_ref, before_ref, after_ref, o_ref, s_ref, g_ref):
    n, _, nz, nr, cg, w = own_ref.shape
    nh = nr - 2
    ch = n * cg
    build(own_ref, before_ref, after_ref, 0, s_ref)
    for z in range(nz):
        for h in range(nh):
            g_ref[z, :, pl.ds(h * w, w)] = block_of(own_ref, 1, h + 1, z).astype(BF)
    core = core_ref[0]
    for a in range(3):
        for b in range(3):
            total = None
            for z in range(nz):
                part = lax.dot_general(
                    g_ref[z],
                    s_ref[z + a, pl.ds(3 * b * ch, 3 * ch), :],
                    (((1,), (1,)), ((), ())),
                    preferred_element_type=F32,
                )
                total = part if total is None else total + part
            for c in range(3):
                for d in range(n):
                    slot = (d % 2) ^ core
                    o_ref[slot, d // 2, 9 * a + 3 * b + c] = total[d * cg : (d + 1) * cg, c * ch : (c + 1) * ch]


def weights_kernel(core_ref, mine_ref, other_ref, wt_ref, wf_ref):
    m, taps, cg, ch = mine_ref.shape
    first = core_ref[0] == 0
    for t in range(taps):
        a, bc = t // 9, t % 9
        parts = []
        for q in range(m):
            mine, other = mine_ref[q, t].astype(F32), other_ref[q, t].astype(F32)
            parts += [jnp.where(first, mine, other), jnp.where(first, other, mine)]
        block = jnp.concatenate(parts, 0)
        wt_ref[a, :, pl.ds(bc * ch, ch)] = block.astype(BF)
        wf_ref[2 - a, :, pl.ds((8 - bc) * ch, ch)] = block.T.astype(BF)


def conv_kernel(own_ref, before_ref, after_ref, wt_ref, wf_ref, o_ref, s_ref):
    n, _, nz, nr, cg, w = own_ref.shape
    nh = nr - 2
    for k, w_ref in enumerate((wt_ref, wf_ref)):
        build(own_ref, before_ref, after_ref, k, s_ref.at[k])
        for z in range(nz):
            total = None
            for a in range(3):
                part = jnp.dot(w_ref[a], s_ref[k, z + a], preferred_element_type=F32)
                total = part if total is None else total + part
            for d in range(n):
                for h in range(nh):
                    o_ref[d, k, z, h] = total[d * cg : (d + 1) * cg, h * w : (h + 1) * w]


def body(activations, weight, grad_out):
    nz, rows, cg, w = activations.shape
    n = lax.axis_size(FILT)
    chips = lax.axis_size(CHIPS)
    ns = lax.axis_size(SPACE)
    ch = n * cg
    nr = rows // n + 2
    nh = nr - 2
    norm = float(nz * ns * rows * w) ** (-0.5)
    core = lax.axis_index("core").astype(jnp.int32).reshape(1)
    up = [(i, i + 1) for i in range(ns - 1)]
    down = [(j, i) for i, j in up]
    swap = [(0, 1), (1, 0)]
    sds = jax.ShapeDtypeStruct

    (packed,) = call(pack_kernel, [sds((n, 2, nz, nr, cg, w), BF)], [activations, grad_out], name="pack")
    own = lax.all_to_all(packed, FILT, 0, 0, tiled=True)

    flat_w = weight.transpose(0, 1, 2, 4, 3).reshape(27, cg, ch)
    spread = jnp.broadcast_to(flat_w[None], (chips, 27, cg, ch))
    mine = lax.all_to_all(spread, CHIPS, 0, 0, tiled=True)
    other = lax.ppermute(mine, "core", swap)
    wt, wf = call(
        weights_kernel, [sds((3, ch, 9 * ch), BF)] * 2, [core, mine, other], smem=1, name="weights"
    )

    before = lax.ppermute(own[:, :, nz - 1], SPACE, up)
    after = lax.ppermute(own[:, :, 0], SPACE, down)

    (partial,) = call(
        wgrad_kernel,
        [sds((2, chips, 27, cg, ch), F32)],
        [core, own, before, after],
        scratch=[pltpu.VMEM((nz + 2, 9 * ch, nh * w), BF), pltpu.VMEM((nz, ch, nh * w), BF)],
        smem=1,
        flops=2 * 27 * ch * ch * nz * nh * w,
        name="wgrad",
    )
    pair = partial[0] + lax.ppermute(partial[1], "core", swap)
    pieces = lax.all_to_all(pair, CHIPS, 0, 0, tiled=True).reshape(chips, 27, cg, ch)
    group = pieces.sum(0)

    (blocks,) = call(
        conv_kernel,
        [sds((n, 2, nz, nh, cg, w), F32)],
        [own, before, after, wt, wf],
        scratch=[pltpu.VMEM((2, nz + 2, 9 * ch, nh * w), BF)],
        flops=2 * 2 * 27 * ch * ch * nz * nh * w,
        name="conv",
    )
    back = lax.all_to_all(blocks, FILT, 0, 0, tiled=True)
    back = back.transpose(1, 2, 0, 3, 4, 5).reshape(2, nz, rows, cg, w)

    padded = jnp.pad(group, ((0, ns - 27), (0, 0), (0, 0)))
    shares = lax.all_to_all(padded, SPACE, 0, 0, tiled=True)
    tap = shares.sum(0) * norm
    taps = lax.all_to_all(jnp.broadcast_to(tap[None], (ns, cg, ch)), SPACE, 0, 0, tiled=True)
    weight_grad = taps[:27].reshape(3, 3, 3, cg, ch).transpose(0, 1, 2, 4, 3)
    return back[0], back[1], weight_grad


def solution(mesh):
    fine = Mesh(mesh.devices.reshape(8, 4, 2, 4, 2), SPACE + FILT)
    return jax.shard_map(
        body,
        mesh=fine,
        in_specs=(
            P(SPACE, None, FILT, None),
            P(None, None, None, None, FILT),
            P(SPACE, None, FILT, None),
        ),
        out_specs=(
            P(SPACE, None, FILT, None),
            P(SPACE, None, FILT, None),
            P(None, None, None, None, FILT),
        ),
        check_vma=False,
    )
```

time: 575 us -> 144 us (0.25)
  waiting for transfers between devices: 432 us -> 53.2 us
  local copies, waits for them, and re-layouts: 35.8 us -> 9.17 us
  between operations: 15 us -> 0.76 us
  Pallas kernels: 0 us -> 12.1 us
  starting transfers between devices: 56.8 us -> 47.7 us
  matrix products: 8.31 us -> 0 us
    psum x1 -> x0, waiting for transfers between devices: 306 us -> none  [body(): weight_grad = lax.psum(shared, 'space') * norm_factor]
    unnamed x3 -> x0, waiting for transfers between devices: 123 us -> none
    all_to_all x4 -> x5, waiting for transfers between devices: 3.76 us -> 39.2 us  [the longest x1 11.1 us: body(): lax.all_to_all(jnp.broadcast_to(tap[None], (ns, cg, ch)), SPACE, 0, 0, ti...]
    all_gather x1 -> x0, blocking collectives: 17.9 us -> none  [body(): full_weight = lax.all_gather(weight, 'filt', axis=4, tiled=True)]
    all_to_all x0 -> x1, blocking collectives: none -> 16.9 us  [body(): own = lax.all_to_all(packed, FILT, 0, 0, tiled=True)]
    ppermute x8 -> x4, starting transfers between devices: 25.5 us -> 10.6 us  [the longest x1 5.46 us: body(): before = lax.ppermute(own[:, :, nz - 1], SPACE, up)]
    ppermute x8 -> x4, waiting for transfers between devices: 0.02 us -> 14 us  [the longest x1 14 us: body(): after = lax.ppermute(own[:, :, 0], SPACE, down)]
    pallas_call x0 -> x4, Pallas kernels: none -> 12.1 us  [call(): pl.pallas_call(kernel, out_shape=tuple(outs), in_specs=specs, out_specs=t...]
  transfers between devices with their start and end apart: 14 -> 9, of which waited for: 3 -> 6; matrix products, arithmetic and copies ran while one was open for 8% -> 4% of each run, Pallas kernels for 0% -> 5%
where the time goes in v1:
time: 144 us; the launch traced here: 142 us
  waiting for transfers between devices  53.2 us (37%)
  starting transfers between devices  47.7 us (33%)
  blocking collectives  16.9 us (12%)
  Pallas kernels  12.1 us (8%)
  local copies, waits for them, and re-layouts  9.17 us (6%)
  other arithmetic  2.26 us (2%)
    all_to_all x1, blocking collectives, body(): own = lax.all_to_all(packed, FILT, 0, 0, tiled=True)  16.9 us
    all_to_all x1, starting transfers between devices, body(): shares = lax.all_to_all(padded, SPACE, 0, 0, tiled=True)  14.6 us
    ppermute x1, waiting for transfers between devices, body(): after = lax.ppermute(own[:, :, 0], SPACE, down)  14 us
    pallas_call x4, Pallas kernels, call(): pl.pallas_call(kernel, out_shape=tuple(outs), in_specs=specs, out_specs=t...  12.1 us
    all_to_all x1, waiting for transfers between devices, body(): lax.all_to_all(jnp.broadcast_to(tap[None], (ns, cg, ch)), SPACE, 0, 0, ti...  11.1 us
    all_to_all x1, waiting for transfers between devices, body(): lax.all_to_all(pair, CHIPS, 0, 0, tiled=True).reshape(chips, 27, cg, ch)  9.43 us
    all_to_all x1, waiting for transfers between devices, body(): back = lax.all_to_all(blocks, FILT, 0, 0, tiled=True)  8.55 us
    all_to_all x1, starting transfers between devices, body(): lax.all_to_all(jnp.broadcast_to(tap[None], (ns, cg, ch)), SPACE, 0, 0, ti...  7.05 us
  transfers between devices with their start and end apart: 9, of which 6 were waited for; matrix products, arithmetic and copies ran while one was open for 4% of the time, Pallas kernels for 5%

profile of v1, /device:TPU:6, one launch (start us, length us, event | category | flops | bytes accessed | tf_op | source)
XLA Modules:
  0.0 142.1 jit_solution(6524991029530554704)
XLA Ops:
  0.6 1.8 %pack.1 = bf16[16,2,2,4,8,128]{5,4,3,2,1,0:T(8,128)(2,1)} custom-call(bf16[2,32,8,128]{3,2,1,0:T(8,128)(2,1)} %x_ref.1, bf16[2,32,8,128]{3,2,1,0:T(8,128)(2,1)} %g_ref.1), custom_call_target="tpu_custom_call" | custom-call | bytes 786432 | tf_op jit(solution)/shard_map/pack/pallas_call | solution.py:24
  2.5 1.1 copy.21
  3.6 16.9 %all_to_all.30 = bf16[16,2,2,4,8,128]{5,4,3,1,2,0:T(8,128)(2,1)S(1)} all-to-all(bf16[16,2,2,4,8,128]{5,4,3,1,2,0:T(8,128)(2,1)S(1)} %copy.21), channel_id=1, replica_groups=mesh['y'=8,'zh'=4,'zl'=2,'x'=4,'core'=2] {'zl','x','core'}, dimensions={0} | all-to-all | bytes 1048576 | tf_op jit(solution)/shard_map/all_to_all | solution.py:157
  20.5 1.3 collective-permute-start.1
  21.8 5.5 %collective-permute-start = (bf16[16,2,4,8,128]{4,3,2,1,0:T(8,128)(2,1)S(1)}, bf16[16,2,4,8,128]{4,3,2,1,0:T(8,128)(2,1)S(1)}, u32[]{:S(2)}, u32[]{:S(2)}) collective-permute-start(bf16[16,2,4,8,128]{4,3,2,1,0:T(8,128)(2,1)S(1)} %get-tuple-element.10), channel_id=1, source_target_pairs={{0,16},{16,32},{32,48},{48,64},{64,80},{80,96},{96,112},{112,128},... | collective-permute-start | bytes 786440 | tf_op jit(solution)/shard_map/ppermute | solution.py:167
  27.3 0.9 copy.24.own_ref
  28.1 14.0 %collective-permute-done.1.after_ref = bf16[16,2,4,8,128]{4,3,2,1,0:T(8,128)(2,1)S(1)} collective-permute-done((bf16[16,2,4,8,128]{4,3,2,1,0:T(8,128)(2,1)S(1)}, bf16[16,2,4,8,128]{4,3,2,1,0:T(8,128)(2,1)S(1)}, u32[]{:S(2)}, u32[]{:S(2)}) %collective-permute-start.1) | collective-permute-done | bytes 262176 | tf_op jit(solution)/shard_map/ppermute | solution.py:168
  42.1 0.7 copy-done.3
  42.9 3.7 %wgrad.1 = f32[2,8,27,8,128]{4,3,2,1,0:T(8,128)} custom-call(s32[1]{0:T(128)} %bitcast.2.core_ref, bf16[16,2,2,4,8,128]{5,4,3,2,1,0:T(8,128)(2,1)} %copy.24.own_ref, bf16[16,2,4,8,128]{4,3,2,1,0:T(8,128)(2,1)} %copy-done.4, bf16[16,2,4,8,128]{4,3,2,1,0:T(8,128)(2,1)} %copy-done.3), custom_call_target="tpu_custom_call" | custom-call | flops 452984832 | bytes 2818052 | tf_op jit(solution)/shard_map/wgrad/pallas_call | solution.py:24
  46.6 1.4 slice_bitcast_fusion
  48.0 1.9 %collective-permute-start.3 = (f32[8,27,8,128]{3,2,1,0:T(8,128)S(1)}, f32[8,27,8,128]{3,2,1,0:T(8,128)}, u32[]{:S(2)}, u32[]{:S(2)}) collective-permute-start(f32[8,27,8,128]{3,2,1,0:T(8,128)S(1)} %slice_bitcast_fusion), channel_id=1, source_target_pairs={{0,1},{1,0},{2,3},{3,2},{4,5},{5,4},{6,7},{7,6},{8,9},{9,8},{10,11... | collective-permute-start | bytes 2654216 | tf_op jit(solution)/shard_map/ppermute | solution.py:179
  49.9 0.8 broadcast_in_dim.14
  50.8 4.5 %all-to-all-start.1 = ((bf16[8,27,8,128]{3,2,1,0:T(8,128)(2,1)}), bf16[8,27,8,128]{3,2,1,0:T(8,128)(2,1)S(1)}, u32[]{:S(2)}, u32[]{:S(2)}) async-start(bf16[8,27,8,128]{3,2,1,0:T(8,128)(2,1)} %broadcast_in_dim.14), calls=%async_computation.1 | async-start | bytes 884736 | tf_op jit(solution)/shard_map/all_to_all | solution.py:161
  55.3 2.2 %fusion = f32[8,27,8,128]{3,2,1,0:T(8,128)} fusion(f32[8,27,8,128]{3,2,1,0:T(8,128)} %collective-permute-done.3, f32[2,8,27,8,128]{4,3,2,1,0:T(8,128)S(1)} %copy-done), kind=kLoop, calls=%fused_computation.2 | loop fusion | flops 221184 | bytes 2654208 | tf_op jit(solution)/shard_map/add | solution.py:179
  57.4 5.1 %all-to-all-done.1.mine_ref = bf16[8,27,8,128]{3,2,1,0:T(8,128)(2,1)S(1)} async-done(((bf16[8,27,8,128]{3,2,1,0:T(8,128)(2,1)}), bf16[8,27,8,128]{3,2,1,0:T(8,128)(2,1)S(1)}, u32[]{:S(2)}, u32[]{:S(2)}) %all-to-all-start.1) | async-done | bytes 442400 | tf_op jit(solution)/shard_map/all_to_all | solution.py:161
  62.5 5.5 %all-to-all-start.3 = ((f32[8,27,8,128]{3,2,1,0:T(8,128)}), f32[8,27,8,128]{3,2,1,0:T(8,128)S(1)}, u32[]{:S(2)}, u32[]{:S(2)}) async-start(f32[8,27,8,128]{3,2,1,0:T(8,128)} %fusion), calls=%async_computation.3 | async-start | bytes 1769472 | tf_op jit(solution)/shard_map/all_to_all | solution.py:180
  68.1 1.9 %collective-permute-start.2 = (bf16[8,27,8,128]{3,2,1,0:T(8,128)(2,1)S(1)}, bf16[8,27,8,128]{3,2,1,0:T(8,128)(2,1)S(1)}, u32[]{:S(2)}, u32[]{:S(2)}) collective-permute-start(bf16[8,27,8,128]{3,2,1,0:T(8,128)(2,1)S(1)} %all-to-all-done.1.mine_ref), channel_id=1, source_target_pairs={{0,1},{1,0},{2,3},{3,2},{4,5},{5,4},{6,7},{7,6},{8,9},{9,8},{10,11... | collective-permute-start | bytes 1327112 | tf_op jit(solution)/shard_map/ppermute | solution.py:162
  70.0 9.4 %all-to-all-done.3 = f32[8,27,8,128]{3,2,1,0:T(8,128)S(1)} async-done(((f32[8,27,8,128]{3,2,1,0:T(8,128)}), f32[8,27,8,128]{3,2,1,0:T(8,128)S(1)}, u32[]{:S(2)}, u32[]{:S(2)}) %all-to-all-start.3) | async-done | bytes 884768 | tf_op jit(solution)/shard_map/all_to_all | solution.py:180
  79.5 0.7 pad.4
  80.1 14.6 %all-to-all-start.4 = ((f32[32,8,128]{2,1,0:T(8,128)}), f32[32,8,128]{2,1,0:T(8,128)S(1)}, u32[]{:S(2)}, u32[]{:S(2)}) async-start(f32[32,8,128]{2,1,0:T(8,128)} %pad.4), calls=%async_computation.4 | async-start | bytes 262144 | tf_op jit(solution)/shard_map/all_to_all | solution.py:195
  94.8 0.7 copy-done.2
  95.5 2.7 %weights.1 = (bf16[3,128,1152]{2,1,0:T(8,128)(2,1)}, bf16[3,128,1152]{2,1,0:T(8,128)(2,1)}) custom-call(s32[1]{0:T(128)} %bitcast.2.core_ref, bf16[8,27,8,128]{3,2,1,0:T(8,128)(2,1)} %copy-done.1, bf16[8,27,8,128]{3,2,1,0:T(8,128)(2,1)} %copy-done.2), custom_call_target="tpu_custom_call" | custom-call | bytes 2654212 | tf_op jit(solution)/shard_map/weights/pallas_call | solution.py:24
  98.2 3.9 %conv.1 = f32[16,2,2,2,8,128]{5,4,3,2,1,0:T(8,128)} custom-call(bf16[16,2,2,4,8,128]{5,4,3,2,1,0:T(8,128)(2,1)} %copy.24.own_ref, bf16[16,2,4,8,128]{4,3,2,1,0:T(8,128)(2,1)} %copy-done.4, bf16[16,2,4,8,128]{4,3,2,1,0:T(8,128)(2,1)} %copy-done.3, bf16[3,128,1152]{2,1,0:T(8,128)(2,1)} %get-tuple-element.5.wt_ref, bf16[3,128,1152]{2,1,0:T(8,128)(2,1)} %get-tuple-element.6.wf_ref), custom_call_target="tpu_custom_call" | custom-call | flops 905969664 | bytes 3342336 | tf_op jit(solution)/shard_map/conv/pallas_call | solution.py:24
  102.1 5.1 %all-to-all-done.4 = f32[32,8,128]{2,1,0:T(8,128)S(1)} async-done(((f32[32,8,128]{2,1,0:T(8,128)}), f32[32,8,128]{2,1,0:T(8,128)S(1)}, u32[]{:S(2)}, u32[]{:S(2)}) %all-to-all-start.4) | async-done | bytes 131104 | tf_op jit(solution)/shard_map/all_to_all | solution.py:195
  107.2 5.4 %all-to-all-start.2 = ((f32[16,2,2,2,8,128]{5,4,3,2,1,0:T(8,128)}), f32[16,2,2,2,8,128]{5,4,3,2,1,0:T(8,128)S(1)}, u32[]{:S(2)}, u32[]{:S(2)}) async-start(f32[16,2,2,2,8,128]{5,4,3,2,1,0:T(8,128)} %conv.1), calls=%async_computation.2 | async-start | bytes 1048576 | tf_op jit(solution)/shard_map/all_to_all | solution.py:191
  112.7 8.5 %all-to-all-done.2 = f32[16,2,2,2,8,128]{5,4,3,2,1,0:T(8,128)S(1)} async-done(((f32[16,2,2,2,8,128]{5,4,3,2,1,0:T(8,128)}), f32[16,2,2,2,8,128]{5,4,3,2,1,0:T(8,128)S(1)}, u32[]{:S(2)}, u32[]{:S(2)}) %all-to-all-start.2) | async-done | bytes 524320 | tf_op jit(solution)/shard_map/all_to_all | solution.py:191
  121.2 0.7 broadcast_in_dim.15
  121.9 7.0 %all-to-all-start.5 = ((f32[32,8,128]{2,1,0:T(8,128)}), f32[32,8,128]{2,1,0:T(8,128)S(1)}, u32[]{:S(2)}, u32[]{:S(2)}) async-start(f32[32,8,128]{2,1,0:T(8,128)} %broadcast_in_dim.15), calls=%async_computation.5 | async-start | bytes 262144 | tf_op jit(solution)/shard_map/all_to_all | solution.py:197
  129.0 0.7 copy.26
  129.7 0.7 copy.25
  130.4 11.1 %all-to-all-done.5 = f32[32,8,128]{2,1,0:T(8,128)S(1)} async-done(((f32[32,8,128]{2,1,0:T(8,128)}), f32[32,8,128]{2,1,0:T(8,128)S(1)}, u32[]{:S(2)}, u32[]{:S(2)}) %all-to-all-start.5) | async-done | bytes 131104 | tf_op jit(solution)/shard_map/all_to_all | solution.py:197
  141.5 0.7 slice.36
  (18 shorter events, 0.3 us)
Async XLA Ops:
  20.5 21.6 %collective-permute-start.1 = (bf16[16,2,4,8,128]{4,3,2,1,0:T(8,128)(2,1)S(1)}, bf16[16,2,4,8,128]{4,3,2,1,0:T(8,128)(2,1)S(1)}, u32[]{:S(2)}, u32[]{:S(2)}) collective-permute-start(bf16[16,2,4,8,128]{4,3,2,1,0:T(8,128)(2,1)S(1)} %get-tuple-element.9), channel_id=1, source_target_pairs={{16,0},{32,16},{48,32},{64,48},{80,64},{96,80},{112,96},{128,112},... | collective-permute-start | bytes 786440 | tf_op jit(solution)/shard_map/ppermute | solution.py:168
  21.8 20.3 %collective-permute-start = (bf16[16,2,4,8,128]{4,3,2,1,0:T(8,128)(2,1)S(1)}, bf16[16,2,4,8,128]{4,3,2,1,0:T(8,128)(2,1)S(1)}, u32[]{:S(2)}, u32[]{:S(2)}) collective-permute-start(bf16[16,2,4,8,128]{4,3,2,1,0:T(8,128)(2,1)S(1)} %get-tuple-element.10), channel_id=1, source_target_pairs={{0,16},{16,32},{32,48},{48,64},{64,80},{80,96},{96,112},{112,128},... | collective-permute-start | bytes 786440 | tf_op jit(solution)/shard_map/ppermute | solution.py:167
  42.1 0.7 copy-start.3
  42.1 0.8 copy-start.4
  42.9 7.0 %copy-start.5 = (bf16[3,3,3,128,8]{3,4,2,1,0:T(8,128)(2,1)S(1)}, bf16[3,3,3,128,8]{3,4,2,1,0:T(8,128)(2,1)}, u32[]{:S(2)}) copy-start(bf16[3,3,3,128,8]{3,4,2,1,0:T(8,128)(2,1)} %param.4) | copy-start | bytes 165892
  46.6 8.6 %copy-start = (f32[2,8,27,8,128]{4,3,2,1,0:T(8,128)S(1)}, f32[2,8,27,8,128]{4,3,2,1,0:T(8,128)}, u32[]{:S(2)}) copy-start(f32[2,8,27,8,128]{4,3,2,1,0:T(8,128)} %wgrad.1) | copy-start | bytes 5308420
  48.0 7.3 %collective-permute-start.3 = (f32[8,27,8,128]{3,2,1,0:T(8,128)S(1)}, f32[8,27,8,128]{3,2,1,0:T(8,128)}, u32[]{:S(2)}, u32[]{:S(2)}) collective-permute-start(f32[8,27,8,128]{3,2,1,0:T(8,128)S(1)} %slice_bitcast_fusion), channel_id=1, source_target_pairs={{0,1},{1,0},{2,3},{3,2},{4,5},{5,4},{6,7},{7,6},{8,9},{9,8},{10,11... | collective-permute-start | bytes 2654216 | tf_op jit(solution)/shard_map/ppermute | solution.py:179
  50.8 11.8 %all-to-all-start.1 = ((bf16[8,27,8,128]{3,2,1,0:T(8,128)(2,1)}), bf16[8,27,8,128]{3,2,1,0:T(8,128)(2,1)S(1)}, u32[]{:S(2)}, u32[]{:S(2)}) async-start(bf16[8,27,8,128]{3,2,1,0:T(8,128)(2,1)} %broadcast_in_dim.14), calls=%async_computation.1 | async-start | bytes 884736 | tf_op jit(solution)/shard_map/all_to_all | solution.py:161
  62.5 32.2 %copy-start.1 = (bf16[8,27,8,128]{3,2,1,0:T(8,128)(2,1)}, bf16[8,27,8,128]{3,2,1,0:T(8,128)(2,1)S(1)}, u32[]{:S(2)}) copy-start(bf16[8,27,8,128]{3,2,1,0:T(8,128)(2,1)S(1)} %all-to-all-done.1.mine_ref) | copy-start | bytes 1327108
  62.5 16.9 %all-to-all-start.3 = ((f32[8,27,8,128]{3,2,1,0:T(8,128)}), f32[8,27,8,128]{3,2,1,0:T(8,128)S(1)}, u32[]{:S(2)}, u32[]{:S(2)}) async-start(f32[8,27,8,128]{3,2,1,0:T(8,128)} %fusion), calls=%async_computation.3 | async-start | bytes 1769472 | tf_op jit(solution)/shard_map/all_to_all | solution.py:180
  68.1 26.7 %collective-permute-start.2 = (bf16[8,27,8,128]{3,2,1,0:T(8,128)(2,1)S(1)}, bf16[8,27,8,128]{3,2,1,0:T(8,128)(2,1)S(1)}, u32[]{:S(2)}, u32[]{:S(2)}) collective-permute-start(bf16[8,27,8,128]{3,2,1,0:T(8,128)(2,1)S(1)} %all-to-all-done.1.mine_ref), channel_id=1, source_target_pairs={{0,1},{1,0},{2,3},{3,2},{4,5},{5,4},{6,7},{7,6},{8,9},{9,8},{10,11... | collective-permute-start | bytes 1327112 | tf_op jit(solution)/shard_map/ppermute | solution.py:162
  80.1 27.1 %all-to-all-start.4 = ((f32[32,8,128]{2,1,0:T(8,128)}), f32[32,8,128]{2,1,0:T(8,128)S(1)}, u32[]{:S(2)}, u32[]{:S(2)}) async-start(f32[32,8,128]{2,1,0:T(8,128)} %pad.4), calls=%async_computation.4 | async-start | bytes 262144 | tf_op jit(solution)/shard_map/all_to_all | solution.py:195
  94.8 0.8 copy-start.2
  107.2 14.0 %all-to-all-start.2 = ((f32[16,2,2,2,8,128]{5,4,3,2,1,0:T(8,128)}), f32[16,2,2,2,8,128]{5,4,3,2,1,0:T(8,128)S(1)}, u32[]{:S(2)}, u32[]{:S(2)}) async-start(f32[16,2,2,2,8,128]{5,4,3,2,1,0:T(8,128)} %conv.1), calls=%async_computation.2 | async-start | bytes 1048576 | tf_op jit(solution)/shard_map/all_to_all | solution.py:191
  121.9 19.6 %all-to-all-start.5 = ((f32[32,8,128]{2,1,0:T(8,128)}), f32[32,8,128]{2,1,0:T(8,128)S(1)}, u32[]{:S(2)}, u32[]{:S(2)}) async-start(f32[32,8,128]{2,1,0:T(8,128)} %broadcast_in_dim.15), calls=%async_computation.5 | async-start | bytes 262144 | tf_op jit(solution)/shard_map/all_to_all | solution.py:197

commit v2 on v1

v2 whole, which is shorter than its diff:
```python
import jax
import jax.numpy as jnp
from jax import lax
from jax.experimental import pallas as pl
from jax.experimental.pallas import tpu as pltpu
from jax.sharding import Mesh
from jax.sharding import PartitionSpec as P


SPACE = ("y", "zh")
FILT = ("zl", "x", "core")
CHIPS = ("zl", "x")
BF, F32 = jnp.bfloat16, jnp.float32


def vmem_specs(n):
    return [pl.BlockSpec(memory_space=pltpu.VMEM)] * n


def call(kernel, outs, ins, scratch=(), smem=0, flops=0):
    specs = [pl.BlockSpec(memory_space=pltpu.SMEM)] * smem + vmem_specs(len(ins) - smem)
    moved = sum(a.size * a.dtype.itemsize for a in ins) + sum(o.size * o.dtype.itemsize for o in outs)
    return pl.pallas_call(
        kernel,
        out_shape=tuple(outs),
        in_specs=specs,
        out_specs=tuple(vmem_specs(len(outs))),
        scratch_shapes=list(scratch),
        cost_estimate=pl.CostEstimate(flops=flops, transcendentals=0, bytes_accessed=moved),
    )(*ins)


def pack_kernel(x_ref, o_ref):
    n, nz, nr = o_ref.shape[:3]
    rows = x_ref.shape[1]
    zero = jnp.zeros(x_ref.shape[2:], x_ref.dtype)
    for z in range(nz):
        for d in range(n):
            for r in range(nr):
                h = d * (nr - 2) + r - 1
                o_ref[d, z, r] = x_ref[z, h] if 0 <= h < rows else zero


def shifted(value):
    lane = lax.broadcasted_iota(jnp.int32, value.shape, 1)
    w = value.shape[1]
    left = jnp.where(lane == 0, 0.0, pltpu.roll(value, 1, 1))
    right = jnp.where(lane == w - 1, 0.0, pltpu.roll(value, w - 1, 1))
    return left.astype(BF), value.astype(BF), right.astype(BF)


def block_of(ref, r, z=None):
    n = ref.shape[0]
    parts = [(ref[d, r] if z is None else ref[d, z, r]).astype(F32) for d in range(n)]
    return jnp.concatenate(parts, 0)


def build(own_ref, before_ref, after_ref, s_ref):
    n, nz, nr, cg, w = own_ref.shape
    nh, ch = nr - 2, n * cg
    planes = [(before_ref, None)] + [(own_ref, z) for z in range(nz)] + [(after_ref, None)]
    for p, (ref, z) in enumerate(planes):
        for r in range(nr):
            for c, v in enumerate(shifted(block_of(ref, r, z))):
                for h in range(nh):
                    b = r - h
                    if 0 <= b < 3:
                        s_ref[p, pl.ds((3 * b + c) * ch, ch), pl.ds(h * w, w)] = v


def wgrad_kernel(core_ref, x_ref, before_ref, after_ref, g_ref, keep_ref, send_ref, s_ref, t_ref, o_ref, sems):
    n, nz, nr, cg, w = x_ref.shape
    nh, ch = nr - 2, n * cg
    build(x_ref, before_ref, after_ref, s_ref)
    for z in range(nz):
        for h in range(nh):
            t_ref[z, :, pl.ds(h * w, w)] = block_of(g_ref, h + 1, z).astype(BF)
    core = core_ref[0]
    for a in range(3):
        for b in range(3):
            total = None
            for z in range(nz):
                part = lax.dot_general(
                    t_ref[z],
                    s_ref[z + a, pl.ds(3 * b * ch, 3 * ch), :],
                    (((1,), (1,)), ((), ())),
                    preferred_element_type=F32,
                )
                total = part if total is None else total + part
            for c in range(3):
                for d in range(n):
                    slot = (d % 2) ^ core
                    o_ref[slot, d // 2, 9 * a + 3 * b + c] = total[d * cg : (d + 1) * cg, c * ch : (c + 1) * ch]
    copies = [
        pltpu.make_async_copy(o_ref.at[1], send_ref, sems.at[1]),
        pltpu.make_async_copy(o_ref.at[0], keep_ref, sems.at[0]),
    ]
    for copy in copies:
        copy.start()
    for copy in copies:
        copy.wait()


def weights_kernel(core_ref, mine_ref, other_ref, wt_ref, wf_ref):
    m, taps, _, ch = mine_ref.shape
    first = core_ref[0] == 0
    for t in range(taps):
        a, bc = t // 9, t % 9
        parts = []
        for q in range(m):
            mine, other = mine_ref[q, t].astype(F32), other_ref[q, t].astype(F32)
            parts += [jnp.where(first, mine, other), jnp.where(first, other, mine)]
        block = jnp.concatenate(parts, 0)
        wt_ref[a, :, pl.ds(bc * ch, ch)] = block.astype(BF)
        wf_ref[2 - a, :, pl.ds((8 - bc) * ch, ch)] = block.T.astype(BF)


def conv_kernel(x_ref, xb_ref, xa_ref, g_ref, gb_ref, ga_ref, wt_ref, wf_ref, o_ref, s_ref):
    n, nz, nr, cg, w = x_ref.shape
    nh = nr - 2
    for k, (refs, w_ref) in enumerate((((x_ref, xb_ref, xa_ref), wt_ref), ((g_ref, gb_ref, ga_ref), wf_ref))):
        build(*refs, s_ref.at[k])
        for z in range(nz):
            total = None
            for a in range(3):
                part = jnp.dot(w_ref[a], s_ref[k, z + a], preferred_element_type=F32)
                total = part if total is None else total + part
            for d in range(n):
                for h in range(nh):
                    o_ref[d, k, z, h] = total[d * cg : (d + 1) * cg, h * w : (h + 1) * w]


def swap_all(array, axes):
    return lax.all_to_all(array, axes, 0, 0, tiled=True)


def step(activations, weight, grad_out):
    nz, rows, cg, w = activations.shape
    n = lax.axis_size(FILT)
    chips = lax.axis_size(CHIPS)
    ns = lax.axis_size(SPACE)
    ch = n * cg
    nr = rows // n + 2
    nh = nr - 2
    norm = float(nz * ns * rows * w) ** (-0.5)
    core = lax.axis_index("core").astype(jnp.int32).reshape(1)
    up = [(i, i + 1) for i in range(ns - 1)]
    down = [(j, i) for i, j in up]
    swap = [(0, 1), (1, 0)]
    sds = jax.ShapeDtypeStruct
    packed = [sds((n, nz, nr, cg, w), BF)]

    (px,) = call(pack_kernel, packed, [activations])
    x = swap_all(px, FILT)
    grad_out, px = lax.optimization_barrier((grad_out, px))
    (pg,) = call(pack_kernel, packed, [grad_out])
    g = swap_all(pg, FILT)

    flat_w = weight.transpose(0, 1, 2, 4, 3).reshape(27, cg, ch)
    flat_w, pg = lax.optimization_barrier((flat_w, pg))
    mine = swap_all(jnp.broadcast_to(flat_w[None], (chips, 27, cg, ch)), CHIPS)
    other = lax.ppermute(mine, "core", swap)
    wt, wf = call(weights_kernel, [sds((3, ch, 9 * ch), BF)] * 2, [core, mine, other], smem=1)

    xb = lax.ppermute(x[:, nz - 1], SPACE, up)
    xa = lax.ppermute(x[:, 0], SPACE, down)
    gb = lax.ppermute(g[:, nz - 1], SPACE, up)
    ga = lax.ppermute(g[:, 0], SPACE, down)

    any_spec = pl.BlockSpec(memory_space=pl.ANY)
    keep, send = pl.pallas_call(
        wgrad_kernel,
        out_shape=(sds((chips, 27, cg, ch), F32),) * 2,
        in_specs=[pl.BlockSpec(memory_space=pltpu.SMEM)] + vmem_specs(4),
        out_specs=(any_spec, any_spec),
        scratch_shapes=[
            pltpu.VMEM((nz + 2, 9 * ch, nh * w), BF),
            pltpu.VMEM((nz, ch, nh * w), BF),
            pltpu.VMEM((2, chips, 27, cg, ch), F32),
            pltpu.SemaphoreType.DMA((2,)),
        ],
        cost_estimate=pl.CostEstimate(
            flops=2 * 27 * ch * ch * nz * nh * w, transcendentals=0, bytes_accessed=4 * 27 * ch * ch
        ),
        name="wgrad",
    )(core, x, xb, xa, g)
    pair = keep + lax.ppermute(send, "core", swap)
    group = swap_all(pair, CHIPS).reshape(chips, 27, cg, ch).sum(0)

    (blocks,) = call(
        conv_kernel,
        [sds((n, 2, nz, nh, cg, w), F32)],
        [x, xb, xa, g, gb, ga, wt, wf],
        scratch=[pltpu.VMEM((2, nz + 2, 9 * ch, nh * w), BF)],
        flops=2 * 2 * 27 * ch * ch * nz * nh * w,
    )
    group, blocks = lax.optimization_barrier((group, blocks))
    back = swap_all(blocks, FILT)
    back = back.transpose(1, 2, 0, 3, 4, 5).reshape(2, nz, rows, cg, w)

    padded = jnp.pad(group, ((0, ns - 27), (0, 0), (0, 0)))
    shares = swap_all(padded, SPACE)
    tap = shares.sum(0) * norm
    taps = swap_all(jnp.broadcast_to(tap[None], (ns, cg, ch)), SPACE)
    weight_grad = taps[:27].reshape(3, 3, 3, cg, ch).transpose(0, 1, 2, 4, 3)
    return back[0], back[1], weight_grad


def solution(mesh):
    fine = Mesh(mesh.devices.reshape(8, 4, 2, 4, 2), SPACE + FILT)
    return jax.shard_map(
        step,
        mesh=fine,
        in_specs=(
            P(SPACE, None, FILT, None),
            P(None, None, None, None, FILT),
            P(SPACE, None, FILT, None),
        ),
        out_specs=(
            P(SPACE, None, FILT, None),
            P(SPACE, None, FILT, None),
            P(None, None, None, None, FILT),
        ),
        check_vma=False,
    )
```

time: 144 us -> 145 us (level)
  the two profiles are of different devices: /device:TPU:6 before, /device:TPU:1 now
where the time goes in v2:
time: 145 us; the launch traced here: 144 us
  starting transfers between devices  49.4 us (34%)
  blocking collectives  38.3 us (26%)
  waiting for transfers between devices  35.9 us (25%)
  Pallas kernels  13.6 us (9%)
  local copies, waits for them, and re-layouts  5.11 us (4%)
    all_to_all x2, blocking collectives, swap_all(): return lax.all_to_all(array, axes, 0, 0, tiled=True)  38.3 us
    all_to_all x5, starting transfers between devices, swap_all(): return lax.all_to_all(array, axes, 0, 0, tiled=True)  31.6 us
    all_to_all x5, waiting for transfers between devices, swap_all(): return lax.all_to_all(array, axes, 0, 0, tiled=True)  24.2 us
    pallas_call x4, Pallas kernels, call(): pl.pallas_call(kernel, out_shape=tuple(outs), in_specs=specs, out_specs=t...  9.92 us
    ppermute x1, waiting for transfers between devices, step(): xa = lax.ppermute(x[:, 0], SPACE, down)  8.28 us
    ppermute x1, starting transfers between devices, step(): gb = lax.ppermute(g[:, nz - 1], SPACE, up)  4.99 us
    ppermute x1, starting transfers between devices, step(): pair = keep + lax.ppermute(send, 'core', swap)  4.08 us
    pallas_call x1, Pallas kernels, step(): pl.pallas_call(wgrad_kernel, out_shape=(sds((chips, 27, cg, ch), F32),) *...  3.72 us
  transfers between devices with their start and end apart: 11, of which 6 were waited for; matrix products, arithmetic and copies ran while one was open for 2% of the time, Pallas kernels for 6%

profile of v2, /device:TPU:1, one launch (start us, length us, event | category | flops | bytes accessed | tf_op | source)
XLA Modules:
  0.0 144.2 jit_solution(13096319692452665060)
XLA Ops:
  0.6 1.6 %shard_map.58 = bf16[16,2,4,8,128]{4,3,2,1,0:T(8,128)(2,1)} custom-call(bf16[2,32,8,128]{3,2,1,0:T(8,128)(2,1)} %x_ref.1), custom_call_target="tpu_custom_call" | custom-call | bytes 393216 | tf_op jit(solution)/shard_map/pallas_call | solution.py:23
  2.3 10.2 %all-to-all-start = ((bf16[16,2,4,8,128]{4,3,2,1,0:T(8,128)(2,1)}), bf16[16,2,4,8,128]{4,3,2,1,0:T(8,128)(2,1)S(1)}, u32[]{:S(2)}, u32[]{:S(2)}) async-start(bf16[16,2,4,8,128]{4,3,2,1,0:T(8,128)(2,1)} %shard_map.58), calls=%async_computation | async-start | bytes 524288 | tf_op jit(solution)/shard_map/all_to_all | solution.py:134
  12.4 1.6 %shard_map.59 = bf16[16,2,4,8,128]{4,3,2,1,0:T(8,128)(2,1)} custom-call(bf16[2,32,8,128]{3,2,1,0:T(8,128)(2,1)} %x_ref.2), custom_call_target="tpu_custom_call" | custom-call | bytes 393216 | tf_op jit(solution)/shard_map/pallas_call | solution.py:23
  14.1 5.6 %all-to-all-done.x_ref = bf16[16,2,4,8,128]{4,3,2,1,0:T(8,128)(2,1)S(1)} async-done(((bf16[16,2,4,8,128]{4,3,2,1,0:T(8,128)(2,1)}), bf16[16,2,4,8,128]{4,3,2,1,0:T(8,128)(2,1)S(1)}, u32[]{:S(2)}, u32[]{:S(2)}) %all-to-all-start) | async-done | bytes 262176 | tf_op jit(solution)/shard_map/all_to_all | solution.py:134
  19.7 4.3 %all-to-all-start.1 = ((bf16[16,2,4,8,128]{4,3,2,1,0:T(8,128)(2,1)}), bf16[16,2,4,8,128]{4,3,2,1,0:T(8,128)(2,1)S(1)}, u32[]{:S(2)}, u32[]{:S(2)}) async-start(bf16[16,2,4,8,128]{4,3,2,1,0:T(8,128)(2,1)} %shard_map.59), calls=%async_computation.1 | async-start | bytes 524288 | tf_op jit(solution)/shard_map/all_to_all | solution.py:134
  24.0 3.2 %collective-permute-start = (bf16[16,4,8,128]{3,2,1,0:T(8,128)(2,1)S(1)}, bf16[16,4,8,128]{3,2,1,0:T(8,128)(2,1)S(1)}, u32[]{:S(2)}, u32[]{:S(2)}) collective-permute-start(bf16[16,4,8,128]{3,2,1,0:T(8,128)(2,1)S(1)} %get-tuple-element.24), channel_id=1, source_target_pairs={{0,16},{16,32},{32,48},{48,64},{64,80},{80,96},{96,112},{112,128},... | collective-permute-start | bytes 393224 | tf_op jit(solution)/shard_map/ppermute | solution.py:165
  27.2 1.3 collective-permute-start.1
  28.5 2.7 %all-to-all-done.1.g_ref = bf16[16,2,4,8,128]{4,3,2,1,0:T(8,128)(2,1)S(1)} async-done(((bf16[16,2,4,8,128]{4,3,2,1,0:T(8,128)(2,1)}), bf16[16,2,4,8,128]{4,3,2,1,0:T(8,128)(2,1)S(1)}, u32[]{:S(2)}, u32[]{:S(2)}) %all-to-all-start.1) | async-done | bytes 262176 | tf_op jit(solution)/shard_map/all_to_all | solution.py:134
  31.2 8.3 %collective-permute-done.1.after_ref.xa_ref = bf16[16,4,8,128]{3,2,1,0:T(8,128)(2,1)S(1)} collective-permute-done((bf16[16,4,8,128]{3,2,1,0:T(8,128)(2,1)S(1)}, bf16[16,4,8,128]{3,2,1,0:T(8,128)(2,1)S(1)}, u32[]{:S(2)}, u32[]{:S(2)}) %collective-permute-start.1) | collective-permute-done | bytes 131104 | tf_op jit(solution)/shard_map/ppermute | solution.py:166
  39.5 0.7 copy-done.8
  40.2 3.7 %wgrad.1 = (f32[8,27,8,128]{3,2,1,0:T(8,128)}, f32[8,27,8,128]{3,2,1,0:T(8,128)}) custom-call(s32[1]{0:T(128)} %bitcast.core_ref, bf16[16,2,4,8,128]{4,3,2,1,0:T(8,128)(2,1)} %copy-done.1, bf16[16,4,8,128]{3,2,1,0:T(8,128)(2,1)} %copy-done.7, bf16[16,4,8,128]{3,2,1,0:T(8,128)(2,1)} %copy-done.8, bf16[16,2,4,8,128]{4,3,2,1,0:T(8,128)(2,1)} %copy-done.2), custom_call_target="tpu_custom_call" | custom-call | flops 452984832 | bytes 1769472 | tf_op jit(solution)/shard_map/wgrad/pallas_call | solution.py:171
  43.9 4.1 %collective-permute-start.2 = (f32[8,27,8,128]{3,2,1,0:T(8,128)}, f32[8,27,8,128]{3,2,1,0:T(8,128)S(1)}, u32[]{:S(2)}, u32[]{:S(2)}) collective-permute-start(f32[8,27,8,128]{3,2,1,0:T(8,128)} %get-tuple-element.13), channel_id=1, source_target_pairs={{0,1},{1,0},{2,3},{3,2},{4,5},{5,4},{6,7},{7,6},{8,9},{9,8},{10,11... | collective-permute-start | bytes 2654216 | tf_op jit(solution)/shard_map/ppermute | solution.py:187
  48.0 0.8 broadcast_in_dim.4
  48.8 4.2 %all-to-all-start.3 = ((bf16[8,27,8,128]{3,2,1,0:T(8,128)(2,1)}), bf16[8,27,8,128]{3,2,1,0:T(8,128)(2,1)S(1)}, u32[]{:S(2)}, u32[]{:S(2)}) async-start(bf16[8,27,8,128]{3,2,1,0:T(8,128)(2,1)} %broadcast_in_dim.4), calls=%async_computation.3 | async-start | bytes 884736 | tf_op jit(solution)/shard_map/all_to_all | solution.py:134
  53.1 1.0 add.5
  54.1 6.8 %all-to-all-done.3.mine_ref = bf16[8,27,8,128]{3,2,1,0:T(8,128)(2,1)S(1)} async-done(((bf16[8,27,8,128]{3,2,1,0:T(8,128)(2,1)}), bf16[8,27,8,128]{3,2,1,0:T(8,128)(2,1)S(1)}, u32[]{:S(2)}, u32[]{:S(2)}) %all-to-all-start.3) | async-done | bytes 442400 | tf_op jit(solution)/shard_map/all_to_all | solution.py:134
  61.0 4.3 %all-to-all-start.2 = ((f32[8,27,8,128]{3,2,1,0:T(8,128)}), f32[8,27,8,128]{3,2,1,0:T(8,128)S(1)}, u32[]{:S(2)}, u32[]{:S(2)}) async-start(f32[8,27,8,128]{3,2,1,0:T(8,128)} %add.5), calls=%async_computation.2 | async-start | bytes 1769472 | tf_op jit(solution)/shard_map/all_to_all | solution.py:134
  65.2 2.9 %collective-permute-start.5 = (bf16[8,27,8,128]{3,2,1,0:T(8,128)(2,1)S(1)}, bf16[8,27,8,128]{3,2,1,0:T(8,128)(2,1)S(1)}, u32[]{:S(2)}, u32[]{:S(2)}) collective-permute-start(bf16[8,27,8,128]{3,2,1,0:T(8,128)(2,1)S(1)} %all-to-all-done.3.mine_ref), channel_id=1, source_target_pairs={{0,1},{1,0},{2,3},{3,2},{4,5},{5,4},{6,7},{7,6},{8,9},{9,8},{10,11... | collective-permute-start | bytes 1327112 | tf_op jit(solution)/shard_map/ppermute | solution.py:162
  68.2 5.0 %collective-permute-start.3 = (bf16[16,4,8,128]{3,2,1,0:T(8,128)(2,1)S(1)}, bf16[16,4,8,128]{3,2,1,0:T(8,128)(2,1)S(1)}, u32[]{:S(2)}, u32[]{:S(2)}) collective-permute-start(bf16[16,4,8,128]{3,2,1,0:T(8,128)(2,1)S(1)} %get-tuple-element.22), channel_id=1, source_target_pairs={{0,16},{16,32},{32,48},{48,64},{64,80},{80,96},{96,112},{112,128},... | collective-permute-start | bytes 393224 | tf_op jit(solution)/shard_map/ppermute | solution.py:167
  73.2 1.3 collective-permute-start.4
  74.5 0.8 copy-done.5
  75.3 2.7 %shard_map.60 = (bf16[3,128,1152]{2,1,0:T(8,128)(2,1)}, bf16[3,128,1152]{2,1,0:T(8,128)(2,1)}) custom-call(s32[1]{0:T(128)} %bitcast.core_ref, bf16[8,27,8,128]{3,2,1,0:T(8,128)(2,1)} %copy-done, bf16[8,27,8,128]{3,2,1,0:T(8,128)(2,1)} %copy-done.5), custom_call_target="tpu_custom_call" | custom-call | bytes 2654212 | tf_op jit(solution)/shard_map/pallas_call | solution.py:23
  78.0 3.4 %collective-permute-done.4.ga_ref = bf16[16,4,8,128]{3,2,1,0:T(8,128)(2,1)S(1)} collective-permute-done((bf16[16,4,8,128]{3,2,1,0:T(8,128)(2,1)S(1)}, bf16[16,4,8,128]{3,2,1,0:T(8,128)(2,1)S(1)}, u32[]{:S(2)}, u32[]{:S(2)}) %collective-permute-start.4) | collective-permute-done | bytes 131104 | tf_op jit(solution)/shard_map/ppermute | solution.py:168
  81.4 0.7 copy-done.10
  82.0 4.0 %shard_map.61 = f32[16,2,2,2,8,128]{5,4,3,2,1,0:T(8,128)} custom-call(bf16[16,2,4,8,128]{4,3,2,1,0:T(8,128)(2,1)} %copy-done.1, bf16[16,4,8,128]{3,2,1,0:T(8,128)(2,1)} %copy-done.7, bf16[16,4,8,128]{3,2,1,0:T(8,128)(2,1)} %copy-done.8, bf16[16,2,4,8,128]{4,3,2,1,0:T(8,128)(2,1)} %copy-done.2, bf16[16,4,8,128]{3,2,1,0:T(8,128)(2,1)} %copy-done.9, ...), custom_call_target="tpu_custom_call" | custom-call | flops 905969664 | bytes 3342336 | tf_op jit(solution)/shard_map/pallas_call | solution.py:23
  86.1 23.8 %all_to_all.35 = f32[32,8,128]{2,1,0:T(8,128)S(1)} all-to-all(f32[32,8,128]{2,1,0:T(8,128)S(1)} %pad.4), channel_id=1, replica_groups=mesh['y'=8,'zh'=4,'zl'=2,'x'=4,'core'=2] {'y','zh'}, dimensions={0} | all-to-all | bytes 262144 | tf_op jit(solution)/shard_map/all_to_all | solution.py:134
  109.9 14.5 %all_to_all.36 = f32[32,8,128]{2,1,0:T(8,128)S(1)} all-to-all(f32[32,8,128]{2,1,0:T(8,128)S(1)} %broadcast_in_dim.5), channel_id=1, replica_groups=mesh['y'=8,'zh'=4,'zl'=2,'x'=4,'core'=2] {'y','zh'}, dimensions={0} | all-to-all | bytes 262144 | tf_op jit(solution)/shard_map/all_to_all | solution.py:134
  124.4 8.7 %all-to-all-start.4 = ((f32[16,2,2,2,8,128]{5,4,3,2,1,0:T(8,128)}), f32[16,2,2,2,8,128]{5,4,3,2,1,0:T(8,128)S(1)}, u32[]{:S(2)}, u32[]{:S(2)}) async-start(f32[16,2,2,2,8,128]{5,4,3,2,1,0:T(8,128)} %shard_map.61), calls=%async_computation.4 | async-start | bytes 1048576 | tf_op jit(solution)/shard_map/all_to_all | solution.py:134
  133.1 0.7 slice.36
  133.7 9.0 %all-to-all-done.4 = f32[16,2,2,2,8,128]{5,4,3,2,1,0:T(8,128)S(1)} async-done(((f32[16,2,2,2,8,128]{5,4,3,2,1,0:T(8,128)}), f32[16,2,2,2,8,128]{5,4,3,2,1,0:T(8,128)S(1)}, u32[]{:S(2)}, u32[]{:S(2)}) %all-to-all-start.4) | async-done | bytes 524320 | tf_op jit(solution)/shard_map/all_to_all | solution.py:134
  142.8 0.7 copy.30
  143.5 0.7 copy.31
  (32 shorter events, 0.2 us)
Async XLA Ops:
  2.3 17.4 %all-to-all-start = ((bf16[16,2,4,8,128]{4,3,2,1,0:T(8,128)(2,1)}), bf16[16,2,4,8,128]{4,3,2,1,0:T(8,128)(2,1)S(1)}, u32[]{:S(2)}, u32[]{:S(2)}) async-start(bf16[16,2,4,8,128]{4,3,2,1,0:T(8,128)(2,1)} %shard_map.58), calls=%async_computation | async-start | bytes 524288 | tf_op jit(solution)/shard_map/all_to_all | solution.py:134
  19.7 4.3 %copy-start.1 = (bf16[16,2,4,8,128]{4,3,2,1,0:T(8,128)(2,1)}, bf16[16,2,4,8,128]{4,3,2,1,0:T(8,128)(2,1)S(1)}, u32[]{:S(2)}) copy-start(bf16[16,2,4,8,128]{4,3,2,1,0:T(8,128)(2,1)S(1)} %all-to-all-done.x_ref) | copy-start | bytes 786436
  19.7 11.5 %all-to-all-start.1 = ((bf16[16,2,4,8,128]{4,3,2,1,0:T(8,128)(2,1)}), bf16[16,2,4,8,128]{4,3,2,1,0:T(8,128)(2,1)S(1)}, u32[]{:S(2)}, u32[]{:S(2)}) async-start(bf16[16,2,4,8,128]{4,3,2,1,0:T(8,128)(2,1)} %shard_map.59), calls=%async_computation.1 | async-start | bytes 524288 | tf_op jit(solution)/shard_map/all_to_all | solution.py:134
  24.0 7.2 %collective-permute-start = (bf16[16,4,8,128]{3,2,1,0:T(8,128)(2,1)S(1)}, bf16[16,4,8,128]{3,2,1,0:T(8,128)(2,1)S(1)}, u32[]{:S(2)}, u32[]{:S(2)}) collective-permute-start(bf16[16,4,8,128]{3,2,1,0:T(8,128)(2,1)S(1)} %get-tuple-element.24), channel_id=1, source_target_pairs={{0,16},{16,32},{32,48},{48,64},{64,80},{80,96},{96,112},{112,128},... | collective-permute-start | bytes 393224 | tf_op jit(solution)/shard_map/ppermute | solution.py:165
  27.2 12.3 %collective-permute-start.1 = (bf16[16,4,8,128]{3,2,1,0:T(8,128)(2,1)S(1)}, bf16[16,4,8,128]{3,2,1,0:T(8,128)(2,1)S(1)}, u32[]{:S(2)}, u32[]{:S(2)}) collective-permute-start(bf16[16,4,8,128]{3,2,1,0:T(8,128)(2,1)S(1)} %get-tuple-element.23), channel_id=1, source_target_pairs={{16,0},{32,16},{48,32},{64,48},{80,64},{96,80},{112,96},{128,112},... | collective-permute-start | bytes 393224 | tf_op jit(solution)/shard_map/ppermute | solution.py:166
  31.2 8.3 %copy-start.2 = (bf16[16,2,4,8,128]{4,3,2,1,0:T(8,128)(2,1)}, bf16[16,2,4,8,128]{4,3,2,1,0:T(8,128)(2,1)S(1)}, u32[]{:S(2)}) copy-start(bf16[16,2,4,8,128]{4,3,2,1,0:T(8,128)(2,1)S(1)} %all-to-all-done.1.g_ref) | copy-start | bytes 786436
  31.2 8.3 %copy-start.7 = (bf16[16,4,8,128]{3,2,1,0:T(8,128)(2,1)}, bf16[16,4,8,128]{3,2,1,0:T(8,128)(2,1)S(1)}, u32[]{:S(2)}) copy-start(bf16[16,4,8,128]{3,2,1,0:T(8,128)(2,1)S(1)} %collective-permute-done.before_ref.xb_ref) | copy-start | bytes 393220
  39.5 0.7 copy-start.8
  40.2 7.8 %copy-start.6 = (bf16[3,3,3,128,8]{3,4,2,1,0:T(8,128)(2,1)S(1)}, bf16[3,3,3,128,8]{3,4,2,1,0:T(8,128)(2,1)}, u32[]{:S(2)}) copy-start(bf16[3,3,3,128,8]{3,4,2,1,0:T(8,128)(2,1)} %param.4) | copy-start | bytes 165892
  43.9 9.2 %copy-start.4 = (f32[8,27,8,128]{3,2,1,0:T(8,128)S(1)}, f32[8,27,8,128]{3,2,1,0:T(8,128)}, u32[]{:S(2)}) copy-start(f32[8,27,8,128]{3,2,1,0:T(8,128)} %get-tuple-element.12) | copy-start | bytes 2654212
  43.9 9.2 %collective-permute-start.2 = (f32[8,27,8,128]{3,2,1,0:T(8,128)}, f32[8,27,8,128]{3,2,1,0:T(8,128)S(1)}, u32[]{:S(2)}, u32[]{:S(2)}) collective-permute-start(f32[8,27,8,128]{3,2,1,0:T(8,128)} %get-tuple-element.13), channel_id=1, source_target_pairs={{0,1},{1,0},{2,3},{3,2},{4,5},{5,4},{6,7},{7,6},{8,9},{9,8},{10,11... | collective-permute-start | bytes 2654216 | tf_op jit(solution)/shard_map/ppermute | solution.py:187
  48.8 12.1 %all-to-all-start.3 = ((bf16[8,27,8,128]{3,2,1,0:T(8,128)(2,1)}), bf16[8,27,8,128]{3,2,1,0:T(8,128)(2,1)S(1)}, u32[]{:S(2)}, u32[]{:S(2)}) async-start(bf16[8,27,8,128]{3,2,1,0:T(8,128)(2,1)} %broadcast_in_dim.4), calls=%async_computation.3 | async-start | bytes 884736 | tf_op jit(solution)/shard_map/all_to_all | solution.py:134
  54.1 14.1 %copy-start.3 = (bf16[16,2,4,8,128]{4,3,2,1,0:T(8,128)(2,1)S(1)}, bf16[16,2,4,8,128]{4,3,2,1,0:T(8,128)(2,1)}, u32[]{:S(2)}) copy-start(bf16[16,2,4,8,128]{4,3,2,1,0:T(8,128)(2,1)} %copy-done.2) | copy-start | bytes 786436
  61.0 4.3 %copy-start = (bf16[8,27,8,128]{3,2,1,0:T(8,128)(2,1)}, bf16[8,27,8,128]{3,2,1,0:T(8,128)(2,1)S(1)}, u32[]{:S(2)}) copy-start(bf16[8,27,8,128]{3,2,1,0:T(8,128)(2,1)S(1)} %all-to-all-done.3.mine_ref) | copy-start | bytes 1327108
  61.0 25.0 %all-to-all-start.2 = ((f32[8,27,8,128]{3,2,1,0:T(8,128)}), f32[8,27,8,128]{3,2,1,0:T(8,128)S(1)}, u32[]{:S(2)}, u32[]{:S(2)}) async-start(f32[8,27,8,128]{3,2,1,0:T(8,128)} %add.5), calls=%async_computation.2 | async-start | bytes 1769472 | tf_op jit(solution)/shard_map/all_to_all | solution.py:134
  65.2 9.3 %collective-permute-start.5 = (bf16[8,27,8,128]{3,2,1,0:T(8,128)(2,1)S(1)}, bf16[8,27,8,128]{3,2,1,0:T(8,128)(2,1)S(1)}, u32[]{:S(2)}, u32[]{:S(2)}) collective-permute-start(bf16[8,27,8,128]{3,2,1,0:T(8,128)(2,1)S(1)} %all-to-all-done.3.mine_ref), channel_id=1, source_target_pairs={{0,1},{1,0},{2,3},{3,2},{4,5},{5,4},{6,7},{7,6},{8,9},{9,8},{10,11... | collective-permute-start | bytes 1327112 | tf_op jit(solution)/shard_map/ppermute | solution.py:162
  68.2 9.7 %collective-permute-start.3 = (bf16[16,4,8,128]{3,2,1,0:T(8,128)(2,1)S(1)}, bf16[16,4,8,128]{3,2,1,0:T(8,128)(2,1)S(1)}, u32[]{:S(2)}, u32[]{:S(2)}) collective-permute-start(bf16[16,4,8,128]{3,2,1,0:T(8,128)(2,1)S(1)} %get-tuple-element.22), channel_id=1, source_target_pairs={{0,16},{16,32},{32,48},{48,64},{64,80},{80,96},{96,112},{112,128},... | collective-permute-start | bytes 393224 | tf_op jit(solution)/shard_map/ppermute | solution.py:167
  73.2 8.2 %collective-permute-start.4 = (bf16[16,4,8,128]{3,2,1,0:T(8,128)(2,1)S(1)}, bf16[16,4,8,128]{3,2,1,0:T(8,128)(2,1)S(1)}, u32[]{:S(2)}, u32[]{:S(2)}) collective-permute-start(bf16[16,4,8,128]{3,2,1,0:T(8,128)(2,1)S(1)} %get-tuple-element.21), channel_id=1, source_target_pairs={{16,0},{32,16},{48,32},{64,48},{80,64},{96,80},{112,96},{128,112},... | collective-permute-start | bytes 393224 | tf_op jit(solution)/shard_map/ppermute | solution.py:168
  74.5 0.8 copy-start.5
  78.0 3.4 %copy-start.9 = (bf16[16,4,8,128]{3,2,1,0:T(8,128)(2,1)}, bf16[16,4,8,128]{3,2,1,0:T(8,128)(2,1)S(1)}, u32[]{:S(2)}) copy-start(bf16[16,4,8,128]{3,2,1,0:T(8,128)(2,1)S(1)} %collective-permute-done.3.gb_ref) | copy-start | bytes 393220
  81.4 0.7 copy-start.10
  124.4 18.4 %all-to-all-start.4 = ((f32[16,2,2,2,8,128]{5,4,3,2,1,0:T(8,128)}), f32[16,2,2,2,8,128]{5,4,3,2,1,0:T(8,128)S(1)}, u32[]{:S(2)}, u32[]{:S(2)}) async-start(f32[16,2,2,2,8,128]{5,4,3,2,1,0:T(8,128)} %shard_map.61), calls=%async_computation.4 | async-start | bytes 1048576 | tf_op jit(solution)/shard_map/all_to_all | solution.py:134

commit v3 on v2

--- a/solution.py
+++ b/solution.py
@@ -30,15 +30,31 @@
     )(*ins)
 
 
-def pack_kernel(x_ref, o_ref):
-    n, nz, nr = o_ref.shape[:3]
+def pack_kernel(x_ref, g_ref, o_ref):
+    n, _, nz, nr = o_ref.shape[:4]
     rows = x_ref.shape[1]
     zero = jnp.zeros(x_ref.shape[2:], x_ref.dtype)
-    for z in range(nz):
-        for d in range(n):
+    for k, ref in enumerate((x_ref, g_ref)):
+        for z in range(nz):
+            for d in range(n):
+                for r in range(nr):
+                    h = d * (nr - 2) + r - 1
+                    o_ref[d, k, z, r] = ref[z, h] if 0 <= h < rows else zero
+
+
+def pack_more_kernel(w_ref, before_ref, after_ref, o_ref):
+    chips, total = o_ref.shape[:2]
+    taps = w_ref.shape[0]
+    rows = before_ref.shape[0]
+    nr = (total - taps) // 2
+    zero = jnp.zeros(w_ref.shape[1:], w_ref.dtype)
+    for q in range(chips):
+        for t in range(taps):
+            o_ref[q, t] = w_ref[t]
+        for p, ref in enumerate((before_ref, after_ref)):
             for r in range(nr):
-                h = d * (nr - 2) + r - 1
-                o_ref[d, z, r] = x_ref[z, h] if 0 <= h < rows else zero
+                h = q * (nr - 2) + r - 1
+                o_ref[q, taps + p * nr + r] = ref[h] if 0 <= h < rows else zero
 
 
 def shifted(value):
@@ -49,32 +65,49 @@
     return left.astype(BF), value.astype(BF), right.astype(BF)
 
 
-def block_of(ref, r, z=None):
-    n = ref.shape[0]
-    parts = [(ref[d, r] if z is None else ref[d, z, r]).astype(F32) for d in range(n)]
+def stack(parts):
+    return jnp.concatenate([p.astype(F32) for p in parts], 0)
+
+
+def by_core(first, mine, other):
+    parts = []
+    for m, o in zip(mine, other):
+        m, o = m.astype(F32), o.astype(F32)
+        parts += [jnp.where(first, m, o), jnp.where(first, o, m)]
     return jnp.concatenate(parts, 0)
 
 
-def build(own_ref, before_ref, after_ref, s_ref):
-    n, nz, nr, cg, w = own_ref.shape
-    nh, ch = nr - 2, n * cg
-    planes = [(before_ref, None)] + [(own_ref, z) for z in range(nz)] + [(after_ref, None)]
-    for p, (ref, z) in enumerate(planes):
+def build(planes, sizes, s_ref):
+    nr, ch, w = sizes
+    for p, plane in enumerate(planes):
         for r in range(nr):
-            for c, v in enumerate(shifted(block_of(ref, r, z))):
-                for h in range(nh):
+            for c, v in enumerate(shifted(plane(r))):
+                for h in range(nr - 2):
                     b = r - h
                     if 0 <= b < 3:
                         s_ref[p, pl.ds((3 * b + c) * ch, ch), pl.ds(h * w, w)] = v
 
 
-def wgrad_kernel(core_ref, x_ref, before_ref, after_ref, g_ref, keep_ref, send_ref, s_ref, t_ref, o_ref, sems):
-    n, nz, nr, cg, w = x_ref.shape
+def own_plane(own_ref, k, z):
+    return lambda r: stack([own_ref[d, k, z, r] for d in range(own_ref.shape[0])])
+
+
+def halo_plane(ref):
+    return lambda r: stack([ref[d, r] for d in range(ref.shape[0])])
+
+
+def x_planes(own_ref, before_ref, after_ref):
+    inner = [own_plane(own_ref, 0, z) for z in range(own_ref.shape[2])]
+    return [halo_plane(before_ref)] + inner + [halo_plane(after_ref)]
+
+
+def wgrad_kernel(core_ref, own_ref, before_ref, after_ref, keep_ref, send_ref, s_ref, t_ref, o_ref, sems):
+    n, _, nz, nr, cg, w = own_ref.shape
     nh, ch = nr - 2, n * cg
-    build(x_ref, before_ref, after_ref, s_ref)
+    build(x_planes(own_ref, before_ref, after_ref), (nr, ch, w), s_ref)
     for z in range(nz):
         for h in range(nh):
-            t_ref[z, :, pl.ds(h * w, w)] = block_of(g_ref, h + 1, z).astype(BF)
+            t_ref[z, :, pl.ds(h * w, w)] = own_plane(own_ref, 1, z)(h + 1).astype(BF)
     core = core_ref[0]
     for a in range(3):
         for b in range(3):
@@ -101,25 +134,31 @@
         copy.wait()
 
 
-def weights_kernel(core_ref, mine_ref, other_ref, wt_ref, wf_ref):
-    m, taps, _, ch = mine_ref.shape
-    first = core_ref[0] == 0
+def conv_kernel(core_ref, own_ref, before_ref, after_ref, mine_ref, other_ref, o_ref, s_ref, wt_ref, wf_ref):
+    n, _, nz, nr, cg, w = own_ref.shape
+    nh, ch = nr - 2, n * cg
+    chips, total = mine_ref.shape[:2]
+    taps = 27
+    span = (total - taps) // 2
+    core = core_ref[0]
+    first = core == 0
     for t in range(taps):
         a, bc = t // 9, t % 9
-        parts = []
-        for q in range(m):
-            mine, other = mine_ref[q, t].astype(F32), other_ref[q, t].astype(F32)
-            parts += [jnp.where(first, mine, other), jnp.where(first, other, mine)]
-        block = jnp.concatenate(parts, 0)
+        block = by_core(first, [mine_ref[q, t] for q in range(chips)], [other_ref[q, t] for q in range(chips)])
         wt_ref[a, :, pl.ds(bc * ch, ch)] = block.astype(BF)
         wf_ref[2 - a, :, pl.ds((8 - bc) * ch, ch)] = block.T.astype(BF)
 
-
-def conv_kernel(x_ref, xb_ref, xa_ref, g_ref, gb_ref, ga_ref, wt_ref, wf_ref, o_ref, s_ref):
-    n, nz, nr, cg, w = x_ref.shape
-    nh = nr - 2
-    for k, (refs, w_ref) in enumerate((((x_ref, xb_ref, xa_ref), wt_ref), ((g_ref, gb_ref, ga_ref), wf_ref))):
-        build(*refs, s_ref.at[k])
+    def g_halo(p):
+        def rows(r):
+            i = taps + p * span + r + core * nh
+            return by_core(first, [mine_ref[q, i] for q in range(chips)], [other_ref[q, i] for q in range(chips)])
+
+        return rows
+
+    g_planes = [g_halo(0)] + [own_plane(own_ref, 1, z) for z in range(nz)] + [g_halo(1)]
+    build(x_planes(own_ref, before_ref, after_ref), (nr, ch, w), s_ref.at[0])
+    build(g_planes, (nr, ch, w), s_ref.at[1])
+    for k, w_ref in enumerate((wt_ref, wf_ref)):
         for z in range(nz):
             total = None
             for a in range(3):
@@ -148,30 +187,24 @@
     down = [(j, i) for i, j in up]
     swap = [(0, 1), (1, 0)]
     sds = jax.ShapeDtypeStruct
-    packed = [sds((n, nz, nr, cg, w), BF)]
-
-    (px,) = call(pack_kernel, packed, [activations])
-    x = swap_all(px, FILT)
-    grad_out, px = lax.optimization_barrier((grad_out, px))
-    (pg,) = call(pack_kernel, packed, [grad_out])
-    g = swap_all(pg, FILT)
+    gb = lax.ppermute(grad_out[nz - 1], SPACE, up)
+    ga = lax.ppermute(grad_out[0], SPACE, down)
+    (packed,) = call(pack_kernel, [sds((n, 2, nz, nr, cg, w), BF)], [activations, grad_out])
+    own = swap_all(packed, FILT)
+    xb = lax.ppermute(own[:, 0, nz - 1], SPACE, up)
+    xa = lax.ppermute(own[:, 0, 0], SPACE, down)
 
     flat_w = weight.transpose(0, 1, 2, 4, 3).reshape(27, cg, ch)
-    flat_w, pg = lax.optimization_barrier((flat_w, pg))
-    mine = swap_all(jnp.broadcast_to(flat_w[None], (chips, 27, cg, ch)), CHIPS)
+    span = rows // chips + 2
+    (more,) = call(pack_more_kernel, [sds((chips, 27 + 2 * span, cg, ch), BF)], [flat_w, gb, ga])
+    mine = swap_all(more, CHIPS)
     other = lax.ppermute(mine, "core", swap)
-    wt, wf = call(weights_kernel, [sds((3, ch, 9 * ch), BF)] * 2, [core, mine, other], smem=1)
-
-    xb = lax.ppermute(x[:, nz - 1], SPACE, up)
-    xa = lax.ppermute(x[:, 0], SPACE, down)
-    gb = lax.ppermute(g[:, nz - 1], SPACE, up)
-    ga = lax.ppermute(g[:, 0], SPACE, down)
 
     any_spec = pl.BlockSpec(memory_space=pl.ANY)
     keep, send = pl.pallas_call(
         wgrad_kernel,
         out_shape=(sds((chips, 27, cg, ch), F32),) * 2,
-        in_specs=[pl.BlockSpec(memory_space=pltpu.SMEM)] + vmem_specs(4),
+        in_specs=[pl.BlockSpec(memory_space=pltpu.SMEM)] + vmem_specs(3),
         out_specs=(any_spec, any_spec),
         scratch_shapes=[
             pltpu.VMEM((nz + 2, 9 * ch, nh * w), BF),
@@ -183,15 +216,16 @@
             flops=2 * 27 * ch * ch * nz * nh * w, transcendentals=0, bytes_accessed=4 * 27 * ch * ch
         ),
         name="wgrad",
-    )(core, x, xb, xa, g)
+    )(core, own, xb, xa)
     pair = keep + lax.ppermute(send, "core", swap)
     group = swap_all(pair, CHIPS).reshape(chips, 27, cg, ch).sum(0)
 
     (blocks,) = call(
         conv_kernel,
         [sds((n, 2, nz, nh, cg, w), F32)],
-        [x, xb, xa, g, gb, ga, wt, wf],
-        scratch=[pltpu.VMEM((2, nz + 2, 9 * ch, nh * w), BF)],
+        [core, own, xb, xa, mine, other],
+        scratch=[pltpu.VMEM((2, nz + 2, 9 * ch, nh * w), BF)] + [pltpu.VMEM((3, ch, 9 * ch), BF)] * 2,
+        smem=1,
         flops=2 * 2 * 27 * ch * ch * nz * nh * w,
     )
     group, blocks = lax.optimization_barrier((group, blocks))

time: 145 us -> 135 us (0.931)
  waiting for transfers between devices: 35.9 us -> 21.4 us
  starting transfers between devices: 49.4 us -> 56.7 us
  Pallas kernels: 13.6 us -> 11.3 us
    all_to_all x5 -> x4, waiting for transfers between devices: 24.2 us -> 14.3 us  [swap_all(): return lax.all_to_all(array, axes, 0, 0, tiled=True)]
    ppermute x4, waiting for transfers between devices: 11.7 us -> 3.22 us  [the longest x1 1.28 us: step(): gb = lax.ppermute(grad_out[nz - 1], SPACE, up)]
    all_to_all x5 -> x4, starting transfers between devices: 31.6 us -> 35.9 us  [swap_all(): return lax.all_to_all(array, axes, 0, 0, tiled=True)]
    ppermute x4, starting transfers between devices: 10.7 us -> 14.2 us  [the longest x1 6.75 us: step(): xb = lax.ppermute(own[:, 0, nz - 1], SPACE, up)]
    pallas_call x4 -> x3, Pallas kernels: 9.92 us -> 7.63 us  [call(): pl.pallas_call(kernel, out_shape=tuple(outs), in_specs=specs, out_specs=t...]
    ppermute x1, waiting for transfers between devices: 0.01 us -> 2.24 us  [step(): pair = keep + lax.ppermute(send, 'core', swap)]
    ppermute x1, waiting for transfers between devices: 0.01 us -> 1.68 us  [step(): other = lax.ppermute(mine, 'core', swap)]
  transfers between devices with their start and end apart: 11 -> 10, of which waited for: 6 -> 8; matrix products, arithmetic and copies ran while one was open for 2% -> 2% of each run, Pallas kernels for 6% -> 7%
where the time goes in v3:
time: 135 us; the launch traced here: 134 us
  starting transfers between devices  56.7 us (42%)
  blocking collectives  37.6 us (28%)
  waiting for transfers between devices  21.4 us (16%)
  Pallas kernels  11.3 us (8%)
  local copies, waits for them, and re-layouts  4.31 us (3%)
  other arithmetic  2.29 us (2%)
    all_to_all x2, blocking collectives, swap_all(): return lax.all_to_all(array, axes, 0, 0, tiled=True)  37.6 us
    all_to_all x4, starting transfers between devices, swap_all(): return lax.all_to_all(array, axes, 0, 0, tiled=True)  35.9 us
    all_to_all x4, waiting for transfers between devices, swap_all(): return lax.all_to_all(array, axes, 0, 0, tiled=True)  14.3 us
    pallas_call x3, Pallas kernels, call(): pl.pallas_call(kernel, out_shape=tuple(outs), in_specs=specs, out_specs=t...  7.63 us
    ppermute x1, starting transfers between devices, step(): xb = lax.ppermute(own[:, 0, nz - 1], SPACE, up)  6.75 us
    ppermute x1, starting transfers between devices, step(): gb = lax.ppermute(grad_out[nz - 1], SPACE, up)  4.89 us
    ppermute x1, starting transfers between devices, step(): pair = keep + lax.ppermute(send, 'core', swap)  4.01 us
    pallas_call x1, Pallas kernels, step(): pl.pallas_call(wgrad_kernel, out_shape=(sds((chips, 27, cg, ch), F32),) *...  3.66 us
  transfers between devices with their start and end apart: 10, of which 8 were waited for; matrix products, arithmetic and copies ran while one was open for 2% of the time, Pallas kernels for 7%

profile of v3, /device:TPU:1, one launch (start us, length us, event | category | flops | bytes accessed | tf_op | source)
XLA Modules:
  0.0 134.4 jit_solution(13320922126206929034)
XLA Ops:
  0.6 1.8 %shard_map.58 = bf16[16,2,2,4,8,128]{5,4,3,2,1,0:T(8,128)(2,1)} custom-call(bf16[2,32,8,128]{3,2,1,0:T(8,128)(2,1)} %x_ref.1, bf16[2,32,8,128]{3,2,1,0:T(8,128)(2,1)} %g_ref.1), custom_call_target="tpu_custom_call" | custom-call | bytes 786432 | tf_op jit(solution)/shard_map/pallas_call | solution.py:23
  2.5 10.3 %all-to-all-start = ((bf16[16,2,2,4,8,128]{5,4,3,2,1,0:T(8,128)(2,1)}), bf16[16,2,2,4,8,128]{5,4,3,2,1,0:T(8,128)(2,1)S(1)}, u32[]{:S(2)}, u32[]{:S(2)}) async-start(bf16[16,2,2,4,8,128]{5,4,3,2,1,0:T(8,128)(2,1)} %shard_map.58), calls=%async_computation | async-start | bytes 1048576 | tf_op jit(solution)/shard_map/all_to_all | solution.py:173
  12.8 1.3 collective-permute-start.4
  14.1 4.9 %collective-permute-start.3 = (bf16[32,8,128]{2,1,0:T(8,128)(2,1)S(1)}, bf16[32,8,128]{2,1,0:T(8,128)(2,1)S(1)}, u32[]{:S(2)}, u32[]{:S(2)}) collective-permute-start(bf16[32,8,128]{2,1,0:T(8,128)(2,1)S(1)} %get-tuple-element.16), channel_id=1, source_target_pairs={{0,16},{16,32},{32,48},{48,64},{64,80},{80,96},{96,112},{112,128},... | collective-permute-start | bytes 196616 | tf_op jit(solution)/shard_map/ppermute | solution.py:190
  19.0 0.0 collective-permute-done.4.after_ref
  19.0 1.3 collective-permute-done.3.before_ref
  20.3 0.6 copy-done.4
  21.0 1.8 %shard_map.59 = bf16[8,39,8,128]{3,2,1,0:T(8,128)(2,1)} custom-call(bf16[27,8,128]{2,1,0:T(8,128)(2,1)} %bitcast.26, bf16[32,8,128]{2,1,0:T(8,128)(2,1)} %copy-done.4, bf16[32,8,128]{2,1,0:T(8,128)(2,1)} %copy-done.3), custom_call_target="tpu_custom_call" | custom-call | bytes 825344 | tf_op jit(solution)/shard_map/pallas_call | solution.py:23
  22.8 1.2 all-to-all-done.own_ref
  23.9 7.0 %all-to-all-start.2 = ((bf16[8,39,8,128]{3,2,1,0:T(8,128)(2,1)}), bf16[8,39,8,128]{3,2,1,0:T(8,128)(2,1)S(1)}, u32[]{:S(2)}, u32[]{:S(2)}) async-start(bf16[8,39,8,128]{3,2,1,0:T(8,128)(2,1)} %shard_map.59), calls=%async_computation.2 | async-start | bytes 1277952 | tf_op jit(solution)/shard_map/all_to_all | solution.py:173
  31.0 1.3 collective-permute-start.1
  32.3 6.8 %collective-permute-start = (bf16[16,4,8,128]{3,2,1,0:T(8,128)(2,1)S(1)}, bf16[16,4,8,128]{3,2,1,0:T(8,128)(2,1)S(1)}, u32[]{:S(2)}, u32[]{:S(2)}) collective-permute-start(bf16[16,4,8,128]{3,2,1,0:T(8,128)(2,1)S(1)} %get-tuple-element.14), channel_id=1, source_target_pairs={{0,16},{16,32},{32,48},{48,64},{64,80},{80,96},{96,112},{112,128},... | collective-permute-start | bytes 393224 | tf_op jit(solution)/shard_map/ppermute | solution.py:194
  39.0 0.8 collective-permute-done.1.after_ref
  39.8 1.2 collective-permute-done.before_ref
  40.9 0.7 copy-done.7
  41.6 3.7 %wgrad.1 = (f32[8,27,8,128]{3,2,1,0:T(8,128)}, f32[8,27,8,128]{3,2,1,0:T(8,128)}) custom-call(s32[1]{0:T(128)} %bitcast.core_ref, bf16[16,2,2,4,8,128]{5,4,3,2,1,0:T(8,128)(2,1)} %copy-done, bf16[16,4,8,128]{3,2,1,0:T(8,128)(2,1)} %copy-done.7, bf16[16,4,8,128]{3,2,1,0:T(8,128)(2,1)} %copy-done.6), custom_call_target="tpu_custom_call" | custom-call | flops 452984832 | bytes 1769472 | tf_op jit(solution)/shard_map/wgrad/pallas_call | solution.py:204
  45.3 4.0 %collective-permute-start.2 = (f32[8,27,8,128]{3,2,1,0:T(8,128)}, f32[8,27,8,128]{3,2,1,0:T(8,128)S(1)}, u32[]{:S(2)}, u32[]{:S(2)}) collective-permute-start(f32[8,27,8,128]{3,2,1,0:T(8,128)} %get-tuple-element.8), channel_id=1, source_target_pairs={{0,1},{1,0},{2,3},{3,2},{4,5},{5,4},{6,7},{7,6},{8,9},{9,8},{10,11... | collective-permute-start | bytes 2654216 | tf_op jit(solution)/shard_map/ppermute | solution.py:220
  49.3 2.2 %collective-permute-done.2 = f32[8,27,8,128]{3,2,1,0:T(8,128)S(1)} collective-permute-done((f32[8,27,8,128]{3,2,1,0:T(8,128)}, f32[8,27,8,128]{3,2,1,0:T(8,128)S(1)}, u32[]{:S(2)}, u32[]{:S(2)}) %collective-permute-start.2) | collective-permute-done | bytes 884768 | tf_op jit(solution)/shard_map/ppermute | solution.py:220
  51.5 2.2 %add.5 = f32[8,27,8,128]{3,2,1,0:T(8,128)} add(f32[8,27,8,128]{3,2,1,0:T(8,128)} %get-tuple-element.7, f32[8,27,8,128]{3,2,1,0:T(8,128)S(1)} %collective-permute-done.2) | non-fusion elementwise | flops 221184 | bytes 2654208 | tf_op jit(solution)/shard_map/add | solution.py:220
  53.7 11.6 %all-to-all-start.1 = ((f32[8,27,8,128]{3,2,1,0:T(8,128)}), f32[8,27,8,128]{3,2,1,0:T(8,128)S(1)}, u32[]{:S(2)}, u32[]{:S(2)}) async-start(f32[8,27,8,128]{3,2,1,0:T(8,128)} %add.5), calls=%async_computation.1 | async-start | bytes 1769472 | tf_op jit(solution)/shard_map/all_to_all | solution.py:173
  65.3 2.6 %collective-permute-start.5 = (bf16[8,39,8,128]{3,2,1,0:T(8,128)(2,1)S(1)}, bf16[8,39,8,128]{3,2,1,0:T(8,128)(2,1)S(1)}, u32[]{:S(2)}, u32[]{:S(2)}) collective-permute-start(bf16[8,39,8,128]{3,2,1,0:T(8,128)(2,1)S(1)} %all-to-all-done.2.mine_ref), channel_id=1, source_target_pairs={{0,1},{1,0},{2,3},{3,2},{4,5},{5,4},{6,7},{7,6},{8,9},{9,8},{10,11... | collective-permute-start | bytes 1916936 | tf_op jit(solution)/shard_map/ppermute | solution.py:201
  67.9 1.7 %collective-permute-done.5.other_ref = bf16[8,39,8,128]{3,2,1,0:T(8,128)(2,1)S(1)} collective-permute-done((bf16[8,39,8,128]{3,2,1,0:T(8,128)(2,1)S(1)}, bf16[8,39,8,128]{3,2,1,0:T(8,128)(2,1)S(1)}, u32[]{:S(2)}, u32[]{:S(2)}) %collective-permute-start.5) | collective-permute-done | bytes 639008 | tf_op jit(solution)/shard_map/ppermute | solution.py:201
  69.6 0.8 copy-done.5
  70.4 4.0 %shard_map.60 = f32[16,2,2,2,8,128]{5,4,3,2,1,0:T(8,128)} custom-call(s32[1]{0:T(128)} %bitcast.core_ref, bf16[16,2,2,4,8,128]{5,4,3,2,1,0:T(8,128)(2,1)} %copy-done, bf16[16,4,8,128]{3,2,1,0:T(8,128)(2,1)} %copy-done.7, bf16[16,4,8,128]{3,2,1,0:T(8,128)(2,1)} %copy-done.6, bf16[8,39,8,128]{3,2,1,0:T(8,128)(2,1)} %copy-done.1, bf16[8,39,8,128]{3,2,1,0:T(8,128)(2,1)} %copy-done.5), custom_call_target="tpu_custom_call" | custom-call | flops 905969664 | bytes 2588676 | tf_op jit(solution)/shard_map/pallas_call | solution.py:23
  74.4 4.1 %all-to-all-done.1 = f32[8,27,8,128]{3,2,1,0:T(8,128)S(1)} async-done(((f32[8,27,8,128]{3,2,1,0:T(8,128)}), f32[8,27,8,128]{3,2,1,0:T(8,128)S(1)}, u32[]{:S(2)}, u32[]{:S(2)}) %all-to-all-start.1) | async-done | bytes 884768 | tf_op jit(solution)/shard_map/all_to_all | solution.py:173
  78.6 23.1 %all_to_all.30 = f32[32,8,128]{2,1,0:T(8,128)S(1)} all-to-all(f32[32,8,128]{2,1,0:T(8,128)S(1)} %pad.4), channel_id=1, replica_groups=mesh['y'=8,'zh'=4,'zl'=2,'x'=4,'core'=2] {'y','zh'}, dimensions={0} | all-to-all | bytes 262144 | tf_op jit(solution)/shard_map/all_to_all | solution.py:173
  101.8 14.5 %all_to_all.31 = f32[32,8,128]{2,1,0:T(8,128)S(1)} all-to-all(f32[32,8,128]{2,1,0:T(8,128)S(1)} %broadcast_in_dim.2), channel_id=1, replica_groups=mesh['y'=8,'zh'=4,'zl'=2,'x'=4,'core'=2] {'y','zh'}, dimensions={0} | all-to-all | bytes 262144 | tf_op jit(solution)/shard_map/all_to_all | solution.py:173
  116.3 7.0 %all-to-all-start.3 = ((f32[16,2,2,2,8,128]{5,4,3,2,1,0:T(8,128)}), f32[16,2,2,2,8,128]{5,4,3,2,1,0:T(8,128)S(1)}, u32[]{:S(2)}, u32[]{:S(2)}) async-start(f32[16,2,2,2,8,128]{5,4,3,2,1,0:T(8,128)} %shard_map.60), calls=%async_computation.3 | async-start | bytes 1048576 | tf_op jit(solution)/shard_map/all_to_all | solution.py:173
  123.3 0.7 slice.34
  123.9 9.0 %all-to-all-done.3 = f32[16,2,2,2,8,128]{5,4,3,2,1,0:T(8,128)S(1)} async-done(((f32[16,2,2,2,8,128]{5,4,3,2,1,0:T(8,128)}), f32[16,2,2,2,8,128]{5,4,3,2,1,0:T(8,128)S(1)}, u32[]{:S(2)}, u32[]{:S(2)}) %all-to-all-start.3) | async-done | bytes 524320 | tf_op jit(solution)/shard_map/all_to_all | solution.py:173
  133.0 0.7 copy.21
  133.7 0.7 copy.20
  (22 shorter events, 0.2 us)
Async XLA Ops:
  2.5 10.3 %copy-start.2 = (bf16[2,32,8,128]{3,2,1,0:T(8,128)(2,1)S(1)}, bf16[2,32,8,128]{3,2,1,0:T(8,128)(2,1)}, u32[]{:S(2)}) copy-start(bf16[2,32,8,128]{3,2,1,0:T(8,128)(2,1)} %g_ref.1) | copy-start | bytes 393220
  2.5 21.5 %all-to-all-start = ((bf16[16,2,2,4,8,128]{5,4,3,2,1,0:T(8,128)(2,1)}), bf16[16,2,2,4,8,128]{5,4,3,2,1,0:T(8,128)(2,1)S(1)}, u32[]{:S(2)}, u32[]{:S(2)}) async-start(bf16[16,2,2,4,8,128]{5,4,3,2,1,0:T(8,128)(2,1)} %shard_map.58), calls=%async_computation | async-start | bytes 1048576 | tf_op jit(solution)/shard_map/all_to_all | solution.py:173
  12.8 6.2 %collective-permute-start.4 = (bf16[32,8,128]{2,1,0:T(8,128)(2,1)S(1)}, bf16[32,8,128]{2,1,0:T(8,128)(2,1)S(1)}, u32[]{:S(2)}, u32[]{:S(2)}) collective-permute-start(bf16[32,8,128]{2,1,0:T(8,128)(2,1)S(1)} %get-tuple-element.15), channel_id=1, source_target_pairs={{16,0},{32,16},{48,32},{64,48},{80,64},{96,80},{112,96},{128,112},... | collective-permute-start | bytes 196616 | tf_op jit(solution)/shard_map/ppermute | solution.py:191
  14.1 6.2 %collective-permute-start.3 = (bf16[32,8,128]{2,1,0:T(8,128)(2,1)S(1)}, bf16[32,8,128]{2,1,0:T(8,128)(2,1)S(1)}, u32[]{:S(2)}, u32[]{:S(2)}) collective-permute-start(bf16[32,8,128]{2,1,0:T(8,128)(2,1)S(1)} %get-tuple-element.16), channel_id=1, source_target_pairs={{0,16},{16,32},{32,48},{48,64},{64,80},{80,96},{96,112},{112,128},... | collective-permute-start | bytes 196616 | tf_op jit(solution)/shard_map/ppermute | solution.py:190
  19.0 1.3 copy-start.3
  20.3 0.6 copy-start.4
  23.9 7.0 %copy-start = (bf16[16,2,2,4,8,128]{5,4,3,2,1,0:T(8,128)(2,1)}, bf16[16,2,2,4,8,128]{5,4,3,2,1,0:T(8,128)(2,1)S(1)}, u32[]{:S(2)}) copy-start(bf16[16,2,2,4,8,128]{5,4,3,2,1,0:T(8,128)(2,1)S(1)} %all-to-all-done.own_ref) | copy-start | bytes 1572868
  23.9 29.8 %all-to-all-start.2 = ((bf16[8,39,8,128]{3,2,1,0:T(8,128)(2,1)}), bf16[8,39,8,128]{3,2,1,0:T(8,128)(2,1)S(1)}, u32[]{:S(2)}, u32[]{:S(2)}) async-start(bf16[8,39,8,128]{3,2,1,0:T(8,128)(2,1)} %shard_map.59), calls=%async_computation.2 | async-start | bytes 1277952 | tf_op jit(solution)/shard_map/all_to_all | solution.py:173
  31.0 8.8 %collective-permute-start.1 = (bf16[16,4,8,128]{3,2,1,0:T(8,128)(2,1)S(1)}, bf16[16,4,8,128]{3,2,1,0:T(8,128)(2,1)S(1)}, u32[]{:S(2)}, u32[]{:S(2)}) collective-permute-start(bf16[16,4,8,128]{3,2,1,0:T(8,128)(2,1)S(1)} %get-tuple-element.13), channel_id=1, source_target_pairs={{16,0},{32,16},{48,32},{64,48},{80,64},{96,80},{112,96},{128,112},... | collective-permute-start | bytes 393224 | tf_op jit(solution)/shard_map/ppermute | solution.py:195
  32.3 8.7 %collective-permute-start = (bf16[16,4,8,128]{3,2,1,0:T(8,128)(2,1)S(1)}, bf16[16,4,8,128]{3,2,1,0:T(8,128)(2,1)S(1)}, u32[]{:S(2)}, u32[]{:S(2)}) collective-permute-start(bf16[16,4,8,128]{3,2,1,0:T(8,128)(2,1)S(1)} %get-tuple-element.14), channel_id=1, source_target_pairs={{0,16},{16,32},{32,48},{48,64},{64,80},{80,96},{96,112},{112,128},... | collective-permute-start | bytes 393224 | tf_op jit(solution)/shard_map/ppermute | solution.py:194
  39.8 1.2 copy-start.6
  40.9 0.7 copy-start.7
  45.3 6.3 %collective-permute-start.2 = (f32[8,27,8,128]{3,2,1,0:T(8,128)}, f32[8,27,8,128]{3,2,1,0:T(8,128)S(1)}, u32[]{:S(2)}, u32[]{:S(2)}) collective-permute-start(f32[8,27,8,128]{3,2,1,0:T(8,128)} %get-tuple-element.8), channel_id=1, source_target_pairs={{0,1},{1,0},{2,3},{3,2},{4,5},{5,4},{6,7},{7,6},{8,9},{9,8},{10,11... | collective-permute-start | bytes 2654216 | tf_op jit(solution)/shard_map/ppermute | solution.py:220
  53.7 11.6 %copy-start.1 = (bf16[8,39,8,128]{3,2,1,0:T(8,128)(2,1)}, bf16[8,39,8,128]{3,2,1,0:T(8,128)(2,1)S(1)}, u32[]{:S(2)}) copy-start(bf16[8,39,8,128]{3,2,1,0:T(8,128)(2,1)S(1)} %all-to-all-done.2.mine_ref) | copy-start | bytes 1916932
  53.7 24.8 %all-to-all-start.1 = ((f32[8,27,8,128]{3,2,1,0:T(8,128)}), f32[8,27,8,128]{3,2,1,0:T(8,128)S(1)}, u32[]{:S(2)}, u32[]{:S(2)}) async-start(f32[8,27,8,128]{3,2,1,0:T(8,128)} %add.5), calls=%async_computation.1 | async-start | bytes 1769472 | tf_op jit(solution)/shard_map/all_to_all | solution.py:173
  65.3 4.2 %collective-permute-start.5 = (bf16[8,39,8,128]{3,2,1,0:T(8,128)(2,1)S(1)}, bf16[8,39,8,128]{3,2,1,0:T(8,128)(2,1)S(1)}, u32[]{:S(2)}, u32[]{:S(2)}) collective-permute-start(bf16[8,39,8,128]{3,2,1,0:T(8,128)(2,1)S(1)} %all-to-all-done.2.mine_ref), channel_id=1, source_target_pairs={{0,1},{1,0},{2,3},{3,2},{4,5},{5,4},{6,7},{7,6},{8,9},{9,8},{10,11... | collective-permute-start | bytes 1916936 | tf_op jit(solution)/shard_map/ppermute | solution.py:201
  69.6 0.8 copy-start.5
  116.3 16.7 %all-to-all-start.3 = ((f32[16,2,2,2,8,128]{5,4,3,2,1,0:T(8,128)}), f32[16,2,2,2,8,128]{5,4,3,2,1,0:T(8,128)S(1)}, u32[]{:S(2)}, u32[]{:S(2)}) async-start(f32[16,2,2,2,8,128]{5,4,3,2,1,0:T(8,128)} %shard_map.60), calls=%async_computation.3 | async-start | bytes 1048576 | tf_op jit(solution)/shard_map/all_to_all | solution.py:173

commit v4 on v3

--- a/solution.py
+++ b/solution.py
@@ -134,13 +134,19 @@
         copy.wait()
 
 
-def conv_kernel(core_ref, own_ref, before_ref, after_ref, mine_ref, other_ref, o_ref, s_ref, wt_ref, wf_ref):
+def place_of(index):
+    return index >> 3, (index >> 1) & 3, index & 1
+
+
+def conv_kernel(
+    f_ref, own_ref, before_ref, after_ref, mine_ref, other_ref, keep_ref, send_ref, s_ref, wt_ref, wf_ref, o_ref, sems
+):
     n, _, nz, nr, cg, w = own_ref.shape
     nh, ch = nr - 2, n * cg
     chips, total = mine_ref.shape[:2]
     taps = 27
     span = (total - taps) // 2
-    core = core_ref[0]
+    zl, x, core = place_of(f_ref[0])
     first = core == 0
     for t in range(taps):
         a, bc = t // 9, t % 9
@@ -165,8 +171,30 @@
                 part = jnp.dot(w_ref[a], s_ref[k, z + a], preferred_element_type=F32)
                 total = part if total is None else total + part
             for d in range(n):
+                dzl, dx, dcore = place_of(d)
+                slot = (dcore ^ core, dzl ^ zl, (dx - x) & 3)
                 for h in range(nh):
-                    o_ref[d, k, z, h] = total[d * cg : (d + 1) * cg, h * w : (h + 1) * w]
+                    o_ref[(*slot, k, z, h)] = total[d * cg : (d + 1) * cg, h * w : (h + 1) * w]
+    copies = [
+        pltpu.make_async_copy(o_ref.at[1], send_ref, sems.at[1]),
+        pltpu.make_async_copy(o_ref.at[0], keep_ref, sems.at[0]),
+    ]
+    for copy in copies:
+        copy.start()
+    for copy in copies:
+        copy.wait()
+
+
+def place_kernel(f_ref, *refs):
+    parts, outs = refs[:-2], refs[-2:]
+    zl, x, core = place_of(f_ref[0])
+    for dx, ref in enumerate(parts):
+        for j in range(ref.shape[0]):
+            source = ((zl ^ (j >> 1)) * 4 + ((x - dx) & 3)) * 2 + (core ^ (j & 1))
+            for k, o_ref in enumerate(outs):
+                for z in range(ref.shape[2]):
+                    for h in range(ref.shape[3]):
+                        o_ref[z, source * ref.shape[3] + h] = ref[j, k, z, h]
 
 
 def swap_all(array, axes):
@@ -218,26 +246,41 @@
         name="wgrad",
     )(core, own, xb, xa)
     pair = keep + lax.ppermute(send, "core", swap)
-    group = swap_all(pair, CHIPS).reshape(chips, 27, cg, ch).sum(0)
-
-    (blocks,) = call(
+    pieces = swap_all(pair, CHIPS).reshape(chips, 27, cg, ch)
+    group = pieces.sum(0)
+
+    index = lax.axis_index(FILT).astype(jnp.int32).reshape(1)
+    keep, send = pl.pallas_call(
         conv_kernel,
-        [sds((n, 2, nz, nh, cg, w), F32)],
-        [core, own, xb, xa, mine, other],
-        scratch=[pltpu.VMEM((2, nz + 2, 9 * ch, nh * w), BF)] + [pltpu.VMEM((3, ch, 9 * ch), BF)] * 2,
-        smem=1,
-        flops=2 * 2 * 27 * ch * ch * nz * nh * w,
-    )
-    group, blocks = lax.optimization_barrier((group, blocks))
-    back = swap_all(blocks, FILT)
-    back = back.transpose(1, 2, 0, 3, 4, 5).reshape(2, nz, rows, cg, w)
+        out_shape=(sds((2, 4, 2, nz, nh, cg, w), F32),) * 2,
+        in_specs=[pl.BlockSpec(memory_space=pltpu.SMEM)] + vmem_specs(5),
+        out_specs=(any_spec, any_spec),
+        scratch_shapes=[
+            pltpu.VMEM((2, nz + 2, 9 * ch, nh * w), BF),
+            pltpu.VMEM((3, ch, 9 * ch), BF),
+            pltpu.VMEM((3, ch, 9 * ch), BF),
+            pltpu.VMEM((2, 2, 4, 2, nz, nh, cg, w), F32),
+            pltpu.SemaphoreType.DMA((2,)),
+        ],
+        cost_estimate=pl.CostEstimate(
+            flops=4 * 27 * ch * ch * nz * nh * w, transcendentals=0, bytes_accessed=4 * 27 * ch * ch
+        ),
+        name="conv",
+    )(index, own, xb, xa, mine, other)
+    got = lax.ppermute(send, "core", swap)
+    far = lax.ppermute(jnp.stack([keep[1], got[1]]), "zl", swap)
+    blocks = [jnp.stack([keep[0, j], got[0, j], far[0, j], far[1, j]]) for j in range(4)]
+    blocks = blocks[:1] + [
+        lax.ppermute(blocks[j], "x", [(i, (i + j) % 4) for i in range(4)]) for j in range(1, 4)
+    ]
+    output, grad_in = call(place_kernel, [sds((nz, rows, cg, w), F32)] * 2, [index, *blocks], smem=1)
 
     padded = jnp.pad(group, ((0, ns - 27), (0, 0), (0, 0)))
     shares = swap_all(padded, SPACE)
     tap = shares.sum(0) * norm
     taps = swap_all(jnp.broadcast_to(tap[None], (ns, cg, ch)), SPACE)
     weight_grad = taps[:27].reshape(3, 3, 3, cg, ch).transpose(0, 1, 2, 4, 3)
-    return back[0], back[1], weight_grad
+    return output, grad_in, weight_grad
 
 
 def solution(mesh):

time: 135 us -> 123 us (0.911)
  the two profiles are of different devices: /device:TPU:1 before, /device:TPU:6 now
where the time goes in v4:
time: 123 us; the launch traced here: 122 us
  starting transfers between devices  79.5 us (65%)
  waiting for transfers between devices  19.4 us (16%)
  Pallas kernels  13.2 us (11%)
  local copies, waits for them, and re-layouts  5.78 us (5%)
  other arithmetic  2.97 us (2%)
    all_to_all x5, starting transfers between devices, swap_all(): return lax.all_to_all(array, axes, 0, 0, tiled=True)  45.5 us
    all_to_all x5, waiting for transfers between devices, swap_all(): return lax.all_to_all(array, axes, 0, 0, tiled=True)  9.14 us
    ppermute x3, starting transfers between devices, step(): lax.ppermute(blocks[j], 'x', [(i, (i + j) % 4) for i in range(4)])  9.1 us
    ppermute x1, starting transfers between devices, step(): xb = lax.ppermute(own[:, 0, nz - 1], SPACE, up)  7.03 us
    pallas_call x3, Pallas kernels, call(): pl.pallas_call(kernel, out_shape=tuple(outs), in_specs=specs, out_specs=t...  5.54 us
    ppermute x1, starting transfers between devices, step(): gb = lax.ppermute(grad_out[nz - 1], SPACE, up)  5.45 us
    ppermute x3, waiting for transfers between devices, step(): lax.ppermute(blocks[j], 'x', [(i, (i + j) % 4) for i in range(4)])  4.95 us
    pallas_call x1, Pallas kernels, step(): pl.pallas_call(conv_kernel, out_shape=(sds((2, 4, 2, nz, nh, cg, w), F32)...  3.95 us
  transfers between devices with their start and end apart: 16, of which 9 were waited for; matrix products, arithmetic and copies ran while one was open for 4% of the time, Pallas kernels for 9%

profile of v4, /device:TPU:6, one launch (start us, length us, event | category | flops | bytes accessed | tf_op | source)
XLA Modules:
  0.0 121.7 jit_solution(14146822935555843509)
XLA Ops:
  0.6 1.8 %shard_map.58 = bf16[16,2,2,4,8,128]{5,4,3,2,1,0:T(8,128)(2,1)} custom-call(bf16[2,32,8,128]{3,2,1,0:T(8,128)(2,1)} %x_ref.1, bf16[2,32,8,128]{3,2,1,0:T(8,128)(2,1)} %g_ref.1), custom_call_target="tpu_custom_call" | custom-call | bytes 786432 | tf_op jit(solution)/shard_map/pallas_call | solution.py:23
  2.5 9.3 %all-to-all-start = ((bf16[16,2,2,4,8,128]{5,4,3,2,1,0:T(8,128)(2,1)}), bf16[16,2,2,4,8,128]{5,4,3,2,1,0:T(8,128)(2,1)S(1)}, u32[]{:S(2)}, u32[]{:S(2)}) async-start(bf16[16,2,2,4,8,128]{5,4,3,2,1,0:T(8,128)(2,1)} %shard_map.58), calls=%async_computation | async-start | bytes 1048576 | tf_op jit(solution)/shard_map/all_to_all | solution.py:201
  11.8 1.3 %collective-permute-start.3 = (bf16[32,8,128]{2,1,0:T(8,128)(2,1)S(1)}, bf16[32,8,128]{2,1,0:T(8,128)(2,1)S(1)}, u32[]{:S(2)}, u32[]{:S(2)}) collective-permute-start(bf16[32,8,128]{2,1,0:T(8,128)(2,1)S(1)} %get-tuple-element.33), channel_id=1, source_target_pairs={{16,0},{32,16},{48,32},{64,48},{80,64},{96,80},{112,96},{128,112},... | collective-permute-start | bytes 196616 | tf_op jit(solution)/shard_map/ppermute | solution.py:219
  13.1 5.4 %collective-permute-start.2 = (bf16[32,8,128]{2,1,0:T(8,128)(2,1)S(1)}, bf16[32,8,128]{2,1,0:T(8,128)(2,1)S(1)}, u32[]{:S(2)}, u32[]{:S(2)}) collective-permute-start(bf16[32,8,128]{2,1,0:T(8,128)(2,1)S(1)} %get-tuple-element.34), channel_id=1, source_target_pairs={{0,16},{16,32},{32,48},{48,64},{64,80},{80,96},{96,112},{112,128},... | collective-permute-start | bytes 196616 | tf_op jit(solution)/shard_map/ppermute | solution.py:218
  18.9 1.6 %collective-permute-done.2.before_ref = bf16[32,8,128]{2,1,0:T(8,128)(2,1)S(1)} collective-permute-done((bf16[32,8,128]{2,1,0:T(8,128)(2,1)S(1)}, bf16[32,8,128]{2,1,0:T(8,128)(2,1)S(1)}, u32[]{:S(2)}, u32[]{:S(2)}) %collective-permute-start.2) | collective-permute-done | bytes 65568 | tf_op jit(solution)/shard_map/ppermute | solution.py:218
  21.1 1.8 %shard_map.59 = bf16[8,39,8,128]{3,2,1,0:T(8,128)(2,1)} custom-call(bf16[27,8,128]{2,1,0:T(8,128)(2,1)} %bitcast.53, bf16[32,8,128]{2,1,0:T(8,128)(2,1)} %copy-done.8, bf16[32,8,128]{2,1,0:T(8,128)(2,1)} %copy-done.7), custom_call_target="tpu_custom_call" | custom-call | bytes 825344 | tf_op jit(solution)/shard_map/pallas_call | solution.py:23
  22.9 8.2 %all-to-all-start.1 = ((bf16[8,39,8,128]{3,2,1,0:T(8,128)(2,1)}), bf16[8,39,8,128]{3,2,1,0:T(8,128)(2,1)S(1)}, u32[]{:S(2)}, u32[]{:S(2)}) async-start(bf16[8,39,8,128]{3,2,1,0:T(8,128)(2,1)} %shard_map.59), calls=%async_computation.1 | async-start | bytes 1277952 | tf_op jit(solution)/shard_map/all_to_all | solution.py:201
  31.1 1.3 %collective-permute-start.1 = (bf16[16,4,8,128]{3,2,1,0:T(8,128)(2,1)S(1)}, bf16[16,4,8,128]{3,2,1,0:T(8,128)(2,1)S(1)}, u32[]{:S(2)}, u32[]{:S(2)}) collective-permute-start(bf16[16,4,8,128]{3,2,1,0:T(8,128)(2,1)S(1)} %get-tuple-element.15), channel_id=1, source_target_pairs={{16,0},{32,16},{48,32},{64,48},{80,64},{96,80},{112,96},{128,112},... | collective-permute-start | bytes 393224 | tf_op jit(solution)/shard_map/ppermute | solution.py:223
  32.4 7.0 %collective-permute-start = (bf16[16,4,8,128]{3,2,1,0:T(8,128)(2,1)S(1)}, bf16[16,4,8,128]{3,2,1,0:T(8,128)(2,1)S(1)}, u32[]{:S(2)}, u32[]{:S(2)}) collective-permute-start(bf16[16,4,8,128]{3,2,1,0:T(8,128)(2,1)S(1)} %get-tuple-element.16), channel_id=1, source_target_pairs={{0,16},{16,32},{32,48},{48,64},{64,80},{80,96},{96,112},{112,128},... | collective-permute-start | bytes 393224 | tf_op jit(solution)/shard_map/ppermute | solution.py:222
  39.5 1.2 collective-permute-done.1.after_ref
  40.7 1.3 %collective-permute-done.before_ref = bf16[16,4,8,128]{3,2,1,0:T(8,128)(2,1)S(1)} collective-permute-done((bf16[16,4,8,128]{3,2,1,0:T(8,128)(2,1)S(1)}, bf16[16,4,8,128]{3,2,1,0:T(8,128)(2,1)S(1)}, u32[]{:S(2)}, u32[]{:S(2)}) %collective-permute-start) | collective-permute-done | bytes 131104 | tf_op jit(solution)/shard_map/ppermute | solution.py:222
  42.6 3.7 %wgrad.1 = (f32[8,27,8,128]{3,2,1,0:T(8,128)}, f32[8,27,8,128]{3,2,1,0:T(8,128)}) custom-call(s32[1]{0:T(128)} %bitcast.23.core_ref, bf16[16,2,2,4,8,128]{5,4,3,2,1,0:T(8,128)(2,1)} %copy-done, bf16[16,4,8,128]{3,2,1,0:T(8,128)(2,1)} %copy-done.11, bf16[16,4,8,128]{3,2,1,0:T(8,128)(2,1)} %copy-done.10), custom_call_target="tpu_custom_call" | custom-call | flops 452984832 | bytes 1769472 | tf_op jit(solution)/shard_map/wgrad/pallas_call | solution.py:232
  46.3 1.9 %collective-permute-start.10 = (f32[8,27,8,128]{3,2,1,0:T(8,128)}, f32[8,27,8,128]{3,2,1,0:T(8,128)S(1)}, u32[]{:S(2)}, u32[]{:S(2)}) collective-permute-start(f32[8,27,8,128]{3,2,1,0:T(8,128)} %get-tuple-element.14), channel_id=1, source_target_pairs={{0,1},{1,0},{2,3},{3,2},{4,5},{5,4},{6,7},{7,6},{8,9},{9,8},{10,11... | collective-permute-start | bytes 2654216 | tf_op jit(solution)/shard_map/ppermute | solution.py:248
  48.3 2.4 %collective-permute-start.4 = (bf16[8,39,8,128]{3,2,1,0:T(8,128)(2,1)S(1)}, bf16[8,39,8,128]{3,2,1,0:T(8,128)(2,1)S(1)}, u32[]{:S(2)}, u32[]{:S(2)}) collective-permute-start(bf16[8,39,8,128]{3,2,1,0:T(8,128)(2,1)S(1)} %all-to-all-done.1.mine_ref), channel_id=1, source_target_pairs={{0,1},{1,0},{2,3},{3,2},{4,5},{5,4},{6,7},{7,6},{8,9},{9,8},{10,11... | collective-permute-start | bytes 1916936 | tf_op jit(solution)/shard_map/ppermute | solution.py:229
  50.9 2.2 %add.13 = f32[8,27,8,128]{3,2,1,0:T(8,128)} add(f32[8,27,8,128]{3,2,1,0:T(8,128)} %get-tuple-element.13, f32[8,27,8,128]{3,2,1,0:T(8,128)S(1)} %collective-permute-done.10) | non-fusion elementwise | flops 221184 | bytes 2654208 | tf_op jit(solution)/shard_map/add | solution.py:248
  53.0 11.9 %all-to-all-start.2 = ((f32[8,27,8,128]{3,2,1,0:T(8,128)}), f32[8,27,8,128]{3,2,1,0:T(8,128)S(1)}, u32[]{:S(2)}, u32[]{:S(2)}) async-start(f32[8,27,8,128]{3,2,1,0:T(8,128)} %add.13), calls=%async_computation.2 | async-start | bytes 1769472 | tf_op jit(solution)/shard_map/all_to_all | solution.py:201
  64.9 0.9 copy-done.9
  65.8 3.9 %conv.1 = (f32[2,4,2,2,2,8,128]{6,5,4,3,2,1,0:T(8,128)}, f32[2,4,2,2,2,8,128]{6,5,4,3,2,1,0:T(8,128)}) custom-call(s32[1]{0:T(128)} %bitcast.f_ref, bf16[16,2,2,4,8,128]{5,4,3,2,1,0:T(8,128)(2,1)} %copy-done, bf16[16,4,8,128]{3,2,1,0:T(8,128)(2,1)} %copy-done.11, bf16[16,4,8,128]{3,2,1,0:T(8,128)(2,1)} %copy-done.10, bf16[8,39,8,128]{3,2,1,0:T(8,128)(2,1)} %copy-done.1, ...), custom_call_target="tpu_custom_call" | custom-call | flops 905969664 | bytes 1769472 | tf_op jit(solution)/shard_map/conv/pallas_call | solution.py:253
  69.7 1.9 %collective-permute-start.5 = (f32[2,4,2,2,2,8,128]{6,5,4,3,2,1,0:T(8,128)}, f32[2,4,2,2,2,8,128]{6,5,4,3,2,1,0:T(8,128)S(1)}, u32[]{:S(2)}, u32[]{:S(2)}) collective-permute-start(f32[2,4,2,2,2,8,128]{6,5,4,3,2,1,0:T(8,128)} %get-tuple-element.10), channel_id=1, source_target_pairs={{0,1},{1,0},{2,3},{3,2},{4,5},{5,4},{6,7},{7,6},{8,9},{9,8},{10,11... | collective-permute-start | bytes 786440 | tf_op jit(solution)/shard_map/ppermute | solution.py:270
  71.7 0.9 slice.75
  72.6 0.8 collective-permute-done.5
  73.4 3.5 %collective-permute-start.6 = (f32[2,4,2,2,2,8,128]{6,5,4,3,2,1,0:T(8,128)S(1)}, f32[2,4,2,2,2,8,128]{6,5,4,3,2,1,0:T(8,128)S(1)}, u32[]{:S(2)}, u32[]{:S(2)}) collective-permute-start(f32[2,4,2,2,2,8,128]{6,5,4,3,2,1,0:T(8,128)S(1)} %pad_maximum_fusion), channel_id=1, source_target_pairs={{0,8},{8,0},{1,9},{9,1},{2,10},{10,2},{3,11},{11,3},{4,12},{12,4},... | collective-permute-start | bytes 786440 | tf_op jit(solution)/shard_map/ppermute | solution.py:271
  77.1 0.7 pad.4
  77.7 12.2 %all-to-all-start.3 = ((f32[32,8,128]{2,1,0:T(8,128)}), f32[32,8,128]{2,1,0:T(8,128)S(1)}, u32[]{:S(2)}, u32[]{:S(2)}) async-start(f32[32,8,128]{2,1,0:T(8,128)} %pad.4), calls=%async_computation.3 | async-start | bytes 262144 | tf_op jit(solution)/shard_map/all_to_all | solution.py:201
  90.0 3.2 %collective-permute-start.7 = (f32[4,2,2,2,8,128]{5,4,3,2,1,0:T(8,128)S(1)}, f32[4,2,2,2,8,128]{5,4,3,2,1,0:T(8,128)S(1)}, u32[]{:S(2)}, u32[]{:S(2)}) collective-permute-start(f32[4,2,2,2,8,128]{5,4,3,2,1,0:T(8,128)S(1)} %pad_maximum_fusion.2), channel_id=1, source_target_pairs={{0,2},{2,4},{4,6},{6,0},{1,3},{3,5},{5,7},{7,1},{8,10},{10,12},{12... | collective-permute-start | bytes 393224 | tf_op jit(solution)/shard_map/ppermute | solution.py:274
  93.2 9.1 %all-to-all-done.3 = f32[32,8,128]{2,1,0:T(8,128)S(1)} async-done(((f32[32,8,128]{2,1,0:T(8,128)}), f32[32,8,128]{2,1,0:T(8,128)S(1)}, u32[]{:S(2)}, u32[]{:S(2)}) %all-to-all-start.3) | async-done | bytes 131104 | tf_op jit(solution)/shard_map/all_to_all | solution.py:201
  103.0 3.9 %all-to-all-start.4 = ((f32[32,8,128]{2,1,0:T(8,128)}), f32[32,8,128]{2,1,0:T(8,128)S(1)}, u32[]{:S(2)}, u32[]{:S(2)}) async-start(f32[32,8,128]{2,1,0:T(8,128)} %broadcast_in_dim.2), calls=%async_computation.4 | async-start | bytes 262144 | tf_op jit(solution)/shard_map/all_to_all | solution.py:201
  106.9 3.5 %collective-permute-start.8 = (f32[4,2,2,2,8,128]{5,4,3,2,1,0:T(8,128)S(1)}, f32[4,2,2,2,8,128]{5,4,3,2,1,0:T(8,128)S(1)}, u32[]{:S(2)}, u32[]{:S(2)}) collective-permute-start(f32[4,2,2,2,8,128]{5,4,3,2,1,0:T(8,128)S(1)} %pad_maximum_fusion.3), channel_id=1, source_target_pairs={{0,4},{2,6},{4,0},{6,2},{1,5},{3,7},{5,1},{7,3},{8,12},{10,14},{12... | collective-permute-start | bytes 393224 | tf_op jit(solution)/shard_map/ppermute | solution.py:274
  110.4 2.5 %collective-permute-start.9 = (f32[4,2,2,2,8,128]{5,4,3,2,1,0:T(8,128)S(1)}, f32[4,2,2,2,8,128]{5,4,3,2,1,0:T(8,128)S(1)}, u32[]{:S(2)}, u32[]{:S(2)}) collective-permute-start(f32[4,2,2,2,8,128]{5,4,3,2,1,0:T(8,128)S(1)} %pad_maximum_fusion.4), channel_id=1, source_target_pairs={{0,6},{2,0},{4,2},{6,4},{1,7},{3,1},{5,3},{7,5},{8,14},{10,8},{12,... | collective-permute-start | bytes 393224 | tf_op jit(solution)/shard_map/ppermute | solution.py:274
  113.5 2.4 %collective-permute-done.8.refs_2_ = f32[4,2,2,2,8,128]{5,4,3,2,1,0:T(8,128)S(1)} collective-permute-done((f32[4,2,2,2,8,128]{5,4,3,2,1,0:T(8,128)S(1)}, f32[4,2,2,2,8,128]{5,4,3,2,1,0:T(8,128)S(1)}, u32[]{:S(2)}, u32[]{:S(2)}) %collective-permute-start.8) | collective-permute-done | bytes 131104 | tf_op jit(solution)/shard_map/ppermute | solution.py:274
  116.0 2.5 %collective-permute-done.9.refs_3_ = f32[4,2,2,2,8,128]{5,4,3,2,1,0:T(8,128)S(1)} collective-permute-done((f32[4,2,2,2,8,128]{5,4,3,2,1,0:T(8,128)S(1)}, f32[4,2,2,2,8,128]{5,4,3,2,1,0:T(8,128)S(1)}, u32[]{:S(2)}, u32[]{:S(2)}) %collective-permute-start.9) | collective-permute-done | bytes 131104 | tf_op jit(solution)/shard_map/ppermute | solution.py:274
  119.1 1.9 %shard_map.60 = (f32[2,32,8,128]{3,2,1,0:T(8,128)}, f32[2,32,8,128]{3,2,1,0:T(8,128)}) custom-call(s32[1]{0:T(128)} %bitcast.f_ref, f32[4,2,2,2,8,128]{5,4,3,2,1,0:T(8,128)} %pad_maximum_fusion.1.refs_0_, f32[4,2,2,2,8,128]{5,4,3,2,1,0:T(8,128)} %copy-done.4, f32[4,2,2,2,8,128]{5,4,3,2,1,0:T(8,128)} %copy-done.5, f32[4,2,2,2,8,128]{5,4,3,2,1,0:T(8,128)} %copy-done.6), custom_call_target="tpu_custom_call" | custom-call | bytes 1048580 | tf_op jit(solution)/shard_map/pallas_call | solution.py:23
  (48 shorter events, 4.6 us)
Async XLA Ops:
  2.4 9.4 %copy-start.2 = (bf16[2,32,8,128]{3,2,1,0:T(8,128)(2,1)S(1)}, bf16[2,32,8,128]{3,2,1,0:T(8,128)(2,1)}, u32[]{:S(2)}) copy-start(bf16[2,32,8,128]{3,2,1,0:T(8,128)(2,1)} %g_ref.1) | copy-start | bytes 393220
  2.5 20.4 %all-to-all-start = ((bf16[16,2,2,4,8,128]{5,4,3,2,1,0:T(8,128)(2,1)}), bf16[16,2,2,4,8,128]{5,4,3,2,1,0:T(8,128)(2,1)S(1)}, u32[]{:S(2)}, u32[]{:S(2)}) async-start(bf16[16,2,2,4,8,128]{5,4,3,2,1,0:T(8,128)(2,1)} %shard_map.58), calls=%async_computation | async-start | bytes 1048576 | tf_op jit(solution)/shard_map/all_to_all | solution.py:201
  11.8 7.1 %collective-permute-start.3 = (bf16[32,8,128]{2,1,0:T(8,128)(2,1)S(1)}, bf16[32,8,128]{2,1,0:T(8,128)(2,1)S(1)}, u32[]{:S(2)}, u32[]{:S(2)}) collective-permute-start(bf16[32,8,128]{2,1,0:T(8,128)(2,1)S(1)} %get-tuple-element.33), channel_id=1, source_target_pairs={{16,0},{32,16},{48,32},{64,48},{80,64},{96,80},{112,96},{128,112},... | collective-permute-start | bytes 196616 | tf_op jit(solution)/shard_map/ppermute | solution.py:219
  13.1 7.3 %collective-permute-start.2 = (bf16[32,8,128]{2,1,0:T(8,128)(2,1)S(1)}, bf16[32,8,128]{2,1,0:T(8,128)(2,1)S(1)}, u32[]{:S(2)}, u32[]{:S(2)}) collective-permute-start(bf16[32,8,128]{2,1,0:T(8,128)(2,1)S(1)} %get-tuple-element.34), channel_id=1, source_target_pairs={{0,16},{16,32},{32,48},{48,64},{64,80},{80,96},{96,112},{112,128},... | collective-permute-start | bytes 196616 | tf_op jit(solution)/shard_map/ppermute | solution.py:218
  18.9 1.6 %copy-start.7 = (bf16[32,8,128]{2,1,0:T(8,128)(2,1)}, bf16[32,8,128]{2,1,0:T(8,128)(2,1)S(1)}, u32[]{:S(2)}) copy-start(bf16[32,8,128]{2,1,0:T(8,128)(2,1)S(1)} %collective-permute-done.3.after_ref) | copy-start | bytes 196612
  20.5 0.6 copy-start.8
  22.9 8.2 %copy-start = (bf16[16,2,2,4,8,128]{5,4,3,2,1,0:T(8,128)(2,1)}, bf16[16,2,2,4,8,128]{5,4,3,2,1,0:T(8,128)(2,1)S(1)}, u32[]{:S(2)}) copy-start(bf16[16,2,2,4,8,128]{5,4,3,2,1,0:T(8,128)(2,1)S(1)} %all-to-all-done.own_ref) | copy-start | bytes 1572868
  22.9 25.4 %all-to-all-start.1 = ((bf16[8,39,8,128]{3,2,1,0:T(8,128)(2,1)}), bf16[8,39,8,128]{3,2,1,0:T(8,128)(2,1)S(1)}, u32[]{:S(2)}, u32[]{:S(2)}) async-start(bf16[8,39,8,128]{3,2,1,0:T(8,128)(2,1)} %shard_map.59), calls=%async_computation.1 | async-start | bytes 1277952 | tf_op jit(solution)/shard_map/all_to_all | solution.py:201
  31.1 9.5 %collective-permute-start.1 = (bf16[16,4,8,128]{3,2,1,0:T(8,128)(2,1)S(1)}, bf16[16,4,8,128]{3,2,1,0:T(8,128)(2,1)S(1)}, u32[]{:S(2)}, u32[]{:S(2)}) collective-permute-start(bf16[16,4,8,128]{3,2,1,0:T(8,128)(2,1)S(1)} %get-tuple-element.15), channel_id=1, source_target_pairs={{16,0},{32,16},{48,32},{64,48},{80,64},{96,80},{112,96},{128,112},... | collective-permute-start | bytes 393224 | tf_op jit(solution)/shard_map/ppermute | solution.py:223
  32.4 9.5 %collective-permute-start = (bf16[16,4,8,128]{3,2,1,0:T(8,128)(2,1)S(1)}, bf16[16,4,8,128]{3,2,1,0:T(8,128)(2,1)S(1)}, u32[]{:S(2)}, u32[]{:S(2)}) collective-permute-start(bf16[16,4,8,128]{3,2,1,0:T(8,128)(2,1)S(1)} %get-tuple-element.16), channel_id=1, source_target_pairs={{0,16},{16,32},{32,48},{48,64},{64,80},{80,96},{96,112},{112,128},... | collective-permute-start | bytes 393224 | tf_op jit(solution)/shard_map/ppermute | solution.py:222
  40.7 1.3 %copy-start.10 = (bf16[16,4,8,128]{3,2,1,0:T(8,128)(2,1)}, bf16[16,4,8,128]{3,2,1,0:T(8,128)(2,1)S(1)}, u32[]{:S(2)}) copy-start(bf16[16,4,8,128]{3,2,1,0:T(8,128)(2,1)S(1)} %collective-permute-done.1.after_ref) | copy-start | bytes 393220
  42.0 0.6 copy-start.11
  46.3 4.5 %collective-permute-start.10 = (f32[8,27,8,128]{3,2,1,0:T(8,128)}, f32[8,27,8,128]{3,2,1,0:T(8,128)S(1)}, u32[]{:S(2)}, u32[]{:S(2)}) collective-permute-start(f32[8,27,8,128]{3,2,1,0:T(8,128)} %get-tuple-element.14), channel_id=1, source_target_pairs={{0,1},{1,0},{2,3},{3,2},{4,5},{5,4},{6,7},{7,6},{8,9},{9,8},{10,11... | collective-permute-start | bytes 2654216 | tf_op jit(solution)/shard_map/ppermute | solution.py:248
  48.3 4.8 %copy-start.1 = (bf16[8,39,8,128]{3,2,1,0:T(8,128)(2,1)}, bf16[8,39,8,128]{3,2,1,0:T(8,128)(2,1)S(1)}, u32[]{:S(2)}) copy-start(bf16[8,39,8,128]{3,2,1,0:T(8,128)(2,1)S(1)} %all-to-all-done.1.mine_ref) | copy-start | bytes 1916932
  48.3 16.6 %collective-permute-start.4 = (bf16[8,39,8,128]{3,2,1,0:T(8,128)(2,1)S(1)}, bf16[8,39,8,128]{3,2,1,0:T(8,128)(2,1)S(1)}, u32[]{:S(2)}, u32[]{:S(2)}) collective-permute-start(bf16[8,39,8,128]{3,2,1,0:T(8,128)(2,1)S(1)} %all-to-all-done.1.mine_ref), channel_id=1, source_target_pairs={{0,1},{1,0},{2,3},{3,2},{4,5},{5,4},{6,7},{7,6},{8,9},{9,8},{10,11... | collective-permute-start | bytes 1916936 | tf_op jit(solution)/shard_map/ppermute | solution.py:229
  53.0 24.0 %all-to-all-start.2 = ((f32[8,27,8,128]{3,2,1,0:T(8,128)}), f32[8,27,8,128]{3,2,1,0:T(8,128)S(1)}, u32[]{:S(2)}, u32[]{:S(2)}) async-start(f32[8,27,8,128]{3,2,1,0:T(8,128)} %add.13), calls=%async_computation.2 | async-start | bytes 1769472 | tf_op jit(solution)/shard_map/all_to_all | solution.py:201
  64.9 0.9 copy-start.9
  69.7 3.6 %collective-permute-start.5 = (f32[2,4,2,2,2,8,128]{6,5,4,3,2,1,0:T(8,128)}, f32[2,4,2,2,2,8,128]{6,5,4,3,2,1,0:T(8,128)S(1)}, u32[]{:S(2)}, u32[]{:S(2)}) collective-permute-start(f32[2,4,2,2,2,8,128]{6,5,4,3,2,1,0:T(8,128)} %get-tuple-element.10), channel_id=1, source_target_pairs={{0,1},{1,0},{2,3},{3,2},{4,5},{5,4},{6,7},{7,6},{8,9},{9,8},{10,11... | collective-permute-start | bytes 786440 | tf_op jit(solution)/shard_map/ppermute | solution.py:270
  73.4 3.6 %copy-start.3 = (f32[2,4,2,2,2,8,128]{6,5,4,3,2,1,0:T(8,128)S(1)}, f32[2,4,2,2,2,8,128]{6,5,4,3,2,1,0:T(8,128)}, u32[]{:S(2)}) copy-start(f32[2,4,2,2,2,8,128]{6,5,4,3,2,1,0:T(8,128)} %get-tuple-element.9) | copy-start | bytes 786436
  73.4 16.5 %collective-permute-start.6 = (f32[2,4,2,2,2,8,128]{6,5,4,3,2,1,0:T(8,128)S(1)}, f32[2,4,2,2,2,8,128]{6,5,4,3,2,1,0:T(8,128)S(1)}, u32[]{:S(2)}, u32[]{:S(2)}) collective-permute-start(f32[2,4,2,2,2,8,128]{6,5,4,3,2,1,0:T(8,128)S(1)} %pad_maximum_fusion), channel_id=1, source_target_pairs={{0,8},{8,0},{1,9},{9,1},{2,10},{10,2},{3,11},{11,3},{4,12},{12,4},... | collective-permute-start | bytes 786440 | tf_op jit(solution)/shard_map/ppermute | solution.py:271
  77.7 24.6 %all-to-all-start.3 = ((f32[32,8,128]{2,1,0:T(8,128)}), f32[32,8,128]{2,1,0:T(8,128)S(1)}, u32[]{:S(2)}, u32[]{:S(2)}) async-start(f32[32,8,128]{2,1,0:T(8,128)} %pad.4), calls=%async_computation.3 | async-start | bytes 262144 | tf_op jit(solution)/shard_map/all_to_all | solution.py:201
  90.0 23.5 %collective-permute-start.7 = (f32[4,2,2,2,8,128]{5,4,3,2,1,0:T(8,128)S(1)}, f32[4,2,2,2,8,128]{5,4,3,2,1,0:T(8,128)S(1)}, u32[]{:S(2)}, u32[]{:S(2)}) collective-permute-start(f32[4,2,2,2,8,128]{5,4,3,2,1,0:T(8,128)S(1)} %pad_maximum_fusion.2), channel_id=1, source_target_pairs={{0,2},{2,4},{4,6},{6,0},{1,3},{3,5},{5,7},{7,1},{8,10},{10,12},{12... | collective-permute-start | bytes 393224 | tf_op jit(solution)/shard_map/ppermute | solution.py:274
  103.0 18.0 %all-to-all-start.4 = ((f32[32,8,128]{2,1,0:T(8,128)}), f32[32,8,128]{2,1,0:T(8,128)S(1)}, u32[]{:S(2)}, u32[]{:S(2)}) async-start(f32[32,8,128]{2,1,0:T(8,128)} %broadcast_in_dim.2), calls=%async_computation.4 | async-start | bytes 262144 | tf_op jit(solution)/shard_map/all_to_all | solution.py:201
  106.9 9.1 %collective-permute-start.8 = (f32[4,2,2,2,8,128]{5,4,3,2,1,0:T(8,128)S(1)}, f32[4,2,2,2,8,128]{5,4,3,2,1,0:T(8,128)S(1)}, u32[]{:S(2)}, u32[]{:S(2)}) collective-permute-start(f32[4,2,2,2,8,128]{5,4,3,2,1,0:T(8,128)S(1)} %pad_maximum_fusion.3), channel_id=1, source_target_pairs={{0,4},{2,6},{4,0},{6,2},{1,5},{3,7},{5,1},{7,3},{8,12},{10,14},{12... | collective-permute-start | bytes 393224 | tf_op jit(solution)/shard_map/ppermute | solution.py:274
  110.4 8.1 %collective-permute-start.9 = (f32[4,2,2,2,8,128]{5,4,3,2,1,0:T(8,128)S(1)}, f32[4,2,2,2,8,128]{5,4,3,2,1,0:T(8,128)S(1)}, u32[]{:S(2)}, u32[]{:S(2)}) collective-permute-start(f32[4,2,2,2,8,128]{5,4,3,2,1,0:T(8,128)S(1)} %pad_maximum_fusion.4), channel_id=1, source_target_pairs={{0,6},{2,0},{4,2},{6,4},{1,7},{3,1},{5,3},{7,5},{8,14},{10,8},{12,... | collective-permute-start | bytes 393224 | tf_op jit(solution)/shard_map/ppermute | solution.py:274
  113.5 5.0 %copy-start.4 = (f32[4,2,2,2,8,128]{5,4,3,2,1,0:T(8,128)}, f32[4,2,2,2,8,128]{5,4,3,2,1,0:T(8,128)S(1)}, u32[]{:S(2)}) copy-start(f32[4,2,2,2,8,128]{5,4,3,2,1,0:T(8,128)S(1)} %collective-permute-done.7.refs_1_) | copy-start | bytes 393220
  116.0 2.5 %copy-start.5 = (f32[4,2,2,2,8,128]{5,4,3,2,1,0:T(8,128)}, f32[4,2,2,2,8,128]{5,4,3,2,1,0:T(8,128)S(1)}, u32[]{:S(2)}) copy-start(f32[4,2,2,2,8,128]{5,4,3,2,1,0:T(8,128)S(1)} %collective-permute-done.8.refs_2_) | copy-start | bytes 393220
  118.5 0.6 copy-start.6

commit v5 on v4

--- a/solution.py
+++ b/solution.py
@@ -30,6 +30,14 @@
     )(*ins)
 
 
+def place_of(index):
+    return (index >> 3) & 1, (index >> 1) & 3, index & 1
+
+
+def odd_slab(index):
+    return (index >> 4) & 1 == 1
+
+
 def pack_kernel(x_ref, g_ref, o_ref):
     n, _, nz, nr = o_ref.shape[:4]
     rows = x_ref.shape[1]
@@ -42,19 +50,30 @@
                     o_ref[d, k, z, r] = ref[z, h] if 0 <= h < rows else zero
 
 
-def pack_more_kernel(w_ref, before_ref, after_ref, o_ref):
+def halo_pick(index):
+    odd = odd_slab(index)
+
+    def pick(side, even, odd_side):
+        even, odd_side = even.astype(F32), odd_side.astype(F32)
+        return jnp.where(odd == (side == 0), even, odd_side).astype(BF)
+
+    return pick
+
+
+def pack_more_kernel(p_ref, w_ref, even_ref, odd_ref, o_ref):
     chips, total = o_ref.shape[:2]
     taps = w_ref.shape[0]
-    rows = before_ref.shape[0]
+    rows = even_ref.shape[0]
     nr = (total - taps) // 2
+    pick = halo_pick(p_ref[0])
     zero = jnp.zeros(w_ref.shape[1:], w_ref.dtype)
     for q in range(chips):
         for t in range(taps):
             o_ref[q, t] = w_ref[t]
-        for p, ref in enumerate((before_ref, after_ref)):
+        for p in range(2):
             for r in range(nr):
                 h = q * (nr - 2) + r - 1
-                o_ref[q, taps + p * nr + r] = ref[h] if 0 <= h < rows else zero
+                o_ref[q, taps + p * nr + r] = pick(p, even_ref[h], odd_ref[h]) if 0 <= h < rows else zero
 
 
 def shifted(value):
@@ -92,23 +111,29 @@
     return lambda r: stack([own_ref[d, k, z, r] for d in range(own_ref.shape[0])])
 
 
-def halo_plane(ref):
-    return lambda r: stack([ref[d, r] for d in range(ref.shape[0])])
-
-
-def x_planes(own_ref, before_ref, after_ref):
+def halo_plane(index, side, even_ref, odd_ref):
+    take_even = odd_slab(index) == (side == 0)
+
+    def rows(r):
+        n = even_ref.shape[0]
+        return jnp.where(take_even, stack([even_ref[d, r] for d in range(n)]), stack([odd_ref[d, r] for d in range(n)]))
+
+    return rows
+
+
+def x_planes(index, own_ref, even_ref, odd_ref):
     inner = [own_plane(own_ref, 0, z) for z in range(own_ref.shape[2])]
-    return [halo_plane(before_ref)] + inner + [halo_plane(after_ref)]
-
-
-def wgrad_kernel(core_ref, own_ref, before_ref, after_ref, keep_ref, send_ref, s_ref, t_ref, o_ref, sems):
+    return [halo_plane(index, 0, even_ref, odd_ref)] + inner + [halo_plane(index, 1, even_ref, odd_ref)]
+
+
+def wgrad_kernel(p_ref, own_ref, even_ref, odd_ref, keep_ref, send_ref, s_ref, t_ref, o_ref, sems):
     n, _, nz, nr, cg, w = own_ref.shape
     nh, ch = nr - 2, n * cg
-    build(x_planes(own_ref, before_ref, after_ref), (nr, ch, w), s_ref)
+    build(x_planes(p_ref[0], own_ref, even_ref, odd_ref), (nr, ch, w), s_ref)
     for z in range(nz):
         for h in range(nh):
             t_ref[z, :, pl.ds(h * w, w)] = own_plane(own_ref, 1, z)(h + 1).astype(BF)
-    core = core_ref[0]
+    core = place_of(p_ref[0])[2]
     for a in range(3):
         for b in range(3):
             total = None
@@ -134,19 +159,15 @@
         copy.wait()
 
 
-def place_of(index):
-    return index >> 3, (index >> 1) & 3, index & 1
-
-
 def conv_kernel(
-    f_ref, own_ref, before_ref, after_ref, mine_ref, other_ref, keep_ref, send_ref, s_ref, wt_ref, wf_ref, o_ref, sems
+    p_ref, own_ref, even_ref, odd_ref, mine_ref, other_ref, keep_ref, send_ref, s_ref, wt_ref, wf_ref, o_ref, sems
 ):
     n, _, nz, nr, cg, w = own_ref.shape
     nh, ch = nr - 2, n * cg
     chips, total = mine_ref.shape[:2]
     taps = 27
     span = (total - taps) // 2
-    zl, x, core = place_of(f_ref[0])
+    zl, x, core = place_of(p_ref[0])
     first = core == 0
     for t in range(taps):
         a, bc = t // 9, t % 9
@@ -162,7 +183,7 @@
         return rows
 
     g_planes = [g_halo(0)] + [own_plane(own_ref, 1, z) for z in range(nz)] + [g_halo(1)]
-    build(x_planes(own_ref, before_ref, after_ref), (nr, ch, w), s_ref.at[0])
+    build(x_planes(p_ref[0], own_ref, even_ref, odd_ref), (nr, ch, w), s_ref.at[0])
     build(g_planes, (nr, ch, w), s_ref.at[1])
     for k, w_ref in enumerate((wt_ref, wf_ref)):
         for z in range(nz):
@@ -172,7 +193,7 @@
                 total = part if total is None else total + part
             for d in range(n):
                 dzl, dx, dcore = place_of(d)
-                slot = (dcore ^ core, dzl ^ zl, (dx - x) & 3)
+                slot = (dcore ^ core, dzl ^ zl, dx ^ x)
                 for h in range(nh):
                     o_ref[(*slot, k, z, h)] = total[d * cg : (d + 1) * cg, h * w : (h + 1) * w]
     copies = [
@@ -185,12 +206,12 @@
         copy.wait()
 
 
-def place_kernel(f_ref, *refs):
+def place_kernel(p_ref, *refs):
     parts, outs = refs[:-2], refs[-2:]
-    zl, x, core = place_of(f_ref[0])
+    zl, x, core = place_of(p_ref[0])
     for dx, ref in enumerate(parts):
         for j in range(ref.shape[0]):
-            source = ((zl ^ (j >> 1)) * 4 + ((x - dx) & 3)) * 2 + (core ^ (j & 1))
+            source = ((zl ^ (j >> 1)) * 4 + (x ^ dx)) * 2 + (core ^ (j & 1))
             for k, o_ref in enumerate(outs):
                 for z in range(ref.shape[2]):
                     for h in range(ref.shape[3]):
@@ -210,21 +231,29 @@
     nr = rows // n + 2
     nh = nr - 2
     norm = float(nz * ns * rows * w) ** (-0.5)
-    core = lax.axis_index("core").astype(jnp.int32).reshape(1)
-    up = [(i, i + 1) for i in range(ns - 1)]
-    down = [(j, i) for i, j in up]
+    index = lax.axis_index(SPACE + FILT).astype(jnp.int32).reshape(1)
+    parity = lax.axis_index(SPACE).astype(jnp.int32) & 1
+    sides = [(nz - 1) * (1 - parity), (nz - 1) * parity]
+    pairs = [[(i, i + 1) for i in range(first, ns - 1, 2)] for first in (0, 1)]
+    pairs = [p + [(j, i) for i, j in p] for p in pairs]
     swap = [(0, 1), (1, 0)]
     sds = jax.ShapeDtypeStruct
-    gb = lax.ppermute(grad_out[nz - 1], SPACE, up)
-    ga = lax.ppermute(grad_out[0], SPACE, down)
+    g_halos = [
+        lax.ppermute(lax.dynamic_slice(grad_out, (side, 0, 0, 0), (1, rows, cg, w))[0], SPACE, pair)
+        for side, pair in zip(sides, pairs)
+    ]
     (packed,) = call(pack_kernel, [sds((n, 2, nz, nr, cg, w), BF)], [activations, grad_out])
     own = swap_all(packed, FILT)
-    xb = lax.ppermute(own[:, 0, nz - 1], SPACE, up)
-    xa = lax.ppermute(own[:, 0, 0], SPACE, down)
+    x_halos = [
+        lax.ppermute(
+            lax.dynamic_slice(own, (0, 0, side, 0, 0, 0), (n, 1, 1, nr, cg, w))[:, 0, 0], SPACE, pair
+        )
+        for side, pair in zip(sides, pairs)
+    ]
 
     flat_w = weight.transpose(0, 1, 2, 4, 3).reshape(27, cg, ch)
     span = rows // chips + 2
-    (more,) = call(pack_more_kernel, [sds((chips, 27 + 2 * span, cg, ch), BF)], [flat_w, gb, ga])
+    (more,) = call(pack_more_kernel, [sds((chips, 27 + 2 * span, cg, ch), BF)], [index, flat_w, *g_halos], smem=1)
     mine = swap_all(more, CHIPS)
     other = lax.ppermute(mine, "core", swap)
 
@@ -244,12 +273,11 @@
             flops=2 * 27 * ch * ch * nz * nh * w, transcendentals=0, bytes_accessed=4 * 27 * ch * ch
         ),
         name="wgrad",
-    )(core, own, xb, xa)
+    )(index, own, *x_halos)
     pair = keep + lax.ppermute(send, "core", swap)
     pieces = swap_all(pair, CHIPS).reshape(chips, 27, cg, ch)
     group = pieces.sum(0)
 
-    index = lax.axis_index(FILT).astype(jnp.int32).reshape(1)
     keep, send = pl.pallas_call(
         conv_kernel,
         out_shape=(sds((2, 4, 2, nz, nh, cg, w), F32),) * 2,
@@ -266,12 +294,13 @@
             flops=4 * 27 * ch * ch * nz * nh * w, transcendentals=0, bytes_accessed=4 * 27 * ch * ch
         ),
         name="conv",
-    )(index, own, xb, xa, mine, other)
+    )(index, own, *x_halos, mine, other)
     got = lax.ppermute(send, "core", swap)
+    group, got = lax.optimization_barrier((group, got))
     far = lax.ppermute(jnp.stack([keep[1], got[1]]), "zl", swap)
     blocks = [jnp.stack([keep[0, j], got[0, j], far[0, j], far[1, j]]) for j in range(4)]
     blocks = blocks[:1] + [
-        lax.ppermute(blocks[j], "x", [(i, (i + j) % 4) for i in range(4)]) for j in range(1, 4)
+        lax.ppermute(blocks[j], "x", [(i, i ^ j) for i in range(4)]) for j in range(1, 4)
     ]
     output, grad_in = call(place_kernel, [sds((nz, rows, cg, w), F32)] * 2, [index, *blocks], smem=1)
 

time: 123 us -> 126 us (1.024)
  the two profiles are of different devices: /device:TPU:6 before, /device:TPU:8 now
where the time goes in v5:
time: 126 us; the launch traced here: 125 us
  starting transfers between devices  72.8 us (58%)
  waiting for transfers between devices  29.6 us (23%)
  Pallas kernels  13.2 us (10%)
  local copies, waits for them, and re-layouts  5.9 us (5%)
  other arithmetic  2.97 us (2%)
    all_to_all x5, starting transfers between devices, swap_all(): return lax.all_to_all(array, axes, 0, 0, tiled=True)  33.4 us
    ppermute x2, starting transfers between devices, step(): lax.ppermute(lax.dynamic_slice(grad_out, (side, 0, 0, 0), (1, rows, cg, w...  12.5 us
    ppermute x3, starting transfers between devices, step(): lax.ppermute(blocks[j], 'x', [(i, i ^ j) for i in range(4)])  10.4 us
    all_to_all x5, waiting for transfers between devices, swap_all(): return lax.all_to_all(array, axes, 0, 0, tiled=True)  10 us
    ppermute x2, starting transfers between devices, step(): lax.ppermute(lax.dynamic_slice(own, (0, 0, side, 0, 0, 0), (n, 1, 1, nr,...  7.17 us
    ppermute x2, waiting for transfers between devices, step(): lax.ppermute(lax.dynamic_slice(grad_out, (side, 0, 0, 0), (1, rows, cg, w...  5.87 us
    pallas_call x3, Pallas kernels, call(): pl.pallas_call(kernel, out_shape=tuple(outs), in_specs=specs, out_specs=t...  5.55 us
    ppermute x3, waiting for transfers between devices, step(): lax.ppermute(blocks[j], 'x', [(i, i ^ j) for i in range(4)])  4.82 us
  transfers between devices with their start and end apart: 16, of which 10 were waited for; matrix products, arithmetic and copies ran while one was open for 4% of the time, Pallas kernels for 9%

profile of v5, /device:TPU:8, one launch (start us, length us, event | category | flops | bytes accessed | tf_op | source)
XLA Modules:
  0.0 125.4 jit_solution(4423092585810536158)
XLA Ops:
  0.6 1.8 %shard_map.58 = bf16[16,2,2,4,8,128]{5,4,3,2,1,0:T(8,128)(2,1)} custom-call(bf16[2,32,8,128]{3,2,1,0:T(8,128)(2,1)} %x_ref.1, bf16[2,32,8,128]{3,2,1,0:T(8,128)(2,1)} %g_ref.1), custom_call_target="tpu_custom_call" | custom-call | bytes 786432 | tf_op jit(solution)/shard_map/pallas_call | solution.py:23
  2.5 6.3 %all-to-all-start = ((bf16[16,2,2,4,8,128]{5,4,3,2,1,0:T(8,128)(2,1)}), bf16[16,2,2,4,8,128]{5,4,3,2,1,0:T(8,128)(2,1)S(1)}, u32[]{:S(2)}, u32[]{:S(2)}) async-start(bf16[16,2,2,4,8,128]{5,4,3,2,1,0:T(8,128)(2,1)} %shard_map.58), calls=%async_computation | async-start | bytes 1048576 | tf_op jit(solution)/shard_map/all_to_all | solution.py:222
  8.8 9.9 %collective-permute-start.3 = (bf16[32,8,128]{2,1,0:T(8,128)(2,1)S(1)}, bf16[32,8,128]{2,1,0:T(8,128)(2,1)S(1)}, u32[]{:S(2)}, u32[]{:S(2)}) collective-permute-start(bf16[32,8,128]{2,1,0:T(8,128)(2,1)S(1)} %get-tuple-element.37), channel_id=1, source_target_pairs={{16,32},{48,64},{80,96},{112,128},{144,160},{176,192},{208,224},{2... | collective-permute-start | bytes 196616 | tf_op jit(solution)/shard_map/ppermute | solution.py:242
  18.8 2.6 %collective-permute-start.2 = (bf16[32,8,128]{2,1,0:T(8,128)(2,1)S(1)}, bf16[32,8,128]{2,1,0:T(8,128)(2,1)S(1)}, u32[]{:S(2)}, u32[]{:S(2)}) collective-permute-start(bf16[32,8,128]{2,1,0:T(8,128)(2,1)S(1)} %get-tuple-element.38), channel_id=1, source_target_pairs={{0,16},{32,48},{64,80},{96,112},{128,144},{160,176},{192,208},{224... | collective-permute-start | bytes 196616 | tf_op jit(solution)/shard_map/ppermute | solution.py:242
  21.4 1.3 %collective-permute-done.3.odd_ref = bf16[32,8,128]{2,1,0:T(8,128)(2,1)S(1)} collective-permute-done((bf16[32,8,128]{2,1,0:T(8,128)(2,1)S(1)}, bf16[32,8,128]{2,1,0:T(8,128)(2,1)S(1)}, u32[]{:S(2)}, u32[]{:S(2)}) %collective-permute-start.3) | collective-permute-done | bytes 65568 | tf_op jit(solution)/shard_map/ppermute | solution.py:242
  22.7 4.5 %collective-permute-done.2.even_ref = bf16[32,8,128]{2,1,0:T(8,128)(2,1)S(1)} collective-permute-done((bf16[32,8,128]{2,1,0:T(8,128)(2,1)S(1)}, bf16[32,8,128]{2,1,0:T(8,128)(2,1)S(1)}, u32[]{:S(2)}, u32[]{:S(2)}) %collective-permute-start.2) | collective-permute-done | bytes 65568 | tf_op jit(solution)/shard_map/ppermute | solution.py:242
  27.9 1.8 %shard_map.59 = bf16[8,39,8,128]{3,2,1,0:T(8,128)(2,1)} custom-call(s32[1]{0:T(128)} %bitcast.p_ref, bf16[27,8,128]{2,1,0:T(8,128)(2,1)} %bitcast.48, bf16[32,8,128]{2,1,0:T(8,128)(2,1)} %copy-done.8, bf16[32,8,128]{2,1,0:T(8,128)(2,1)} %copy-done.7), custom_call_target="tpu_custom_call" | custom-call | bytes 825348 | tf_op jit(solution)/shard_map/pallas_call | solution.py:23
  29.7 4.5 %all-to-all-start.1 = ((bf16[8,39,8,128]{3,2,1,0:T(8,128)(2,1)}), bf16[8,39,8,128]{3,2,1,0:T(8,128)(2,1)S(1)}, u32[]{:S(2)}, u32[]{:S(2)}) async-start(bf16[8,39,8,128]{3,2,1,0:T(8,128)(2,1)} %shard_map.59), calls=%async_computation.1 | async-start | bytes 1277952 | tf_op jit(solution)/shard_map/all_to_all | solution.py:222
  34.2 2.9 %collective-permute-start.1 = (bf16[16,4,8,128]{3,2,1,0:T(8,128)(2,1)S(1)}, bf16[16,4,8,128]{3,2,1,0:T(8,128)(2,1)S(1)}, u32[]{:S(2)}, u32[]{:S(2)}) collective-permute-start(bf16[16,4,8,128]{3,2,1,0:T(8,128)(2,1)S(1)} %get-tuple-element.19), channel_id=1, source_target_pairs={{16,32},{48,64},{80,96},{112,128},{144,160},{176,192},{208,224},{2... | collective-permute-start | bytes 393224 | tf_op jit(solution)/shard_map/ppermute | solution.py:248
  37.1 4.3 %collective-permute-start = (bf16[16,4,8,128]{3,2,1,0:T(8,128)(2,1)S(1)}, bf16[16,4,8,128]{3,2,1,0:T(8,128)(2,1)S(1)}, u32[]{:S(2)}, u32[]{:S(2)}) collective-permute-start(bf16[16,4,8,128]{3,2,1,0:T(8,128)(2,1)S(1)} %get-tuple-element.20), channel_id=1, source_target_pairs={{0,16},{32,48},{64,80},{96,112},{128,144},{160,176},{192,208},{224... | collective-permute-start | bytes 393224 | tf_op jit(solution)/shard_map/ppermute | solution.py:248
  41.4 3.7 %collective-permute-done.1.odd_ref = bf16[16,4,8,128]{3,2,1,0:T(8,128)(2,1)S(1)} collective-permute-done((bf16[16,4,8,128]{3,2,1,0:T(8,128)(2,1)S(1)}, bf16[16,4,8,128]{3,2,1,0:T(8,128)(2,1)S(1)}, u32[]{:S(2)}, u32[]{:S(2)}) %collective-permute-start.1) | collective-permute-done | bytes 131104 | tf_op jit(solution)/shard_map/ppermute | solution.py:248
  46.4 3.7 %wgrad.1 = (f32[8,27,8,128]{3,2,1,0:T(8,128)}, f32[8,27,8,128]{3,2,1,0:T(8,128)}) custom-call(s32[1]{0:T(128)} %bitcast.p_ref, bf16[16,2,2,4,8,128]{5,4,3,2,1,0:T(8,128)(2,1)} %copy-done, bf16[16,4,8,128]{3,2,1,0:T(8,128)(2,1)} %copy-done.11, bf16[16,4,8,128]{3,2,1,0:T(8,128)(2,1)} %copy-done.10), custom_call_target="tpu_custom_call" | custom-call | flops 452984832 | bytes 1769472 | tf_op jit(solution)/shard_map/wgrad/pallas_call | solution.py:261
  50.1 1.9 %collective-permute-start.5 = (f32[8,27,8,128]{3,2,1,0:T(8,128)}, f32[8,27,8,128]{3,2,1,0:T(8,128)S(1)}, u32[]{:S(2)}, u32[]{:S(2)}) collective-permute-start(f32[8,27,8,128]{3,2,1,0:T(8,128)} %get-tuple-element.13), channel_id=1, source_target_pairs={{0,1},{1,0},{2,3},{3,2},{4,5},{5,4},{6,7},{7,6},{8,9},{9,8},{10,11... | collective-permute-start | bytes 2654216 | tf_op jit(solution)/shard_map/ppermute | solution.py:277
  52.0 2.6 %collective-permute-done.5 = f32[8,27,8,128]{3,2,1,0:T(8,128)S(1)} collective-permute-done((f32[8,27,8,128]{3,2,1,0:T(8,128)}, f32[8,27,8,128]{3,2,1,0:T(8,128)S(1)}, u32[]{:S(2)}, u32[]{:S(2)}) %collective-permute-start.5) | collective-permute-done | bytes 884768 | tf_op jit(solution)/shard_map/ppermute | solution.py:277
  54.6 2.2 %add.36 = f32[8,27,8,128]{3,2,1,0:T(8,128)} add(f32[8,27,8,128]{3,2,1,0:T(8,128)} %get-tuple-element.12, f32[8,27,8,128]{3,2,1,0:T(8,128)S(1)} %collective-permute-done.5) | non-fusion elementwise | flops 221184 | bytes 2654208 | tf_op jit(solution)/shard_map/add | solution.py:277
  56.8 8.1 %all-to-all-start.2 = ((f32[8,27,8,128]{3,2,1,0:T(8,128)}), f32[8,27,8,128]{3,2,1,0:T(8,128)S(1)}, u32[]{:S(2)}, u32[]{:S(2)}) async-start(f32[8,27,8,128]{3,2,1,0:T(8,128)} %add.36), calls=%async_computation.2 | async-start | bytes 1769472 | tf_op jit(solution)/shard_map/all_to_all | solution.py:222
  64.9 1.9 %collective-permute-start.4 = (bf16[8,39,8,128]{3,2,1,0:T(8,128)(2,1)S(1)}, bf16[8,39,8,128]{3,2,1,0:T(8,128)(2,1)S(1)}, u32[]{:S(2)}, u32[]{:S(2)}) collective-permute-start(bf16[8,39,8,128]{3,2,1,0:T(8,128)(2,1)S(1)} %all-to-all-done.1.mine_ref), channel_id=1, source_target_pairs={{0,1},{1,0},{2,3},{3,2},{4,5},{5,4},{6,7},{7,6},{8,9},{9,8},{10,11... | collective-permute-start | bytes 1916936 | tf_op jit(solution)/shard_map/ppermute | solution.py:258
  66.8 2.0 %collective-permute-done.4.other_ref = bf16[8,39,8,128]{3,2,1,0:T(8,128)(2,1)S(1)} collective-permute-done((bf16[8,39,8,128]{3,2,1,0:T(8,128)(2,1)S(1)}, bf16[8,39,8,128]{3,2,1,0:T(8,128)(2,1)S(1)}, u32[]{:S(2)}, u32[]{:S(2)}) %collective-permute-start.4) | collective-permute-done | bytes 639008 | tf_op jit(solution)/shard_map/ppermute | solution.py:258
  68.9 0.8 copy-done.9
  69.7 3.9 %conv.1 = (f32[2,4,2,2,2,8,128]{6,5,4,3,2,1,0:T(8,128)}, f32[2,4,2,2,2,8,128]{6,5,4,3,2,1,0:T(8,128)}) custom-call(s32[1]{0:T(128)} %bitcast.p_ref, bf16[16,2,2,4,8,128]{5,4,3,2,1,0:T(8,128)(2,1)} %copy-done, bf16[16,4,8,128]{3,2,1,0:T(8,128)(2,1)} %copy-done.11, bf16[16,4,8,128]{3,2,1,0:T(8,128)(2,1)} %copy-done.10, bf16[8,39,8,128]{3,2,1,0:T(8,128)(2,1)} %copy-done.1, ...), custom_call_target="tpu_custom_call" | custom-call | flops 905969664 | bytes 1769472 | tf_op jit(solution)/shard_map/conv/pallas_call | solution.py:281
  73.7 2.2 %collective-permute-start.6 = (f32[2,4,2,2,2,8,128]{6,5,4,3,2,1,0:T(8,128)}, f32[2,4,2,2,2,8,128]{6,5,4,3,2,1,0:T(8,128)S(1)}, u32[]{:S(2)}, u32[]{:S(2)}) collective-permute-start(f32[2,4,2,2,2,8,128]{6,5,4,3,2,1,0:T(8,128)} %get-tuple-element.14), channel_id=1, source_target_pairs={{0,1},{1,0},{2,3},{3,2},{4,5},{5,4},{6,7},{7,6},{8,9},{9,8},{10,11... | collective-permute-start | bytes 786440 | tf_op jit(solution)/shard_map/ppermute | solution.py:298
  75.8 0.9 slice.59
  76.8 1.4 %all-to-all-done.2 = f32[8,27,8,128]{3,2,1,0:T(8,128)S(1)} async-done(((f32[8,27,8,128]{3,2,1,0:T(8,128)}), f32[8,27,8,128]{3,2,1,0:T(8,128)S(1)}, u32[]{:S(2)}, u32[]{:S(2)}) %all-to-all-start.2) | async-done | bytes 884768 | tf_op jit(solution)/shard_map/all_to_all | solution.py:222
  79.0 10.3 %all-to-all-start.3 = ((f32[32,8,128]{2,1,0:T(8,128)}), f32[32,8,128]{2,1,0:T(8,128)S(1)}, u32[]{:S(2)}, u32[]{:S(2)}) async-start(f32[32,8,128]{2,1,0:T(8,128)} %pad.4), calls=%async_computation.3 | async-start | bytes 262144 | tf_op jit(solution)/shard_map/all_to_all | solution.py:222
  89.4 3.4 %collective-permute-start.7 = (f32[2,4,2,2,2,8,128]{6,5,4,3,2,1,0:T(8,128)S(1)}, f32[2,4,2,2,2,8,128]{6,5,4,3,2,1,0:T(8,128)S(1)}, u32[]{:S(2)}, u32[]{:S(2)}) collective-permute-start(f32[2,4,2,2,2,8,128]{6,5,4,3,2,1,0:T(8,128)S(1)} %pad_maximum_fusion), channel_id=1, source_target_pairs={{0,8},{8,0},{1,9},{9,1},{2,10},{10,2},{3,11},{11,3},{4,12},{12,4},... | collective-permute-start | bytes 786440 | tf_op jit(solution)/shard_map/ppermute | solution.py:300
  92.8 8.6 %all-to-all-done.3 = f32[32,8,128]{2,1,0:T(8,128)S(1)} async-done(((f32[32,8,128]{2,1,0:T(8,128)}), f32[32,8,128]{2,1,0:T(8,128)S(1)}, u32[]{:S(2)}, u32[]{:S(2)}) %all-to-all-start.3) | async-done | bytes 131104 | tf_op jit(solution)/shard_map/all_to_all | solution.py:222
  102.0 4.1 %all-to-all-start.4 = ((f32[32,8,128]{2,1,0:T(8,128)}), f32[32,8,128]{2,1,0:T(8,128)S(1)}, u32[]{:S(2)}, u32[]{:S(2)}) async-start(f32[32,8,128]{2,1,0:T(8,128)} %broadcast_in_dim.2), calls=%async_computation.4 | async-start | bytes 262144 | tf_op jit(solution)/shard_map/all_to_all | solution.py:222
  106.2 3.3 %collective-permute-start.8 = (f32[4,2,2,2,8,128]{5,4,3,2,1,0:T(8,128)S(1)}, f32[4,2,2,2,8,128]{5,4,3,2,1,0:T(8,128)S(1)}, u32[]{:S(2)}, u32[]{:S(2)}) collective-permute-start(f32[4,2,2,2,8,128]{5,4,3,2,1,0:T(8,128)S(1)} %pad_maximum_fusion.2), channel_id=1, source_target_pairs={{0,2},{2,0},{4,6},{6,4},{1,3},{3,1},{5,7},{7,5},{8,10},{10,8},{12,... | collective-permute-start | bytes 393224 | tf_op jit(solution)/shard_map/ppermute | solution.py:303
  109.5 4.6 %collective-permute-start.9 = (f32[4,2,2,2,8,128]{5,4,3,2,1,0:T(8,128)S(1)}, f32[4,2,2,2,8,128]{5,4,3,2,1,0:T(8,128)S(1)}, u32[]{:S(2)}, u32[]{:S(2)}) collective-permute-start(f32[4,2,2,2,8,128]{5,4,3,2,1,0:T(8,128)S(1)} %pad_maximum_fusion.3), channel_id=1, source_target_pairs={{0,4},{2,6},{4,0},{6,2},{1,5},{3,7},{5,1},{7,3},{8,12},{10,14},{12... | collective-permute-start | bytes 393224 | tf_op jit(solution)/shard_map/ppermute | solution.py:303
  114.1 2.6 %collective-permute-start.10 = (f32[4,2,2,2,8,128]{5,4,3,2,1,0:T(8,128)S(1)}, f32[4,2,2,2,8,128]{5,4,3,2,1,0:T(8,128)S(1)}, u32[]{:S(2)}, u32[]{:S(2)}) collective-permute-start(f32[4,2,2,2,8,128]{5,4,3,2,1,0:T(8,128)S(1)} %pad_maximum_fusion.4), channel_id=1, source_target_pairs={{0,6},{2,4},{4,2},{6,0},{1,7},{3,5},{5,3},{7,1},{8,14},{10,12},{12... | collective-permute-start | bytes 393224 | tf_op jit(solution)/shard_map/ppermute | solution.py:303
  117.9 4.3 %collective-permute-done.10.refs_3_ = f32[4,2,2,2,8,128]{5,4,3,2,1,0:T(8,128)S(1)} collective-permute-done((f32[4,2,2,2,8,128]{5,4,3,2,1,0:T(8,128)S(1)}, f32[4,2,2,2,8,128]{5,4,3,2,1,0:T(8,128)S(1)}, u32[]{:S(2)}, u32[]{:S(2)}) %collective-permute-start.10) | collective-permute-done | bytes 131104 | tf_op jit(solution)/shard_map/ppermute | solution.py:303
  122.8 1.9 %shard_map.60 = (f32[2,32,8,128]{3,2,1,0:T(8,128)}, f32[2,32,8,128]{3,2,1,0:T(8,128)}) custom-call(s32[1]{0:T(128)} %bitcast.p_ref, f32[4,2,2,2,8,128]{5,4,3,2,1,0:T(8,128)} %pad_maximum_fusion.1.refs_0_, f32[4,2,2,2,8,128]{5,4,3,2,1,0:T(8,128)} %copy-done.4, f32[4,2,2,2,8,128]{5,4,3,2,1,0:T(8,128)} %copy-done.5, f32[4,2,2,2,8,128]{5,4,3,2,1,0:T(8,128)} %copy-done.6), custom_call_target="tpu_custom_call" | custom-call | bytes 1048580 | tf_op jit(solution)/shard_map/pallas_call | solution.py:23
  (48 shorter events, 6.0 us)
Async XLA Ops:
  2.4 6.4 %copy-start.2 = (bf16[2,32,8,128]{3,2,1,0:T(8,128)(2,1)S(1)}, bf16[2,32,8,128]{3,2,1,0:T(8,128)(2,1)}, u32[]{:S(2)}) copy-start(bf16[2,32,8,128]{3,2,1,0:T(8,128)(2,1)} %g_ref.1) | copy-start | bytes 393220
  2.5 27.2 %all-to-all-start = ((bf16[16,2,2,4,8,128]{5,4,3,2,1,0:T(8,128)(2,1)}), bf16[16,2,2,4,8,128]{5,4,3,2,1,0:T(8,128)(2,1)S(1)}, u32[]{:S(2)}, u32[]{:S(2)}) async-start(bf16[16,2,2,4,8,128]{5,4,3,2,1,0:T(8,128)(2,1)} %shard_map.58), calls=%async_computation | async-start | bytes 1048576 | tf_op jit(solution)/shard_map/all_to_all | solution.py:222
  8.8 13.9 %collective-permute-start.3 = (bf16[32,8,128]{2,1,0:T(8,128)(2,1)S(1)}, bf16[32,8,128]{2,1,0:T(8,128)(2,1)S(1)}, u32[]{:S(2)}, u32[]{:S(2)}) collective-permute-start(bf16[32,8,128]{2,1,0:T(8,128)(2,1)S(1)} %get-tuple-element.37), channel_id=1, source_target_pairs={{16,32},{48,64},{80,96},{112,128},{144,160},{176,192},{208,224},{2... | collective-permute-start | bytes 196616 | tf_op jit(solution)/shard_map/ppermute | solution.py:242
  18.8 8.5 %collective-permute-start.2 = (bf16[32,8,128]{2,1,0:T(8,128)(2,1)S(1)}, bf16[32,8,128]{2,1,0:T(8,128)(2,1)S(1)}, u32[]{:S(2)}, u32[]{:S(2)}) collective-permute-start(bf16[32,8,128]{2,1,0:T(8,128)(2,1)S(1)} %get-tuple-element.38), channel_id=1, source_target_pairs={{0,16},{32,48},{64,80},{96,112},{128,144},{160,176},{192,208},{224... | collective-permute-start | bytes 196616 | tf_op jit(solution)/shard_map/ppermute | solution.py:242
  22.7 4.5 %copy-start.7 = (bf16[32,8,128]{2,1,0:T(8,128)(2,1)}, bf16[32,8,128]{2,1,0:T(8,128)(2,1)S(1)}, u32[]{:S(2)}) copy-start(bf16[32,8,128]{2,1,0:T(8,128)(2,1)S(1)} %collective-permute-done.3.odd_ref) | copy-start | bytes 196612
  27.2 0.6 copy-start.8
  29.7 4.5 %copy-start = (bf16[16,2,2,4,8,128]{5,4,3,2,1,0:T(8,128)(2,1)}, bf16[16,2,2,4,8,128]{5,4,3,2,1,0:T(8,128)(2,1)S(1)}, u32[]{:S(2)}) copy-start(bf16[16,2,2,4,8,128]{5,4,3,2,1,0:T(8,128)(2,1)S(1)} %all-to-all-done.own_ref) | copy-start | bytes 1572868
  29.7 27.1 %all-to-all-start.1 = ((bf16[8,39,8,128]{3,2,1,0:T(8,128)(2,1)}), bf16[8,39,8,128]{3,2,1,0:T(8,128)(2,1)S(1)}, u32[]{:S(2)}, u32[]{:S(2)}) async-start(bf16[8,39,8,128]{3,2,1,0:T(8,128)(2,1)} %shard_map.59), calls=%async_computation.1 | async-start | bytes 1277952 | tf_op jit(solution)/shard_map/all_to_all | solution.py:222
  34.2 10.9 %collective-permute-start.1 = (bf16[16,4,8,128]{3,2,1,0:T(8,128)(2,1)S(1)}, bf16[16,4,8,128]{3,2,1,0:T(8,128)(2,1)S(1)}, u32[]{:S(2)}, u32[]{:S(2)}) collective-permute-start(bf16[16,4,8,128]{3,2,1,0:T(8,128)(2,1)S(1)} %get-tuple-element.19), channel_id=1, source_target_pairs={{16,32},{48,64},{80,96},{112,128},{144,160},{176,192},{208,224},{2... | collective-permute-start | bytes 393224 | tf_op jit(solution)/shard_map/ppermute | solution.py:248
  37.1 8.5 %collective-permute-start = (bf16[16,4,8,128]{3,2,1,0:T(8,128)(2,1)S(1)}, bf16[16,4,8,128]{3,2,1,0:T(8,128)(2,1)S(1)}, u32[]{:S(2)}, u32[]{:S(2)}) collective-permute-start(bf16[16,4,8,128]{3,2,1,0:T(8,128)(2,1)S(1)} %get-tuple-element.20), channel_id=1, source_target_pairs={{0,16},{32,48},{64,80},{96,112},{128,144},{160,176},{192,208},{224... | collective-permute-start | bytes 393224 | tf_op jit(solution)/shard_map/ppermute | solution.py:248
  45.1 0.6 copy-start.10
  45.8 0.6 copy-start.11
  50.1 4.5 %collective-permute-start.5 = (f32[8,27,8,128]{3,2,1,0:T(8,128)}, f32[8,27,8,128]{3,2,1,0:T(8,128)S(1)}, u32[]{:S(2)}, u32[]{:S(2)}) collective-permute-start(f32[8,27,8,128]{3,2,1,0:T(8,128)} %get-tuple-element.13), channel_id=1, source_target_pairs={{0,1},{1,0},{2,3},{3,2},{4,5},{5,4},{6,7},{7,6},{8,9},{9,8},{10,11... | collective-permute-start | bytes 2654216 | tf_op jit(solution)/shard_map/ppermute | solution.py:277
  56.8 8.1 %copy-start.1 = (bf16[8,39,8,128]{3,2,1,0:T(8,128)(2,1)}, bf16[8,39,8,128]{3,2,1,0:T(8,128)(2,1)S(1)}, u32[]{:S(2)}) copy-start(bf16[8,39,8,128]{3,2,1,0:T(8,128)(2,1)S(1)} %all-to-all-done.1.mine_ref) | copy-start | bytes 1916932
  56.8 21.4 %all-to-all-start.2 = ((f32[8,27,8,128]{3,2,1,0:T(8,128)}), f32[8,27,8,128]{3,2,1,0:T(8,128)S(1)}, u32[]{:S(2)}, u32[]{:S(2)}) async-start(f32[8,27,8,128]{3,2,1,0:T(8,128)} %add.36), calls=%async_computation.2 | async-start | bytes 1769472 | tf_op jit(solution)/shard_map/all_to_all | solution.py:222
  64.9 4.0 %collective-permute-start.4 = (bf16[8,39,8,128]{3,2,1,0:T(8,128)(2,1)S(1)}, bf16[8,39,8,128]{3,2,1,0:T(8,128)(2,1)S(1)}, u32[]{:S(2)}, u32[]{:S(2)}) collective-permute-start(bf16[8,39,8,128]{3,2,1,0:T(8,128)(2,1)S(1)} %all-to-all-done.1.mine_ref), channel_id=1, source_target_pairs={{0,1},{1,0},{2,3},{3,2},{4,5},{5,4},{6,7},{7,6},{8,9},{9,8},{10,11... | collective-permute-start | bytes 1916936 | tf_op jit(solution)/shard_map/ppermute | solution.py:258
  68.9 0.8 copy-start.9
  73.6 3.1 %copy-start.3 = (f32[2,4,2,2,2,8,128]{6,5,4,3,2,1,0:T(8,128)S(1)}, f32[2,4,2,2,2,8,128]{6,5,4,3,2,1,0:T(8,128)}, u32[]{:S(2)}) copy-start(f32[2,4,2,2,2,8,128]{6,5,4,3,2,1,0:T(8,128)} %get-tuple-element.11) | copy-start | bytes 786436
  73.7 4.6 %collective-permute-start.6 = (f32[2,4,2,2,2,8,128]{6,5,4,3,2,1,0:T(8,128)}, f32[2,4,2,2,2,8,128]{6,5,4,3,2,1,0:T(8,128)S(1)}, u32[]{:S(2)}, u32[]{:S(2)}) collective-permute-start(f32[2,4,2,2,2,8,128]{6,5,4,3,2,1,0:T(8,128)} %get-tuple-element.14), channel_id=1, source_target_pairs={{0,1},{1,0},{2,3},{3,2},{4,5},{5,4},{6,7},{7,6},{8,9},{9,8},{10,11... | collective-permute-start | bytes 786440 | tf_op jit(solution)/shard_map/ppermute | solution.py:298
  79.0 22.4 %all-to-all-start.3 = ((f32[32,8,128]{2,1,0:T(8,128)}), f32[32,8,128]{2,1,0:T(8,128)S(1)}, u32[]{:S(2)}, u32[]{:S(2)}) async-start(f32[32,8,128]{2,1,0:T(8,128)} %pad.4), calls=%async_computation.3 | async-start | bytes 262144 | tf_op jit(solution)/shard_map/all_to_all | solution.py:222
  89.4 16.8 %collective-permute-start.7 = (f32[2,4,2,2,2,8,128]{6,5,4,3,2,1,0:T(8,128)S(1)}, f32[2,4,2,2,2,8,128]{6,5,4,3,2,1,0:T(8,128)S(1)}, u32[]{:S(2)}, u32[]{:S(2)}) collective-permute-start(f32[2,4,2,2,2,8,128]{6,5,4,3,2,1,0:T(8,128)S(1)} %pad_maximum_fusion), channel_id=1, source_target_pairs={{0,8},{8,0},{1,9},{9,1},{2,10},{10,2},{3,11},{11,3},{4,12},{12,4},... | collective-permute-start | bytes 786440 | tf_op jit(solution)/shard_map/ppermute | solution.py:300
  102.0 22.7 %all-to-all-start.4 = ((f32[32,8,128]{2,1,0:T(8,128)}), f32[32,8,128]{2,1,0:T(8,128)S(1)}, u32[]{:S(2)}, u32[]{:S(2)}) async-start(f32[32,8,128]{2,1,0:T(8,128)} %broadcast_in_dim.2), calls=%async_computation.4 | async-start | bytes 262144 | tf_op jit(solution)/shard_map/all_to_all | solution.py:222
  106.2 11.1 %collective-permute-start.8 = (f32[4,2,2,2,8,128]{5,4,3,2,1,0:T(8,128)S(1)}, f32[4,2,2,2,8,128]{5,4,3,2,1,0:T(8,128)S(1)}, u32[]{:S(2)}, u32[]{:S(2)}) collective-permute-start(f32[4,2,2,2,8,128]{5,4,3,2,1,0:T(8,128)S(1)} %pad_maximum_fusion.2), channel_id=1, source_target_pairs={{0,2},{2,0},{4,6},{6,4},{1,3},{3,1},{5,7},{7,5},{8,10},{10,8},{12,... | collective-permute-start | bytes 393224 | tf_op jit(solution)/shard_map/ppermute | solution.py:303
  109.5 8.4 %collective-permute-start.9 = (f32[4,2,2,2,8,128]{5,4,3,2,1,0:T(8,128)S(1)}, f32[4,2,2,2,8,128]{5,4,3,2,1,0:T(8,128)S(1)}, u32[]{:S(2)}, u32[]{:S(2)}) collective-permute-start(f32[4,2,2,2,8,128]{5,4,3,2,1,0:T(8,128)S(1)} %pad_maximum_fusion.3), channel_id=1, source_target_pairs={{0,4},{2,6},{4,0},{6,2},{1,5},{3,7},{5,1},{7,3},{8,12},{10,14},{12... | collective-permute-start | bytes 393224 | tf_op jit(solution)/shard_map/ppermute | solution.py:303
  114.1 8.1 %collective-permute-start.10 = (f32[4,2,2,2,8,128]{5,4,3,2,1,0:T(8,128)S(1)}, f32[4,2,2,2,8,128]{5,4,3,2,1,0:T(8,128)S(1)}, u32[]{:S(2)}, u32[]{:S(2)}) collective-permute-start(f32[4,2,2,2,8,128]{5,4,3,2,1,0:T(8,128)S(1)} %pad_maximum_fusion.4), channel_id=1, source_target_pairs={{0,6},{2,4},{4,2},{6,0},{1,7},{3,5},{5,3},{7,1},{8,14},{10,12},{12... | collective-permute-start | bytes 393224 | tf_op jit(solution)/shard_map/ppermute | solution.py:303
  117.4 4.8 %copy-start.4 = (f32[4,2,2,2,8,128]{5,4,3,2,1,0:T(8,128)}, f32[4,2,2,2,8,128]{5,4,3,2,1,0:T(8,128)S(1)}, u32[]{:S(2)}) copy-start(f32[4,2,2,2,8,128]{5,4,3,2,1,0:T(8,128)S(1)} %collective-permute-done.8.refs_1_) | copy-start | bytes 393220
  117.9 4.3 %copy-start.5 = (f32[4,2,2,2,8,128]{5,4,3,2,1,0:T(8,128)}, f32[4,2,2,2,8,128]{5,4,3,2,1,0:T(8,128)S(1)}, u32[]{:S(2)}) copy-start(f32[4,2,2,2,8,128]{5,4,3,2,1,0:T(8,128)S(1)} %collective-permute-done.9.refs_2_) | copy-start | bytes 393220
  122.2 0.6 copy-start.6

commit v6 on v5

--- a/solution.py
+++ b/solution.py
@@ -160,7 +160,7 @@
 
 
 def conv_kernel(
-    p_ref, own_ref, even_ref, odd_ref, mine_ref, other_ref, keep_ref, send_ref, s_ref, wt_ref, wf_ref, o_ref, sems
+    p_ref, own_ref, even_ref, odd_ref, mine_ref, other_ref, out0, out1, out2, out3, s_ref, wt_ref, wf_ref, o_ref, sems
 ):
     n, _, nz, nr, cg, w = own_ref.shape
     nh, ch = nr - 2, n * cg
@@ -193,13 +193,10 @@
                 total = part if total is None else total + part
             for d in range(n):
                 dzl, dx, dcore = place_of(d)
-                slot = (dcore ^ core, dzl ^ zl, dx ^ x)
+                slot = (2 * (dzl ^ zl) + (dcore ^ core), dx ^ x)
                 for h in range(nh):
                     o_ref[(*slot, k, z, h)] = total[d * cg : (d + 1) * cg, h * w : (h + 1) * w]
-    copies = [
-        pltpu.make_async_copy(o_ref.at[1], send_ref, sems.at[1]),
-        pltpu.make_async_copy(o_ref.at[0], keep_ref, sems.at[0]),
-    ]
+    copies = [pltpu.make_async_copy(o_ref.at[j], ref, sems.at[j]) for j, ref in enumerate((out0, out1, out2, out3))]
     for copy in copies:
         copy.start()
     for copy in copies:
@@ -274,34 +271,37 @@
         ),
         name="wgrad",
     )(index, own, *x_halos)
-    pair = keep + lax.ppermute(send, "core", swap)
+    got = lax.ppermute(send, "core", swap)
+    pair = keep + got
     pieces = swap_all(pair, CHIPS).reshape(chips, 27, cg, ch)
     group = pieces.sum(0)
 
-    keep, send = pl.pallas_call(
+    near = pl.pallas_call(
         conv_kernel,
-        out_shape=(sds((2, 4, 2, nz, nh, cg, w), F32),) * 2,
+        out_shape=(sds((4, 2, nz, nh, cg, w), F32),) * 4,
         in_specs=[pl.BlockSpec(memory_space=pltpu.SMEM)] + vmem_specs(5),
-        out_specs=(any_spec, any_spec),
+        out_specs=(any_spec,) * 4,
         scratch_shapes=[
             pltpu.VMEM((2, nz + 2, 9 * ch, nh * w), BF),
             pltpu.VMEM((3, ch, 9 * ch), BF),
             pltpu.VMEM((3, ch, 9 * ch), BF),
-            pltpu.VMEM((2, 2, 4, 2, nz, nh, cg, w), F32),
-            pltpu.SemaphoreType.DMA((2,)),
+            pltpu.VMEM((4, 4, 2, nz, nh, cg, w), F32),
+            pltpu.SemaphoreType.DMA((4,)),
         ],
         cost_estimate=pl.CostEstimate(
             flops=4 * 27 * ch * ch * nz * nh * w, transcendentals=0, bytes_accessed=4 * 27 * ch * ch
         ),
         name="conv",
     )(index, own, *x_halos, mine, other)
-    got = lax.ppermute(send, "core", swap)
-    group, got = lax.optimization_barrier((group, got))
-    far = lax.ppermute(jnp.stack([keep[1], got[1]]), "zl", swap)
-    blocks = [jnp.stack([keep[0, j], got[0, j], far[0, j], far[1, j]]) for j in range(4)]
-    blocks = blocks[:1] + [
-        lax.ppermute(blocks[j], "x", [(i, i ^ j) for i in range(4)]) for j in range(1, 4)
-    ]
+    near = (
+        near[0],
+        lax.ppermute(near[1], "core", swap),
+        lax.ppermute(near[2], "zl", swap),
+        lax.ppermute(near[3], ("zl", "core"), [(i, 3 - i) for i in range(4)]),
+    )
+    _, near = lax.optimization_barrier((group, near))
+    blocks = [jnp.stack([part[j] for part in near]) for j in range(4)]
+    blocks = blocks[:1] + [lax.ppermute(blocks[j], "x", [(i, i ^ j) for i in range(4)]) for j in range(1, 4)]
     output, grad_in = call(place_kernel, [sds((nz, rows, cg, w), F32)] * 2, [index, *blocks], smem=1)
 
     padded = jnp.pad(group, ((0, ns - 27), (0, 0), (0, 0)))

time: 126 us -> 132 us (1.048)
  starting transfers between devices: 72.8 us -> 76.1 us
  waiting for transfers between devices: 29.6 us -> 32.9 us
    ppermute x1, waiting for transfers between devices: 0.01 us -> 2.6 us  [step(): got = lax.ppermute(send, 'core', swap)]
    ppermute x2 -> x3, starting transfers between devices: 5.29 us -> 7.88 us  [the longest x1 3.92 us: step(): lax.ppermute(near[2], 'zl', swap)]
    ppermute x2 -> x3, waiting for transfers between devices: 2.6 us -> 4.97 us  [the longest x1 3.4 us: step(): lax.ppermute(near[3], ('zl', 'core'), [(i, 3 - i) for i in range(4)])]
  transfers between devices with their start and end apart: 16 -> 17, of which waited for: 10 -> 10; matrix products, arithmetic and copies ran while one was open for 4% -> 3% of each run, Pallas kernels for 9% -> 9%
where the time goes in v6:
time: 132 us; the launch traced here: 131 us
  starting transfers between devices  76.1 us (58%)
  waiting for transfers between devices  32.9 us (25%)
  Pallas kernels  13.2 us (10%)
  local copies, waits for them, and re-layouts  4.99 us (4%)
  other arithmetic  3.01 us (2%)
    all_to_all x5, starting transfers between devices, swap_all(): return lax.all_to_all(array, axes, 0, 0, tiled=True)  33.4 us
    ppermute x2, starting transfers between devices, step(): lax.ppermute(lax.dynamic_slice(grad_out, (side, 0, 0, 0), (1, rows, cg, w...  12.5 us
    ppermute x3, starting transfers between devices, step(): lax.ppermute(blocks[j], 'x', [(i, i ^ j) for i in range(4)])  11.3 us
    all_to_all x5, waiting for transfers between devices, swap_all(): return lax.all_to_all(array, axes, 0, 0, tiled=True)  8.82 us
    ppermute x2, starting transfers between devices, step(): lax.ppermute(lax.dynamic_slice(own, (0, 0, side, 0, 0, 0), (n, 1, 1, nr,...  7.17 us
    ppermute x2, waiting for transfers between devices, step(): lax.ppermute(lax.dynamic_slice(grad_out, (side, 0, 0, 0), (1, rows, cg, w...  5.87 us
    pallas_call x3, Pallas kernels, call(): pl.pallas_call(kernel, out_shape=tuple(outs), in_specs=specs, out_specs=t...  5.56 us
    ppermute x3, waiting for transfers between devices, step(): lax.ppermute(blocks[j], 'x', [(i, i ^ j) for i in range(4)])  4.31 us
  transfers between devices with their start and end apart: 17, of which 10 were waited for; matrix products, arithmetic and copies ran while one was open for 3% of the time, Pallas kernels for 9%

profile of v6, /device:TPU:8, one launch (start us, length us, event | category | flops | bytes accessed | tf_op | source)
XLA Modules:
  0.0 131.1 jit_solution(1761041542159976151)
XLA Ops:
  0.6 1.8 %shard_map.58 = bf16[16,2,2,4,8,128]{5,4,3,2,1,0:T(8,128)(2,1)} custom-call(bf16[2,32,8,128]{3,2,1,0:T(8,128)(2,1)} %x_ref.1, bf16[2,32,8,128]{3,2,1,0:T(8,128)(2,1)} %g_ref.1), custom_call_target="tpu_custom_call" | custom-call | bytes 786432 | tf_op jit(solution)/shard_map/pallas_call | solution.py:23
  2.5 6.3 %all-to-all-start = ((bf16[16,2,2,4,8,128]{5,4,3,2,1,0:T(8,128)(2,1)}), bf16[16,2,2,4,8,128]{5,4,3,2,1,0:T(8,128)(2,1)S(1)}, u32[]{:S(2)}, u32[]{:S(2)}) async-start(bf16[16,2,2,4,8,128]{5,4,3,2,1,0:T(8,128)(2,1)} %shard_map.58), calls=%async_computation | async-start | bytes 1048576 | tf_op jit(solution)/shard_map/all_to_all | solution.py:219
  8.9 9.9 %collective-permute-start.4 = (bf16[32,8,128]{2,1,0:T(8,128)(2,1)S(1)}, bf16[32,8,128]{2,1,0:T(8,128)(2,1)S(1)}, u32[]{:S(2)}, u32[]{:S(2)}) collective-permute-start(bf16[32,8,128]{2,1,0:T(8,128)(2,1)S(1)} %get-tuple-element.45), channel_id=1, source_target_pairs={{16,32},{48,64},{80,96},{112,128},{144,160},{176,192},{208,224},{2... | collective-permute-start | bytes 196616 | tf_op jit(solution)/shard_map/ppermute | solution.py:239
  18.8 2.6 %collective-permute-start.3 = (bf16[32,8,128]{2,1,0:T(8,128)(2,1)S(1)}, bf16[32,8,128]{2,1,0:T(8,128)(2,1)S(1)}, u32[]{:S(2)}, u32[]{:S(2)}) collective-permute-start(bf16[32,8,128]{2,1,0:T(8,128)(2,1)S(1)} %get-tuple-element.46), channel_id=1, source_target_pairs={{0,16},{32,48},{64,80},{96,112},{128,144},{160,176},{192,208},{224... | collective-permute-start | bytes 196616 | tf_op jit(solution)/shard_map/ppermute | solution.py:239
  21.4 1.3 %collective-permute-done.4.odd_ref = bf16[32,8,128]{2,1,0:T(8,128)(2,1)S(1)} collective-permute-done((bf16[32,8,128]{2,1,0:T(8,128)(2,1)S(1)}, bf16[32,8,128]{2,1,0:T(8,128)(2,1)S(1)}, u32[]{:S(2)}, u32[]{:S(2)}) %collective-permute-start.4) | collective-permute-done | bytes 65568 | tf_op jit(solution)/shard_map/ppermute | solution.py:239
  22.7 4.5 %collective-permute-done.3.even_ref = bf16[32,8,128]{2,1,0:T(8,128)(2,1)S(1)} collective-permute-done((bf16[32,8,128]{2,1,0:T(8,128)(2,1)S(1)}, bf16[32,8,128]{2,1,0:T(8,128)(2,1)S(1)}, u32[]{:S(2)}, u32[]{:S(2)}) %collective-permute-start.3) | collective-permute-done | bytes 65568 | tf_op jit(solution)/shard_map/ppermute | solution.py:239
  27.9 1.8 %shard_map.59 = bf16[8,39,8,128]{3,2,1,0:T(8,128)(2,1)} custom-call(s32[1]{0:T(128)} %bitcast.p_ref, bf16[27,8,128]{2,1,0:T(8,128)(2,1)} %bitcast.16, bf16[32,8,128]{2,1,0:T(8,128)(2,1)} %copy-done.8, bf16[32,8,128]{2,1,0:T(8,128)(2,1)} %copy-done.7), custom_call_target="tpu_custom_call" | custom-call | bytes 825348 | tf_op jit(solution)/shard_map/pallas_call | solution.py:23
  29.7 4.5 %all-to-all-start.2 = ((bf16[8,39,8,128]{3,2,1,0:T(8,128)(2,1)}), bf16[8,39,8,128]{3,2,1,0:T(8,128)(2,1)S(1)}, u32[]{:S(2)}, u32[]{:S(2)}) async-start(bf16[8,39,8,128]{3,2,1,0:T(8,128)(2,1)} %shard_map.59), calls=%async_computation.2 | async-start | bytes 1277952 | tf_op jit(solution)/shard_map/all_to_all | solution.py:219
  34.2 2.9 %collective-permute-start.1 = (bf16[16,4,8,128]{3,2,1,0:T(8,128)(2,1)S(1)}, bf16[16,4,8,128]{3,2,1,0:T(8,128)(2,1)S(1)}, u32[]{:S(2)}, u32[]{:S(2)}) collective-permute-start(bf16[16,4,8,128]{3,2,1,0:T(8,128)(2,1)S(1)} %get-tuple-element.27), channel_id=1, source_target_pairs={{16,32},{48,64},{80,96},{112,128},{144,160},{176,192},{208,224},{2... | collective-permute-start | bytes 393224 | tf_op jit(solution)/shard_map/ppermute | solution.py:245
  37.1 4.3 %collective-permute-start = (bf16[16,4,8,128]{3,2,1,0:T(8,128)(2,1)S(1)}, bf16[16,4,8,128]{3,2,1,0:T(8,128)(2,1)S(1)}, u32[]{:S(2)}, u32[]{:S(2)}) collective-permute-start(bf16[16,4,8,128]{3,2,1,0:T(8,128)(2,1)S(1)} %get-tuple-element.28), channel_id=1, source_target_pairs={{0,16},{32,48},{64,80},{96,112},{128,144},{160,176},{192,208},{224... | collective-permute-start | bytes 393224 | tf_op jit(solution)/shard_map/ppermute | solution.py:245
  41.4 3.7 %collective-permute-done.1.odd_ref = bf16[16,4,8,128]{3,2,1,0:T(8,128)(2,1)S(1)} collective-permute-done((bf16[16,4,8,128]{3,2,1,0:T(8,128)(2,1)S(1)}, bf16[16,4,8,128]{3,2,1,0:T(8,128)(2,1)S(1)}, u32[]{:S(2)}, u32[]{:S(2)}) %collective-permute-start.1) | collective-permute-done | bytes 131104 | tf_op jit(solution)/shard_map/ppermute | solution.py:245
  46.4 3.7 %wgrad.1 = (f32[8,27,8,128]{3,2,1,0:T(8,128)}, f32[8,27,8,128]{3,2,1,0:T(8,128)}) custom-call(s32[1]{0:T(128)} %bitcast.p_ref, bf16[16,2,2,4,8,128]{5,4,3,2,1,0:T(8,128)(2,1)} %copy-done, bf16[16,4,8,128]{3,2,1,0:T(8,128)(2,1)} %copy-done.11, bf16[16,4,8,128]{3,2,1,0:T(8,128)(2,1)} %copy-done.10), custom_call_target="tpu_custom_call" | custom-call | flops 452984832 | bytes 1769472 | tf_op jit(solution)/shard_map/wgrad/pallas_call | solution.py:258
  50.1 1.9 %collective-permute-start.2 = (f32[8,27,8,128]{3,2,1,0:T(8,128)}, f32[8,27,8,128]{3,2,1,0:T(8,128)S(1)}, u32[]{:S(2)}, u32[]{:S(2)}) collective-permute-start(f32[8,27,8,128]{3,2,1,0:T(8,128)} %get-tuple-element.16), channel_id=1, source_target_pairs={{0,1},{1,0},{2,3},{3,2},{4,5},{5,4},{6,7},{7,6},{8,9},{9,8},{10,11... | collective-permute-start | bytes 2654216 | tf_op jit(solution)/shard_map/ppermute | solution.py:274
  52.1 2.6 %collective-permute-done.2 = f32[8,27,8,128]{3,2,1,0:T(8,128)S(1)} collective-permute-done((f32[8,27,8,128]{3,2,1,0:T(8,128)}, f32[8,27,8,128]{3,2,1,0:T(8,128)S(1)}, u32[]{:S(2)}, u32[]{:S(2)}) %collective-permute-start.2) | collective-permute-done | bytes 884768 | tf_op jit(solution)/shard_map/ppermute | solution.py:274
  54.7 2.2 %add.36 = f32[8,27,8,128]{3,2,1,0:T(8,128)} add(f32[8,27,8,128]{3,2,1,0:T(8,128)} %get-tuple-element.15, f32[8,27,8,128]{3,2,1,0:T(8,128)S(1)} %collective-permute-done.2) | non-fusion elementwise | flops 221184 | bytes 2654208 | tf_op jit(solution)/shard_map/add | solution.py:275
  56.9 8.1 %all-to-all-start.1 = ((f32[8,27,8,128]{3,2,1,0:T(8,128)}), f32[8,27,8,128]{3,2,1,0:T(8,128)S(1)}, u32[]{:S(2)}, u32[]{:S(2)}) async-start(f32[8,27,8,128]{3,2,1,0:T(8,128)} %add.36), calls=%async_computation.1 | async-start | bytes 1769472 | tf_op jit(solution)/shard_map/all_to_all | solution.py:219
  65.0 1.9 %collective-permute-start.5 = (bf16[8,39,8,128]{3,2,1,0:T(8,128)(2,1)S(1)}, bf16[8,39,8,128]{3,2,1,0:T(8,128)(2,1)S(1)}, u32[]{:S(2)}, u32[]{:S(2)}) collective-permute-start(bf16[8,39,8,128]{3,2,1,0:T(8,128)(2,1)S(1)} %all-to-all-done.2.mine_ref), channel_id=1, source_target_pairs={{0,1},{1,0},{2,3},{3,2},{4,5},{5,4},{6,7},{7,6},{8,9},{9,8},{10,11... | collective-permute-start | bytes 1916936 | tf_op jit(solution)/shard_map/ppermute | solution.py:255
  66.9 2.0 %collective-permute-done.5.other_ref = bf16[8,39,8,128]{3,2,1,0:T(8,128)(2,1)S(1)} collective-permute-done((bf16[8,39,8,128]{3,2,1,0:T(8,128)(2,1)S(1)}, bf16[8,39,8,128]{3,2,1,0:T(8,128)(2,1)S(1)}, u32[]{:S(2)}, u32[]{:S(2)}) %collective-permute-start.5) | collective-permute-done | bytes 639008 | tf_op jit(solution)/shard_map/ppermute | solution.py:255
  69.8 4.0 %conv.1 = (f32[4,2,2,2,8,128]{5,4,3,2,1,0:T(8,128)}, f32[4,2,2,2,8,128]{5,4,3,2,1,0:T(8,128)}, f32[4,2,2,2,8,128]{5,4,3,2,1,0:T(8,128)}, f32[4,2,2,2,8,128]{5,4,3,2,1,0:T(8,128)}) custom-call(s32[1]{0:T(128)} %bitcast.p_ref, bf16[16,2,2,4,8,128]{5,4,3,2,1,0:T(8,128)(2,1)} %copy-done, bf16[16,4,8,128]{3,2,1,0:T(8,128)(2,1)} %copy-done.11, ...), custom_call_target="tpu_custom_call" | custom-call | flops 905969664 | bytes 1769472 | tf_op jit(solution)/shard_map/conv/pallas_call | solution.py:279
  73.8 2.0 %collective-permute-start.6 = (f32[4,2,2,2,8,128]{5,4,3,2,1,0:T(8,128)}, f32[4,2,2,2,8,128]{5,4,3,2,1,0:T(8,128)S(1)}, u32[]{:S(2)}, u32[]{:S(2)}) collective-permute-start(f32[4,2,2,2,8,128]{5,4,3,2,1,0:T(8,128)} %get-tuple-element.18), channel_id=1, source_target_pairs={{0,1},{1,0},{2,3},{3,2},{4,5},{5,4},{6,7},{7,6},{8,9},{9,8},{10,11... | collective-permute-start | bytes 393224 | tf_op jit(solution)/shard_map/ppermute | solution.py:298
  75.8 3.9 %collective-permute-start.7 = (f32[4,2,2,2,8,128]{5,4,3,2,1,0:T(8,128)}, f32[4,2,2,2,8,128]{5,4,3,2,1,0:T(8,128)S(1)}, u32[]{:S(2)}, u32[]{:S(2)}) collective-permute-start(f32[4,2,2,2,8,128]{5,4,3,2,1,0:T(8,128)} %get-tuple-element.19), channel_id=1, source_target_pairs={{0,8},{8,0},{1,9},{9,1},{2,10},{10,2},{3,11},{11,3},{4,12},{12,4},... | collective-permute-start | bytes 393224 | tf_op jit(solution)/shard_map/ppermute | solution.py:299
  79.7 1.9 %collective-permute-start.8 = (f32[4,2,2,2,8,128]{5,4,3,2,1,0:T(8,128)}, f32[4,2,2,2,8,128]{5,4,3,2,1,0:T(8,128)S(1)}, u32[]{:S(2)}, u32[]{:S(2)}) collective-permute-start(f32[4,2,2,2,8,128]{5,4,3,2,1,0:T(8,128)} %get-tuple-element.20), channel_id=1, source_target_pairs={{0,9},{1,8},{8,1},{9,0},{2,11},{3,10},{10,3},{11,2},{4,13},{5,12},... | collective-permute-start | bytes 393224 | tf_op jit(solution)/shard_map/ppermute | solution.py:300
  82.4 1.6 %collective-permute-done.7 = f32[4,2,2,2,8,128]{5,4,3,2,1,0:T(8,128)S(1)} collective-permute-done((f32[4,2,2,2,8,128]{5,4,3,2,1,0:T(8,128)}, f32[4,2,2,2,8,128]{5,4,3,2,1,0:T(8,128)S(1)}, u32[]{:S(2)}, u32[]{:S(2)}) %collective-permute-start.7) | collective-permute-done | bytes 131104 | tf_op jit(solution)/shard_map/ppermute | solution.py:299
  84.0 3.4 %collective-permute-done.8 = f32[4,2,2,2,8,128]{5,4,3,2,1,0:T(8,128)S(1)} collective-permute-done((f32[4,2,2,2,8,128]{5,4,3,2,1,0:T(8,128)}, f32[4,2,2,2,8,128]{5,4,3,2,1,0:T(8,128)S(1)}, u32[]{:S(2)}, u32[]{:S(2)}) %collective-permute-start.8) | collective-permute-done | bytes 131104 | tf_op jit(solution)/shard_map/ppermute | solution.py:300
  87.4 10.5 %all-to-all-start.3 = ((f32[32,8,128]{2,1,0:T(8,128)}), f32[32,8,128]{2,1,0:T(8,128)S(1)}, u32[]{:S(2)}, u32[]{:S(2)}) async-start(f32[32,8,128]{2,1,0:T(8,128)} %pad.4), calls=%async_computation.3 | async-start | bytes 262144 | tf_op jit(solution)/shard_map/all_to_all | solution.py:219
  97.9 3.4 %collective-permute-start.9 = (f32[4,2,2,2,8,128]{5,4,3,2,1,0:T(8,128)S(1)}, f32[4,2,2,2,8,128]{5,4,3,2,1,0:T(8,128)S(1)}, u32[]{:S(2)}, u32[]{:S(2)}) collective-permute-start(f32[4,2,2,2,8,128]{5,4,3,2,1,0:T(8,128)S(1)} %pad_maximum_fusion.1), channel_id=1, source_target_pairs={{0,2},{2,0},{4,6},{6,4},{1,3},{3,1},{5,7},{7,5},{8,10},{10,8},{12,... | collective-permute-start | bytes 393224 | tf_op jit(solution)/shard_map/ppermute | solution.py:304
  101.3 8.8 %all-to-all-done.3 = f32[32,8,128]{2,1,0:T(8,128)S(1)} async-done(((f32[32,8,128]{2,1,0:T(8,128)}), f32[32,8,128]{2,1,0:T(8,128)S(1)}, u32[]{:S(2)}, u32[]{:S(2)}) %all-to-all-start.3) | async-done | bytes 131104 | tf_op jit(solution)/shard_map/all_to_all | solution.py:219
  110.8 4.0 %all-to-all-start.4 = ((f32[32,8,128]{2,1,0:T(8,128)}), f32[32,8,128]{2,1,0:T(8,128)S(1)}, u32[]{:S(2)}, u32[]{:S(2)}) async-start(f32[32,8,128]{2,1,0:T(8,128)} %broadcast_in_dim.2), calls=%async_computation.4 | async-start | bytes 262144 | tf_op jit(solution)/shard_map/all_to_all | solution.py:219
  114.9 4.9 %collective-permute-start.10 = (f32[4,2,2,2,8,128]{5,4,3,2,1,0:T(8,128)S(1)}, f32[4,2,2,2,8,128]{5,4,3,2,1,0:T(8,128)S(1)}, u32[]{:S(2)}, u32[]{:S(2)}) collective-permute-start(f32[4,2,2,2,8,128]{5,4,3,2,1,0:T(8,128)S(1)} %pad_maximum_fusion.2), channel_id=1, source_target_pairs={{0,4},{2,6},{4,0},{6,2},{1,5},{3,7},{5,1},{7,3},{8,12},{10,14},{12... | collective-permute-start | bytes 393224 | tf_op jit(solution)/shard_map/ppermute | solution.py:304
  119.8 3.1 %collective-permute-start.11 = (f32[4,2,2,2,8,128]{5,4,3,2,1,0:T(8,128)S(1)}, f32[4,2,2,2,8,128]{5,4,3,2,1,0:T(8,128)S(1)}, u32[]{:S(2)}, u32[]{:S(2)}) collective-permute-start(f32[4,2,2,2,8,128]{5,4,3,2,1,0:T(8,128)S(1)} %pad_maximum_fusion.3), channel_id=1, source_target_pairs={{0,6},{2,4},{4,2},{6,0},{1,7},{3,5},{5,3},{7,1},{8,14},{10,12},{12... | collective-permute-start | bytes 393224 | tf_op jit(solution)/shard_map/ppermute | solution.py:304
  123.6 4.3 %collective-permute-done.11.refs_3_ = f32[4,2,2,2,8,128]{5,4,3,2,1,0:T(8,128)S(1)} collective-permute-done((f32[4,2,2,2,8,128]{5,4,3,2,1,0:T(8,128)S(1)}, f32[4,2,2,2,8,128]{5,4,3,2,1,0:T(8,128)S(1)}, u32[]{:S(2)}, u32[]{:S(2)}) %collective-permute-start.11) | collective-permute-done | bytes 131104 | tf_op jit(solution)/shard_map/ppermute | solution.py:304
  128.5 1.9 %shard_map.60 = (f32[2,32,8,128]{3,2,1,0:T(8,128)}, f32[2,32,8,128]{3,2,1,0:T(8,128)}) custom-call(s32[1]{0:T(128)} %bitcast.p_ref, f32[4,2,2,2,8,128]{5,4,3,2,1,0:T(8,128)} %pad_maximum_fusion.refs_0_, f32[4,2,2,2,8,128]{5,4,3,2,1,0:T(8,128)} %copy-done.3, f32[4,2,2,2,8,128]{5,4,3,2,1,0:T(8,128)} %copy-done.4, f32[4,2,2,2,8,128]{5,4,3,2,1,0:T(8,128)} %copy-done.5), custom_call_target="tpu_custom_call" | custom-call | bytes 1048580 | tf_op jit(solution)/shard_map/pallas_call | solution.py:23
  (46 shorter events, 6.3 us)
Async XLA Ops:
  2.5 6.4 %copy-start.2 = (bf16[2,32,8,128]{3,2,1,0:T(8,128)(2,1)S(1)}, bf16[2,32,8,128]{3,2,1,0:T(8,128)(2,1)}, u32[]{:S(2)}) copy-start(bf16[2,32,8,128]{3,2,1,0:T(8,128)(2,1)} %g_ref.1) | copy-start | bytes 393220
  2.5 27.2 %all-to-all-start = ((bf16[16,2,2,4,8,128]{5,4,3,2,1,0:T(8,128)(2,1)}), bf16[16,2,2,4,8,128]{5,4,3,2,1,0:T(8,128)(2,1)S(1)}, u32[]{:S(2)}, u32[]{:S(2)}) async-start(bf16[16,2,2,4,8,128]{5,4,3,2,1,0:T(8,128)(2,1)} %shard_map.58), calls=%async_computation | async-start | bytes 1048576 | tf_op jit(solution)/shard_map/all_to_all | solution.py:219
  8.9 13.9 %collective-permute-start.4 = (bf16[32,8,128]{2,1,0:T(8,128)(2,1)S(1)}, bf16[32,8,128]{2,1,0:T(8,128)(2,1)S(1)}, u32[]{:S(2)}, u32[]{:S(2)}) collective-permute-start(bf16[32,8,128]{2,1,0:T(8,128)(2,1)S(1)} %get-tuple-element.45), channel_id=1, source_target_pairs={{16,32},{48,64},{80,96},{112,128},{144,160},{176,192},{208,224},{2... | collective-permute-start | bytes 196616 | tf_op jit(solution)/shard_map/ppermute | solution.py:239
  18.8 8.5 %collective-permute-start.3 = (bf16[32,8,128]{2,1,0:T(8,128)(2,1)S(1)}, bf16[32,8,128]{2,1,0:T(8,128)(2,1)S(1)}, u32[]{:S(2)}, u32[]{:S(2)}) collective-permute-start(bf16[32,8,128]{2,1,0:T(8,128)(2,1)S(1)} %get-tuple-element.46), channel_id=1, source_target_pairs={{0,16},{32,48},{64,80},{96,112},{128,144},{160,176},{192,208},{224... | collective-permute-start | bytes 196616 | tf_op jit(solution)/shard_map/ppermute | solution.py:239
  22.7 4.5 %copy-start.7 = (bf16[32,8,128]{2,1,0:T(8,128)(2,1)}, bf16[32,8,128]{2,1,0:T(8,128)(2,1)S(1)}, u32[]{:S(2)}) copy-start(bf16[32,8,128]{2,1,0:T(8,128)(2,1)S(1)} %collective-permute-done.4.odd_ref) | copy-start | bytes 196612
  27.3 0.6 copy-start.8
  29.7 4.5 %copy-start = (bf16[16,2,2,4,8,128]{5,4,3,2,1,0:T(8,128)(2,1)}, bf16[16,2,2,4,8,128]{5,4,3,2,1,0:T(8,128)(2,1)S(1)}, u32[]{:S(2)}) copy-start(bf16[16,2,2,4,8,128]{5,4,3,2,1,0:T(8,128)(2,1)S(1)} %all-to-all-done.own_ref) | copy-start | bytes 1572868
  29.7 27.2 %all-to-all-start.2 = ((bf16[8,39,8,128]{3,2,1,0:T(8,128)(2,1)}), bf16[8,39,8,128]{3,2,1,0:T(8,128)(2,1)S(1)}, u32[]{:S(2)}, u32[]{:S(2)}) async-start(bf16[8,39,8,128]{3,2,1,0:T(8,128)(2,1)} %shard_map.59), calls=%async_computation.2 | async-start | bytes 1277952 | tf_op jit(solution)/shard_map/all_to_all | solution.py:219
  34.2 10.9 %collective-permute-start.1 = (bf16[16,4,8,128]{3,2,1,0:T(8,128)(2,1)S(1)}, bf16[16,4,8,128]{3,2,1,0:T(8,128)(2,1)S(1)}, u32[]{:S(2)}, u32[]{:S(2)}) collective-permute-start(bf16[16,4,8,128]{3,2,1,0:T(8,128)(2,1)S(1)} %get-tuple-element.27), channel_id=1, source_target_pairs={{16,32},{48,64},{80,96},{112,128},{144,160},{176,192},{208,224},{2... | collective-permute-start | bytes 393224 | tf_op jit(solution)/shard_map/ppermute | solution.py:245
  37.1 8.5 %collective-permute-start = (bf16[16,4,8,128]{3,2,1,0:T(8,128)(2,1)S(1)}, bf16[16,4,8,128]{3,2,1,0:T(8,128)(2,1)S(1)}, u32[]{:S(2)}, u32[]{:S(2)}) collective-permute-start(bf16[16,4,8,128]{3,2,1,0:T(8,128)(2,1)S(1)} %get-tuple-element.28), channel_id=1, source_target_pairs={{0,16},{32,48},{64,80},{96,112},{128,144},{160,176},{192,208},{224... | collective-permute-start | bytes 393224 | tf_op jit(solution)/shard_map/ppermute | solution.py:245
  45.1 0.7 copy-start.10
  45.8 0.7 copy-start.11
  50.1 4.5 %collective-permute-start.2 = (f32[8,27,8,128]{3,2,1,0:T(8,128)}, f32[8,27,8,128]{3,2,1,0:T(8,128)S(1)}, u32[]{:S(2)}, u32[]{:S(2)}) collective-permute-start(f32[8,27,8,128]{3,2,1,0:T(8,128)} %get-tuple-element.16), channel_id=1, source_target_pairs={{0,1},{1,0},{2,3},{3,2},{4,5},{5,4},{6,7},{7,6},{8,9},{9,8},{10,11... | collective-permute-start | bytes 2654216 | tf_op jit(solution)/shard_map/ppermute | solution.py:274
  56.9 8.1 %copy-start.1 = (bf16[8,39,8,128]{3,2,1,0:T(8,128)(2,1)}, bf16[8,39,8,128]{3,2,1,0:T(8,128)(2,1)S(1)}, u32[]{:S(2)}) copy-start(bf16[8,39,8,128]{3,2,1,0:T(8,128)(2,1)S(1)} %all-to-all-done.2.mine_ref) | copy-start | bytes 1916932
  56.9 24.8 %all-to-all-start.1 = ((f32[8,27,8,128]{3,2,1,0:T(8,128)}), f32[8,27,8,128]{3,2,1,0:T(8,128)S(1)}, u32[]{:S(2)}, u32[]{:S(2)}) async-start(f32[8,27,8,128]{3,2,1,0:T(8,128)} %add.36), calls=%async_computation.1 | async-start | bytes 1769472 | tf_op jit(solution)/shard_map/all_to_all | solution.py:219
  65.0 4.0 %collective-permute-start.5 = (bf16[8,39,8,128]{3,2,1,0:T(8,128)(2,1)S(1)}, bf16[8,39,8,128]{3,2,1,0:T(8,128)(2,1)S(1)}, u32[]{:S(2)}, u32[]{:S(2)}) collective-permute-start(bf16[8,39,8,128]{3,2,1,0:T(8,128)(2,1)S(1)} %all-to-all-done.2.mine_ref), channel_id=1, source_target_pairs={{0,1},{1,0},{2,3},{3,2},{4,5},{5,4},{6,7},{7,6},{8,9},{9,8},{10,11... | collective-permute-start | bytes 1916936 | tf_op jit(solution)/shard_map/ppermute | solution.py:255
  69.0 0.8 copy-start.9
  73.8 8.6 %collective-permute-start.6 = (f32[4,2,2,2,8,128]{5,4,3,2,1,0:T(8,128)}, f32[4,2,2,2,8,128]{5,4,3,2,1,0:T(8,128)S(1)}, u32[]{:S(2)}, u32[]{:S(2)}) collective-permute-start(f32[4,2,2,2,8,128]{5,4,3,2,1,0:T(8,128)} %get-tuple-element.18), channel_id=1, source_target_pairs={{0,1},{1,0},{2,3},{3,2},{4,5},{5,4},{6,7},{7,6},{8,9},{9,8},{10,11... | collective-permute-start | bytes 393224 | tf_op jit(solution)/shard_map/ppermute | solution.py:298
  75.8 8.2 %collective-permute-start.7 = (f32[4,2,2,2,8,128]{5,4,3,2,1,0:T(8,128)}, f32[4,2,2,2,8,128]{5,4,3,2,1,0:T(8,128)S(1)}, u32[]{:S(2)}, u32[]{:S(2)}) collective-permute-start(f32[4,2,2,2,8,128]{5,4,3,2,1,0:T(8,128)} %get-tuple-element.19), channel_id=1, source_target_pairs={{0,8},{8,0},{1,9},{9,1},{2,10},{10,2},{3,11},{11,3},{4,12},{12,4},... | collective-permute-start | bytes 393224 | tf_op jit(solution)/shard_map/ppermute | solution.py:299
  79.7 7.6 %collective-permute-start.8 = (f32[4,2,2,2,8,128]{5,4,3,2,1,0:T(8,128)}, f32[4,2,2,2,8,128]{5,4,3,2,1,0:T(8,128)S(1)}, u32[]{:S(2)}, u32[]{:S(2)}) collective-permute-start(f32[4,2,2,2,8,128]{5,4,3,2,1,0:T(8,128)} %get-tuple-element.20), channel_id=1, source_target_pairs={{0,9},{1,8},{8,1},{9,0},{2,11},{3,10},{10,3},{11,2},{4,13},{5,12},... | collective-permute-start | bytes 393224 | tf_op jit(solution)/shard_map/ppermute | solution.py:300
  87.4 10.5 %copy-start.6 = (f32[4,2,2,2,8,128]{5,4,3,2,1,0:T(8,128)S(1)}, f32[4,2,2,2,8,128]{5,4,3,2,1,0:T(8,128)}, u32[]{:S(2)}) copy-start(f32[4,2,2,2,8,128]{5,4,3,2,1,0:T(8,128)} %get-tuple-element.21) | copy-start | bytes 393220
  87.4 22.8 %all-to-all-start.3 = ((f32[32,8,128]{2,1,0:T(8,128)}), f32[32,8,128]{2,1,0:T(8,128)S(1)}, u32[]{:S(2)}, u32[]{:S(2)}) async-start(f32[32,8,128]{2,1,0:T(8,128)} %pad.4), calls=%async_computation.3 | async-start | bytes 262144 | tf_op jit(solution)/shard_map/all_to_all | solution.py:219
  97.9 25.6 %collective-permute-start.9 = (f32[4,2,2,2,8,128]{5,4,3,2,1,0:T(8,128)S(1)}, f32[4,2,2,2,8,128]{5,4,3,2,1,0:T(8,128)S(1)}, u32[]{:S(2)}, u32[]{:S(2)}) collective-permute-start(f32[4,2,2,2,8,128]{5,4,3,2,1,0:T(8,128)S(1)} %pad_maximum_fusion.1), channel_id=1, source_target_pairs={{0,2},{2,0},{4,6},{6,4},{1,3},{3,1},{5,7},{7,5},{8,10},{10,8},{12,... | collective-permute-start | bytes 393224 | tf_op jit(solution)/shard_map/ppermute | solution.py:304
  110.8 19.6 %all-to-all-start.4 = ((f32[32,8,128]{2,1,0:T(8,128)}), f32[32,8,128]{2,1,0:T(8,128)S(1)}, u32[]{:S(2)}, u32[]{:S(2)}) async-start(f32[32,8,128]{2,1,0:T(8,128)} %broadcast_in_dim.2), calls=%async_computation.4 | async-start | bytes 262144 | tf_op jit(solution)/shard_map/all_to_all | solution.py:219
  114.9 8.7 %collective-permute-start.10 = (f32[4,2,2,2,8,128]{5,4,3,2,1,0:T(8,128)S(1)}, f32[4,2,2,2,8,128]{5,4,3,2,1,0:T(8,128)S(1)}, u32[]{:S(2)}, u32[]{:S(2)}) collective-permute-start(f32[4,2,2,2,8,128]{5,4,3,2,1,0:T(8,128)S(1)} %pad_maximum_fusion.2), channel_id=1, source_target_pairs={{0,4},{2,6},{4,0},{6,2},{1,5},{3,7},{5,1},{7,3},{8,12},{10,14},{12... | collective-permute-start | bytes 393224 | tf_op jit(solution)/shard_map/ppermute | solution.py:304
  119.8 8.1 %collective-permute-start.11 = (f32[4,2,2,2,8,128]{5,4,3,2,1,0:T(8,128)S(1)}, f32[4,2,2,2,8,128]{5,4,3,2,1,0:T(8,128)S(1)}, u32[]{:S(2)}, u32[]{:S(2)}) collective-permute-start(f32[4,2,2,2,8,128]{5,4,3,2,1,0:T(8,128)S(1)} %pad_maximum_fusion.3), channel_id=1, source_target_pairs={{0,6},{2,4},{4,2},{6,0},{1,7},{3,5},{5,3},{7,1},{8,14},{10,12},{12... | collective-permute-start | bytes 393224 | tf_op jit(solution)/shard_map/ppermute | solution.py:304
  123.6 4.3 %copy-start.3 = (f32[4,2,2,2,8,128]{5,4,3,2,1,0:T(8,128)}, f32[4,2,2,2,8,128]{5,4,3,2,1,0:T(8,128)S(1)}, u32[]{:S(2)}) copy-start(f32[4,2,2,2,8,128]{5,4,3,2,1,0:T(8,128)S(1)} %collective-permute-done.9.refs_1_) | copy-start | bytes 393220
  123.6 4.3 %copy-start.4 = (f32[4,2,2,2,8,128]{5,4,3,2,1,0:T(8,128)}, f32[4,2,2,2,8,128]{5,4,3,2,1,0:T(8,128)S(1)}, u32[]{:S(2)}) copy-start(f32[4,2,2,2,8,128]{5,4,3,2,1,0:T(8,128)S(1)} %collective-permute-done.10.refs_2_) | copy-start | bytes 393220
  127.9 0.6 copy-start.5

commit v7 on v6

--- a/solution.py
+++ b/solution.py
@@ -299,15 +299,17 @@
         lax.ppermute(near[2], "zl", swap),
         lax.ppermute(near[3], ("zl", "core"), [(i, 3 - i) for i in range(4)]),
     )
-    _, near = lax.optimization_barrier((group, near))
-    blocks = [jnp.stack([part[j] for part in near]) for j in range(4)]
-    blocks = blocks[:1] + [lax.ppermute(blocks[j], "x", [(i, i ^ j) for i in range(4)]) for j in range(1, 4)]
-    output, grad_in = call(place_kernel, [sds((nz, rows, cg, w), F32)] * 2, [index, *blocks], smem=1)
 
     padded = jnp.pad(group, ((0, ns - 27), (0, 0), (0, 0)))
     shares = swap_all(padded, SPACE)
+    _, near = lax.optimization_barrier((shares, near))
     tap = shares.sum(0) * norm
     taps = swap_all(jnp.broadcast_to(tap[None], (ns, cg, ch)), SPACE)
+    blocks = {j: jnp.stack([part[j] for part in near]) for j in (2, 1, 3, 0)}
+    blocks = {j: lax.ppermute(b, "x", [(i, i ^ j) for i in range(4)]) if j else b for j, b in blocks.items()}
+    output, grad_in = call(
+        place_kernel, [sds((nz, rows, cg, w), F32)] * 2, [index] + [blocks[j] for j in range(4)], smem=1
+    )
     weight_grad = taps[:27].reshape(3, 3, 3, cg, ch).transpose(0, 1, 2, 4, 3)
     return output, grad_in, weight_grad
 

time: 132 us -> 139 us (1.053)
  the two profiles are of different devices: /device:TPU:8 before, /device:TPU:6 now
where the time goes in v7:
time: 139 us; the launch traced here: 137 us
  starting transfers between devices  86 us (62%)
  waiting for transfers between devices  29.1 us (21%)
  Pallas kernels  13.2 us (9%)
  local copies, waits for them, and re-layouts  4.83 us (3%)
  other arithmetic  2.95 us (2%)
    all_to_all x5, starting transfers between devices, swap_all(): return lax.all_to_all(array, axes, 0, 0, tiled=True)  45.1 us
    ppermute x3, starting transfers between devices, step(): lax.ppermute(b, 'x', [(i, i ^ j) for i in range(4)])  10.4 us
    ppermute x2, starting transfers between devices, step(): lax.ppermute(lax.dynamic_slice(grad_out, (side, 0, 0, 0), (1, rows, cg, w...  9.87 us
    all_to_all x5, waiting for transfers between devices, swap_all(): return lax.all_to_all(array, axes, 0, 0, tiled=True)  9.71 us
    ppermute x2, starting transfers between devices, step(): lax.ppermute(lax.dynamic_slice(own, (0, 0, side, 0, 0, 0), (n, 1, 1, nr,...  9.2 us
    pallas_call x3, Pallas kernels, call(): pl.pallas_call(kernel, out_shape=tuple(outs), in_specs=specs, out_specs=t...  5.55 us
    ppermute x3, waiting for transfers between devices, step(): lax.ppermute(b, 'x', [(i, i ^ j) for i in range(4)])  4.04 us
    ppermute x2, waiting for transfers between devices, step(): lax.ppermute(lax.dynamic_slice(own, (0, 0, side, 0, 0, 0), (n, 1, 1, nr,...  3.97 us
  transfers between devices with their start and end apart: 17, of which 8 were waited for; matrix products, arithmetic and copies ran while one was open for 3% of the time, Pallas kernels for 8%

profile of v7, /device:TPU:6, one launch (start us, length us, event | category | flops | bytes accessed | tf_op | source)
XLA Modules:
  0.0 136.9 jit_solution(14696990092282947501)
XLA Ops:
  0.6 1.8 %shard_map.58 = bf16[16,2,2,4,8,128]{5,4,3,2,1,0:T(8,128)(2,1)} custom-call(bf16[2,32,8,128]{3,2,1,0:T(8,128)(2,1)} %x_ref.1, bf16[2,32,8,128]{3,2,1,0:T(8,128)(2,1)} %g_ref.1), custom_call_target="tpu_custom_call" | custom-call | bytes 786432 | tf_op jit(solution)/shard_map/pallas_call | solution.py:23
  2.5 9.3 %all-to-all-start = ((bf16[16,2,2,4,8,128]{5,4,3,2,1,0:T(8,128)(2,1)}), bf16[16,2,2,4,8,128]{5,4,3,2,1,0:T(8,128)(2,1)S(1)}, u32[]{:S(2)}, u32[]{:S(2)}) async-start(bf16[16,2,2,4,8,128]{5,4,3,2,1,0:T(8,128)(2,1)} %shard_map.58), calls=%async_computation | async-start | bytes 1048576 | tf_op jit(solution)/shard_map/all_to_all | solution.py:219
  11.8 0.7 collective-permute-start.4
  12.5 9.2 %collective-permute-start.3 = (bf16[32,8,128]{2,1,0:T(8,128)(2,1)S(1)}, bf16[32,8,128]{2,1,0:T(8,128)(2,1)S(1)}, u32[]{:S(2)}, u32[]{:S(2)}) collective-permute-start(bf16[32,8,128]{2,1,0:T(8,128)(2,1)S(1)} %get-tuple-element.46), channel_id=1, source_target_pairs={{0,16},{32,48},{64,80},{96,112},{128,144},{160,176},{192,208},{224... | collective-permute-start | bytes 196616 | tf_op jit(solution)/shard_map/ppermute | solution.py:239
  21.8 3.6 %collective-permute-done.3.even_ref = bf16[32,8,128]{2,1,0:T(8,128)(2,1)S(1)} collective-permute-done((bf16[32,8,128]{2,1,0:T(8,128)(2,1)S(1)}, bf16[32,8,128]{2,1,0:T(8,128)(2,1)S(1)}, u32[]{:S(2)}, u32[]{:S(2)}) %collective-permute-start.3) | collective-permute-done | bytes 65568 | tf_op jit(solution)/shard_map/ppermute | solution.py:239
  26.0 1.8 %shard_map.59 = bf16[8,39,8,128]{3,2,1,0:T(8,128)(2,1)} custom-call(s32[1]{0:T(128)} %bitcast.p_ref, bf16[27,8,128]{2,1,0:T(8,128)(2,1)} %bitcast.16, bf16[32,8,128]{2,1,0:T(8,128)(2,1)} %copy-done.8, bf16[32,8,128]{2,1,0:T(8,128)(2,1)} %copy-done.7), custom_call_target="tpu_custom_call" | custom-call | bytes 825348 | tf_op jit(solution)/shard_map/pallas_call | solution.py:23
  27.8 4.8 %all-to-all-start.3 = ((bf16[8,39,8,128]{3,2,1,0:T(8,128)(2,1)}), bf16[8,39,8,128]{3,2,1,0:T(8,128)(2,1)S(1)}, u32[]{:S(2)}, u32[]{:S(2)}) async-start(bf16[8,39,8,128]{3,2,1,0:T(8,128)(2,1)} %shard_map.59), calls=%async_computation.3 | async-start | bytes 1277952 | tf_op jit(solution)/shard_map/all_to_all | solution.py:219
  32.6 0.7 collective-permute-start.1
  33.3 8.5 %collective-permute-start = (bf16[16,4,8,128]{3,2,1,0:T(8,128)(2,1)S(1)}, bf16[16,4,8,128]{3,2,1,0:T(8,128)(2,1)S(1)}, u32[]{:S(2)}, u32[]{:S(2)}) collective-permute-start(bf16[16,4,8,128]{3,2,1,0:T(8,128)(2,1)S(1)} %get-tuple-element.28), channel_id=1, source_target_pairs={{0,16},{32,48},{64,80},{96,112},{128,144},{160,176},{192,208},{224... | collective-permute-start | bytes 393224 | tf_op jit(solution)/shard_map/ppermute | solution.py:245
  41.9 4.0 %collective-permute-done.even_ref = bf16[16,4,8,128]{3,2,1,0:T(8,128)(2,1)S(1)} collective-permute-done((bf16[16,4,8,128]{3,2,1,0:T(8,128)(2,1)S(1)}, bf16[16,4,8,128]{3,2,1,0:T(8,128)(2,1)S(1)}, u32[]{:S(2)}, u32[]{:S(2)}) %collective-permute-start) | collective-permute-done | bytes 131104 | tf_op jit(solution)/shard_map/ppermute | solution.py:245
  46.5 3.7 %wgrad.1 = (f32[8,27,8,128]{3,2,1,0:T(8,128)}, f32[8,27,8,128]{3,2,1,0:T(8,128)}) custom-call(s32[1]{0:T(128)} %bitcast.p_ref, bf16[16,2,2,4,8,128]{5,4,3,2,1,0:T(8,128)(2,1)} %copy-done, bf16[16,4,8,128]{3,2,1,0:T(8,128)(2,1)} %copy-done.11, bf16[16,4,8,128]{3,2,1,0:T(8,128)(2,1)} %copy-done.10), custom_call_target="tpu_custom_call" | custom-call | flops 452984832 | bytes 1769472 | tf_op jit(solution)/shard_map/wgrad/pallas_call | solution.py:258
  50.2 1.9 %collective-permute-start.2 = (f32[8,27,8,128]{3,2,1,0:T(8,128)}, f32[8,27,8,128]{3,2,1,0:T(8,128)S(1)}, u32[]{:S(2)}, u32[]{:S(2)}) collective-permute-start(f32[8,27,8,128]{3,2,1,0:T(8,128)} %get-tuple-element.16), channel_id=1, source_target_pairs={{0,1},{1,0},{2,3},{3,2},{4,5},{5,4},{6,7},{7,6},{8,9},{9,8},{10,11... | collective-permute-start | bytes 2654216 | tf_op jit(solution)/shard_map/ppermute | solution.py:274
  52.1 2.6 %collective-permute-done.2 = f32[8,27,8,128]{3,2,1,0:T(8,128)S(1)} collective-permute-done((f32[8,27,8,128]{3,2,1,0:T(8,128)}, f32[8,27,8,128]{3,2,1,0:T(8,128)S(1)}, u32[]{:S(2)}, u32[]{:S(2)}) %collective-permute-start.2) | collective-permute-done | bytes 884768 | tf_op jit(solution)/shard_map/ppermute | solution.py:274
  54.7 2.2 %add.36 = f32[8,27,8,128]{3,2,1,0:T(8,128)} add(f32[8,27,8,128]{3,2,1,0:T(8,128)} %get-tuple-element.15, f32[8,27,8,128]{3,2,1,0:T(8,128)S(1)} %collective-permute-done.2) | non-fusion elementwise | flops 221184 | bytes 2654208 | tf_op jit(solution)/shard_map/add | solution.py:275
  56.9 8.5 %all-to-all-start.1 = ((f32[8,27,8,128]{3,2,1,0:T(8,128)}), f32[8,27,8,128]{3,2,1,0:T(8,128)S(1)}, u32[]{:S(2)}, u32[]{:S(2)}) async-start(f32[8,27,8,128]{3,2,1,0:T(8,128)} %add.36), calls=%async_computation.1 | async-start | bytes 1769472 | tf_op jit(solution)/shard_map/all_to_all | solution.py:219
  65.4 1.9 %collective-permute-start.5 = (bf16[8,39,8,128]{3,2,1,0:T(8,128)(2,1)S(1)}, bf16[8,39,8,128]{3,2,1,0:T(8,128)(2,1)S(1)}, u32[]{:S(2)}, u32[]{:S(2)}) collective-permute-start(bf16[8,39,8,128]{3,2,1,0:T(8,128)(2,1)S(1)} %all-to-all-done.3.mine_ref), channel_id=1, source_target_pairs={{0,1},{1,0},{2,3},{3,2},{4,5},{5,4},{6,7},{7,6},{8,9},{9,8},{10,11... | collective-permute-start | bytes 1916936 | tf_op jit(solution)/shard_map/ppermute | solution.py:255
  67.3 9.7 %all-to-all-done.1 = f32[8,27,8,128]{3,2,1,0:T(8,128)S(1)} async-done(((f32[8,27,8,128]{3,2,1,0:T(8,128)}), f32[8,27,8,128]{3,2,1,0:T(8,128)S(1)}, u32[]{:S(2)}, u32[]{:S(2)}) %all-to-all-start.1) | async-done | bytes 884768 | tf_op jit(solution)/shard_map/all_to_all | solution.py:219
  77.0 0.7 pad.4
  77.7 10.1 %all-to-all-start.2 = ((f32[32,8,128]{2,1,0:T(8,128)}), f32[32,8,128]{2,1,0:T(8,128)S(1)}, u32[]{:S(2)}, u32[]{:S(2)}) async-start(f32[32,8,128]{2,1,0:T(8,128)} %pad.4), calls=%async_computation.2 | async-start | bytes 262144 | tf_op jit(solution)/shard_map/all_to_all | solution.py:219
  87.9 0.8 copy-done.9
  88.7 4.0 %conv.1 = (f32[4,2,2,2,8,128]{5,4,3,2,1,0:T(8,128)}, f32[4,2,2,2,8,128]{5,4,3,2,1,0:T(8,128)}, f32[4,2,2,2,8,128]{5,4,3,2,1,0:T(8,128)}, f32[4,2,2,2,8,128]{5,4,3,2,1,0:T(8,128)}) custom-call(s32[1]{0:T(128)} %bitcast.p_ref, bf16[16,2,2,4,8,128]{5,4,3,2,1,0:T(8,128)(2,1)} %copy-done, bf16[16,4,8,128]{3,2,1,0:T(8,128)(2,1)} %copy-done.11, ...), custom_call_target="tpu_custom_call" | custom-call | flops 905969664 | bytes 1769472 | tf_op jit(solution)/shard_map/conv/pallas_call | solution.py:279
  92.7 1.9 %collective-permute-start.6 = (f32[4,2,2,2,8,128]{5,4,3,2,1,0:T(8,128)}, f32[4,2,2,2,8,128]{5,4,3,2,1,0:T(8,128)S(1)}, u32[]{:S(2)}, u32[]{:S(2)}) collective-permute-start(f32[4,2,2,2,8,128]{5,4,3,2,1,0:T(8,128)} %get-tuple-element.18), channel_id=1, source_target_pairs={{0,1},{1,0},{2,3},{3,2},{4,5},{5,4},{6,7},{7,6},{8,9},{9,8},{10,11... | collective-permute-start | bytes 393224 | tf_op jit(solution)/shard_map/ppermute | solution.py:298
  94.6 3.3 %collective-permute-start.7 = (f32[4,2,2,2,8,128]{5,4,3,2,1,0:T(8,128)}, f32[4,2,2,2,8,128]{5,4,3,2,1,0:T(8,128)S(1)}, u32[]{:S(2)}, u32[]{:S(2)}) collective-permute-start(f32[4,2,2,2,8,128]{5,4,3,2,1,0:T(8,128)} %get-tuple-element.19), channel_id=1, source_target_pairs={{0,8},{8,0},{1,9},{9,1},{2,10},{10,2},{3,11},{11,3},{4,12},{12,4},... | collective-permute-start | bytes 393224 | tf_op jit(solution)/shard_map/ppermute | solution.py:299
  97.9 2.3 %collective-permute-start.8 = (f32[4,2,2,2,8,128]{5,4,3,2,1,0:T(8,128)}, f32[4,2,2,2,8,128]{5,4,3,2,1,0:T(8,128)S(1)}, u32[]{:S(2)}, u32[]{:S(2)}) collective-permute-start(f32[4,2,2,2,8,128]{5,4,3,2,1,0:T(8,128)} %get-tuple-element.20), channel_id=1, source_target_pairs={{0,9},{1,8},{8,1},{9,0},{2,11},{3,10},{10,3},{11,2},{4,13},{5,12},... | collective-permute-start | bytes 393224 | tf_op jit(solution)/shard_map/ppermute | solution.py:300
  100.3 2.3 %collective-permute-done.7 = f32[4,2,2,2,8,128]{5,4,3,2,1,0:T(8,128)S(1)} collective-permute-done((f32[4,2,2,2,8,128]{5,4,3,2,1,0:T(8,128)}, f32[4,2,2,2,8,128]{5,4,3,2,1,0:T(8,128)S(1)}, u32[]{:S(2)}, u32[]{:S(2)}) %collective-permute-start.7) | collective-permute-done | bytes 131104 | tf_op jit(solution)/shard_map/ppermute | solution.py:299
  102.6 2.8 %collective-permute-done.8 = f32[4,2,2,2,8,128]{5,4,3,2,1,0:T(8,128)S(1)} collective-permute-done((f32[4,2,2,2,8,128]{5,4,3,2,1,0:T(8,128)}, f32[4,2,2,2,8,128]{5,4,3,2,1,0:T(8,128)S(1)}, u32[]{:S(2)}, u32[]{:S(2)}) %collective-permute-start.8) | collective-permute-done | bytes 131104 | tf_op jit(solution)/shard_map/ppermute | solution.py:300
  106.1 12.3 %all-to-all-start.4 = ((f32[32,8,128]{2,1,0:T(8,128)}), f32[32,8,128]{2,1,0:T(8,128)S(1)}, u32[]{:S(2)}, u32[]{:S(2)}) async-start(f32[32,8,128]{2,1,0:T(8,128)} %broadcast_in_dim.2), calls=%async_computation.4 | async-start | bytes 262144 | tf_op jit(solution)/shard_map/all_to_all | solution.py:219
  118.5 2.3 %collective-permute-start.9 = (f32[4,2,2,2,8,128]{5,4,3,2,1,0:T(8,128)S(1)}, f32[4,2,2,2,8,128]{5,4,3,2,1,0:T(8,128)S(1)}, u32[]{:S(2)}, u32[]{:S(2)}) collective-permute-start(f32[4,2,2,2,8,128]{5,4,3,2,1,0:T(8,128)S(1)} %pad_maximum_fusion.1), channel_id=1, source_target_pairs={{0,2},{2,0},{4,6},{6,4},{1,3},{3,1},{5,7},{7,5},{8,10},{10,8},{12,... | collective-permute-start | bytes 393224 | tf_op jit(solution)/shard_map/ppermute | solution.py:309
  120.9 4.7 %collective-permute-start.10 = (f32[4,2,2,2,8,128]{5,4,3,2,1,0:T(8,128)S(1)}, f32[4,2,2,2,8,128]{5,4,3,2,1,0:T(8,128)S(1)}, u32[]{:S(2)}, u32[]{:S(2)}) collective-permute-start(f32[4,2,2,2,8,128]{5,4,3,2,1,0:T(8,128)S(1)} %pad_maximum_fusion.2), channel_id=1, source_target_pairs={{0,4},{2,6},{4,0},{6,2},{1,5},{3,7},{5,1},{7,3},{8,12},{10,14},{12... | collective-permute-start | bytes 393224 | tf_op jit(solution)/shard_map/ppermute | solution.py:309
  125.6 3.4 %collective-permute-start.11 = (f32[4,2,2,2,8,128]{5,4,3,2,1,0:T(8,128)S(1)}, f32[4,2,2,2,8,128]{5,4,3,2,1,0:T(8,128)S(1)}, u32[]{:S(2)}, u32[]{:S(2)}) collective-permute-start(f32[4,2,2,2,8,128]{5,4,3,2,1,0:T(8,128)S(1)} %pad_maximum_fusion.3), channel_id=1, source_target_pairs={{0,6},{2,4},{4,2},{6,0},{1,7},{3,5},{5,3},{7,1},{8,14},{10,12},{12... | collective-permute-start | bytes 393224 | tf_op jit(solution)/shard_map/ppermute | solution.py:309
  129.8 3.9 %collective-permute-done.11.refs_3_ = f32[4,2,2,2,8,128]{5,4,3,2,1,0:T(8,128)S(1)} collective-permute-done((f32[4,2,2,2,8,128]{5,4,3,2,1,0:T(8,128)S(1)}, f32[4,2,2,2,8,128]{5,4,3,2,1,0:T(8,128)S(1)}, u32[]{:S(2)}, u32[]{:S(2)}) %collective-permute-start.11) | collective-permute-done | bytes 131104 | tf_op jit(solution)/shard_map/ppermute | solution.py:309
  134.4 1.9 %shard_map.60 = (f32[2,32,8,128]{3,2,1,0:T(8,128)}, f32[2,32,8,128]{3,2,1,0:T(8,128)}) custom-call(s32[1]{0:T(128)} %bitcast.p_ref, f32[4,2,2,2,8,128]{5,4,3,2,1,0:T(8,128)} %pad_maximum_fusion.refs_0_, f32[4,2,2,2,8,128]{5,4,3,2,1,0:T(8,128)} %copy-done.3, f32[4,2,2,2,8,128]{5,4,3,2,1,0:T(8,128)} %copy-done.4, f32[4,2,2,2,8,128]{5,4,3,2,1,0:T(8,128)} %copy-done.5), custom_call_target="tpu_custom_call" | custom-call | bytes 1048580 | tf_op jit(solution)/shard_map/pallas_call | solution.py:23
  (46 shorter events, 4.3 us)
Async XLA Ops:
  2.4 9.4 %copy-start.2 = (bf16[2,32,8,128]{3,2,1,0:T(8,128)(2,1)S(1)}, bf16[2,32,8,128]{3,2,1,0:T(8,128)(2,1)}, u32[]{:S(2)}) copy-start(bf16[2,32,8,128]{3,2,1,0:T(8,128)(2,1)} %g_ref.1) | copy-start | bytes 393220
  2.5 25.3 %all-to-all-start = ((bf16[16,2,2,4,8,128]{5,4,3,2,1,0:T(8,128)(2,1)}), bf16[16,2,2,4,8,128]{5,4,3,2,1,0:T(8,128)(2,1)S(1)}, u32[]{:S(2)}, u32[]{:S(2)}) async-start(bf16[16,2,2,4,8,128]{5,4,3,2,1,0:T(8,128)(2,1)} %shard_map.58), calls=%async_computation | async-start | bytes 1048576 | tf_op jit(solution)/shard_map/all_to_all | solution.py:219
  11.8 9.9 %collective-permute-start.4 = (bf16[32,8,128]{2,1,0:T(8,128)(2,1)S(1)}, bf16[32,8,128]{2,1,0:T(8,128)(2,1)S(1)}, u32[]{:S(2)}, u32[]{:S(2)}) collective-permute-start(bf16[32,8,128]{2,1,0:T(8,128)(2,1)S(1)} %get-tuple-element.45), channel_id=1, source_target_pairs={{16,32},{48,64},{80,96},{112,128},{144,160},{176,192},{208,224},{2... | collective-permute-start | bytes 196616 | tf_op jit(solution)/shard_map/ppermute | solution.py:239
  12.5 12.9 %collective-permute-start.3 = (bf16[32,8,128]{2,1,0:T(8,128)(2,1)S(1)}, bf16[32,8,128]{2,1,0:T(8,128)(2,1)S(1)}, u32[]{:S(2)}, u32[]{:S(2)}) collective-permute-start(bf16[32,8,128]{2,1,0:T(8,128)(2,1)S(1)} %get-tuple-element.46), channel_id=1, source_target_pairs={{0,16},{32,48},{64,80},{96,112},{128,144},{160,176},{192,208},{224... | collective-permute-start | bytes 196616 | tf_op jit(solution)/shard_map/ppermute | solution.py:239
  21.7 3.6 %copy-start.7 = (bf16[32,8,128]{2,1,0:T(8,128)(2,1)}, bf16[32,8,128]{2,1,0:T(8,128)(2,1)S(1)}, u32[]{:S(2)}) copy-start(bf16[32,8,128]{2,1,0:T(8,128)(2,1)S(1)} %collective-permute-done.4.odd_ref) | copy-start | bytes 196612
  25.4 0.6 copy-start.8
  27.8 4.8 %copy-start = (bf16[16,2,2,4,8,128]{5,4,3,2,1,0:T(8,128)(2,1)}, bf16[16,2,2,4,8,128]{5,4,3,2,1,0:T(8,128)(2,1)S(1)}, u32[]{:S(2)}) copy-start(bf16[16,2,2,4,8,128]{5,4,3,2,1,0:T(8,128)(2,1)S(1)} %all-to-all-done.own_ref) | copy-start | bytes 1572868
  27.8 29.1 %all-to-all-start.3 = ((bf16[8,39,8,128]{3,2,1,0:T(8,128)(2,1)}), bf16[8,39,8,128]{3,2,1,0:T(8,128)(2,1)S(1)}, u32[]{:S(2)}, u32[]{:S(2)}) async-start(bf16[8,39,8,128]{3,2,1,0:T(8,128)(2,1)} %shard_map.59), calls=%async_computation.3 | async-start | bytes 1277952 | tf_op jit(solution)/shard_map/all_to_all | solution.py:219
  32.6 9.2 %collective-permute-start.1 = (bf16[16,4,8,128]{3,2,1,0:T(8,128)(2,1)S(1)}, bf16[16,4,8,128]{3,2,1,0:T(8,128)(2,1)S(1)}, u32[]{:S(2)}, u32[]{:S(2)}) collective-permute-start(bf16[16,4,8,128]{3,2,1,0:T(8,128)(2,1)S(1)} %get-tuple-element.27), channel_id=1, source_target_pairs={{16,32},{48,64},{80,96},{112,128},{144,160},{176,192},{208,224},{2... | collective-permute-start | bytes 393224 | tf_op jit(solution)/shard_map/ppermute | solution.py:245
  33.3 12.5 %collective-permute-start = (bf16[16,4,8,128]{3,2,1,0:T(8,128)(2,1)S(1)}, bf16[16,4,8,128]{3,2,1,0:T(8,128)(2,1)S(1)}, u32[]{:S(2)}, u32[]{:S(2)}) collective-permute-start(bf16[16,4,8,128]{3,2,1,0:T(8,128)(2,1)S(1)} %get-tuple-element.28), channel_id=1, source_target_pairs={{0,16},{32,48},{64,80},{96,112},{128,144},{160,176},{192,208},{224... | collective-permute-start | bytes 393224 | tf_op jit(solution)/shard_map/ppermute | solution.py:245
  41.8 4.0 %copy-start.10 = (bf16[16,4,8,128]{3,2,1,0:T(8,128)(2,1)}, bf16[16,4,8,128]{3,2,1,0:T(8,128)(2,1)S(1)}, u32[]{:S(2)}) copy-start(bf16[16,4,8,128]{3,2,1,0:T(8,128)(2,1)S(1)} %collective-permute-done.1.odd_ref) | copy-start | bytes 393220
  45.8 0.7 copy-start.11
  50.2 4.5 %collective-permute-start.2 = (f32[8,27,8,128]{3,2,1,0:T(8,128)}, f32[8,27,8,128]{3,2,1,0:T(8,128)S(1)}, u32[]{:S(2)}, u32[]{:S(2)}) collective-permute-start(f32[8,27,8,128]{3,2,1,0:T(8,128)} %get-tuple-element.16), channel_id=1, source_target_pairs={{0,1},{1,0},{2,3},{3,2},{4,5},{5,4},{6,7},{7,6},{8,9},{9,8},{10,11... | collective-permute-start | bytes 2654216 | tf_op jit(solution)/shard_map/ppermute | solution.py:274
  56.9 8.5 %copy-start.1 = (bf16[8,39,8,128]{3,2,1,0:T(8,128)(2,1)}, bf16[8,39,8,128]{3,2,1,0:T(8,128)(2,1)S(1)}, u32[]{:S(2)}) copy-start(bf16[8,39,8,128]{3,2,1,0:T(8,128)(2,1)S(1)} %all-to-all-done.3.mine_ref) | copy-start | bytes 1916932
  56.9 20.1 %all-to-all-start.1 = ((f32[8,27,8,128]{3,2,1,0:T(8,128)}), f32[8,27,8,128]{3,2,1,0:T(8,128)S(1)}, u32[]{:S(2)}, u32[]{:S(2)}) async-start(f32[8,27,8,128]{3,2,1,0:T(8,128)} %add.36), calls=%async_computation.1 | async-start | bytes 1769472 | tf_op jit(solution)/shard_map/all_to_all | solution.py:219
  65.4 22.5 %collective-permute-start.5 = (bf16[8,39,8,128]{3,2,1,0:T(8,128)(2,1)S(1)}, bf16[8,39,8,128]{3,2,1,0:T(8,128)(2,1)S(1)}, u32[]{:S(2)}, u32[]{:S(2)}) collective-permute-start(bf16[8,39,8,128]{3,2,1,0:T(8,128)(2,1)S(1)} %all-to-all-done.3.mine_ref), channel_id=1, source_target_pairs={{0,1},{1,0},{2,3},{3,2},{4,5},{5,4},{6,7},{7,6},{8,9},{9,8},{10,11... | collective-permute-start | bytes 1916936 | tf_op jit(solution)/shard_map/ppermute | solution.py:255
  77.7 27.7 %all-to-all-start.2 = ((f32[32,8,128]{2,1,0:T(8,128)}), f32[32,8,128]{2,1,0:T(8,128)S(1)}, u32[]{:S(2)}, u32[]{:S(2)}) async-start(f32[32,8,128]{2,1,0:T(8,128)} %pad.4), calls=%async_computation.2 | async-start | bytes 262144 | tf_op jit(solution)/shard_map/all_to_all | solution.py:219
  87.9 0.8 copy-start.9
  92.7 7.6 %collective-permute-start.6 = (f32[4,2,2,2,8,128]{5,4,3,2,1,0:T(8,128)}, f32[4,2,2,2,8,128]{5,4,3,2,1,0:T(8,128)S(1)}, u32[]{:S(2)}, u32[]{:S(2)}) collective-permute-start(f32[4,2,2,2,8,128]{5,4,3,2,1,0:T(8,128)} %get-tuple-element.18), channel_id=1, source_target_pairs={{0,1},{1,0},{2,3},{3,2},{4,5},{5,4},{6,7},{7,6},{8,9},{9,8},{10,11... | collective-permute-start | bytes 393224 | tf_op jit(solution)/shard_map/ppermute | solution.py:298
  94.6 8.0 %collective-permute-start.7 = (f32[4,2,2,2,8,128]{5,4,3,2,1,0:T(8,128)}, f32[4,2,2,2,8,128]{5,4,3,2,1,0:T(8,128)S(1)}, u32[]{:S(2)}, u32[]{:S(2)}) collective-permute-start(f32[4,2,2,2,8,128]{5,4,3,2,1,0:T(8,128)} %get-tuple-element.19), channel_id=1, source_target_pairs={{0,8},{8,0},{1,9},{9,1},{2,10},{10,2},{3,11},{11,3},{4,12},{12,4},... | collective-permute-start | bytes 393224 | tf_op jit(solution)/shard_map/ppermute | solution.py:299
  97.9 7.5 %collective-permute-start.8 = (f32[4,2,2,2,8,128]{5,4,3,2,1,0:T(8,128)}, f32[4,2,2,2,8,128]{5,4,3,2,1,0:T(8,128)S(1)}, u32[]{:S(2)}, u32[]{:S(2)}) collective-permute-start(f32[4,2,2,2,8,128]{5,4,3,2,1,0:T(8,128)} %get-tuple-element.20), channel_id=1, source_target_pairs={{0,9},{1,8},{8,1},{9,0},{2,11},{3,10},{10,3},{11,2},{4,13},{5,12},... | collective-permute-start | bytes 393224 | tf_op jit(solution)/shard_map/ppermute | solution.py:300
  106.1 12.3 %copy-start.6 = (f32[4,2,2,2,8,128]{5,4,3,2,1,0:T(8,128)S(1)}, f32[4,2,2,2,8,128]{5,4,3,2,1,0:T(8,128)}, u32[]{:S(2)}) copy-start(f32[4,2,2,2,8,128]{5,4,3,2,1,0:T(8,128)} %get-tuple-element.21) | copy-start | bytes 393220
  106.1 30.2 %all-to-all-start.4 = ((f32[32,8,128]{2,1,0:T(8,128)}), f32[32,8,128]{2,1,0:T(8,128)S(1)}, u32[]{:S(2)}, u32[]{:S(2)}) async-start(f32[32,8,128]{2,1,0:T(8,128)} %broadcast_in_dim.2), calls=%async_computation.4 | async-start | bytes 262144 | tf_op jit(solution)/shard_map/all_to_all | solution.py:219
  118.5 11.1 %collective-permute-start.9 = (f32[4,2,2,2,8,128]{5,4,3,2,1,0:T(8,128)S(1)}, f32[4,2,2,2,8,128]{5,4,3,2,1,0:T(8,128)S(1)}, u32[]{:S(2)}, u32[]{:S(2)}) collective-permute-start(f32[4,2,2,2,8,128]{5,4,3,2,1,0:T(8,128)S(1)} %pad_maximum_fusion.1), channel_id=1, source_target_pairs={{0,2},{2,0},{4,6},{6,4},{1,3},{3,1},{5,7},{7,5},{8,10},{10,8},{12,... | collective-permute-start | bytes 393224 | tf_op jit(solution)/shard_map/ppermute | solution.py:309
  120.9 8.9 %collective-permute-start.10 = (f32[4,2,2,2,8,128]{5,4,3,2,1,0:T(8,128)S(1)}, f32[4,2,2,2,8,128]{5,4,3,2,1,0:T(8,128)S(1)}, u32[]{:S(2)}, u32[]{:S(2)}) collective-permute-start(f32[4,2,2,2,8,128]{5,4,3,2,1,0:T(8,128)S(1)} %pad_maximum_fusion.2), channel_id=1, source_target_pairs={{0,4},{2,6},{4,0},{6,2},{1,5},{3,7},{5,1},{7,3},{8,12},{10,14},{12... | collective-permute-start | bytes 393224 | tf_op jit(solution)/shard_map/ppermute | solution.py:309
  125.6 8.1 %collective-permute-start.11 = (f32[4,2,2,2,8,128]{5,4,3,2,1,0:T(8,128)S(1)}, f32[4,2,2,2,8,128]{5,4,3,2,1,0:T(8,128)S(1)}, u32[]{:S(2)}, u32[]{:S(2)}) collective-permute-start(f32[4,2,2,2,8,128]{5,4,3,2,1,0:T(8,128)S(1)} %pad_maximum_fusion.3), channel_id=1, source_target_pairs={{0,6},{2,4},{4,2},{6,0},{1,7},{3,5},{5,3},{7,1},{8,14},{10,12},{12... | collective-permute-start | bytes 393224 | tf_op jit(solution)/shard_map/ppermute | solution.py:309
  129.7 4.0 %copy-start.3 = (f32[4,2,2,2,8,128]{5,4,3,2,1,0:T(8,128)}, f32[4,2,2,2,8,128]{5,4,3,2,1,0:T(8,128)S(1)}, u32[]{:S(2)}) copy-start(f32[4,2,2,2,8,128]{5,4,3,2,1,0:T(8,128)S(1)} %collective-permute-done.9.refs_1_) | copy-start | bytes 393220
  129.8 3.9 %copy-start.4 = (f32[4,2,2,2,8,128]{5,4,3,2,1,0:T(8,128)}, f32[4,2,2,2,8,128]{5,4,3,2,1,0:T(8,128)S(1)}, u32[]{:S(2)}) copy-start(f32[4,2,2,2,8,128]{5,4,3,2,1,0:T(8,128)S(1)} %collective-permute-done.10.refs_2_) | copy-start | bytes 393220
  133.7 0.6 copy-start.5

commit v8 on v7

--- a/solution.py
+++ b/solution.py
@@ -1,3 +1,6 @@
+import functools
+import math
+
 import jax
 import jax.numpy as jnp
 from jax import lax
@@ -19,15 +22,22 @@
 
 def call(kernel, outs, ins, scratch=(), smem=0, flops=0):
     specs = [pl.BlockSpec(memory_space=pltpu.SMEM)] * smem + vmem_specs(len(ins) - smem)
-    moved = sum(a.size * a.dtype.itemsize for a in ins) + sum(o.size * o.dtype.itemsize for o in outs)
-    return pl.pallas_call(
+    moved = sum(a.size * a.dtype.itemsize for a in ins) + sum(math.prod(o.shape) * 4 for o in outs)
+    one = len(outs) == 1
+    out_specs = vmem_specs(len(outs))
+    result = pl.pallas_call(
         kernel,
-        out_shape=tuple(outs),
+        out_shape=outs[0] if one else tuple(outs),
         in_specs=specs,
-        out_specs=tuple(vmem_specs(len(outs))),
+        out_specs=out_specs[0] if one else tuple(out_specs),
         scratch_shapes=list(scratch),
         cost_estimate=pl.CostEstimate(flops=flops, transcendentals=0, bytes_accessed=moved),
     )(*ins)
+    return (result,) if one else result
+
+
+def near_core(array):
+    return pltpu.with_memory_space_constraint(array, pltpu.VMEM)
 
 
 def place_of(index):
@@ -126,14 +136,14 @@
     return [halo_plane(index, 0, even_ref, odd_ref)] + inner + [halo_plane(index, 1, even_ref, odd_ref)]
 
 
-def wgrad_kernel(p_ref, own_ref, even_ref, odd_ref, keep_ref, send_ref, s_ref, t_ref, o_ref, sems):
+def wgrad_kernel(p_ref, own_ref, even_ref, odd_ref, keep_ref, send_ref, s_ref, t_ref):
     n, _, nz, nr, cg, w = own_ref.shape
     nh, ch = nr - 2, n * cg
     build(x_planes(p_ref[0], own_ref, even_ref, odd_ref), (nr, ch, w), s_ref)
     for z in range(nz):
         for h in range(nh):
             t_ref[z, :, pl.ds(h * w, w)] = own_plane(own_ref, 1, z)(h + 1).astype(BF)
-    core = place_of(p_ref[0])[2]
+    first = place_of(p_ref[0])[2] == 0
     for a in range(3):
         for b in range(3):
             total = None
@@ -146,21 +156,17 @@
                 )
                 total = part if total is None else total + part
             for c in range(3):
-                for d in range(n):
-                    slot = (d % 2) ^ core
-                    o_ref[slot, d // 2, 9 * a + 3 * b + c] = total[d * cg : (d + 1) * cg, c * ch : (c + 1) * ch]
-    copies = [
-        pltpu.make_async_copy(o_ref.at[1], send_ref, sems.at[1]),
-        pltpu.make_async_copy(o_ref.at[0], keep_ref, sems.at[0]),
-    ]
-    for copy in copies:
-        copy.start()
-    for copy in copies:
-        copy.wait()
+                tap = 9 * a + 3 * b + c
+                for q in range(n // 2):
+                    left, right = [
+                        total[d * cg : (d + 1) * cg, c * ch : (c + 1) * ch] for d in (2 * q, 2 * q + 1)
+                    ]
+                    keep_ref[q, tap] = jnp.where(first, left, right)
+                    send_ref[q, tap] = jnp.where(first, right, left)
 
 
 def conv_kernel(
-    p_ref, own_ref, even_ref, odd_ref, mine_ref, other_ref, out0, out1, out2, out3, s_ref, wt_ref, wf_ref, o_ref, sems
+    p_ref, own_ref, even_ref, odd_ref, mine_ref, other_ref, out0, out1, out2, out3, s_ref, wt_ref, wf_ref
 ):
     n, _, nz, nr, cg, w = own_ref.shape
     nh, ch = nr - 2, n * cg
@@ -169,6 +175,11 @@
     span = (total - taps) // 2
     zl, x, core = place_of(p_ref[0])
     first = core == 0
+    outs = (out0, out1, out2, out3)
+
+    def targets(dx):
+        return [[zl_to * 8 + dx * 2 + core_to for core_to in range(2)] for zl_to in range(2)]
+
     for t in range(taps):
         a, bc = t // 9, t % 9
         block = by_core(first, [mine_ref[q, t] for q in range(chips)], [other_ref[q, t] for q in range(chips)])
@@ -191,16 +202,38 @@
             for a in range(3):
                 part = jnp.dot(w_ref[a], s_ref[k, z + a], preferred_element_type=F32)
                 total = part if total is None else total + part
-            for d in range(n):
-                dzl, dx, dcore = place_of(d)
-                slot = (2 * (dzl ^ zl) + (dcore ^ core), dx ^ x)
+            for dx in range(4):
                 for h in range(nh):
-                    o_ref[(*slot, k, z, h)] = total[d * cg : (d + 1) * cg, h * w : (h + 1) * w]
-    copies = [pltpu.make_async_copy(o_ref.at[j], ref, sems.at[j]) for j, ref in enumerate((out0, out1, out2, out3))]
-    for copy in copies:
-        copy.start()
-    for copy in copies:
-        copy.wait()
+                    tiles = [[total[d * cg : (d + 1) * cg, h * w : (h + 1) * w] for d in pair] for pair in targets(dx)]
+                    tiles = [
+                        [jnp.where(core == 0, t[0], t[1]), jnp.where(core == 0, t[1], t[0])] for t in tiles
+                    ]
+                    for j in range(2):
+                        low = jnp.where(zl == 0, tiles[0][j], tiles[1][j])
+                        high = jnp.where(zl == 0, tiles[1][j], tiles[0][j])
+                        outs[j][dx ^ x, k, z, h] = low
+                        outs[2 + j][dx ^ x, k, z, h] = high
+
+
+def chips_add_kernel(pieces_ref, o_ref):
+    taps = pieces_ref.shape[1]
+    for t in range(o_ref.shape[0]):
+        if t < taps:
+            total = pieces_ref[0, t]
+            for q in range(1, pieces_ref.shape[0]):
+                total = total + pieces_ref[q, t]
+        else:
+            total = jnp.zeros(o_ref.shape[1:], F32)
+        o_ref[t] = total
+
+
+def space_add_kernel(shares_ref, o_ref, *, norm):
+    total = shares_ref[0]
+    for j in range(1, shares_ref.shape[0]):
+        total = total + shares_ref[j]
+    total = total * norm
+    for j in range(o_ref.shape[0]):
+        o_ref[j] = total
 
 
 def place_kernel(p_ref, *refs):
@@ -239,7 +272,7 @@
         lax.ppermute(lax.dynamic_slice(grad_out, (side, 0, 0, 0), (1, rows, cg, w))[0], SPACE, pair)
         for side, pair in zip(sides, pairs)
     ]
-    (packed,) = call(pack_kernel, [sds((n, 2, nz, nr, cg, w), BF)], [activations, grad_out])
+    (packed,) = call(pack_kernel, [pltpu.VMEM((n, 2, nz, nr, cg, w), BF)], [activations, grad_out])
     own = swap_all(packed, FILT)
     x_halos = [
         lax.ppermute(
@@ -247,68 +280,49 @@
         )
         for side, pair in zip(sides, pairs)
     ]
+    local = [index, near_core(own), *map(near_core, x_halos)]
 
     flat_w = weight.transpose(0, 1, 2, 4, 3).reshape(27, cg, ch)
     span = rows // chips + 2
-    (more,) = call(pack_more_kernel, [sds((chips, 27 + 2 * span, cg, ch), BF)], [index, flat_w, *g_halos], smem=1)
+    (more,) = call(pack_more_kernel, [sds((chips, 27 + 2 * span, cg, ch), BF)], [index, flat_w, *map(near_core, g_halos)], smem=1)
     mine = swap_all(more, CHIPS)
     other = lax.ppermute(mine, "core", swap)
 
-    any_spec = pl.BlockSpec(memory_space=pl.ANY)
-    keep, send = pl.pallas_call(
+    keep, send = call(
         wgrad_kernel,
-        out_shape=(sds((chips, 27, cg, ch), F32),) * 2,
-        in_specs=[pl.BlockSpec(memory_space=pltpu.SMEM)] + vmem_specs(3),
-        out_specs=(any_spec, any_spec),
-        scratch_shapes=[
-            pltpu.VMEM((nz + 2, 9 * ch, nh * w), BF),
-            pltpu.VMEM((nz, ch, nh * w), BF),
-            pltpu.VMEM((2, chips, 27, cg, ch), F32),
-            pltpu.SemaphoreType.DMA((2,)),
-        ],
-        cost_estimate=pl.CostEstimate(
-            flops=2 * 27 * ch * ch * nz * nh * w, transcendentals=0, bytes_accessed=4 * 27 * ch * ch
-        ),
-        name="wgrad",
-    )(index, own, *x_halos)
+        [pltpu.VMEM((chips, 27, cg, ch), F32)] * 2,
+        local,
+        scratch=[pltpu.VMEM((nz + 2, 9 * ch, nh * w), BF), pltpu.VMEM((nz, ch, nh * w), BF)],
+        smem=1,
+        flops=2 * 27 * ch * ch * nz * nh * w,
+    )
     got = lax.ppermute(send, "core", swap)
     pair = keep + got
     pieces = swap_all(pair, CHIPS).reshape(chips, 27, cg, ch)
-    group = pieces.sum(0)
-
-    near = pl.pallas_call(
+    (padded,) = call(chips_add_kernel, [pltpu.VMEM((ns, cg, ch), F32)], [near_core(pieces)])
+
+    near = call(
         conv_kernel,
-        out_shape=(sds((4, 2, nz, nh, cg, w), F32),) * 4,
-        in_specs=[pl.BlockSpec(memory_space=pltpu.SMEM)] + vmem_specs(5),
-        out_specs=(any_spec,) * 4,
-        scratch_shapes=[
-            pltpu.VMEM((2, nz + 2, 9 * ch, nh * w), BF),
-            pltpu.VMEM((3, ch, 9 * ch), BF),
-            pltpu.VMEM((3, ch, 9 * ch), BF),
-            pltpu.VMEM((4, 4, 2, nz, nh, cg, w), F32),
-            pltpu.SemaphoreType.DMA((4,)),
-        ],
-        cost_estimate=pl.CostEstimate(
-            flops=4 * 27 * ch * ch * nz * nh * w, transcendentals=0, bytes_accessed=4 * 27 * ch * ch
-        ),
-        name="conv",
-    )(index, own, *x_halos, mine, other)
+        [pltpu.VMEM((4, 2, nz, nh, cg, w), F32)] * 4,
+        local + [mine, other],
+        scratch=[pltpu.VMEM((2, nz + 2, 9 * ch, nh * w), BF)] + [pltpu.VMEM((3, ch, 9 * ch), BF)] * 2,
+        smem=1,
+        flops=4 * 27 * ch * ch * nz * nh * w,
+    )
     near = (
         near[0],
         lax.ppermute(near[1], "core", swap),
         lax.ppermute(near[2], "zl", swap),
         lax.ppermute(near[3], ("zl", "core"), [(i, 3 - i) for i in range(4)]),
     )
-
-    padded = jnp.pad(group, ((0, ns - 27), (0, 0), (0, 0)))
     shares = swap_all(padded, SPACE)
     _, near = lax.optimization_barrier((shares, near))
-    tap = shares.sum(0) * norm
-    taps = swap_all(jnp.broadcast_to(tap[None], (ns, cg, ch)), SPACE)
+    (tap,) = call(functools.partial(space_add_kernel, norm=norm), [pltpu.VMEM((ns, cg, ch), F32)], [near_core(shares)])
+    taps = swap_all(tap, SPACE)
     blocks = {j: jnp.stack([part[j] for part in near]) for j in (2, 1, 3, 0)}
     blocks = {j: lax.ppermute(b, "x", [(i, i ^ j) for i in range(4)]) if j else b for j, b in blocks.items()}
     output, grad_in = call(
-        place_kernel, [sds((nz, rows, cg, w), F32)] * 2, [index] + [blocks[j] for j in range(4)], smem=1
+        place_kernel, [sds((nz, rows, cg, w), F32)] * 2, [index] + [near_core(blocks[j]) for j in range(4)], smem=1
     )
     weight_grad = taps[:27].reshape(3, 3, 3, cg, ch).transpose(0, 1, 2, 4, 3)
     return output, grad_in, weight_grad

time: 139 us -> 130 us (0.935)
  local copies, waits for them, and re-layouts: 4.83 us -> 1.56 us
  Pallas kernels: 13.2 us -> 9.99 us
  other arithmetic: 2.95 us -> 1.05 us
    pallas_call x5 -> x7, Pallas kernels: 13.2 us -> 9.99 us  [call(): pl.pallas_call(kernel, out_shape=outs[0] if one else tuple(outs), in_spec...]
    unnamed x24 -> x6, local copies, waits for them, and re-layouts: 2.78 us -> 0.83 us
  transfers between devices with their start and end apart: 17 -> 17, of which waited for: 8 -> 8; matrix products, arithmetic and copies ran while one was open for 3% -> 1% of each run, Pallas kernels for 8% -> 6%
where the time goes in v8:
time: 130 us; the launch traced here: 128 us
  starting transfers between devices  85.4 us (66%)
  waiting for transfers between devices  29.3 us (23%)
  Pallas kernels  9.99 us (8%)
  local copies, waits for them, and re-layouts  1.56 us (1%)
    all_to_all x5, starting transfers between devices, swap_all(): return lax.all_to_all(array, axes, 0, 0, tiled=True)  44.4 us
    ppermute x3, starting transfers between devices, step(): lax.ppermute(b, 'x', [(i, i ^ j) for i in range(4)])  10.4 us
    pallas_call x7, Pallas kernels, call(): pl.pallas_call(kernel, out_shape=outs[0] if one else tuple(outs), in_spec...  9.99 us
    ppermute x2, starting transfers between devices, step(): lax.ppermute(lax.dynamic_slice(grad_out, (side, 0, 0, 0), (1, rows, cg, w...  9.87 us
    all_to_all x5, waiting for transfers between devices, swap_all(): return lax.all_to_all(array, axes, 0, 0, tiled=True)  9.71 us
    ppermute x2, starting transfers between devices, step(): lax.ppermute(lax.dynamic_slice(own, (0, 0, side, 0, 0, 0), (n, 1, 1, nr,...  9.2 us
    ppermute x3, waiting for transfers between devices, step(): lax.ppermute(b, 'x', [(i, i ^ j) for i in range(4)])  4.67 us
    ppermute x2, waiting for transfers between devices, step(): lax.ppermute(lax.dynamic_slice(own, (0, 0, side, 0, 0, 0), (n, 1, 1, nr,...  3.98 us
  transfers between devices with their start and end apart: 17, of which 8 were waited for; matrix products, arithmetic and copies ran while one was open for 1% of the time, Pallas kernels for 6%

profile of v8, /device:TPU:6, one launch (start us, length us, event | category | flops | bytes accessed | tf_op | source)
XLA Modules:
  0.0 128.1 jit_solution(2942398161323174388)
XLA Ops:
  0.6 1.8 %shard_map.58 = bf16[16,2,2,4,8,128]{5,4,3,2,1,0:T(8,128)(2,1)} custom-call(bf16[2,32,8,128]{3,2,1,0:T(8,128)(2,1)} %x_ref.1, bf16[2,32,8,128]{3,2,1,0:T(8,128)(2,1)} %g_ref.1), custom_call_target="tpu_custom_call" | custom-call | bytes 1310720 | tf_op jit(solution)/shard_map/pallas_call | solution.py:28
  2.5 9.3 %all-to-all-start = ((bf16[16,2,2,4,8,128]{5,4,3,2,1,0:T(8,128)(2,1)}), bf16[16,2,2,4,8,128]{5,4,3,2,1,0:T(8,128)(2,1)S(1)}, u32[]{:S(2)}, u32[]{:S(2)}) async-start(bf16[16,2,2,4,8,128]{5,4,3,2,1,0:T(8,128)(2,1)} %shard_map.58), calls=%async_computation | async-start | bytes 1048576 | tf_op jit(solution)/shard_map/all_to_all | solution.py:252
  12.5 9.2 %collective-permute-start.3 = (bf16[32,8,128]{2,1,0:T(8,128)(2,1)S(1)}, bf16[32,8,128]{2,1,0:T(8,128)(2,1)S(1)}, u32[]{:S(2)}, u32[]{:S(2)}) collective-permute-start(bf16[32,8,128]{2,1,0:T(8,128)(2,1)S(1)} %get-tuple-element.46), channel_id=1, source_target_pairs={{0,16},{32,48},{64,80},{96,112},{128,144},{160,176},{192,208},{224... | collective-permute-start | bytes 196616 | tf_op jit(solution)/shard_map/ppermute | solution.py:272
  21.8 3.6 %collective-permute-done.3.even_ref = bf16[32,8,128]{2,1,0:T(8,128)(2,1)S(1)} collective-permute-done((bf16[32,8,128]{2,1,0:T(8,128)(2,1)S(1)}, bf16[32,8,128]{2,1,0:T(8,128)(2,1)S(1)}, u32[]{:S(2)}, u32[]{:S(2)}) %collective-permute-start.3) | collective-permute-done | bytes 65568 | tf_op jit(solution)/shard_map/ppermute | solution.py:272
  25.4 1.8 %shard_map.61 = bf16[8,39,8,128]{3,2,1,0:T(8,128)(2,1)} custom-call(s32[1]{0:T(128)} %bitcast.p_ref, bf16[27,8,128]{2,1,0:T(8,128)(2,1)} %bitcast.16, bf16[32,8,128]{2,1,0:T(8,128)(2,1)S(1)} %collective-permute-done.3.even_ref, bf16[32,8,128]{2,1,0:T(8,128)(2,1)S(1)} %collective-permute-done.4.odd_ref), custom_call_target="tpu_custom_call" | custom-call | bytes 1464324 | tf_op jit(solution)/shard_map/pallas_call | solution.py:28
  27.1 4.8 %all-to-all-start.3 = ((bf16[8,39,8,128]{3,2,1,0:T(8,128)(2,1)}), bf16[8,39,8,128]{3,2,1,0:T(8,128)(2,1)S(1)}, u32[]{:S(2)}, u32[]{:S(2)}) async-start(bf16[8,39,8,128]{3,2,1,0:T(8,128)(2,1)} %shard_map.61), calls=%async_computation.3 | async-start | bytes 1277952 | tf_op jit(solution)/shard_map/all_to_all | solution.py:252
  32.6 8.5 %collective-permute-start = (bf16[16,4,8,128]{3,2,1,0:T(8,128)(2,1)S(1)}, bf16[16,4,8,128]{3,2,1,0:T(8,128)(2,1)S(1)}, u32[]{:S(2)}, u32[]{:S(2)}) collective-permute-start(bf16[16,4,8,128]{3,2,1,0:T(8,128)(2,1)S(1)} %get-tuple-element.28), channel_id=1, source_target_pairs={{0,16},{32,48},{64,80},{96,112},{128,144},{160,176},{192,208},{224... | collective-permute-start | bytes 393224 | tf_op jit(solution)/shard_map/ppermute | solution.py:278
  41.2 4.0 %collective-permute-done.even_ref = bf16[16,4,8,128]{3,2,1,0:T(8,128)(2,1)S(1)} collective-permute-done((bf16[16,4,8,128]{3,2,1,0:T(8,128)(2,1)S(1)}, bf16[16,4,8,128]{3,2,1,0:T(8,128)(2,1)S(1)}, u32[]{:S(2)}, u32[]{:S(2)}) %collective-permute-start) | collective-permute-done | bytes 131104 | tf_op jit(solution)/shard_map/ppermute | solution.py:278
  45.2 1.3 %shard_map.59 = (f32[8,27,8,128]{3,2,1,0:T(8,128)S(1)}, f32[8,27,8,128]{3,2,1,0:T(8,128)S(1)}) custom-call(s32[1]{0:T(128)} %bitcast.p_ref, bf16[16,2,2,4,8,128]{5,4,3,2,1,0:T(8,128)(2,1)S(1)} %all-to-all-done.own_ref, bf16[16,4,8,128]{3,2,1,0:T(8,128)(2,1)S(1)} %collective-permute-done.even_ref, bf16[16,4,8,128]{3,2,1,0:T(8,128)(2,1)S(1)} %collective-permute-done.1.odd_ref), custom_call_target="tpu_custom_call" | custom-call | flops 452984832 | bytes 2555908 | tf_op jit(solution)/shard_map/pallas_call | solution.py:28
  46.5 1.9 %collective-permute-start.2 = (f32[8,27,8,128]{3,2,1,0:T(8,128)S(1)}, f32[8,27,8,128]{3,2,1,0:T(8,128)S(1)}, u32[]{:S(2)}, u32[]{:S(2)}) collective-permute-start(f32[8,27,8,128]{3,2,1,0:T(8,128)S(1)} %get-tuple-element.16), channel_id=1, source_target_pairs={{0,1},{1,0},{2,3},{3,2},{4,5},{5,4},{6,7},{7,6},{8,9},{9,8},{10,11... | collective-permute-start | bytes 2654216 | tf_op jit(solution)/shard_map/ppermute | solution.py:299
  48.4 2.4 %collective-permute-done.2 = f32[8,27,8,128]{3,2,1,0:T(8,128)S(1)} collective-permute-done((f32[8,27,8,128]{3,2,1,0:T(8,128)S(1)}, f32[8,27,8,128]{3,2,1,0:T(8,128)S(1)}, u32[]{:S(2)}, u32[]{:S(2)}) %collective-permute-start.2) | collective-permute-done | bytes 884768 | tf_op jit(solution)/shard_map/ppermute | solution.py:299
  50.8 1.0 add.34
  51.8 8.5 %all-to-all-start.1 = ((f32[8,27,8,128]{3,2,1,0:T(8,128)}), f32[8,27,8,128]{3,2,1,0:T(8,128)S(1)}, u32[]{:S(2)}, u32[]{:S(2)}) async-start(f32[8,27,8,128]{3,2,1,0:T(8,128)} %add.34), calls=%async_computation.1 | async-start | bytes 1769472 | tf_op jit(solution)/shard_map/all_to_all | solution.py:252
  60.3 1.9 %collective-permute-start.5 = (bf16[8,39,8,128]{3,2,1,0:T(8,128)(2,1)S(1)}, bf16[8,39,8,128]{3,2,1,0:T(8,128)(2,1)S(1)}, u32[]{:S(2)}, u32[]{:S(2)}) collective-permute-start(bf16[8,39,8,128]{3,2,1,0:T(8,128)(2,1)S(1)} %all-to-all-done.3.mine_ref), channel_id=1, source_target_pairs={{0,1},{1,0},{2,3},{3,2},{4,5},{5,4},{6,7},{7,6},{8,9},{9,8},{10,11... | collective-permute-start | bytes 1916936 | tf_op jit(solution)/shard_map/ppermute | solution.py:289
  62.2 9.7 %all-to-all-done.1.pieces_ref = f32[8,27,8,128]{3,2,1,0:T(8,128)S(1)} async-done(((f32[8,27,8,128]{3,2,1,0:T(8,128)}), f32[8,27,8,128]{3,2,1,0:T(8,128)S(1)}, u32[]{:S(2)}, u32[]{:S(2)}) %all-to-all-start.1) | async-done | bytes 884768 | tf_op jit(solution)/shard_map/all_to_all | solution.py:252
  71.9 0.7 shard_map.60
  72.6 9.6 %all-to-all-start.2 = ((f32[32,8,128]{2,1,0:T(8,128)}), f32[32,8,128]{2,1,0:T(8,128)S(1)}, u32[]{:S(2)}, u32[]{:S(2)}) async-start(f32[32,8,128]{2,1,0:T(8,128)} %shard_map.60), calls=%async_computation.2 | async-start | bytes 262144 | tf_op jit(solution)/shard_map/all_to_all | solution.py:252
  82.3 0.8 copy-done.2
  83.1 2.9 %shard_map.62 = (f32[4,2,2,2,8,128]{5,4,3,2,1,0:T(8,128)S(1)}, f32[4,2,2,2,8,128]{5,4,3,2,1,0:T(8,128)S(1)}, f32[4,2,2,2,8,128]{5,4,3,2,1,0:T(8,128)S(1)}, f32[4,2,2,2,8,128]{5,4,3,2,1,0:T(8,128)S(1)}) custom-call(s32[1]{0:T(128)} %bitcast.p_ref, bf16[16,2,2,4,8,128]{5,4,3,2,1,0:T(8,128)(2,1)S(1)} %all-to-all-done.own_ref, ...), custom_call_target="tpu_custom_call" | custom-call | flops 905969664 | bytes 2588676 | tf_op jit(solution)/shard_map/pallas_call | solution.py:28
  86.0 1.9 %collective-permute-start.6 = (f32[4,2,2,2,8,128]{5,4,3,2,1,0:T(8,128)S(1)}, f32[4,2,2,2,8,128]{5,4,3,2,1,0:T(8,128)S(1)}, u32[]{:S(2)}, u32[]{:S(2)}) collective-permute-start(f32[4,2,2,2,8,128]{5,4,3,2,1,0:T(8,128)S(1)} %get-tuple-element.18), channel_id=1, source_target_pairs={{0,1},{1,0},{2,3},{3,2},{4,5},{5,4},{6,7},{7,6},{8,9},{9,8},{10,11... | collective-permute-start | bytes 393224 | tf_op jit(solution)/shard_map/ppermute | solution.py:314
  87.9 3.3 %collective-permute-start.7 = (f32[4,2,2,2,8,128]{5,4,3,2,1,0:T(8,128)S(1)}, f32[4,2,2,2,8,128]{5,4,3,2,1,0:T(8,128)S(1)}, u32[]{:S(2)}, u32[]{:S(2)}) collective-permute-start(f32[4,2,2,2,8,128]{5,4,3,2,1,0:T(8,128)S(1)} %get-tuple-element.19), channel_id=1, source_target_pairs={{0,8},{8,0},{1,9},{9,1},{2,10},{10,2},{3,11},{11,3},{4,12},{12,4},... | collective-permute-start | bytes 393224 | tf_op jit(solution)/shard_map/ppermute | solution.py:315
  91.2 2.3 %collective-permute-start.8 = (f32[4,2,2,2,8,128]{5,4,3,2,1,0:T(8,128)S(1)}, f32[4,2,2,2,8,128]{5,4,3,2,1,0:T(8,128)S(1)}, u32[]{:S(2)}, u32[]{:S(2)}) collective-permute-start(f32[4,2,2,2,8,128]{5,4,3,2,1,0:T(8,128)S(1)} %get-tuple-element.20), channel_id=1, source_target_pairs={{0,9},{1,8},{8,1},{9,0},{2,11},{3,10},{10,3},{11,2},{4,13},{5,12},... | collective-permute-start | bytes 393224 | tf_op jit(solution)/shard_map/ppermute | solution.py:316
  93.6 2.1 %collective-permute-done.7 = f32[4,2,2,2,8,128]{5,4,3,2,1,0:T(8,128)S(1)} collective-permute-done((f32[4,2,2,2,8,128]{5,4,3,2,1,0:T(8,128)S(1)}, f32[4,2,2,2,8,128]{5,4,3,2,1,0:T(8,128)S(1)}, u32[]{:S(2)}, u32[]{:S(2)}) %collective-permute-start.7) | collective-permute-done | bytes 131104 | tf_op jit(solution)/shard_map/ppermute | solution.py:315
  95.7 2.8 %collective-permute-done.8 = f32[4,2,2,2,8,128]{5,4,3,2,1,0:T(8,128)S(1)} collective-permute-done((f32[4,2,2,2,8,128]{5,4,3,2,1,0:T(8,128)S(1)}, f32[4,2,2,2,8,128]{5,4,3,2,1,0:T(8,128)S(1)}, u32[]{:S(2)}, u32[]{:S(2)}) %collective-permute-start.8) | collective-permute-done | bytes 131104 | tf_op jit(solution)/shard_map/ppermute | solution.py:316
  98.5 0.7 shard_map.64
  99.2 12.2 %all-to-all-start.4 = ((f32[32,8,128]{2,1,0:T(8,128)}), f32[32,8,128]{2,1,0:T(8,128)S(1)}, u32[]{:S(2)}, u32[]{:S(2)}) async-start(f32[32,8,128]{2,1,0:T(8,128)} %shard_map.64), calls=%async_computation.4 | async-start | bytes 262144 | tf_op jit(solution)/shard_map/all_to_all | solution.py:252
  111.5 2.3 %collective-permute-start.9 = (f32[4,2,2,2,8,128]{5,4,3,2,1,0:T(8,128)S(1)}, f32[4,2,2,2,8,128]{5,4,3,2,1,0:T(8,128)S(1)}, u32[]{:S(2)}, u32[]{:S(2)}) collective-permute-start(f32[4,2,2,2,8,128]{5,4,3,2,1,0:T(8,128)S(1)} %pad_maximum_fusion.1), channel_id=1, source_target_pairs={{0,2},{2,0},{4,6},{6,4},{1,3},{3,1},{5,7},{7,5},{8,10},{10,8},{12,... | collective-permute-start | bytes 393224 | tf_op jit(solution)/shard_map/ppermute | solution.py:323
  113.8 4.7 %collective-permute-start.10 = (f32[4,2,2,2,8,128]{5,4,3,2,1,0:T(8,128)S(1)}, f32[4,2,2,2,8,128]{5,4,3,2,1,0:T(8,128)S(1)}, u32[]{:S(2)}, u32[]{:S(2)}) collective-permute-start(f32[4,2,2,2,8,128]{5,4,3,2,1,0:T(8,128)S(1)} %pad_maximum_fusion.2), channel_id=1, source_target_pairs={{0,4},{2,6},{4,0},{6,2},{1,5},{3,7},{5,1},{7,3},{8,12},{10,14},{12... | collective-permute-start | bytes 393224 | tf_op jit(solution)/shard_map/ppermute | solution.py:323
  118.6 3.4 %collective-permute-start.11 = (f32[4,2,2,2,8,128]{5,4,3,2,1,0:T(8,128)S(1)}, f32[4,2,2,2,8,128]{5,4,3,2,1,0:T(8,128)S(1)}, u32[]{:S(2)}, u32[]{:S(2)}) collective-permute-start(f32[4,2,2,2,8,128]{5,4,3,2,1,0:T(8,128)S(1)} %pad_maximum_fusion.3), channel_id=1, source_target_pairs={{0,6},{2,4},{4,2},{6,0},{1,7},{3,5},{5,3},{7,1},{8,14},{10,12},{12... | collective-permute-start | bytes 393224 | tf_op jit(solution)/shard_map/ppermute | solution.py:323
  122.0 0.7 collective-permute-done.10.refs_2_
  122.7 3.9 %collective-permute-done.11.refs_3_ = f32[4,2,2,2,8,128]{5,4,3,2,1,0:T(8,128)S(1)} collective-permute-done((f32[4,2,2,2,8,128]{5,4,3,2,1,0:T(8,128)S(1)}, f32[4,2,2,2,8,128]{5,4,3,2,1,0:T(8,128)S(1)}, u32[]{:S(2)}, u32[]{:S(2)}) %collective-permute-start.11) | collective-permute-done | bytes 131104 | tf_op jit(solution)/shard_map/ppermute | solution.py:323
  126.7 0.8 shard_map.63
  (25 shorter events, 2.1 us)
Async XLA Ops:
  2.5 9.4 %copy-start.1 = (bf16[2,32,8,128]{3,2,1,0:T(8,128)(2,1)S(1)}, bf16[2,32,8,128]{3,2,1,0:T(8,128)(2,1)}, u32[]{:S(2)}) copy-start(bf16[2,32,8,128]{3,2,1,0:T(8,128)(2,1)} %g_ref.1) | copy-start | bytes 393220
  2.5 24.7 %all-to-all-start = ((bf16[16,2,2,4,8,128]{5,4,3,2,1,0:T(8,128)(2,1)}), bf16[16,2,2,4,8,128]{5,4,3,2,1,0:T(8,128)(2,1)S(1)}, u32[]{:S(2)}, u32[]{:S(2)}) async-start(bf16[16,2,2,4,8,128]{5,4,3,2,1,0:T(8,128)(2,1)} %shard_map.58), calls=%async_computation | async-start | bytes 1048576 | tf_op jit(solution)/shard_map/all_to_all | solution.py:252
  11.9 9.9 %collective-permute-start.4 = (bf16[32,8,128]{2,1,0:T(8,128)(2,1)S(1)}, bf16[32,8,128]{2,1,0:T(8,128)(2,1)S(1)}, u32[]{:S(2)}, u32[]{:S(2)}) collective-permute-start(bf16[32,8,128]{2,1,0:T(8,128)(2,1)S(1)} %get-tuple-element.45), channel_id=1, source_target_pairs={{16,32},{48,64},{80,96},{112,128},{144,160},{176,192},{208,224},{2... | collective-permute-start | bytes 196616 | tf_op jit(solution)/shard_map/ppermute | solution.py:272
  12.5 12.9 %collective-permute-start.3 = (bf16[32,8,128]{2,1,0:T(8,128)(2,1)S(1)}, bf16[32,8,128]{2,1,0:T(8,128)(2,1)S(1)}, u32[]{:S(2)}, u32[]{:S(2)}) collective-permute-start(bf16[32,8,128]{2,1,0:T(8,128)(2,1)S(1)} %get-tuple-element.46), channel_id=1, source_target_pairs={{0,16},{32,48},{64,80},{96,112},{128,144},{160,176},{192,208},{224... | collective-permute-start | bytes 196616 | tf_op jit(solution)/shard_map/ppermute | solution.py:272
  27.1 24.7 %all-to-all-start.3 = ((bf16[8,39,8,128]{3,2,1,0:T(8,128)(2,1)}), bf16[8,39,8,128]{3,2,1,0:T(8,128)(2,1)S(1)}, u32[]{:S(2)}, u32[]{:S(2)}) async-start(bf16[8,39,8,128]{3,2,1,0:T(8,128)(2,1)} %shard_map.61), calls=%async_computation.3 | async-start | bytes 1277952 | tf_op jit(solution)/shard_map/all_to_all | solution.py:252
  32.0 9.2 %collective-permute-start.1 = (bf16[16,4,8,128]{3,2,1,0:T(8,128)(2,1)S(1)}, bf16[16,4,8,128]{3,2,1,0:T(8,128)(2,1)S(1)}, u32[]{:S(2)}, u32[]{:S(2)}) collective-permute-start(bf16[16,4,8,128]{3,2,1,0:T(8,128)(2,1)S(1)} %get-tuple-element.27), channel_id=1, source_target_pairs={{16,32},{48,64},{80,96},{112,128},{144,160},{176,192},{208,224},{2... | collective-permute-start | bytes 393224 | tf_op jit(solution)/shard_map/ppermute | solution.py:278
  32.6 12.5 %collective-permute-start = (bf16[16,4,8,128]{3,2,1,0:T(8,128)(2,1)S(1)}, bf16[16,4,8,128]{3,2,1,0:T(8,128)(2,1)S(1)}, u32[]{:S(2)}, u32[]{:S(2)}) collective-permute-start(bf16[16,4,8,128]{3,2,1,0:T(8,128)(2,1)S(1)} %get-tuple-element.28), channel_id=1, source_target_pairs={{0,16},{32,48},{64,80},{96,112},{128,144},{160,176},{192,208},{224... | collective-permute-start | bytes 393224 | tf_op jit(solution)/shard_map/ppermute | solution.py:278
  46.5 4.3 %collective-permute-start.2 = (f32[8,27,8,128]{3,2,1,0:T(8,128)S(1)}, f32[8,27,8,128]{3,2,1,0:T(8,128)S(1)}, u32[]{:S(2)}, u32[]{:S(2)}) collective-permute-start(f32[8,27,8,128]{3,2,1,0:T(8,128)S(1)} %get-tuple-element.16), channel_id=1, source_target_pairs={{0,1},{1,0},{2,3},{3,2},{4,5},{5,4},{6,7},{7,6},{8,9},{9,8},{10,11... | collective-permute-start | bytes 2654216 | tf_op jit(solution)/shard_map/ppermute | solution.py:299
  51.8 8.5 %copy-start = (bf16[8,39,8,128]{3,2,1,0:T(8,128)(2,1)}, bf16[8,39,8,128]{3,2,1,0:T(8,128)(2,1)S(1)}, u32[]{:S(2)}) copy-start(bf16[8,39,8,128]{3,2,1,0:T(8,128)(2,1)S(1)} %all-to-all-done.3.mine_ref) | copy-start | bytes 1916932
  51.8 20.1 %all-to-all-start.1 = ((f32[8,27,8,128]{3,2,1,0:T(8,128)}), f32[8,27,8,128]{3,2,1,0:T(8,128)S(1)}, u32[]{:S(2)}, u32[]{:S(2)}) async-start(f32[8,27,8,128]{3,2,1,0:T(8,128)} %add.34), calls=%async_computation.1 | async-start | bytes 1769472 | tf_op jit(solution)/shard_map/all_to_all | solution.py:252
  60.3 21.9 %collective-permute-start.5 = (bf16[8,39,8,128]{3,2,1,0:T(8,128)(2,1)S(1)}, bf16[8,39,8,128]{3,2,1,0:T(8,128)(2,1)S(1)}, u32[]{:S(2)}, u32[]{:S(2)}) collective-permute-start(bf16[8,39,8,128]{3,2,1,0:T(8,128)(2,1)S(1)} %all-to-all-done.3.mine_ref), channel_id=1, source_target_pairs={{0,1},{1,0},{2,3},{3,2},{4,5},{5,4},{6,7},{7,6},{8,9},{9,8},{10,11... | collective-permute-start | bytes 1916936 | tf_op jit(solution)/shard_map/ppermute | solution.py:289
  72.6 25.9 %all-to-all-start.2 = ((f32[32,8,128]{2,1,0:T(8,128)}), f32[32,8,128]{2,1,0:T(8,128)S(1)}, u32[]{:S(2)}, u32[]{:S(2)}) async-start(f32[32,8,128]{2,1,0:T(8,128)} %shard_map.60), calls=%async_computation.2 | async-start | bytes 262144 | tf_op jit(solution)/shard_map/all_to_all | solution.py:252
  82.2 0.8 copy-start.2
  86.0 7.6 %collective-permute-start.6 = (f32[4,2,2,2,8,128]{5,4,3,2,1,0:T(8,128)S(1)}, f32[4,2,2,2,8,128]{5,4,3,2,1,0:T(8,128)S(1)}, u32[]{:S(2)}, u32[]{:S(2)}) collective-permute-start(f32[4,2,2,2,8,128]{5,4,3,2,1,0:T(8,128)S(1)} %get-tuple-element.18), channel_id=1, source_target_pairs={{0,1},{1,0},{2,3},{3,2},{4,5},{5,4},{6,7},{7,6},{8,9},{9,8},{10,11... | collective-permute-start | bytes 393224 | tf_op jit(solution)/shard_map/ppermute | solution.py:314
  87.9 7.8 %collective-permute-start.7 = (f32[4,2,2,2,8,128]{5,4,3,2,1,0:T(8,128)S(1)}, f32[4,2,2,2,8,128]{5,4,3,2,1,0:T(8,128)S(1)}, u32[]{:S(2)}, u32[]{:S(2)}) collective-permute-start(f32[4,2,2,2,8,128]{5,4,3,2,1,0:T(8,128)S(1)} %get-tuple-element.19), channel_id=1, source_target_pairs={{0,8},{8,0},{1,9},{9,1},{2,10},{10,2},{3,11},{11,3},{4,12},{12,4},... | collective-permute-start | bytes 393224 | tf_op jit(solution)/shard_map/ppermute | solution.py:315
  91.2 7.3 %collective-permute-start.8 = (f32[4,2,2,2,8,128]{5,4,3,2,1,0:T(8,128)S(1)}, f32[4,2,2,2,8,128]{5,4,3,2,1,0:T(8,128)S(1)}, u32[]{:S(2)}, u32[]{:S(2)}) collective-permute-start(f32[4,2,2,2,8,128]{5,4,3,2,1,0:T(8,128)S(1)} %get-tuple-element.20), channel_id=1, source_target_pairs={{0,9},{1,8},{8,1},{9,0},{2,11},{3,10},{10,3},{11,2},{4,13},{5,12},... | collective-permute-start | bytes 393224 | tf_op jit(solution)/shard_map/ppermute | solution.py:316
  99.2 28.3 %all-to-all-start.4 = ((f32[32,8,128]{2,1,0:T(8,128)}), f32[32,8,128]{2,1,0:T(8,128)S(1)}, u32[]{:S(2)}, u32[]{:S(2)}) async-start(f32[32,8,128]{2,1,0:T(8,128)} %shard_map.64), calls=%async_computation.4 | async-start | bytes 262144 | tf_op jit(solution)/shard_map/all_to_all | solution.py:252
  111.5 10.5 %collective-permute-start.9 = (f32[4,2,2,2,8,128]{5,4,3,2,1,0:T(8,128)S(1)}, f32[4,2,2,2,8,128]{5,4,3,2,1,0:T(8,128)S(1)}, u32[]{:S(2)}, u32[]{:S(2)}) collective-permute-start(f32[4,2,2,2,8,128]{5,4,3,2,1,0:T(8,128)S(1)} %pad_maximum_fusion.1), channel_id=1, source_target_pairs={{0,2},{2,0},{4,6},{6,4},{1,3},{3,1},{5,7},{7,5},{8,10},{10,8},{12,... | collective-permute-start | bytes 393224 | tf_op jit(solution)/shard_map/ppermute | solution.py:323
  113.8 8.9 %collective-permute-start.10 = (f32[4,2,2,2,8,128]{5,4,3,2,1,0:T(8,128)S(1)}, f32[4,2,2,2,8,128]{5,4,3,2,1,0:T(8,128)S(1)}, u32[]{:S(2)}, u32[]{:S(2)}) collective-permute-start(f32[4,2,2,2,8,128]{5,4,3,2,1,0:T(8,128)S(1)} %pad_maximum_fusion.2), channel_id=1, source_target_pairs={{0,4},{2,6},{4,0},{6,2},{1,5},{3,7},{5,1},{7,3},{8,12},{10,14},{12... | collective-permute-start | bytes 393224 | tf_op jit(solution)/shard_map/ppermute | solution.py:323
  118.6 8.1 %collective-permute-start.11 = (f32[4,2,2,2,8,128]{5,4,3,2,1,0:T(8,128)S(1)}, f32[4,2,2,2,8,128]{5,4,3,2,1,0:T(8,128)S(1)}, u32[]{:S(2)}, u32[]{:S(2)}) collective-permute-start(f32[4,2,2,2,8,128]{5,4,3,2,1,0:T(8,128)S(1)} %pad_maximum_fusion.3), channel_id=1, source_target_pairs={{0,6},{2,4},{4,2},{6,0},{1,7},{3,5},{5,3},{7,1},{8,14},{10,12},{12... | collective-permute-start | bytes 393224 | tf_op jit(solution)/shard_map/ppermute | solution.py:323

commit v9 on v8

--- a/solution.py
+++ b/solution.py
@@ -163,6 +163,16 @@
                     ]
                     keep_ref[q, tap] = jnp.where(first, left, right)
                     send_ref[q, tap] = jnp.where(first, right, left)
+
+
+def pair_add_kernel(keep_ref, got_ref, o_ref, sum_ref, sems):
+    count = keep_ref.shape[0]
+    stores = [pltpu.make_async_copy(sum_ref.at[q], o_ref.at[q], sems.at[q]) for q in range(count)]
+    for q in range(count):
+        sum_ref[q] = keep_ref[q] + got_ref[q]
+        stores[q].start()
+    for store in stores:
+        store.wait()
 
 
 def conv_kernel(
@@ -297,7 +307,14 @@
         flops=2 * 27 * ch * ch * nz * nh * w,
     )
     got = lax.ppermute(send, "core", swap)
-    pair = keep + got
+    pair = pl.pallas_call(
+        pair_add_kernel,
+        out_shape=sds((chips, 27, cg, ch), F32),
+        in_specs=vmem_specs(2),
+        out_specs=pl.BlockSpec(memory_space=pl.ANY),
+        scratch_shapes=[pltpu.VMEM((chips, 27, cg, ch), F32), pltpu.SemaphoreType.DMA((chips,))],
+        name="pair_add",
+    )(near_core(keep), near_core(got))
     pieces = swap_all(pair, CHIPS).reshape(chips, 27, cg, ch)
     (padded,) = call(chips_add_kernel, [pltpu.VMEM((ns, cg, ch), F32)], [near_core(pieces)])
 
@@ -316,11 +333,12 @@
         lax.ppermute(near[3], ("zl", "core"), [(i, 3 - i) for i in range(4)]),
     )
     shares = swap_all(padded, SPACE)
-    _, near = lax.optimization_barrier((shares, near))
+    _, near = lax.optimization_barrier((padded, near))
     (tap,) = call(functools.partial(space_add_kernel, norm=norm), [pltpu.VMEM((ns, cg, ch), F32)], [near_core(shares)])
     taps = swap_all(tap, SPACE)
-    blocks = {j: jnp.stack([part[j] for part in near]) for j in (2, 1, 3, 0)}
-    blocks = {j: lax.ppermute(b, "x", [(i, i ^ j) for i in range(4)]) if j else b for j, b in blocks.items()}
+    blocks = {j: jnp.stack([part[j] for part in near]) for j in range(4)}
+    for j in (2, 1, 3):
+        blocks[j] = lax.ppermute(blocks[j], "x", [(i, i ^ j) for i in range(4)])
     output, grad_in = call(
         place_kernel, [sds((nz, rows, cg, w), F32)] * 2, [index] + [near_core(blocks[j]) for j in range(4)], smem=1
     )

time: 130 us -> 122 us (0.938)
  the two profiles are of different devices: /device:TPU:6 before, /device:TPU:8 now
where the time goes in v9:
time: 122 us; the launch traced here: 121 us
  starting transfers between devices  76.3 us (63%)
  waiting for transfers between devices  28.2 us (23%)
  Pallas kernels  10.9 us (9%)
  local copies, waits for them, and re-layouts  4.9 us (4%)
    all_to_all x5, starting transfers between devices, swap_all(): return lax.all_to_all(array, axes, 0, 0, tiled=True)  33 us
    ppermute x2, starting transfers between devices, step(): lax.ppermute(lax.dynamic_slice(grad_out, (side, 0, 0, 0), (1, rows, cg, w...  12.5 us
    ppermute x3, starting transfers between devices, step(): blocks[j] = lax.ppermute(blocks[j], 'x', [(i, i ^ j) for i in range(4)])  12 us
    pallas_call x7, Pallas kernels, call(): pl.pallas_call(kernel, out_shape=outs[0] if one else tuple(outs), in_spec...  9.94 us
    all_to_all x5, waiting for transfers between devices, swap_all(): return lax.all_to_all(array, axes, 0, 0, tiled=True)  8.57 us
    ppermute x2, starting transfers between devices, step(): lax.ppermute(lax.dynamic_slice(own, (0, 0, side, 0, 0, 0), (n, 1, 1, nr,...  7.17 us
    ppermute x2, waiting for transfers between devices, step(): lax.ppermute(lax.dynamic_slice(grad_out, (side, 0, 0, 0), (1, rows, cg, w...  5.87 us
    ppermute x3, waiting for transfers between devices, step(): blocks[j] = lax.ppermute(blocks[j], 'x', [(i, i ^ j) for i in range(4)])  4.95 us
  transfers between devices with their start and end apart: 17, of which 8 were waited for; matrix products, arithmetic and copies ran while one was open for 0% of the time, Pallas kernels for 8%

profile of v9, /device:TPU:8, one launch (start us, length us, event | category | flops | bytes accessed | tf_op | source)
XLA Modules:
  0.0 121.4 jit_solution(2528691673534194589)
XLA Ops:
  0.6 1.8 %shard_map.58 = bf16[16,2,2,4,8,128]{5,4,3,2,1,0:T(8,128)(2,1)} custom-call(bf16[2,32,8,128]{3,2,1,0:T(8,128)(2,1)} %x_ref.1, bf16[2,32,8,128]{3,2,1,0:T(8,128)(2,1)} %g_ref.1), custom_call_target="tpu_custom_call" | custom-call | bytes 1310720 | tf_op jit(solution)/shard_map/pallas_call | solution.py:28
  2.5 6.3 %all-to-all-start = ((bf16[16,2,2,4,8,128]{5,4,3,2,1,0:T(8,128)(2,1)}), bf16[16,2,2,4,8,128]{5,4,3,2,1,0:T(8,128)(2,1)S(1)}, u32[]{:S(2)}, u32[]{:S(2)}) async-start(bf16[16,2,2,4,8,128]{5,4,3,2,1,0:T(8,128)(2,1)} %shard_map.58), calls=%async_computation | async-start | bytes 1048576 | tf_op jit(solution)/shard_map/all_to_all | solution.py:262
  8.9 9.9 %collective-permute-start.4 = (bf16[32,8,128]{2,1,0:T(8,128)(2,1)S(1)}, bf16[32,8,128]{2,1,0:T(8,128)(2,1)S(1)}, u32[]{:S(2)}, u32[]{:S(2)}) collective-permute-start(bf16[32,8,128]{2,1,0:T(8,128)(2,1)S(1)} %get-tuple-element.45), channel_id=1, source_target_pairs={{16,32},{48,64},{80,96},{112,128},{144,160},{176,192},{208,224},{2... | collective-permute-start | bytes 196616 | tf_op jit(solution)/shard_map/ppermute | solution.py:282
  18.8 2.6 %collective-permute-start.3 = (bf16[32,8,128]{2,1,0:T(8,128)(2,1)S(1)}, bf16[32,8,128]{2,1,0:T(8,128)(2,1)S(1)}, u32[]{:S(2)}, u32[]{:S(2)}) collective-permute-start(bf16[32,8,128]{2,1,0:T(8,128)(2,1)S(1)} %get-tuple-element.46), channel_id=1, source_target_pairs={{0,16},{32,48},{64,80},{96,112},{128,144},{160,176},{192,208},{224... | collective-permute-start | bytes 196616 | tf_op jit(solution)/shard_map/ppermute | solution.py:282
  21.4 1.3 %collective-permute-done.4.odd_ref = bf16[32,8,128]{2,1,0:T(8,128)(2,1)S(1)} collective-permute-done((bf16[32,8,128]{2,1,0:T(8,128)(2,1)S(1)}, bf16[32,8,128]{2,1,0:T(8,128)(2,1)S(1)}, u32[]{:S(2)}, u32[]{:S(2)}) %collective-permute-start.4) | collective-permute-done | bytes 65568 | tf_op jit(solution)/shard_map/ppermute | solution.py:282
  22.7 4.5 %collective-permute-done.3.even_ref = bf16[32,8,128]{2,1,0:T(8,128)(2,1)S(1)} collective-permute-done((bf16[32,8,128]{2,1,0:T(8,128)(2,1)S(1)}, bf16[32,8,128]{2,1,0:T(8,128)(2,1)S(1)}, u32[]{:S(2)}, u32[]{:S(2)}) %collective-permute-start.3) | collective-permute-done | bytes 65568 | tf_op jit(solution)/shard_map/ppermute | solution.py:282
  27.3 1.7 %shard_map.61 = bf16[8,39,8,128]{3,2,1,0:T(8,128)(2,1)} custom-call(s32[1]{0:T(128)} %bitcast.p_ref, bf16[27,8,128]{2,1,0:T(8,128)(2,1)} %bitcast.16, bf16[32,8,128]{2,1,0:T(8,128)(2,1)S(1)} %collective-permute-done.3.even_ref, bf16[32,8,128]{2,1,0:T(8,128)(2,1)S(1)} %collective-permute-done.4.odd_ref), custom_call_target="tpu_custom_call" | custom-call | bytes 1464324 | tf_op jit(solution)/shard_map/pallas_call | solution.py:28
  29.0 4.5 %all-to-all-start.2 = ((bf16[8,39,8,128]{3,2,1,0:T(8,128)(2,1)}), bf16[8,39,8,128]{3,2,1,0:T(8,128)(2,1)S(1)}, u32[]{:S(2)}, u32[]{:S(2)}) async-start(bf16[8,39,8,128]{3,2,1,0:T(8,128)(2,1)} %shard_map.61), calls=%async_computation.2 | async-start | bytes 1277952 | tf_op jit(solution)/shard_map/all_to_all | solution.py:262
  33.5 2.9 %collective-permute-start.1 = (bf16[16,4,8,128]{3,2,1,0:T(8,128)(2,1)S(1)}, bf16[16,4,8,128]{3,2,1,0:T(8,128)(2,1)S(1)}, u32[]{:S(2)}, u32[]{:S(2)}) collective-permute-start(bf16[16,4,8,128]{3,2,1,0:T(8,128)(2,1)S(1)} %get-tuple-element.27), channel_id=1, source_target_pairs={{16,32},{48,64},{80,96},{112,128},{144,160},{176,192},{208,224},{2... | collective-permute-start | bytes 393224 | tf_op jit(solution)/shard_map/ppermute | solution.py:288
  36.4 4.3 %collective-permute-start = (bf16[16,4,8,128]{3,2,1,0:T(8,128)(2,1)S(1)}, bf16[16,4,8,128]{3,2,1,0:T(8,128)(2,1)S(1)}, u32[]{:S(2)}, u32[]{:S(2)}) collective-permute-start(bf16[16,4,8,128]{3,2,1,0:T(8,128)(2,1)S(1)} %get-tuple-element.28), channel_id=1, source_target_pairs={{0,16},{32,48},{64,80},{96,112},{128,144},{160,176},{192,208},{224... | collective-permute-start | bytes 393224 | tf_op jit(solution)/shard_map/ppermute | solution.py:288
  40.7 3.7 %collective-permute-done.1.odd_ref = bf16[16,4,8,128]{3,2,1,0:T(8,128)(2,1)S(1)} collective-permute-done((bf16[16,4,8,128]{3,2,1,0:T(8,128)(2,1)S(1)}, bf16[16,4,8,128]{3,2,1,0:T(8,128)(2,1)S(1)}, u32[]{:S(2)}, u32[]{:S(2)}) %collective-permute-start.1) | collective-permute-done | bytes 131104 | tf_op jit(solution)/shard_map/ppermute | solution.py:288
  44.9 1.3 %shard_map.59 = (f32[8,27,8,128]{3,2,1,0:T(8,128)S(1)}, f32[8,27,8,128]{3,2,1,0:T(8,128)S(1)}) custom-call(s32[1]{0:T(128)} %bitcast.p_ref, bf16[16,2,2,4,8,128]{5,4,3,2,1,0:T(8,128)(2,1)S(1)} %all-to-all-done.own_ref, bf16[16,4,8,128]{3,2,1,0:T(8,128)(2,1)S(1)} %collective-permute-done.even_ref, bf16[16,4,8,128]{3,2,1,0:T(8,128)(2,1)S(1)} %collective-permute-done.1.odd_ref), custom_call_target="tpu_custom_call" | custom-call | flops 452984832 | bytes 2555908 | tf_op jit(solution)/shard_map/pallas_call | solution.py:28
  47.1 1.9 %collective-permute-start.2 = (f32[8,27,8,128]{3,2,1,0:T(8,128)S(1)}, f32[8,27,8,128]{3,2,1,0:T(8,128)S(1)}, u32[]{:S(2)}, u32[]{:S(2)}) collective-permute-start(f32[8,27,8,128]{3,2,1,0:T(8,128)S(1)} %get-tuple-element.16), channel_id=1, source_target_pairs={{0,1},{1,0},{2,3},{3,2},{4,5},{5,4},{6,7},{7,6},{8,9},{9,8},{10,11... | collective-permute-start | bytes 2654216 | tf_op jit(solution)/shard_map/ppermute | solution.py:309
  49.0 2.4 %collective-permute-done.2.got_ref = f32[8,27,8,128]{3,2,1,0:T(8,128)S(1)} collective-permute-done((f32[8,27,8,128]{3,2,1,0:T(8,128)S(1)}, f32[8,27,8,128]{3,2,1,0:T(8,128)S(1)}, u32[]{:S(2)}, u32[]{:S(2)}) %collective-permute-start.2) | collective-permute-done | bytes 884768 | tf_op jit(solution)/shard_map/ppermute | solution.py:309
  51.4 0.9 copy-done.2
  52.3 1.2 copy-done.1
  53.5 1.2 copy-done.3
  54.7 1.0 pair_add.1
  55.7 8.3 %all-to-all-start.1 = ((f32[8,27,8,128]{3,2,1,0:T(8,128)}), f32[8,27,8,128]{3,2,1,0:T(8,128)S(1)}, u32[]{:S(2)}, u32[]{:S(2)}) async-start(f32[8,27,8,128]{3,2,1,0:T(8,128)} %pair_add.1), calls=%async_computation.1 | async-start | bytes 1769472 | tf_op jit(solution)/shard_map/all_to_all | solution.py:262
  64.0 1.9 %collective-permute-start.5 = (bf16[8,39,8,128]{3,2,1,0:T(8,128)(2,1)S(1)}, bf16[8,39,8,128]{3,2,1,0:T(8,128)(2,1)}, u32[]{:S(2)}, u32[]{:S(2)}) collective-permute-start(bf16[8,39,8,128]{3,2,1,0:T(8,128)(2,1)S(1)} %all-to-all-done.2.mine_ref), channel_id=1, source_target_pairs={{0,1},{1,0},{2,3},{3,2},{4,5},{5,4},{6,7},{7,6},{8,9},{9,8},{10,11... | collective-permute-start | bytes 1916936 | tf_op jit(solution)/shard_map/ppermute | solution.py:299
  65.9 2.2 %collective-permute-done.5.other_ref = bf16[8,39,8,128]{3,2,1,0:T(8,128)(2,1)} collective-permute-done((bf16[8,39,8,128]{3,2,1,0:T(8,128)(2,1)S(1)}, bf16[8,39,8,128]{3,2,1,0:T(8,128)(2,1)}, u32[]{:S(2)}, u32[]{:S(2)}) %collective-permute-start.5) | collective-permute-done | bytes 639008 | tf_op jit(solution)/shard_map/ppermute | solution.py:299
  68.1 2.9 %shard_map.62 = (f32[4,2,2,2,8,128]{5,4,3,2,1,0:T(8,128)S(1)}, f32[4,2,2,2,8,128]{5,4,3,2,1,0:T(8,128)S(1)}, f32[4,2,2,2,8,128]{5,4,3,2,1,0:T(8,128)S(1)}, f32[4,2,2,2,8,128]{5,4,3,2,1,0:T(8,128)S(1)}) custom-call(s32[1]{0:T(128)} %bitcast.p_ref, bf16[16,2,2,4,8,128]{5,4,3,2,1,0:T(8,128)(2,1)S(1)} %all-to-all-done.own_ref, ...), custom_call_target="tpu_custom_call" | custom-call | flops 905969664 | bytes 2588676 | tf_op jit(solution)/shard_map/pallas_call | solution.py:28
  71.0 2.0 %collective-permute-start.6 = (f32[4,2,2,2,8,128]{5,4,3,2,1,0:T(8,128)S(1)}, f32[4,2,2,2,8,128]{5,4,3,2,1,0:T(8,128)S(1)}, u32[]{:S(2)}, u32[]{:S(2)}) collective-permute-start(f32[4,2,2,2,8,128]{5,4,3,2,1,0:T(8,128)S(1)} %get-tuple-element.18), channel_id=1, source_target_pairs={{0,1},{1,0},{2,3},{3,2},{4,5},{5,4},{6,7},{7,6},{8,9},{9,8},{10,11... | collective-permute-start | bytes 393224 | tf_op jit(solution)/shard_map/ppermute | solution.py:331
  73.0 3.9 %collective-permute-start.7 = (f32[4,2,2,2,8,128]{5,4,3,2,1,0:T(8,128)S(1)}, f32[4,2,2,2,8,128]{5,4,3,2,1,0:T(8,128)S(1)}, u32[]{:S(2)}, u32[]{:S(2)}) collective-permute-start(f32[4,2,2,2,8,128]{5,4,3,2,1,0:T(8,128)S(1)} %get-tuple-element.19), channel_id=1, source_target_pairs={{0,8},{8,0},{1,9},{9,1},{2,10},{10,2},{3,11},{11,3},{4,12},{12,4},... | collective-permute-start | bytes 393224 | tf_op jit(solution)/shard_map/ppermute | solution.py:332
  76.9 1.9 %collective-permute-start.8 = (f32[4,2,2,2,8,128]{5,4,3,2,1,0:T(8,128)S(1)}, f32[4,2,2,2,8,128]{5,4,3,2,1,0:T(8,128)S(1)}, u32[]{:S(2)}, u32[]{:S(2)}) collective-permute-start(f32[4,2,2,2,8,128]{5,4,3,2,1,0:T(8,128)S(1)} %get-tuple-element.20), channel_id=1, source_target_pairs={{0,9},{1,8},{8,1},{9,0},{2,11},{3,10},{10,3},{11,2},{4,13},{5,12},... | collective-permute-start | bytes 393224 | tf_op jit(solution)/shard_map/ppermute | solution.py:333
  79.6 9.8 %all-to-all-start.3 = ((f32[32,8,128]{2,1,0:T(8,128)}), f32[32,8,128]{2,1,0:T(8,128)S(1)}, u32[]{:S(2)}, u32[]{:S(2)}) async-start(f32[32,8,128]{2,1,0:T(8,128)} %shard_map.60), calls=%async_computation.3 | async-start | bytes 262144 | tf_op jit(solution)/shard_map/all_to_all | solution.py:262
  89.5 3.6 %collective-permute-start.9 = (f32[4,2,2,2,8,128]{5,4,3,2,1,0:T(8,128)S(1)}, f32[4,2,2,2,8,128]{5,4,3,2,1,0:T(8,128)S(1)}, u32[]{:S(2)}, u32[]{:S(2)}) collective-permute-start(f32[4,2,2,2,8,128]{5,4,3,2,1,0:T(8,128)S(1)} %pad_maximum_fusion.1), channel_id=1, source_target_pairs={{0,2},{2,0},{4,6},{6,4},{1,3},{3,1},{5,7},{7,5},{8,10},{10,8},{12,... | collective-permute-start | bytes 393224 | tf_op jit(solution)/shard_map/ppermute | solution.py:341
  93.2 8.6 %all-to-all-done.3.shares_ref = f32[32,8,128]{2,1,0:T(8,128)S(1)} async-done(((f32[32,8,128]{2,1,0:T(8,128)}), f32[32,8,128]{2,1,0:T(8,128)S(1)}, u32[]{:S(2)}, u32[]{:S(2)}) %all-to-all-start.3) | async-done | bytes 131104 | tf_op jit(solution)/shard_map/all_to_all | solution.py:262
  102.4 4.1 %all-to-all-start.4 = ((f32[32,8,128]{2,1,0:T(8,128)}), f32[32,8,128]{2,1,0:T(8,128)S(1)}, u32[]{:S(2)}, u32[]{:S(2)}) async-start(f32[32,8,128]{2,1,0:T(8,128)} %shard_map.64), calls=%async_computation.4 | async-start | bytes 262144 | tf_op jit(solution)/shard_map/all_to_all | solution.py:262
  106.5 5.3 %collective-permute-start.10 = (f32[4,2,2,2,8,128]{5,4,3,2,1,0:T(8,128)S(1)}, f32[4,2,2,2,8,128]{5,4,3,2,1,0:T(8,128)S(1)}, u32[]{:S(2)}, u32[]{:S(2)}) collective-permute-start(f32[4,2,2,2,8,128]{5,4,3,2,1,0:T(8,128)S(1)} %pad_maximum_fusion.2), channel_id=1, source_target_pairs={{0,4},{2,6},{4,0},{6,2},{1,5},{3,7},{5,1},{7,3},{8,12},{10,14},{12... | collective-permute-start | bytes 393224 | tf_op jit(solution)/shard_map/ppermute | solution.py:341
  111.8 3.1 %collective-permute-start.11 = (f32[4,2,2,2,8,128]{5,4,3,2,1,0:T(8,128)S(1)}, f32[4,2,2,2,8,128]{5,4,3,2,1,0:T(8,128)S(1)}, u32[]{:S(2)}, u32[]{:S(2)}) collective-permute-start(f32[4,2,2,2,8,128]{5,4,3,2,1,0:T(8,128)S(1)} %pad_maximum_fusion.3), channel_id=1, source_target_pairs={{0,6},{2,4},{4,2},{6,0},{1,7},{3,5},{5,3},{7,1},{8,14},{10,12},{12... | collective-permute-start | bytes 393224 | tf_op jit(solution)/shard_map/ppermute | solution.py:341
  114.9 4.9 %collective-permute-done.11.refs_3_ = f32[4,2,2,2,8,128]{5,4,3,2,1,0:T(8,128)S(1)} collective-permute-done((f32[4,2,2,2,8,128]{5,4,3,2,1,0:T(8,128)S(1)}, f32[4,2,2,2,8,128]{5,4,3,2,1,0:T(8,128)S(1)}, u32[]{:S(2)}, u32[]{:S(2)}) %collective-permute-start.11) | collective-permute-done | bytes 131104 | tf_op jit(solution)/shard_map/ppermute | solution.py:341
  (31 shorter events, 4.5 us)
Async XLA Ops:
  2.5 6.4 %copy-start.5 = (bf16[2,32,8,128]{3,2,1,0:T(8,128)(2,1)S(1)}, bf16[2,32,8,128]{3,2,1,0:T(8,128)(2,1)}, u32[]{:S(2)}) copy-start(bf16[2,32,8,128]{3,2,1,0:T(8,128)(2,1)} %g_ref.1) | copy-start | bytes 393220
  2.5 26.5 %all-to-all-start = ((bf16[16,2,2,4,8,128]{5,4,3,2,1,0:T(8,128)(2,1)}), bf16[16,2,2,4,8,128]{5,4,3,2,1,0:T(8,128)(2,1)S(1)}, u32[]{:S(2)}, u32[]{:S(2)}) async-start(bf16[16,2,2,4,8,128]{5,4,3,2,1,0:T(8,128)(2,1)} %shard_map.58), calls=%async_computation | async-start | bytes 1048576 | tf_op jit(solution)/shard_map/all_to_all | solution.py:262
  8.9 13.9 %collective-permute-start.4 = (bf16[32,8,128]{2,1,0:T(8,128)(2,1)S(1)}, bf16[32,8,128]{2,1,0:T(8,128)(2,1)S(1)}, u32[]{:S(2)}, u32[]{:S(2)}) collective-permute-start(bf16[32,8,128]{2,1,0:T(8,128)(2,1)S(1)} %get-tuple-element.45), channel_id=1, source_target_pairs={{16,32},{48,64},{80,96},{112,128},{144,160},{176,192},{208,224},{2... | collective-permute-start | bytes 196616 | tf_op jit(solution)/shard_map/ppermute | solution.py:282
  18.8 8.5 %collective-permute-start.3 = (bf16[32,8,128]{2,1,0:T(8,128)(2,1)S(1)}, bf16[32,8,128]{2,1,0:T(8,128)(2,1)S(1)}, u32[]{:S(2)}, u32[]{:S(2)}) collective-permute-start(bf16[32,8,128]{2,1,0:T(8,128)(2,1)S(1)} %get-tuple-element.46), channel_id=1, source_target_pairs={{0,16},{32,48},{64,80},{96,112},{128,144},{160,176},{192,208},{224... | collective-permute-start | bytes 196616 | tf_op jit(solution)/shard_map/ppermute | solution.py:282
  29.0 26.7 %all-to-all-start.2 = ((bf16[8,39,8,128]{3,2,1,0:T(8,128)(2,1)}), bf16[8,39,8,128]{3,2,1,0:T(8,128)(2,1)S(1)}, u32[]{:S(2)}, u32[]{:S(2)}) async-start(bf16[8,39,8,128]{3,2,1,0:T(8,128)(2,1)} %shard_map.61), calls=%async_computation.2 | async-start | bytes 1277952 | tf_op jit(solution)/shard_map/all_to_all | solution.py:262
  33.5 10.9 %collective-permute-start.1 = (bf16[16,4,8,128]{3,2,1,0:T(8,128)(2,1)S(1)}, bf16[16,4,8,128]{3,2,1,0:T(8,128)(2,1)S(1)}, u32[]{:S(2)}, u32[]{:S(2)}) collective-permute-start(bf16[16,4,8,128]{3,2,1,0:T(8,128)(2,1)S(1)} %get-tuple-element.27), channel_id=1, source_target_pairs={{16,32},{48,64},{80,96},{112,128},{144,160},{176,192},{208,224},{2... | collective-permute-start | bytes 393224 | tf_op jit(solution)/shard_map/ppermute | solution.py:288
  36.4 8.5 %collective-permute-start = (bf16[16,4,8,128]{3,2,1,0:T(8,128)(2,1)S(1)}, bf16[16,4,8,128]{3,2,1,0:T(8,128)(2,1)S(1)}, u32[]{:S(2)}, u32[]{:S(2)}) collective-permute-start(bf16[16,4,8,128]{3,2,1,0:T(8,128)(2,1)S(1)} %get-tuple-element.28), channel_id=1, source_target_pairs={{0,16},{32,48},{64,80},{96,112},{128,144},{160,176},{192,208},{224... | collective-permute-start | bytes 393224 | tf_op jit(solution)/shard_map/ppermute | solution.py:288
  46.2 0.9 copy-start
  47.1 4.3 %collective-permute-start.2 = (f32[8,27,8,128]{3,2,1,0:T(8,128)S(1)}, f32[8,27,8,128]{3,2,1,0:T(8,128)S(1)}, u32[]{:S(2)}, u32[]{:S(2)}) collective-permute-start(f32[8,27,8,128]{3,2,1,0:T(8,128)S(1)} %get-tuple-element.16), channel_id=1, source_target_pairs={{0,1},{1,0},{2,3},{3,2},{4,5},{5,4},{6,7},{7,6},{8,9},{9,8},{10,11... | collective-permute-start | bytes 2654216 | tf_op jit(solution)/shard_map/ppermute | solution.py:309
  51.4 0.9 copy-start.2
  52.3 1.2 copy-start.1
  53.5 1.2 copy-start.3
  55.7 8.3 %copy-start.4 = (bf16[8,39,8,128]{3,2,1,0:T(8,128)(2,1)}, bf16[8,39,8,128]{3,2,1,0:T(8,128)(2,1)S(1)}, u32[]{:S(2)}) copy-start(bf16[8,39,8,128]{3,2,1,0:T(8,128)(2,1)S(1)} %all-to-all-done.2.mine_ref) | copy-start | bytes 1916932
  55.7 23.2 %all-to-all-start.1 = ((f32[8,27,8,128]{3,2,1,0:T(8,128)}), f32[8,27,8,128]{3,2,1,0:T(8,128)S(1)}, u32[]{:S(2)}, u32[]{:S(2)}) async-start(f32[8,27,8,128]{3,2,1,0:T(8,128)} %pair_add.1), calls=%async_computation.1 | async-start | bytes 1769472 | tf_op jit(solution)/shard_map/all_to_all | solution.py:262
  64.0 4.1 %collective-permute-start.5 = (bf16[8,39,8,128]{3,2,1,0:T(8,128)(2,1)S(1)}, bf16[8,39,8,128]{3,2,1,0:T(8,128)(2,1)}, u32[]{:S(2)}, u32[]{:S(2)}) collective-permute-start(bf16[8,39,8,128]{3,2,1,0:T(8,128)(2,1)S(1)} %all-to-all-done.2.mine_ref), channel_id=1, source_target_pairs={{0,1},{1,0},{2,3},{3,2},{4,5},{5,4},{6,7},{7,6},{8,9},{9,8},{10,11... | collective-permute-start | bytes 1916936 | tf_op jit(solution)/shard_map/ppermute | solution.py:299
  71.0 18.5 %collective-permute-start.6 = (f32[4,2,2,2,8,128]{5,4,3,2,1,0:T(8,128)S(1)}, f32[4,2,2,2,8,128]{5,4,3,2,1,0:T(8,128)S(1)}, u32[]{:S(2)}, u32[]{:S(2)}) collective-permute-start(f32[4,2,2,2,8,128]{5,4,3,2,1,0:T(8,128)S(1)} %get-tuple-element.18), channel_id=1, source_target_pairs={{0,1},{1,0},{2,3},{3,2},{4,5},{5,4},{6,7},{7,6},{8,9},{9,8},{10,11... | collective-permute-start | bytes 393224 | tf_op jit(solution)/shard_map/ppermute | solution.py:331
  73.0 16.4 %collective-permute-start.7 = (f32[4,2,2,2,8,128]{5,4,3,2,1,0:T(8,128)S(1)}, f32[4,2,2,2,8,128]{5,4,3,2,1,0:T(8,128)S(1)}, u32[]{:S(2)}, u32[]{:S(2)}) collective-permute-start(f32[4,2,2,2,8,128]{5,4,3,2,1,0:T(8,128)S(1)} %get-tuple-element.19), channel_id=1, source_target_pairs={{0,8},{8,0},{1,9},{9,1},{2,10},{10,2},{3,11},{11,3},{4,12},{12,4},... | collective-permute-start | bytes 393224 | tf_op jit(solution)/shard_map/ppermute | solution.py:332
  76.9 12.5 %collective-permute-start.8 = (f32[4,2,2,2,8,128]{5,4,3,2,1,0:T(8,128)S(1)}, f32[4,2,2,2,8,128]{5,4,3,2,1,0:T(8,128)S(1)}, u32[]{:S(2)}, u32[]{:S(2)}) collective-permute-start(f32[4,2,2,2,8,128]{5,4,3,2,1,0:T(8,128)S(1)} %get-tuple-element.20), channel_id=1, source_target_pairs={{0,9},{1,8},{8,1},{9,0},{2,11},{3,10},{10,3},{11,2},{4,13},{5,12},... | collective-permute-start | bytes 393224 | tf_op jit(solution)/shard_map/ppermute | solution.py:333
  79.6 22.1 %all-to-all-start.3 = ((f32[32,8,128]{2,1,0:T(8,128)}), f32[32,8,128]{2,1,0:T(8,128)S(1)}, u32[]{:S(2)}, u32[]{:S(2)}) async-start(f32[32,8,128]{2,1,0:T(8,128)} %shard_map.60), calls=%async_computation.3 | async-start | bytes 262144 | tf_op jit(solution)/shard_map/all_to_all | solution.py:262
  89.5 25.4 %collective-permute-start.9 = (f32[4,2,2,2,8,128]{5,4,3,2,1,0:T(8,128)S(1)}, f32[4,2,2,2,8,128]{5,4,3,2,1,0:T(8,128)S(1)}, u32[]{:S(2)}, u32[]{:S(2)}) collective-permute-start(f32[4,2,2,2,8,128]{5,4,3,2,1,0:T(8,128)S(1)} %pad_maximum_fusion.1), channel_id=1, source_target_pairs={{0,2},{2,0},{4,6},{6,4},{1,3},{3,1},{5,7},{7,5},{8,10},{10,8},{12,... | collective-permute-start | bytes 393224 | tf_op jit(solution)/shard_map/ppermute | solution.py:341
  102.4 18.3 %all-to-all-start.4 = ((f32[32,8,128]{2,1,0:T(8,128)}), f32[32,8,128]{2,1,0:T(8,128)S(1)}, u32[]{:S(2)}, u32[]{:S(2)}) async-start(f32[32,8,128]{2,1,0:T(8,128)} %shard_map.64), calls=%async_computation.4 | async-start | bytes 262144 | tf_op jit(solution)/shard_map/all_to_all | solution.py:262
  106.5 8.4 %collective-permute-start.10 = (f32[4,2,2,2,8,128]{5,4,3,2,1,0:T(8,128)S(1)}, f32[4,2,2,2,8,128]{5,4,3,2,1,0:T(8,128)S(1)}, u32[]{:S(2)}, u32[]{:S(2)}) collective-permute-start(f32[4,2,2,2,8,128]{5,4,3,2,1,0:T(8,128)S(1)} %pad_maximum_fusion.2), channel_id=1, source_target_pairs={{0,4},{2,6},{4,0},{6,2},{1,5},{3,7},{5,1},{7,3},{8,12},{10,14},{12... | collective-permute-start | bytes 393224 | tf_op jit(solution)/shard_map/ppermute | solution.py:341
  111.8 8.1 %collective-permute-start.11 = (f32[4,2,2,2,8,128]{5,4,3,2,1,0:T(8,128)S(1)}, f32[4,2,2,2,8,128]{5,4,3,2,1,0:T(8,128)S(1)}, u32[]{:S(2)}, u32[]{:S(2)}) collective-permute-start(f32[4,2,2,2,8,128]{5,4,3,2,1,0:T(8,128)S(1)} %pad_maximum_fusion.3), channel_id=1, source_target_pairs={{0,6},{2,4},{4,2},{6,0},{1,7},{3,5},{5,3},{7,1},{8,14},{10,12},{12... | collective-permute-start | bytes 393224 | tf_op jit(solution)/shard_map/ppermute | solution.py:341

commit v10 on v8

--- a/solution.py
+++ b/solution.py
@@ -316,11 +316,12 @@
         lax.ppermute(near[3], ("zl", "core"), [(i, 3 - i) for i in range(4)]),
     )
     shares = swap_all(padded, SPACE)
-    _, near = lax.optimization_barrier((shares, near))
+    _, near = lax.optimization_barrier((padded, near))
     (tap,) = call(functools.partial(space_add_kernel, norm=norm), [pltpu.VMEM((ns, cg, ch), F32)], [near_core(shares)])
     taps = swap_all(tap, SPACE)
-    blocks = {j: jnp.stack([part[j] for part in near]) for j in (2, 1, 3, 0)}
-    blocks = {j: lax.ppermute(b, "x", [(i, i ^ j) for i in range(4)]) if j else b for j, b in blocks.items()}
+    blocks = {j: jnp.stack([part[j] for part in near]) for j in range(4)}
+    for j in (2, 1, 3):
+        blocks[j] = lax.ppermute(blocks[j], "x", [(i, i ^ j) for i in range(4)])
     output, grad_in = call(
         place_kernel, [sds((nz, rows, cg, w), F32)] * 2, [index] + [near_core(blocks[j]) for j in range(4)], smem=1
     )

time: 130 us -> 118 us (0.908)
  the two profiles are of different devices: /device:TPU:6 before, /device:TPU:8 now
where the time goes in v10:
time: 118 us; the launch traced here: 117 us
  starting transfers between devices  76.3 us (65%)
  waiting for transfers between devices  28.2 us (24%)
  Pallas kernels  10 us (8%)
    all_to_all x5, starting transfers between devices, swap_all(): return lax.all_to_all(array, axes, 0, 0, tiled=True)  33 us
    ppermute x2, starting transfers between devices, step(): lax.ppermute(lax.dynamic_slice(grad_out, (side, 0, 0, 0), (1, rows, cg, w...  12.5 us
    ppermute x3, starting transfers between devices, step(): blocks[j] = lax.ppermute(blocks[j], 'x', [(i, i ^ j) for i in range(4)])  12 us
    pallas_call x7, Pallas kernels, call(): pl.pallas_call(kernel, out_shape=outs[0] if one else tuple(outs), in_spec...  10 us
    all_to_all x5, waiting for transfers between devices, swap_all(): return lax.all_to_all(array, axes, 0, 0, tiled=True)  8.57 us
    ppermute x2, starting transfers between devices, step(): lax.ppermute(lax.dynamic_slice(own, (0, 0, side, 0, 0, 0), (n, 1, 1, nr,...  7.17 us
    ppermute x2, waiting for transfers between devices, step(): lax.ppermute(lax.dynamic_slice(grad_out, (side, 0, 0, 0), (1, rows, cg, w...  5.87 us
    ppermute x3, waiting for transfers between devices, step(): blocks[j] = lax.ppermute(blocks[j], 'x', [(i, i ^ j) for i in range(4)])  4.95 us
  transfers between devices with their start and end apart: 17, of which 8 were waited for; matrix products, arithmetic and copies ran while one was open for 1% of the time, Pallas kernels for 7%

profile of v10, /device:TPU:8, one launch (start us, length us, event | category | flops | bytes accessed | tf_op | source)
XLA Modules:
  0.0 117.2 jit_solution(17193996477350694984)
XLA Ops:
  0.6 1.9 %shard_map.58 = bf16[16,2,2,4,8,128]{5,4,3,2,1,0:T(8,128)(2,1)} custom-call(bf16[2,32,8,128]{3,2,1,0:T(8,128)(2,1)} %x_ref.1, bf16[2,32,8,128]{3,2,1,0:T(8,128)(2,1)} %g_ref.1), custom_call_target="tpu_custom_call" | custom-call | bytes 1310720 | tf_op jit(solution)/shard_map/pallas_call | solution.py:28
  2.5 6.3 %all-to-all-start = ((bf16[16,2,2,4,8,128]{5,4,3,2,1,0:T(8,128)(2,1)}), bf16[16,2,2,4,8,128]{5,4,3,2,1,0:T(8,128)(2,1)S(1)}, u32[]{:S(2)}, u32[]{:S(2)}) async-start(bf16[16,2,2,4,8,128]{5,4,3,2,1,0:T(8,128)(2,1)} %shard_map.58), calls=%async_computation | async-start | bytes 1048576 | tf_op jit(solution)/shard_map/all_to_all | solution.py:252
  8.9 9.9 %collective-permute-start.4 = (bf16[32,8,128]{2,1,0:T(8,128)(2,1)S(1)}, bf16[32,8,128]{2,1,0:T(8,128)(2,1)S(1)}, u32[]{:S(2)}, u32[]{:S(2)}) collective-permute-start(bf16[32,8,128]{2,1,0:T(8,128)(2,1)S(1)} %get-tuple-element.45), channel_id=1, source_target_pairs={{16,32},{48,64},{80,96},{112,128},{144,160},{176,192},{208,224},{2... | collective-permute-start | bytes 196616 | tf_op jit(solution)/shard_map/ppermute | solution.py:272
  18.8 2.6 %collective-permute-start.3 = (bf16[32,8,128]{2,1,0:T(8,128)(2,1)S(1)}, bf16[32,8,128]{2,1,0:T(8,128)(2,1)S(1)}, u32[]{:S(2)}, u32[]{:S(2)}) collective-permute-start(bf16[32,8,128]{2,1,0:T(8,128)(2,1)S(1)} %get-tuple-element.46), channel_id=1, source_target_pairs={{0,16},{32,48},{64,80},{96,112},{128,144},{160,176},{192,208},{224... | collective-permute-start | bytes 196616 | tf_op jit(solution)/shard_map/ppermute | solution.py:272
  21.4 1.3 %collective-permute-done.4.odd_ref = bf16[32,8,128]{2,1,0:T(8,128)(2,1)S(1)} collective-permute-done((bf16[32,8,128]{2,1,0:T(8,128)(2,1)S(1)}, bf16[32,8,128]{2,1,0:T(8,128)(2,1)S(1)}, u32[]{:S(2)}, u32[]{:S(2)}) %collective-permute-start.4) | collective-permute-done | bytes 65568 | tf_op jit(solution)/shard_map/ppermute | solution.py:272
  22.8 4.5 %collective-permute-done.3.even_ref = bf16[32,8,128]{2,1,0:T(8,128)(2,1)S(1)} collective-permute-done((bf16[32,8,128]{2,1,0:T(8,128)(2,1)S(1)}, bf16[32,8,128]{2,1,0:T(8,128)(2,1)S(1)}, u32[]{:S(2)}, u32[]{:S(2)}) %collective-permute-start.3) | collective-permute-done | bytes 65568 | tf_op jit(solution)/shard_map/ppermute | solution.py:272
  27.3 1.8 %shard_map.61 = bf16[8,39,8,128]{3,2,1,0:T(8,128)(2,1)} custom-call(s32[1]{0:T(128)} %bitcast.p_ref, bf16[27,8,128]{2,1,0:T(8,128)(2,1)} %bitcast.16, bf16[32,8,128]{2,1,0:T(8,128)(2,1)S(1)} %collective-permute-done.3.even_ref, bf16[32,8,128]{2,1,0:T(8,128)(2,1)S(1)} %collective-permute-done.4.odd_ref), custom_call_target="tpu_custom_call" | custom-call | bytes 1464324 | tf_op jit(solution)/shard_map/pallas_call | solution.py:28
  29.0 4.5 %all-to-all-start.2 = ((bf16[8,39,8,128]{3,2,1,0:T(8,128)(2,1)}), bf16[8,39,8,128]{3,2,1,0:T(8,128)(2,1)S(1)}, u32[]{:S(2)}, u32[]{:S(2)}) async-start(bf16[8,39,8,128]{3,2,1,0:T(8,128)(2,1)} %shard_map.61), calls=%async_computation.2 | async-start | bytes 1277952 | tf_op jit(solution)/shard_map/all_to_all | solution.py:252
  33.5 2.9 %collective-permute-start.1 = (bf16[16,4,8,128]{3,2,1,0:T(8,128)(2,1)S(1)}, bf16[16,4,8,128]{3,2,1,0:T(8,128)(2,1)S(1)}, u32[]{:S(2)}, u32[]{:S(2)}) collective-permute-start(bf16[16,4,8,128]{3,2,1,0:T(8,128)(2,1)S(1)} %get-tuple-element.27), channel_id=1, source_target_pairs={{16,32},{48,64},{80,96},{112,128},{144,160},{176,192},{208,224},{2... | collective-permute-start | bytes 393224 | tf_op jit(solution)/shard_map/ppermute | solution.py:278
  36.4 4.3 %collective-permute-start = (bf16[16,4,8,128]{3,2,1,0:T(8,128)(2,1)S(1)}, bf16[16,4,8,128]{3,2,1,0:T(8,128)(2,1)S(1)}, u32[]{:S(2)}, u32[]{:S(2)}) collective-permute-start(bf16[16,4,8,128]{3,2,1,0:T(8,128)(2,1)S(1)} %get-tuple-element.28), channel_id=1, source_target_pairs={{0,16},{32,48},{64,80},{96,112},{128,144},{160,176},{192,208},{224... | collective-permute-start | bytes 393224 | tf_op jit(solution)/shard_map/ppermute | solution.py:278
  40.7 3.7 %collective-permute-done.1.odd_ref = bf16[16,4,8,128]{3,2,1,0:T(8,128)(2,1)S(1)} collective-permute-done((bf16[16,4,8,128]{3,2,1,0:T(8,128)(2,1)S(1)}, bf16[16,4,8,128]{3,2,1,0:T(8,128)(2,1)S(1)}, u32[]{:S(2)}, u32[]{:S(2)}) %collective-permute-start.1) | collective-permute-done | bytes 131104 | tf_op jit(solution)/shard_map/ppermute | solution.py:278
  45.0 1.3 %shard_map.59 = (f32[8,27,8,128]{3,2,1,0:T(8,128)S(1)}, f32[8,27,8,128]{3,2,1,0:T(8,128)S(1)}) custom-call(s32[1]{0:T(128)} %bitcast.p_ref, bf16[16,2,2,4,8,128]{5,4,3,2,1,0:T(8,128)(2,1)S(1)} %all-to-all-done.own_ref, bf16[16,4,8,128]{3,2,1,0:T(8,128)(2,1)S(1)} %collective-permute-done.even_ref, bf16[16,4,8,128]{3,2,1,0:T(8,128)(2,1)S(1)} %collective-permute-done.1.odd_ref), custom_call_target="tpu_custom_call" | custom-call | flops 452984832 | bytes 2555908 | tf_op jit(solution)/shard_map/pallas_call | solution.py:28
  46.3 1.9 %collective-permute-start.2 = (f32[8,27,8,128]{3,2,1,0:T(8,128)S(1)}, f32[8,27,8,128]{3,2,1,0:T(8,128)S(1)}, u32[]{:S(2)}, u32[]{:S(2)}) collective-permute-start(f32[8,27,8,128]{3,2,1,0:T(8,128)S(1)} %get-tuple-element.16), channel_id=1, source_target_pairs={{0,1},{1,0},{2,3},{3,2},{4,5},{5,4},{6,7},{7,6},{8,9},{9,8},{10,11... | collective-permute-start | bytes 2654216 | tf_op jit(solution)/shard_map/ppermute | solution.py:299
  48.2 2.4 %collective-permute-done.2 = f32[8,27,8,128]{3,2,1,0:T(8,128)S(1)} collective-permute-done((f32[8,27,8,128]{3,2,1,0:T(8,128)S(1)}, f32[8,27,8,128]{3,2,1,0:T(8,128)S(1)}, u32[]{:S(2)}, u32[]{:S(2)}) %collective-permute-start.2) | collective-permute-done | bytes 884768 | tf_op jit(solution)/shard_map/ppermute | solution.py:299
  50.6 1.0 add.34
  51.6 8.2 %all-to-all-start.1 = ((f32[8,27,8,128]{3,2,1,0:T(8,128)}), f32[8,27,8,128]{3,2,1,0:T(8,128)S(1)}, u32[]{:S(2)}, u32[]{:S(2)}) async-start(f32[8,27,8,128]{3,2,1,0:T(8,128)} %add.34), calls=%async_computation.1 | async-start | bytes 1769472 | tf_op jit(solution)/shard_map/all_to_all | solution.py:252
  59.9 1.9 %collective-permute-start.5 = (bf16[8,39,8,128]{3,2,1,0:T(8,128)(2,1)S(1)}, bf16[8,39,8,128]{3,2,1,0:T(8,128)(2,1)}, u32[]{:S(2)}, u32[]{:S(2)}) collective-permute-start(bf16[8,39,8,128]{3,2,1,0:T(8,128)(2,1)S(1)} %all-to-all-done.2.mine_ref), channel_id=1, source_target_pairs={{0,1},{1,0},{2,3},{3,2},{4,5},{5,4},{6,7},{7,6},{8,9},{9,8},{10,11... | collective-permute-start | bytes 1916936 | tf_op jit(solution)/shard_map/ppermute | solution.py:289
  61.8 2.2 %collective-permute-done.5.other_ref = bf16[8,39,8,128]{3,2,1,0:T(8,128)(2,1)} collective-permute-done((bf16[8,39,8,128]{3,2,1,0:T(8,128)(2,1)S(1)}, bf16[8,39,8,128]{3,2,1,0:T(8,128)(2,1)}, u32[]{:S(2)}, u32[]{:S(2)}) %collective-permute-start.5) | collective-permute-done | bytes 639008 | tf_op jit(solution)/shard_map/ppermute | solution.py:289
  64.0 2.9 %shard_map.62 = (f32[4,2,2,2,8,128]{5,4,3,2,1,0:T(8,128)S(1)}, f32[4,2,2,2,8,128]{5,4,3,2,1,0:T(8,128)S(1)}, f32[4,2,2,2,8,128]{5,4,3,2,1,0:T(8,128)S(1)}, f32[4,2,2,2,8,128]{5,4,3,2,1,0:T(8,128)S(1)}) custom-call(s32[1]{0:T(128)} %bitcast.p_ref, bf16[16,2,2,4,8,128]{5,4,3,2,1,0:T(8,128)(2,1)S(1)} %all-to-all-done.own_ref, ...), custom_call_target="tpu_custom_call" | custom-call | flops 905969664 | bytes 2588676 | tf_op jit(solution)/shard_map/pallas_call | solution.py:28
  66.8 2.0 %collective-permute-start.6 = (f32[4,2,2,2,8,128]{5,4,3,2,1,0:T(8,128)S(1)}, f32[4,2,2,2,8,128]{5,4,3,2,1,0:T(8,128)S(1)}, u32[]{:S(2)}, u32[]{:S(2)}) collective-permute-start(f32[4,2,2,2,8,128]{5,4,3,2,1,0:T(8,128)S(1)} %get-tuple-element.18), channel_id=1, source_target_pairs={{0,1},{1,0},{2,3},{3,2},{4,5},{5,4},{6,7},{7,6},{8,9},{9,8},{10,11... | collective-permute-start | bytes 393224 | tf_op jit(solution)/shard_map/ppermute | solution.py:314
  68.9 3.9 %collective-permute-start.7 = (f32[4,2,2,2,8,128]{5,4,3,2,1,0:T(8,128)S(1)}, f32[4,2,2,2,8,128]{5,4,3,2,1,0:T(8,128)S(1)}, u32[]{:S(2)}, u32[]{:S(2)}) collective-permute-start(f32[4,2,2,2,8,128]{5,4,3,2,1,0:T(8,128)S(1)} %get-tuple-element.19), channel_id=1, source_target_pairs={{0,8},{8,0},{1,9},{9,1},{2,10},{10,2},{3,11},{11,3},{4,12},{12,4},... | collective-permute-start | bytes 393224 | tf_op jit(solution)/shard_map/ppermute | solution.py:315
  72.8 1.9 %collective-permute-start.8 = (f32[4,2,2,2,8,128]{5,4,3,2,1,0:T(8,128)S(1)}, f32[4,2,2,2,8,128]{5,4,3,2,1,0:T(8,128)S(1)}, u32[]{:S(2)}, u32[]{:S(2)}) collective-permute-start(f32[4,2,2,2,8,128]{5,4,3,2,1,0:T(8,128)S(1)} %get-tuple-element.20), channel_id=1, source_target_pairs={{0,9},{1,8},{8,1},{9,0},{2,11},{3,10},{10,3},{11,2},{4,13},{5,12},... | collective-permute-start | bytes 393224 | tf_op jit(solution)/shard_map/ppermute | solution.py:316
  74.8 0.7 shard_map.60
  75.5 9.8 %all-to-all-start.3 = ((f32[32,8,128]{2,1,0:T(8,128)}), f32[32,8,128]{2,1,0:T(8,128)S(1)}, u32[]{:S(2)}, u32[]{:S(2)}) async-start(f32[32,8,128]{2,1,0:T(8,128)} %shard_map.60), calls=%async_computation.3 | async-start | bytes 262144 | tf_op jit(solution)/shard_map/all_to_all | solution.py:252
  85.4 3.6 %collective-permute-start.9 = (f32[4,2,2,2,8,128]{5,4,3,2,1,0:T(8,128)S(1)}, f32[4,2,2,2,8,128]{5,4,3,2,1,0:T(8,128)S(1)}, u32[]{:S(2)}, u32[]{:S(2)}) collective-permute-start(f32[4,2,2,2,8,128]{5,4,3,2,1,0:T(8,128)S(1)} %pad_maximum_fusion.1), channel_id=1, source_target_pairs={{0,2},{2,0},{4,6},{6,4},{1,3},{3,1},{5,7},{7,5},{8,10},{10,8},{12,... | collective-permute-start | bytes 393224 | tf_op jit(solution)/shard_map/ppermute | solution.py:324
  89.0 8.6 %all-to-all-done.3.shares_ref = f32[32,8,128]{2,1,0:T(8,128)S(1)} async-done(((f32[32,8,128]{2,1,0:T(8,128)}), f32[32,8,128]{2,1,0:T(8,128)S(1)}, u32[]{:S(2)}, u32[]{:S(2)}) %all-to-all-start.3) | async-done | bytes 131104 | tf_op jit(solution)/shard_map/all_to_all | solution.py:252
  97.6 0.7 shard_map.64
  98.3 4.1 %all-to-all-start.4 = ((f32[32,8,128]{2,1,0:T(8,128)}), f32[32,8,128]{2,1,0:T(8,128)S(1)}, u32[]{:S(2)}, u32[]{:S(2)}) async-start(f32[32,8,128]{2,1,0:T(8,128)} %shard_map.64), calls=%async_computation.4 | async-start | bytes 262144 | tf_op jit(solution)/shard_map/all_to_all | solution.py:252
  102.4 5.3 %collective-permute-start.10 = (f32[4,2,2,2,8,128]{5,4,3,2,1,0:T(8,128)S(1)}, f32[4,2,2,2,8,128]{5,4,3,2,1,0:T(8,128)S(1)}, u32[]{:S(2)}, u32[]{:S(2)}) collective-permute-start(f32[4,2,2,2,8,128]{5,4,3,2,1,0:T(8,128)S(1)} %pad_maximum_fusion.2), channel_id=1, source_target_pairs={{0,4},{2,6},{4,0},{6,2},{1,5},{3,7},{5,1},{7,3},{8,12},{10,14},{12... | collective-permute-start | bytes 393224 | tf_op jit(solution)/shard_map/ppermute | solution.py:324
  107.7 3.1 %collective-permute-start.11 = (f32[4,2,2,2,8,128]{5,4,3,2,1,0:T(8,128)S(1)}, f32[4,2,2,2,8,128]{5,4,3,2,1,0:T(8,128)S(1)}, u32[]{:S(2)}, u32[]{:S(2)}) collective-permute-start(f32[4,2,2,2,8,128]{5,4,3,2,1,0:T(8,128)S(1)} %pad_maximum_fusion.3), channel_id=1, source_target_pairs={{0,6},{2,4},{4,2},{6,0},{1,7},{3,5},{5,3},{7,1},{8,14},{10,12},{12... | collective-permute-start | bytes 393224 | tf_op jit(solution)/shard_map/ppermute | solution.py:324
  110.8 4.9 %collective-permute-done.11.refs_3_ = f32[4,2,2,2,8,128]{5,4,3,2,1,0:T(8,128)S(1)} collective-permute-done((f32[4,2,2,2,8,128]{5,4,3,2,1,0:T(8,128)S(1)}, f32[4,2,2,2,8,128]{5,4,3,2,1,0:T(8,128)S(1)}, u32[]{:S(2)}, u32[]{:S(2)}) %collective-permute-start.11) | collective-permute-done | bytes 131104 | tf_op jit(solution)/shard_map/ppermute | solution.py:324
  115.7 0.8 shard_map.63
  (23 shorter events, 1.3 us)
Async XLA Ops:
  2.5 6.4 %copy-start.1 = (bf16[2,32,8,128]{3,2,1,0:T(8,128)(2,1)S(1)}, bf16[2,32,8,128]{3,2,1,0:T(8,128)(2,1)}, u32[]{:S(2)}) copy-start(bf16[2,32,8,128]{3,2,1,0:T(8,128)(2,1)} %g_ref.1) | copy-start | bytes 393220
  2.5 26.5 %all-to-all-start = ((bf16[16,2,2,4,8,128]{5,4,3,2,1,0:T(8,128)(2,1)}), bf16[16,2,2,4,8,128]{5,4,3,2,1,0:T(8,128)(2,1)S(1)}, u32[]{:S(2)}, u32[]{:S(2)}) async-start(bf16[16,2,2,4,8,128]{5,4,3,2,1,0:T(8,128)(2,1)} %shard_map.58), calls=%async_computation | async-start | bytes 1048576 | tf_op jit(solution)/shard_map/all_to_all | solution.py:252
  8.9 13.9 %collective-permute-start.4 = (bf16[32,8,128]{2,1,0:T(8,128)(2,1)S(1)}, bf16[32,8,128]{2,1,0:T(8,128)(2,1)S(1)}, u32[]{:S(2)}, u32[]{:S(2)}) collective-permute-start(bf16[32,8,128]{2,1,0:T(8,128)(2,1)S(1)} %get-tuple-element.45), channel_id=1, source_target_pairs={{16,32},{48,64},{80,96},{112,128},{144,160},{176,192},{208,224},{2... | collective-permute-start | bytes 196616 | tf_op jit(solution)/shard_map/ppermute | solution.py:272
  18.8 8.5 %collective-permute-start.3 = (bf16[32,8,128]{2,1,0:T(8,128)(2,1)S(1)}, bf16[32,8,128]{2,1,0:T(8,128)(2,1)S(1)}, u32[]{:S(2)}, u32[]{:S(2)}) collective-permute-start(bf16[32,8,128]{2,1,0:T(8,128)(2,1)S(1)} %get-tuple-element.46), channel_id=1, source_target_pairs={{0,16},{32,48},{64,80},{96,112},{128,144},{160,176},{192,208},{224... | collective-permute-start | bytes 196616 | tf_op jit(solution)/shard_map/ppermute | solution.py:272
  29.0 22.6 %all-to-all-start.2 = ((bf16[8,39,8,128]{3,2,1,0:T(8,128)(2,1)}), bf16[8,39,8,128]{3,2,1,0:T(8,128)(2,1)S(1)}, u32[]{:S(2)}, u32[]{:S(2)}) async-start(bf16[8,39,8,128]{3,2,1,0:T(8,128)(2,1)} %shard_map.61), calls=%async_computation.2 | async-start | bytes 1277952 | tf_op jit(solution)/shard_map/all_to_all | solution.py:252
  33.5 10.9 %collective-permute-start.1 = (bf16[16,4,8,128]{3,2,1,0:T(8,128)(2,1)S(1)}, bf16[16,4,8,128]{3,2,1,0:T(8,128)(2,1)S(1)}, u32[]{:S(2)}, u32[]{:S(2)}) collective-permute-start(bf16[16,4,8,128]{3,2,1,0:T(8,128)(2,1)S(1)} %get-tuple-element.27), channel_id=1, source_target_pairs={{16,32},{48,64},{80,96},{112,128},{144,160},{176,192},{208,224},{2... | collective-permute-start | bytes 393224 | tf_op jit(solution)/shard_map/ppermute | solution.py:278
  36.4 8.5 %collective-permute-start = (bf16[16,4,8,128]{3,2,1,0:T(8,128)(2,1)S(1)}, bf16[16,4,8,128]{3,2,1,0:T(8,128)(2,1)S(1)}, u32[]{:S(2)}, u32[]{:S(2)}) collective-permute-start(bf16[16,4,8,128]{3,2,1,0:T(8,128)(2,1)S(1)} %get-tuple-element.28), channel_id=1, source_target_pairs={{0,16},{32,48},{64,80},{96,112},{128,144},{160,176},{192,208},{224... | collective-permute-start | bytes 393224 | tf_op jit(solution)/shard_map/ppermute | solution.py:278
  46.3 4.3 %collective-permute-start.2 = (f32[8,27,8,128]{3,2,1,0:T(8,128)S(1)}, f32[8,27,8,128]{3,2,1,0:T(8,128)S(1)}, u32[]{:S(2)}, u32[]{:S(2)}) collective-permute-start(f32[8,27,8,128]{3,2,1,0:T(8,128)S(1)} %get-tuple-element.16), channel_id=1, source_target_pairs={{0,1},{1,0},{2,3},{3,2},{4,5},{5,4},{6,7},{7,6},{8,9},{9,8},{10,11... | collective-permute-start | bytes 2654216 | tf_op jit(solution)/shard_map/ppermute | solution.py:299
  51.6 8.3 %copy-start = (bf16[8,39,8,128]{3,2,1,0:T(8,128)(2,1)}, bf16[8,39,8,128]{3,2,1,0:T(8,128)(2,1)S(1)}, u32[]{:S(2)}) copy-start(bf16[8,39,8,128]{3,2,1,0:T(8,128)(2,1)S(1)} %all-to-all-done.2.mine_ref) | copy-start | bytes 1916932
  51.6 23.2 %all-to-all-start.1 = ((f32[8,27,8,128]{3,2,1,0:T(8,128)}), f32[8,27,8,128]{3,2,1,0:T(8,128)S(1)}, u32[]{:S(2)}, u32[]{:S(2)}) async-start(f32[8,27,8,128]{3,2,1,0:T(8,128)} %add.34), calls=%async_computation.1 | async-start | bytes 1769472 | tf_op jit(solution)/shard_map/all_to_all | solution.py:252
  59.9 4.1 %collective-permute-start.5 = (bf16[8,39,8,128]{3,2,1,0:T(8,128)(2,1)S(1)}, bf16[8,39,8,128]{3,2,1,0:T(8,128)(2,1)}, u32[]{:S(2)}, u32[]{:S(2)}) collective-permute-start(bf16[8,39,8,128]{3,2,1,0:T(8,128)(2,1)S(1)} %all-to-all-done.2.mine_ref), channel_id=1, source_target_pairs={{0,1},{1,0},{2,3},{3,2},{4,5},{5,4},{6,7},{7,6},{8,9},{9,8},{10,11... | collective-permute-start | bytes 1916936 | tf_op jit(solution)/shard_map/ppermute | solution.py:289
  66.8 18.5 %collective-permute-start.6 = (f32[4,2,2,2,8,128]{5,4,3,2,1,0:T(8,128)S(1)}, f32[4,2,2,2,8,128]{5,4,3,2,1,0:T(8,128)S(1)}, u32[]{:S(2)}, u32[]{:S(2)}) collective-permute-start(f32[4,2,2,2,8,128]{5,4,3,2,1,0:T(8,128)S(1)} %get-tuple-element.18), channel_id=1, source_target_pairs={{0,1},{1,0},{2,3},{3,2},{4,5},{5,4},{6,7},{7,6},{8,9},{9,8},{10,11... | collective-permute-start | bytes 393224 | tf_op jit(solution)/shard_map/ppermute | solution.py:314
  68.9 16.4 %collective-permute-start.7 = (f32[4,2,2,2,8,128]{5,4,3,2,1,0:T(8,128)S(1)}, f32[4,2,2,2,8,128]{5,4,3,2,1,0:T(8,128)S(1)}, u32[]{:S(2)}, u32[]{:S(2)}) collective-permute-start(f32[4,2,2,2,8,128]{5,4,3,2,1,0:T(8,128)S(1)} %get-tuple-element.19), channel_id=1, source_target_pairs={{0,8},{8,0},{1,9},{9,1},{2,10},{10,2},{3,11},{11,3},{4,12},{12,4},... | collective-permute-start | bytes 393224 | tf_op jit(solution)/shard_map/ppermute | solution.py:315
  72.8 12.5 %collective-permute-start.8 = (f32[4,2,2,2,8,128]{5,4,3,2,1,0:T(8,128)S(1)}, f32[4,2,2,2,8,128]{5,4,3,2,1,0:T(8,128)S(1)}, u32[]{:S(2)}, u32[]{:S(2)}) collective-permute-start(f32[4,2,2,2,8,128]{5,4,3,2,1,0:T(8,128)S(1)} %get-tuple-element.20), channel_id=1, source_target_pairs={{0,9},{1,8},{8,1},{9,0},{2,11},{3,10},{10,3},{11,2},{4,13},{5,12},... | collective-permute-start | bytes 393224 | tf_op jit(solution)/shard_map/ppermute | solution.py:316
  75.5 22.1 %all-to-all-start.3 = ((f32[32,8,128]{2,1,0:T(8,128)}), f32[32,8,128]{2,1,0:T(8,128)S(1)}, u32[]{:S(2)}, u32[]{:S(2)}) async-start(f32[32,8,128]{2,1,0:T(8,128)} %shard_map.60), calls=%async_computation.3 | async-start | bytes 262144 | tf_op jit(solution)/shard_map/all_to_all | solution.py:252
  85.4 25.4 %collective-permute-start.9 = (f32[4,2,2,2,8,128]{5,4,3,2,1,0:T(8,128)S(1)}, f32[4,2,2,2,8,128]{5,4,3,2,1,0:T(8,128)S(1)}, u32[]{:S(2)}, u32[]{:S(2)}) collective-permute-start(f32[4,2,2,2,8,128]{5,4,3,2,1,0:T(8,128)S(1)} %pad_maximum_fusion.1), channel_id=1, source_target_pairs={{0,2},{2,0},{4,6},{6,4},{1,3},{3,1},{5,7},{7,5},{8,10},{10,8},{12,... | collective-permute-start | bytes 393224 | tf_op jit(solution)/shard_map/ppermute | solution.py:324
  98.3 18.3 %all-to-all-start.4 = ((f32[32,8,128]{2,1,0:T(8,128)}), f32[32,8,128]{2,1,0:T(8,128)S(1)}, u32[]{:S(2)}, u32[]{:S(2)}) async-start(f32[32,8,128]{2,1,0:T(8,128)} %shard_map.64), calls=%async_computation.4 | async-start | bytes 262144 | tf_op jit(solution)/shard_map/all_to_all | solution.py:252
  102.4 8.4 %collective-permute-start.10 = (f32[4,2,2,2,8,128]{5,4,3,2,1,0:T(8,128)S(1)}, f32[4,2,2,2,8,128]{5,4,3,2,1,0:T(8,128)S(1)}, u32[]{:S(2)}, u32[]{:S(2)}) collective-permute-start(f32[4,2,2,2,8,128]{5,4,3,2,1,0:T(8,128)S(1)} %pad_maximum_fusion.2), channel_id=1, source_target_pairs={{0,4},{2,6},{4,0},{6,2},{1,5},{3,7},{5,1},{7,3},{8,12},{10,14},{12... | collective-permute-start | bytes 393224 | tf_op jit(solution)/shard_map/ppermute | solution.py:324
  107.7 8.1 %collective-permute-start.11 = (f32[4,2,2,2,8,128]{5,4,3,2,1,0:T(8,128)S(1)}, f32[4,2,2,2,8,128]{5,4,3,2,1,0:T(8,128)S(1)}, u32[]{:S(2)}, u32[]{:S(2)}) collective-permute-start(f32[4,2,2,2,8,128]{5,4,3,2,1,0:T(8,128)S(1)} %pad_maximum_fusion.3), channel_id=1, source_target_pairs={{0,6},{2,4},{4,2},{6,0},{1,7},{3,5},{5,3},{7,1},{8,14},{10,12},{12... | collective-permute-start | bytes 393224 | tf_op jit(solution)/shard_map/ppermute | solution.py:324

commit v11 on v10

--- a/solution.py
+++ b/solution.py
@@ -20,11 +20,14 @@
     return [pl.BlockSpec(memory_space=pltpu.VMEM)] * n
 
 
-def call(kernel, outs, ins, scratch=(), smem=0, flops=0):
+def call(kernel, outs, ins, scratch=(), smem=0, flops=0, copied=0):
     specs = [pl.BlockSpec(memory_space=pltpu.SMEM)] * smem + vmem_specs(len(ins) - smem)
     moved = sum(a.size * a.dtype.itemsize for a in ins) + sum(math.prod(o.shape) * 4 for o in outs)
     one = len(outs) == 1
     out_specs = vmem_specs(len(outs))
+    if copied:
+        out_specs = [pl.BlockSpec(memory_space=pl.ANY)]
+        scratch = [pltpu.VMEM(outs[0].shape, outs[0].dtype), pltpu.SemaphoreType.DMA((copied,))]
     result = pl.pallas_call(
         kernel,
         out_shape=outs[0] if one else tuple(outs),
@@ -48,16 +51,20 @@
     return (index >> 4) & 1 == 1
 
 
-def pack_kernel(x_ref, g_ref, o_ref):
+def pack_kernel(x_ref, g_ref, out_ref, o_ref, sems):
     n, _, nz, nr = o_ref.shape[:4]
     rows = x_ref.shape[1]
     zero = jnp.zeros(x_ref.shape[2:], x_ref.dtype)
-    for k, ref in enumerate((x_ref, g_ref)):
-        for z in range(nz):
-            for d in range(n):
+    copies = [pltpu.make_async_copy(o_ref.at[d], out_ref.at[d], sems.at[d]) for d in range(n)]
+    for d in range(n):
+        for k, ref in enumerate((x_ref, g_ref)):
+            for z in range(nz):
                 for r in range(nr):
                     h = d * (nr - 2) + r - 1
                     o_ref[d, k, z, r] = ref[z, h] if 0 <= h < rows else zero
+        copies[d].start()
+    for copy in copies:
+        copy.wait()
 
 
 def halo_pick(index):
@@ -70,13 +77,14 @@
     return pick
 
 
-def pack_more_kernel(p_ref, w_ref, even_ref, odd_ref, o_ref):
+def pack_more_kernel(p_ref, w_ref, even_ref, odd_ref, out_ref, o_ref, sems):
     chips, total = o_ref.shape[:2]
     taps = w_ref.shape[0]
     rows = even_ref.shape[0]
     nr = (total - taps) // 2
     pick = halo_pick(p_ref[0])
     zero = jnp.zeros(w_ref.shape[1:], w_ref.dtype)
+    copies = [pltpu.make_async_copy(o_ref.at[q], out_ref.at[q], sems.at[q]) for q in range(chips)]
     for q in range(chips):
         for t in range(taps):
             o_ref[q, t] = w_ref[t]
@@ -84,6 +92,9 @@
             for r in range(nr):
                 h = q * (nr - 2) + r - 1
                 o_ref[q, taps + p * nr + r] = pick(p, even_ref[h], odd_ref[h]) if 0 <= h < rows else zero
+        copies[q].start()
+    for copy in copies:
+        copy.wait()
 
 
 def shifted(value):
@@ -272,7 +283,7 @@
         lax.ppermute(lax.dynamic_slice(grad_out, (side, 0, 0, 0), (1, rows, cg, w))[0], SPACE, pair)
         for side, pair in zip(sides, pairs)
     ]
-    (packed,) = call(pack_kernel, [pltpu.VMEM((n, 2, nz, nr, cg, w), BF)], [activations, grad_out])
+    (packed,) = call(pack_kernel, [sds((n, 2, nz, nr, cg, w), BF)], [activations, grad_out], copied=n)
     own = swap_all(packed, FILT)
     x_halos = [
         lax.ppermute(
@@ -284,7 +295,13 @@
 
     flat_w = weight.transpose(0, 1, 2, 4, 3).reshape(27, cg, ch)
     span = rows // chips + 2
-    (more,) = call(pack_more_kernel, [sds((chips, 27 + 2 * span, cg, ch), BF)], [index, flat_w, *map(near_core, g_halos)], smem=1)
+    (more,) = call(
+        pack_more_kernel,
+        [sds((chips, 27 + 2 * span, cg, ch), BF)],
+        [index, flat_w, *map(near_core, g_halos)],
+        smem=1,
+        copied=chips,
+    )
     mine = swap_all(more, CHIPS)
     other = lax.ppermute(mine, "core", swap)
 
@@ -309,14 +326,12 @@
         smem=1,
         flops=4 * 27 * ch * ch * nz * nh * w,
     )
-    near = (
-        near[0],
-        lax.ppermute(near[1], "core", swap),
-        lax.ppermute(near[2], "zl", swap),
-        lax.ppermute(near[3], ("zl", "core"), [(i, 3 - i) for i in range(4)]),
-    )
+    both = lax.ppermute(near[3], ("zl", "core"), [(i, 3 - i) for i in range(4)])
+    across = lax.ppermute(near[2], "zl", swap)
+
     shares = swap_all(padded, SPACE)
-    _, near = lax.optimization_barrier((padded, near))
+    beside = lax.ppermute(near[1], "core", swap)
+    _, near = lax.optimization_barrier((padded, (near[0], beside, across, both)))
     (tap,) = call(functools.partial(space_add_kernel, norm=norm), [pltpu.VMEM((ns, cg, ch), F32)], [near_core(shares)])
     taps = swap_all(tap, SPACE)
     blocks = {j: jnp.stack([part[j] for part in near]) for j in range(4)}

time: 118 us -> 118 us (level)
  no operation moved by 1% of the time
where the time goes in v11:
time: 118 us; the launch traced here: 117 us
  starting transfers between devices  76.3 us (65%)
  waiting for transfers between devices  28.2 us (24%)
  Pallas kernels  10.1 us (9%)
    all_to_all x5, starting transfers between devices, swap_all(): return lax.all_to_all(array, axes, 0, 0, tiled=True)  33 us
    ppermute x2, starting transfers between devices, step(): lax.ppermute(lax.dynamic_slice(grad_out, (side, 0, 0, 0), (1, rows, cg, w...  12.5 us
    ppermute x3, starting transfers between devices, step(): blocks[j] = lax.ppermute(blocks[j], 'x', [(i, i ^ j) for i in range(4)])  12 us
    pallas_call x7, Pallas kernels, call(): pl.pallas_call(kernel, out_shape=outs[0] if one else tuple(outs), in_spec...  10.1 us
    all_to_all x5, waiting for transfers between devices, swap_all(): return lax.all_to_all(array, axes, 0, 0, tiled=True)  8.57 us
    ppermute x2, starting transfers between devices, step(): lax.ppermute(lax.dynamic_slice(own, (0, 0, side, 0, 0, 0), (n, 1, 1, nr,...  7.17 us
    ppermute x2, waiting for transfers between devices, step(): lax.ppermute(lax.dynamic_slice(grad_out, (side, 0, 0, 0), (1, rows, cg, w...  5.87 us
    ppermute x3, waiting for transfers between devices, step(): blocks[j] = lax.ppermute(blocks[j], 'x', [(i, i ^ j) for i in range(4)])  4.95 us
  transfers between devices with their start and end apart: 17, of which 8 were waited for; matrix products, arithmetic and copies ran while one was open for 1% of the time, Pallas kernels for 7%

profile of v11, /device:TPU:8, one launch (start us, length us, event | category | flops | bytes accessed | tf_op | source)
XLA Modules:
  0.0 117.4 jit_solution(12340436693428094908)
XLA Ops:
  0.6 1.9 %shard_map.58 = bf16[16,2,2,4,8,128]{5,4,3,2,1,0:T(8,128)(2,1)} custom-call(bf16[2,32,8,128]{3,2,1,0:T(8,128)(2,1)} %x_ref.1, bf16[2,32,8,128]{3,2,1,0:T(8,128)(2,1)} %g_ref.1), custom_call_target="tpu_custom_call" | custom-call | bytes 1310720 | tf_op jit(solution)/shard_map/pallas_call | solution.py:31
  2.6 6.4 %all-to-all-start = ((bf16[16,2,2,4,8,128]{5,4,3,2,1,0:T(8,128)(2,1)}), bf16[16,2,2,4,8,128]{5,4,3,2,1,0:T(8,128)(2,1)S(1)}, u32[]{:S(2)}, u32[]{:S(2)}) async-start(bf16[16,2,2,4,8,128]{5,4,3,2,1,0:T(8,128)(2,1)} %shard_map.58), calls=%async_computation | async-start | bytes 1048576 | tf_op jit(solution)/shard_map/all_to_all | solution.py:263
  9.0 9.9 %collective-permute-start.4 = (bf16[32,8,128]{2,1,0:T(8,128)(2,1)S(1)}, bf16[32,8,128]{2,1,0:T(8,128)(2,1)S(1)}, u32[]{:S(2)}, u32[]{:S(2)}) collective-permute-start(bf16[32,8,128]{2,1,0:T(8,128)(2,1)S(1)} %get-tuple-element.45), channel_id=1, source_target_pairs={{16,32},{48,64},{80,96},{112,128},{144,160},{176,192},{208,224},{2... | collective-permute-start | bytes 196616 | tf_op jit(solution)/shard_map/ppermute | solution.py:283
  18.9 2.6 %collective-permute-start.3 = (bf16[32,8,128]{2,1,0:T(8,128)(2,1)S(1)}, bf16[32,8,128]{2,1,0:T(8,128)(2,1)S(1)}, u32[]{:S(2)}, u32[]{:S(2)}) collective-permute-start(bf16[32,8,128]{2,1,0:T(8,128)(2,1)S(1)} %get-tuple-element.46), channel_id=1, source_target_pairs={{0,16},{32,48},{64,80},{96,112},{128,144},{160,176},{192,208},{224... | collective-permute-start | bytes 196616 | tf_op jit(solution)/shard_map/ppermute | solution.py:283
  21.5 1.3 %collective-permute-done.4.odd_ref = bf16[32,8,128]{2,1,0:T(8,128)(2,1)S(1)} collective-permute-done((bf16[32,8,128]{2,1,0:T(8,128)(2,1)S(1)}, bf16[32,8,128]{2,1,0:T(8,128)(2,1)S(1)}, u32[]{:S(2)}, u32[]{:S(2)}) %collective-permute-start.4) | collective-permute-done | bytes 65568 | tf_op jit(solution)/shard_map/ppermute | solution.py:283
  22.9 4.5 %collective-permute-done.3.even_ref = bf16[32,8,128]{2,1,0:T(8,128)(2,1)S(1)} collective-permute-done((bf16[32,8,128]{2,1,0:T(8,128)(2,1)S(1)}, bf16[32,8,128]{2,1,0:T(8,128)(2,1)S(1)}, u32[]{:S(2)}, u32[]{:S(2)}) %collective-permute-start.3) | collective-permute-done | bytes 65568 | tf_op jit(solution)/shard_map/ppermute | solution.py:283
  27.4 1.8 %shard_map.61 = bf16[8,39,8,128]{3,2,1,0:T(8,128)(2,1)} custom-call(s32[1]{0:T(128)} %bitcast.p_ref, bf16[27,8,128]{2,1,0:T(8,128)(2,1)} %bitcast.16, bf16[32,8,128]{2,1,0:T(8,128)(2,1)S(1)} %collective-permute-done.3.even_ref, bf16[32,8,128]{2,1,0:T(8,128)(2,1)S(1)} %collective-permute-done.4.odd_ref), custom_call_target="tpu_custom_call" | custom-call | bytes 1464324 | tf_op jit(solution)/shard_map/pallas_call | solution.py:31
  29.2 4.5 %all-to-all-start.2 = ((bf16[8,39,8,128]{3,2,1,0:T(8,128)(2,1)}), bf16[8,39,8,128]{3,2,1,0:T(8,128)(2,1)S(1)}, u32[]{:S(2)}, u32[]{:S(2)}) async-start(bf16[8,39,8,128]{3,2,1,0:T(8,128)(2,1)} %shard_map.61), calls=%async_computation.2 | async-start | bytes 1277952 | tf_op jit(solution)/shard_map/all_to_all | solution.py:263
  33.7 2.9 %collective-permute-start.1 = (bf16[16,4,8,128]{3,2,1,0:T(8,128)(2,1)S(1)}, bf16[16,4,8,128]{3,2,1,0:T(8,128)(2,1)S(1)}, u32[]{:S(2)}, u32[]{:S(2)}) collective-permute-start(bf16[16,4,8,128]{3,2,1,0:T(8,128)(2,1)S(1)} %get-tuple-element.27), channel_id=1, source_target_pairs={{16,32},{48,64},{80,96},{112,128},{144,160},{176,192},{208,224},{2... | collective-permute-start | bytes 393224 | tf_op jit(solution)/shard_map/ppermute | solution.py:289
  36.6 4.3 %collective-permute-start = (bf16[16,4,8,128]{3,2,1,0:T(8,128)(2,1)S(1)}, bf16[16,4,8,128]{3,2,1,0:T(8,128)(2,1)S(1)}, u32[]{:S(2)}, u32[]{:S(2)}) collective-permute-start(bf16[16,4,8,128]{3,2,1,0:T(8,128)(2,1)S(1)} %get-tuple-element.28), channel_id=1, source_target_pairs={{0,16},{32,48},{64,80},{96,112},{128,144},{160,176},{192,208},{224... | collective-permute-start | bytes 393224 | tf_op jit(solution)/shard_map/ppermute | solution.py:289
  40.9 3.7 %collective-permute-done.1.odd_ref = bf16[16,4,8,128]{3,2,1,0:T(8,128)(2,1)S(1)} collective-permute-done((bf16[16,4,8,128]{3,2,1,0:T(8,128)(2,1)S(1)}, bf16[16,4,8,128]{3,2,1,0:T(8,128)(2,1)S(1)}, u32[]{:S(2)}, u32[]{:S(2)}) %collective-permute-start.1) | collective-permute-done | bytes 131104 | tf_op jit(solution)/shard_map/ppermute | solution.py:289
  45.1 1.3 %shard_map.59 = (f32[8,27,8,128]{3,2,1,0:T(8,128)S(1)}, f32[8,27,8,128]{3,2,1,0:T(8,128)S(1)}) custom-call(s32[1]{0:T(128)} %bitcast.p_ref, bf16[16,2,2,4,8,128]{5,4,3,2,1,0:T(8,128)(2,1)S(1)} %all-to-all-done.own_ref, bf16[16,4,8,128]{3,2,1,0:T(8,128)(2,1)S(1)} %collective-permute-done.even_ref, bf16[16,4,8,128]{3,2,1,0:T(8,128)(2,1)S(1)} %collective-permute-done.1.odd_ref), custom_call_target="tpu_custom_call" | custom-call | flops 452984832 | bytes 2555908 | tf_op jit(solution)/shard_map/pallas_call | solution.py:31
  46.4 1.9 %collective-permute-start.2 = (f32[8,27,8,128]{3,2,1,0:T(8,128)S(1)}, f32[8,27,8,128]{3,2,1,0:T(8,128)S(1)}, u32[]{:S(2)}, u32[]{:S(2)}) collective-permute-start(f32[8,27,8,128]{3,2,1,0:T(8,128)S(1)} %get-tuple-element.16), channel_id=1, source_target_pairs={{0,1},{1,0},{2,3},{3,2},{4,5},{5,4},{6,7},{7,6},{8,9},{9,8},{10,11... | collective-permute-start | bytes 2654216 | tf_op jit(solution)/shard_map/ppermute | solution.py:316
  48.3 2.4 %collective-permute-done.2 = f32[8,27,8,128]{3,2,1,0:T(8,128)S(1)} collective-permute-done((f32[8,27,8,128]{3,2,1,0:T(8,128)S(1)}, f32[8,27,8,128]{3,2,1,0:T(8,128)S(1)}, u32[]{:S(2)}, u32[]{:S(2)}) %collective-permute-start.2) | collective-permute-done | bytes 884768 | tf_op jit(solution)/shard_map/ppermute | solution.py:316
  50.7 1.0 add.34
  51.7 8.2 %all-to-all-start.1 = ((f32[8,27,8,128]{3,2,1,0:T(8,128)}), f32[8,27,8,128]{3,2,1,0:T(8,128)S(1)}, u32[]{:S(2)}, u32[]{:S(2)}) async-start(f32[8,27,8,128]{3,2,1,0:T(8,128)} %add.34), calls=%async_computation.1 | async-start | bytes 1769472 | tf_op jit(solution)/shard_map/all_to_all | solution.py:263
  60.0 1.9 %collective-permute-start.5 = (bf16[8,39,8,128]{3,2,1,0:T(8,128)(2,1)S(1)}, bf16[8,39,8,128]{3,2,1,0:T(8,128)(2,1)}, u32[]{:S(2)}, u32[]{:S(2)}) collective-permute-start(bf16[8,39,8,128]{3,2,1,0:T(8,128)(2,1)S(1)} %all-to-all-done.2.mine_ref), channel_id=1, source_target_pairs={{0,1},{1,0},{2,3},{3,2},{4,5},{5,4},{6,7},{7,6},{8,9},{9,8},{10,11... | collective-permute-start | bytes 1916936 | tf_op jit(solution)/shard_map/ppermute | solution.py:306
  61.9 2.2 %collective-permute-done.5.other_ref = bf16[8,39,8,128]{3,2,1,0:T(8,128)(2,1)} collective-permute-done((bf16[8,39,8,128]{3,2,1,0:T(8,128)(2,1)S(1)}, bf16[8,39,8,128]{3,2,1,0:T(8,128)(2,1)}, u32[]{:S(2)}, u32[]{:S(2)}) %collective-permute-start.5) | collective-permute-done | bytes 639008 | tf_op jit(solution)/shard_map/ppermute | solution.py:306
  64.1 2.9 %shard_map.62 = (f32[4,2,2,2,8,128]{5,4,3,2,1,0:T(8,128)S(1)}, f32[4,2,2,2,8,128]{5,4,3,2,1,0:T(8,128)S(1)}, f32[4,2,2,2,8,128]{5,4,3,2,1,0:T(8,128)S(1)}, f32[4,2,2,2,8,128]{5,4,3,2,1,0:T(8,128)S(1)}) custom-call(s32[1]{0:T(128)} %bitcast.p_ref, bf16[16,2,2,4,8,128]{5,4,3,2,1,0:T(8,128)(2,1)S(1)} %all-to-all-done.own_ref, ...), custom_call_target="tpu_custom_call" | custom-call | flops 905969664 | bytes 2588676 | tf_op jit(solution)/shard_map/pallas_call | solution.py:31
  67.0 2.0 %collective-permute-start.6 = (f32[4,2,2,2,8,128]{5,4,3,2,1,0:T(8,128)S(1)}, f32[4,2,2,2,8,128]{5,4,3,2,1,0:T(8,128)S(1)}, u32[]{:S(2)}, u32[]{:S(2)}) collective-permute-start(f32[4,2,2,2,8,128]{5,4,3,2,1,0:T(8,128)S(1)} %get-tuple-element.18), channel_id=1, source_target_pairs={{0,1},{1,0},{2,3},{3,2},{4,5},{5,4},{6,7},{7,6},{8,9},{9,8},{10,11... | collective-permute-start | bytes 393224 | tf_op jit(solution)/shard_map/ppermute | solution.py:333
  69.0 3.9 %collective-permute-start.7 = (f32[4,2,2,2,8,128]{5,4,3,2,1,0:T(8,128)S(1)}, f32[4,2,2,2,8,128]{5,4,3,2,1,0:T(8,128)S(1)}, u32[]{:S(2)}, u32[]{:S(2)}) collective-permute-start(f32[4,2,2,2,8,128]{5,4,3,2,1,0:T(8,128)S(1)} %get-tuple-element.19), channel_id=1, source_target_pairs={{0,8},{8,0},{1,9},{9,1},{2,10},{10,2},{3,11},{11,3},{4,12},{12,4},... | collective-permute-start | bytes 393224 | tf_op jit(solution)/shard_map/ppermute | solution.py:330
  73.0 1.9 %collective-permute-start.8 = (f32[4,2,2,2,8,128]{5,4,3,2,1,0:T(8,128)S(1)}, f32[4,2,2,2,8,128]{5,4,3,2,1,0:T(8,128)S(1)}, u32[]{:S(2)}, u32[]{:S(2)}) collective-permute-start(f32[4,2,2,2,8,128]{5,4,3,2,1,0:T(8,128)S(1)} %get-tuple-element.20), channel_id=1, source_target_pairs={{0,9},{1,8},{8,1},{9,0},{2,11},{3,10},{10,3},{11,2},{4,13},{5,12},... | collective-permute-start | bytes 393224 | tf_op jit(solution)/shard_map/ppermute | solution.py:329
  74.9 0.7 shard_map.60
  75.6 9.8 %all-to-all-start.3 = ((f32[32,8,128]{2,1,0:T(8,128)}), f32[32,8,128]{2,1,0:T(8,128)S(1)}, u32[]{:S(2)}, u32[]{:S(2)}) async-start(f32[32,8,128]{2,1,0:T(8,128)} %shard_map.60), calls=%async_computation.3 | async-start | bytes 262144 | tf_op jit(solution)/shard_map/all_to_all | solution.py:263
  85.5 3.6 %collective-permute-start.9 = (f32[4,2,2,2,8,128]{5,4,3,2,1,0:T(8,128)S(1)}, f32[4,2,2,2,8,128]{5,4,3,2,1,0:T(8,128)S(1)}, u32[]{:S(2)}, u32[]{:S(2)}) collective-permute-start(f32[4,2,2,2,8,128]{5,4,3,2,1,0:T(8,128)S(1)} %pad_maximum_fusion.1), channel_id=1, source_target_pairs={{0,2},{2,0},{4,6},{6,4},{1,3},{3,1},{5,7},{7,5},{8,10},{10,8},{12,... | collective-permute-start | bytes 393224 | tf_op jit(solution)/shard_map/ppermute | solution.py:339
  89.2 8.6 %all-to-all-done.3.shares_ref = f32[32,8,128]{2,1,0:T(8,128)S(1)} async-done(((f32[32,8,128]{2,1,0:T(8,128)}), f32[32,8,128]{2,1,0:T(8,128)S(1)}, u32[]{:S(2)}, u32[]{:S(2)}) %all-to-all-start.3) | async-done | bytes 131104 | tf_op jit(solution)/shard_map/all_to_all | solution.py:263
  97.7 0.7 shard_map.64
  98.4 4.1 %all-to-all-start.4 = ((f32[32,8,128]{2,1,0:T(8,128)}), f32[32,8,128]{2,1,0:T(8,128)S(1)}, u32[]{:S(2)}, u32[]{:S(2)}) async-start(f32[32,8,128]{2,1,0:T(8,128)} %shard_map.64), calls=%async_computation.4 | async-start | bytes 262144 | tf_op jit(solution)/shard_map/all_to_all | solution.py:263
  102.5 5.3 %collective-permute-start.10 = (f32[4,2,2,2,8,128]{5,4,3,2,1,0:T(8,128)S(1)}, f32[4,2,2,2,8,128]{5,4,3,2,1,0:T(8,128)S(1)}, u32[]{:S(2)}, u32[]{:S(2)}) collective-permute-start(f32[4,2,2,2,8,128]{5,4,3,2,1,0:T(8,128)S(1)} %pad_maximum_fusion.2), channel_id=1, source_target_pairs={{0,4},{2,6},{4,0},{6,2},{1,5},{3,7},{5,1},{7,3},{8,12},{10,14},{12... | collective-permute-start | bytes 393224 | tf_op jit(solution)/shard_map/ppermute | solution.py:339
  107.8 3.1 %collective-permute-start.11 = (f32[4,2,2,2,8,128]{5,4,3,2,1,0:T(8,128)S(1)}, f32[4,2,2,2,8,128]{5,4,3,2,1,0:T(8,128)S(1)}, u32[]{:S(2)}, u32[]{:S(2)}) collective-permute-start(f32[4,2,2,2,8,128]{5,4,3,2,1,0:T(8,128)S(1)} %pad_maximum_fusion.3), channel_id=1, source_target_pairs={{0,6},{2,4},{4,2},{6,0},{1,7},{3,5},{5,3},{7,1},{8,14},{10,12},{12... | collective-permute-start | bytes 393224 | tf_op jit(solution)/shard_map/ppermute | solution.py:339
  110.9 4.9 %collective-permute-done.11.refs_3_ = f32[4,2,2,2,8,128]{5,4,3,2,1,0:T(8,128)S(1)} collective-permute-done((f32[4,2,2,2,8,128]{5,4,3,2,1,0:T(8,128)S(1)}, f32[4,2,2,2,8,128]{5,4,3,2,1,0:T(8,128)S(1)}, u32[]{:S(2)}, u32[]{:S(2)}) %collective-permute-start.11) | collective-permute-done | bytes 131104 | tf_op jit(solution)/shard_map/ppermute | solution.py:339
  115.9 0.8 shard_map.63
  (23 shorter events, 1.3 us)
Async XLA Ops:
  2.6 6.4 %copy-start.1 = (bf16[2,32,8,128]{3,2,1,0:T(8,128)(2,1)S(1)}, bf16[2,32,8,128]{3,2,1,0:T(8,128)(2,1)}, u32[]{:S(2)}) copy-start(bf16[2,32,8,128]{3,2,1,0:T(8,128)(2,1)} %g_ref.1) | copy-start | bytes 393220
  2.6 26.6 %all-to-all-start = ((bf16[16,2,2,4,8,128]{5,4,3,2,1,0:T(8,128)(2,1)}), bf16[16,2,2,4,8,128]{5,4,3,2,1,0:T(8,128)(2,1)S(1)}, u32[]{:S(2)}, u32[]{:S(2)}) async-start(bf16[16,2,2,4,8,128]{5,4,3,2,1,0:T(8,128)(2,1)} %shard_map.58), calls=%async_computation | async-start | bytes 1048576 | tf_op jit(solution)/shard_map/all_to_all | solution.py:263
  9.0 13.9 %collective-permute-start.4 = (bf16[32,8,128]{2,1,0:T(8,128)(2,1)S(1)}, bf16[32,8,128]{2,1,0:T(8,128)(2,1)S(1)}, u32[]{:S(2)}, u32[]{:S(2)}) collective-permute-start(bf16[32,8,128]{2,1,0:T(8,128)(2,1)S(1)} %get-tuple-element.45), channel_id=1, source_target_pairs={{16,32},{48,64},{80,96},{112,128},{144,160},{176,192},{208,224},{2... | collective-permute-start | bytes 196616 | tf_op jit(solution)/shard_map/ppermute | solution.py:283
  18.9 8.5 %collective-permute-start.3 = (bf16[32,8,128]{2,1,0:T(8,128)(2,1)S(1)}, bf16[32,8,128]{2,1,0:T(8,128)(2,1)S(1)}, u32[]{:S(2)}, u32[]{:S(2)}) collective-permute-start(bf16[32,8,128]{2,1,0:T(8,128)(2,1)S(1)} %get-tuple-element.46), channel_id=1, source_target_pairs={{0,16},{32,48},{64,80},{96,112},{128,144},{160,176},{192,208},{224... | collective-permute-start | bytes 196616 | tf_op jit(solution)/shard_map/ppermute | solution.py:283
  29.2 22.6 %all-to-all-start.2 = ((bf16[8,39,8,128]{3,2,1,0:T(8,128)(2,1)}), bf16[8,39,8,128]{3,2,1,0:T(8,128)(2,1)S(1)}, u32[]{:S(2)}, u32[]{:S(2)}) async-start(bf16[8,39,8,128]{3,2,1,0:T(8,128)(2,1)} %shard_map.61), calls=%async_computation.2 | async-start | bytes 1277952 | tf_op jit(solution)/shard_map/all_to_all | solution.py:263
  33.7 10.9 %collective-permute-start.1 = (bf16[16,4,8,128]{3,2,1,0:T(8,128)(2,1)S(1)}, bf16[16,4,8,128]{3,2,1,0:T(8,128)(2,1)S(1)}, u32[]{:S(2)}, u32[]{:S(2)}) collective-permute-start(bf16[16,4,8,128]{3,2,1,0:T(8,128)(2,1)S(1)} %get-tuple-element.27), channel_id=1, source_target_pairs={{16,32},{48,64},{80,96},{112,128},{144,160},{176,192},{208,224},{2... | collective-permute-start | bytes 393224 | tf_op jit(solution)/shard_map/ppermute | solution.py:289
  36.6 8.5 %collective-permute-start = (bf16[16,4,8,128]{3,2,1,0:T(8,128)(2,1)S(1)}, bf16[16,4,8,128]{3,2,1,0:T(8,128)(2,1)S(1)}, u32[]{:S(2)}, u32[]{:S(2)}) collective-permute-start(bf16[16,4,8,128]{3,2,1,0:T(8,128)(2,1)S(1)} %get-tuple-element.28), channel_id=1, source_target_pairs={{0,16},{32,48},{64,80},{96,112},{128,144},{160,176},{192,208},{224... | collective-permute-start | bytes 393224 | tf_op jit(solution)/shard_map/ppermute | solution.py:289
  46.4 4.3 %collective-permute-start.2 = (f32[8,27,8,128]{3,2,1,0:T(8,128)S(1)}, f32[8,27,8,128]{3,2,1,0:T(8,128)S(1)}, u32[]{:S(2)}, u32[]{:S(2)}) collective-permute-start(f32[8,27,8,128]{3,2,1,0:T(8,128)S(1)} %get-tuple-element.16), channel_id=1, source_target_pairs={{0,1},{1,0},{2,3},{3,2},{4,5},{5,4},{6,7},{7,6},{8,9},{9,8},{10,11... | collective-permute-start | bytes 2654216 | tf_op jit(solution)/shard_map/ppermute | solution.py:316
  51.7 8.2 %copy-start = (bf16[8,39,8,128]{3,2,1,0:T(8,128)(2,1)}, bf16[8,39,8,128]{3,2,1,0:T(8,128)(2,1)S(1)}, u32[]{:S(2)}) copy-start(bf16[8,39,8,128]{3,2,1,0:T(8,128)(2,1)S(1)} %all-to-all-done.2.mine_ref) | copy-start | bytes 1916932
  51.7 23.1 %all-to-all-start.1 = ((f32[8,27,8,128]{3,2,1,0:T(8,128)}), f32[8,27,8,128]{3,2,1,0:T(8,128)S(1)}, u32[]{:S(2)}, u32[]{:S(2)}) async-start(f32[8,27,8,128]{3,2,1,0:T(8,128)} %add.34), calls=%async_computation.1 | async-start | bytes 1769472 | tf_op jit(solution)/shard_map/all_to_all | solution.py:263
  60.0 4.1 %collective-permute-start.5 = (bf16[8,39,8,128]{3,2,1,0:T(8,128)(2,1)S(1)}, bf16[8,39,8,128]{3,2,1,0:T(8,128)(2,1)}, u32[]{:S(2)}, u32[]{:S(2)}) collective-permute-start(bf16[8,39,8,128]{3,2,1,0:T(8,128)(2,1)S(1)} %all-to-all-done.2.mine_ref), channel_id=1, source_target_pairs={{0,1},{1,0},{2,3},{3,2},{4,5},{5,4},{6,7},{7,6},{8,9},{9,8},{10,11... | collective-permute-start | bytes 1916936 | tf_op jit(solution)/shard_map/ppermute | solution.py:306
  67.0 18.5 %collective-permute-start.6 = (f32[4,2,2,2,8,128]{5,4,3,2,1,0:T(8,128)S(1)}, f32[4,2,2,2,8,128]{5,4,3,2,1,0:T(8,128)S(1)}, u32[]{:S(2)}, u32[]{:S(2)}) collective-permute-start(f32[4,2,2,2,8,128]{5,4,3,2,1,0:T(8,128)S(1)} %get-tuple-element.18), channel_id=1, source_target_pairs={{0,1},{1,0},{2,3},{3,2},{4,5},{5,4},{6,7},{7,6},{8,9},{9,8},{10,11... | collective-permute-start | bytes 393224 | tf_op jit(solution)/shard_map/ppermute | solution.py:333
  69.0 16.4 %collective-permute-start.7 = (f32[4,2,2,2,8,128]{5,4,3,2,1,0:T(8,128)S(1)}, f32[4,2,2,2,8,128]{5,4,3,2,1,0:T(8,128)S(1)}, u32[]{:S(2)}, u32[]{:S(2)}) collective-permute-start(f32[4,2,2,2,8,128]{5,4,3,2,1,0:T(8,128)S(1)} %get-tuple-element.19), channel_id=1, source_target_pairs={{0,8},{8,0},{1,9},{9,1},{2,10},{10,2},{3,11},{11,3},{4,12},{12,4},... | collective-permute-start | bytes 393224 | tf_op jit(solution)/shard_map/ppermute | solution.py:330
  73.0 12.5 %collective-permute-start.8 = (f32[4,2,2,2,8,128]{5,4,3,2,1,0:T(8,128)S(1)}, f32[4,2,2,2,8,128]{5,4,3,2,1,0:T(8,128)S(1)}, u32[]{:S(2)}, u32[]{:S(2)}) collective-permute-start(f32[4,2,2,2,8,128]{5,4,3,2,1,0:T(8,128)S(1)} %get-tuple-element.20), channel_id=1, source_target_pairs={{0,9},{1,8},{8,1},{9,0},{2,11},{3,10},{10,3},{11,2},{4,13},{5,12},... | collective-permute-start | bytes 393224 | tf_op jit(solution)/shard_map/ppermute | solution.py:329
  75.6 22.1 %all-to-all-start.3 = ((f32[32,8,128]{2,1,0:T(8,128)}), f32[32,8,128]{2,1,0:T(8,128)S(1)}, u32[]{:S(2)}, u32[]{:S(2)}) async-start(f32[32,8,128]{2,1,0:T(8,128)} %shard_map.60), calls=%async_computation.3 | async-start | bytes 262144 | tf_op jit(solution)/shard_map/all_to_all | solution.py:263
  85.5 25.4 %collective-permute-start.9 = (f32[4,2,2,2,8,128]{5,4,3,2,1,0:T(8,128)S(1)}, f32[4,2,2,2,8,128]{5,4,3,2,1,0:T(8,128)S(1)}, u32[]{:S(2)}, u32[]{:S(2)}) collective-permute-start(f32[4,2,2,2,8,128]{5,4,3,2,1,0:T(8,128)S(1)} %pad_maximum_fusion.1), channel_id=1, source_target_pairs={{0,2},{2,0},{4,6},{6,4},{1,3},{3,1},{5,7},{7,5},{8,10},{10,8},{12,... | collective-permute-start | bytes 393224 | tf_op jit(solution)/shard_map/ppermute | solution.py:339
  98.4 18.3 %all-to-all-start.4 = ((f32[32,8,128]{2,1,0:T(8,128)}), f32[32,8,128]{2,1,0:T(8,128)S(1)}, u32[]{:S(2)}, u32[]{:S(2)}) async-start(f32[32,8,128]{2,1,0:T(8,128)} %shard_map.64), calls=%async_computation.4 | async-start | bytes 262144 | tf_op jit(solution)/shard_map/all_to_all | solution.py:263
  102.5 8.4 %collective-permute-start.10 = (f32[4,2,2,2,8,128]{5,4,3,2,1,0:T(8,128)S(1)}, f32[4,2,2,2,8,128]{5,4,3,2,1,0:T(8,128)S(1)}, u32[]{:S(2)}, u32[]{:S(2)}) collective-permute-start(f32[4,2,2,2,8,128]{5,4,3,2,1,0:T(8,128)S(1)} %pad_maximum_fusion.2), channel_id=1, source_target_pairs={{0,4},{2,6},{4,0},{6,2},{1,5},{3,7},{5,1},{7,3},{8,12},{10,14},{12... | collective-permute-start | bytes 393224 | tf_op jit(solution)/shard_map/ppermute | solution.py:339
  107.8 8.1 %collective-permute-start.11 = (f32[4,2,2,2,8,128]{5,4,3,2,1,0:T(8,128)S(1)}, f32[4,2,2,2,8,128]{5,4,3,2,1,0:T(8,128)S(1)}, u32[]{:S(2)}, u32[]{:S(2)}) collective-permute-start(f32[4,2,2,2,8,128]{5,4,3,2,1,0:T(8,128)S(1)} %pad_maximum_fusion.3), channel_id=1, source_target_pairs={{0,6},{2,4},{4,2},{6,0},{1,7},{3,5},{5,3},{7,1},{8,14},{10,12},{12... | collective-permute-start | bytes 393224 | tf_op jit(solution)/shard_map/ppermute | solution.py:339
